TPU v7x, 128 devices: a whole 4x4x4 slice. The times are simulated.
128 devices in a mesh: exp: 8 (over z, core), tile: 16 (over y, x).
Axes of the slice: x: 4, y: 4, z: 4, core: 2. Of those that a mesh axis runs over, the one named last changes fastest.
Arguments:
- exposure: bfloat16 [8, 4096, 4096], P('exp', 'tile'), may hold values from -6 to 6
- row_taps: bfloat16 [3, 21], replicated, may hold values from -1.25 to 1.25
- column_taps: bfloat16 [3, 21], replicated, may hold values from -1.25 to 1.25
- basis_coef: float32 [8, 3], P('exp'), may hold values from -2.5 to 2.5
- warp_rows: bfloat16 [64, 128, 128], replicated, may hold values from -0.3 to 1.2
- warp_columns: bfloat16 [64, 128, 128], replicated, may hold values from -0.3 to 1.2
- warp_id: int32 [8, 16, 64], replicated, may hold values from 0 to 63
- route_device: int32 [8, 16, 64], replicated, may hold values from 0 to 127, as said below
- route_slot: int32 [8, 16, 64], replicated, may hold values from 0 to 63
- weight: float32 [8, 16], replicated, may hold values from 0.3 to 3
Outputs:
- coadd_patch: float32 [8192, 16384], P('exp', 'tile')
- difference: float32 [8, 4096, 4096], P('exp', 'tile')
Inputs may be any that keep to these rules, and one draw needn't show every extreme that they name: `route_device`: the blocks of one device (its exposures of its tile, in order) name any one device at most 2 times, and some device is named exactly 2 times by the blocks of every device.
All inputs are finite; a program needn't handle non-finite values.
Results may differ from a plain program's by a relative error of at most 0.0058.
Values may be sent and summed in bfloat16 or wider, within the bound.
No kernel may reach another device: no remote copies, remote signals or barrier semaphores. Data moves between devices by JAX's collectives and lax.ppermute only.
A program may use at most 128 MiB of HBM per device.

v0:
```python
import functools

import jax
import jax.numpy as jnp
from jax import lax
from jax.experimental import pallas as pl
from jax.experimental.pallas import tpu as pltpu
from jax.sharding import PartitionSpec as P

BLOCK = 128
HALF = 10
RIM = 16
CHUNK = 256
SLOT_ROWS = 8
SLOT_COLS = 8
LANES = 4
VMEM_BYTES = 60 * 1024 * 1024
VMEM = pl.BlockSpec(memory_space=pltpu.VMEM)
SMEM = pl.BlockSpec(memory_space=pltpu.SMEM)


def band_matrices(tap_values, depth, width, start, axis):
    grid = (
        lax.broadcasted_iota(jnp.int32, (depth, width), 0)
        - lax.broadcasted_iota(jnp.int32, (depth, width), 1)
        - start
    )
    bands = []
    for taps in tap_values.astype(jnp.float32):
        band = jnp.zeros((depth, width), jnp.float32)
        for tap_index in range(tap_values.shape[1]):
            band = jnp.where(grid == tap_index, taps[tap_index], band)
        bands.append(band.T if axis == 0 else band)
    return jnp.stack(bands).astype(jnp.bfloat16)


def rims(block):
    count = lax.axis_size("tile")
    forward = [(i, i + 1) for i in range(count - 1)]
    backward = [(target, source) for source, target in forward]
    above = lax.ppermute(block[block.shape[0] - RIM :], "tile", forward)
    below = lax.ppermute(block[:RIM], "tile", backward)
    return above, below


def row_step(step, chunks, coef_ref, above_ref, image_ref, below_ref, rows_ref, pass_ref):
    tile_rows = image_ref.shape[0]
    live = (step < chunks).astype(jnp.float32)
    for part in range(tile_rows // BLOCK):
        low = part * BLOCK - RIM
        high = (part + 1) * BLOCK + RIM
        pieces = [image_ref[max(low, 0) : min(high, tile_rows), :]]
        if low < 0:
            pieces.insert(0, above_ref[...])
        if high > tile_rows:
            pieces.append(below_ref[...])
        window = jnp.concatenate(pieces, axis=0)
        summed = jnp.dot(rows_ref[...], window, preferred_element_type=jnp.float32)
        for base in range(pass_ref.shape[0]):
            pass_ref[base, part * BLOCK : (part + 1) * BLOCK, pl.ds(BLOCK + step * CHUNK, CHUNK)] = (
                (coef_ref[0, base] * live) * summed[base * BLOCK : (base + 1) * BLOCK]
            ).astype(jnp.bfloat16)


def column_step(chunk, columns_ref, pass_ref):
    window = pl.ds(pl.multiple_of(chunk * CHUNK, CHUNK), CHUNK + 2 * BLOCK)
    summed = jnp.dot(pass_ref[0, :, window], columns_ref[0], preferred_element_type=jnp.float32)
    for base in range(1, pass_ref.shape[0]):
        summed = summed + jnp.dot(
            pass_ref[base, :, window], columns_ref[base], preferred_element_type=jnp.float32
        )
    return summed


def forward_kernel(
    ident_ref,
    weight_ref,
    coef_ref,
    above_ref,
    image_ref,
    below_ref,
    rows_ref,
    columns_ref,
    warp_rows_ref,
    warp_columns_ref,
    out_ref,
    pass_ref,
    turned_ref,
    *,
    chunks,
):
    step = pl.program_id(0)
    parts = image_ref.shape[0] // BLOCK
    side = CHUNK // BLOCK
    per_tile = parts * chunks * side

    @pl.when(step == 0)
    def _():
        pass_ref[:, :, :BLOCK] = jnp.zeros((pass_ref.shape[0], pass_ref.shape[1], BLOCK), jnp.bfloat16)

    chunk = jnp.maximum(step - 2, 0)
    matched = column_step(chunk, columns_ref, pass_ref).astype(jnp.bfloat16)
    for part in range(parts):
        for inner in range(side):
            index = part * (chunks * side) + chunk * side + inner
            ident = ident_ref[0, index]
            piece = matched[part * BLOCK : (part + 1) * BLOCK, inner * BLOCK : (inner + 1) * BLOCK]
            first = jnp.dot(
                warp_rows_ref[ident], piece, preferred_element_type=jnp.float32
            ).astype(jnp.bfloat16)
            second = lax.dot_general(
                first,
                warp_columns_ref[ident],
                (((1,), (1,)), ((), ())),
                preferred_element_type=jnp.float32,
            )
            turned_ref[pl.ds(index, BLOCK, stride=per_tile), :] = weight_ref[0, 0] * second
    row_step(step, chunks, coef_ref, above_ref, image_ref, below_ref, rows_ref, pass_ref)

    @pl.when(step == chunks + 1)
    def _():
        @pl.loop(0, BLOCK)
        def _(row):
            at = pl.ds(pl.multiple_of(row * per_tile, per_tile), per_tile)
            out_ref[at, :] = turned_ref[at, :].astype(jnp.bfloat16)


def forward(ident, weight, coef, above, image, below, rows, columns, warp_rows, warp_columns):
    tile_rows, width = image.shape
    chunks = width // CHUNK
    bases = columns.shape[0]
    items = tile_rows * width // BLOCK

    def at_column(step):
        return (0, jnp.minimum(step, chunks - 1))

    return pl.pallas_call(
        functools.partial(forward_kernel, chunks=chunks),
        out_shape=jax.ShapeDtypeStruct((items, BLOCK), jnp.bfloat16),
        grid=(chunks + 2,),
        in_specs=[
            SMEM,
            SMEM,
            SMEM,
            pl.BlockSpec((RIM, CHUNK), at_column),
            pl.BlockSpec((tile_rows, CHUNK), at_column),
            pl.BlockSpec((RIM, CHUNK), at_column),
            VMEM,
            VMEM,
            VMEM,
            VMEM,
        ],
        out_specs=pl.BlockSpec((items, BLOCK), lambda step: (0, 0)),
        scratch_shapes=[
            pltpu.VMEM((bases, tile_rows, BLOCK + (chunks + 2) * CHUNK), jnp.bfloat16),
            pltpu.VMEM((items, BLOCK), jnp.float32),
        ],
        compiler_params=pltpu.CompilerParams(
            dimension_semantics=("arbitrary",), vmem_limit_bytes=VMEM_BYTES
        ),
        name="match_warp",
    )(ident, weight, coef, above, image, below, rows, columns, warp_rows, warp_columns)


def slots_kernel(slot_ref, arrived_ref, total_ref, template_ref, coadd_ref, wide_ref, *sums):
    sources, per_tile = slot_ref.shape

    @pl.loop(0, sources)
    def _(source):
        at = pl.ds(pl.multiple_of(source * per_tile, per_tile), per_tile)
        wide_ref[at, :] = arrived_ref[at, :].astype(jnp.float32)
        for sum_ref in sums:
            sum_ref[at, :] = jnp.zeros((per_tile, BLOCK), jnp.float32)

    @pl.loop(0, sources)
    def _(source):
        for first in range(0, per_tile, len(sums)):
            slots = [slot_ref[source, first + lane] for lane in range(len(sums))]
            values = [
                sum_ref[pl.ds(slot, 1), :] + wide_ref[pl.ds(source * per_tile + first + lane, 1), :]
                for lane, (slot, sum_ref) in enumerate(zip(slots, sums))
            ]
            for slot, sum_ref, value in zip(slots, sums, values):
                sum_ref[pl.ds(slot, 1), :] = value

    @pl.loop(0, sources)
    def _(source):
        at = pl.ds(pl.multiple_of(source * per_tile, per_tile), per_tile)
        numerator = sums[0][at, :]
        for sum_ref in sums[1:]:
            numerator = numerator + sum_ref[at, :]
        value = numerator / jnp.maximum(total_ref[at, :], 1.0)
        sums[0][at, :] = value
        coadd_ref[at, :] = value.astype(jnp.bfloat16)

    @pl.loop(0, sources)
    def _(source):
        for item in range(per_tile):
            slot = slot_ref[source, item]
            wide_ref[pl.ds(source * per_tile + item, 1), :] = sums[0][pl.ds(slot, 1), :]

    @pl.loop(0, sources)
    def _(source):
        at = pl.ds(pl.multiple_of(source * per_tile, per_tile), per_tile)
        template_ref[at, :] = wide_ref[at, :].astype(jnp.bfloat16)


def slot_values(slots, arrived, total):
    shape = jax.ShapeDtypeStruct(arrived.shape, jnp.bfloat16)
    wide = pltpu.VMEM(arrived.shape, jnp.float32)
    return pl.pallas_call(
        slots_kernel,
        out_shape=(shape, shape),
        in_specs=[SMEM, VMEM, VMEM],
        out_specs=(VMEM, VMEM),
        scratch_shapes=[wide] * (1 + LANES),
        compiler_params=pltpu.CompilerParams(vmem_limit_bytes=VMEM_BYTES),
        name="slot_values",
    )(slots, arrived, total)


def unwarp_kernel(ident_ref, returned_ref, warp_rows_ref, warp_columns_ref, out_ref, wide_ref):
    per_tile = ident_ref.shape[1]
    across = out_ref.shape[1] // BLOCK

    @pl.loop(0, BLOCK)
    def _(row):
        at = pl.ds(pl.multiple_of(row * per_tile, per_tile), per_tile)
        wide_ref[at, :] = returned_ref[at, :].astype(jnp.float32)

    parts = out_ref.shape[0] // BLOCK

    @pl.loop(0, across // 2)
    def _(pair):
        for part in range(parts):
            for inner in range(2):
                column = pair * 2 + inner
                index = part * across + column
                ident = ident_ref[0, index]
                template = wide_ref[pl.ds(index, BLOCK, stride=per_tile), :].astype(jnp.bfloat16)
                first = lax.dot_general(
                    warp_rows_ref[ident],
                    template,
                    (((0,), (0,)), ((), ())),
                    preferred_element_type=jnp.float32,
                ).astype(jnp.bfloat16)
                out_ref[
                    part * BLOCK : (part + 1) * BLOCK,
                    pl.ds(pl.multiple_of(column * BLOCK, BLOCK), BLOCK),
                ] = jnp.dot(
                    first, warp_columns_ref[ident], preferred_element_type=jnp.float32
                ).astype(jnp.bfloat16)


def unwarp(ident, returned, warp_rows, warp_columns, tile_rows, width):
    return pl.pallas_call(
        unwarp_kernel,
        out_shape=jax.ShapeDtypeStruct((tile_rows, width), jnp.bfloat16),
        in_specs=[SMEM, VMEM, VMEM, VMEM],
        out_specs=VMEM,
        scratch_shapes=[pltpu.VMEM(returned.shape, jnp.float32)],
        compiler_params=pltpu.CompilerParams(vmem_limit_bytes=VMEM_BYTES),
        name="unwarp",
    )(ident, returned, warp_rows, warp_columns)


def subtract_kernel(
    coef_ref,
    above_ref,
    image_ref,
    below_ref,
    exposure_ref,
    rows_ref,
    columns_ref,
    out_ref,
    pass_ref,
    *,
    chunks,
):
    step = pl.program_id(0)

    @pl.when(step == 0)
    def _():
        pass_ref[:, :, :BLOCK] = jnp.zeros((pass_ref.shape[0], pass_ref.shape[1], BLOCK), jnp.bfloat16)

    chunk = jnp.maximum(step - 2, 0)
    out_ref[...] = exposure_ref[...].astype(jnp.float32) - column_step(chunk, columns_ref, pass_ref)
    row_step(step, chunks, coef_ref, above_ref, image_ref, below_ref, rows_ref, pass_ref)


def subtract(coef, above, image, below, exposure, rows, columns):
    tile_rows, width = image.shape
    chunks = width // CHUNK
    bases = columns.shape[0]

    def at_column(step):
        return (0, jnp.minimum(step, chunks - 1))

    def behind(step):
        return (0, jnp.maximum(step - 2, 0))

    return pl.pallas_call(
        functools.partial(subtract_kernel, chunks=chunks),
        out_shape=jax.ShapeDtypeStruct((tile_rows, width), jnp.float32),
        grid=(chunks + 2,),
        in_specs=[
            SMEM,
            pl.BlockSpec((RIM, CHUNK), at_column),
            pl.BlockSpec((tile_rows, CHUNK), at_column),
            pl.BlockSpec((RIM, CHUNK), at_column),
            pl.BlockSpec((tile_rows, CHUNK), behind),
            VMEM,
            VMEM,
        ],
        out_specs=pl.BlockSpec((tile_rows, CHUNK), behind),
        scratch_shapes=[
            pltpu.VMEM((bases, tile_rows, BLOCK + (chunks + 2) * CHUNK), jnp.bfloat16)
        ],
        compiler_params=pltpu.CompilerParams(
            dimension_semantics=("arbitrary",), vmem_limit_bytes=VMEM_BYTES
        ),
        name="match_subtract",
    )(coef, above, image, below, exposure, rows, columns)


def patch_kernel(rows_ref, out_ref, wide_ref):
    slots = SLOT_ROWS * SLOT_COLS

    @pl.loop(0, BLOCK)
    def _(row):
        at = pl.ds(pl.multiple_of(row * slots, slots), slots)
        wide_ref[at, :] = rows_ref[at, :].astype(jnp.float32)

    @pl.loop(0, SLOT_ROWS)
    def _(down):
        for across in range(SLOT_COLS):
            out_ref[
                pl.ds(pl.multiple_of(down * BLOCK, BLOCK), BLOCK),
                across * BLOCK : (across + 1) * BLOCK,
            ] = wide_ref[pl.ds(down * SLOT_COLS + across, BLOCK, stride=slots), :]


def patch(rows):
    return pl.pallas_call(
        patch_kernel,
        out_shape=jax.ShapeDtypeStruct((SLOT_ROWS * BLOCK, SLOT_COLS * BLOCK), jnp.float32),
        in_specs=[VMEM],
        out_specs=VMEM,
        scratch_shapes=[pltpu.VMEM(rows.shape, jnp.float32)],
        compiler_params=pltpu.CompilerParams(vmem_limit_bytes=VMEM_BYTES),
        name="patch",
    )(rows)


def exchange(rows, devices):
    shaped = rows.reshape(devices, -1, BLOCK)
    moved = lax.all_to_all(shaped, ("exp", "tile"), split_axis=0, concat_axis=0, tiled=True)
    return moved.reshape(rows.shape)


def shards(
    exposure,
    row_taps,
    column_taps,
    basis_coef,
    warp_rows,
    warp_columns,
    warp_id,
    route_device,
    route_slot,
    weight,
):
    devices = lax.axis_size("exp") * lax.axis_size("tile")
    image = exposure[0]
    tile_rows, width = image.shape
    per_tile = tile_rows * width // (BLOCK * BLOCK)
    slot_count = SLOT_ROWS * SLOT_COLS
    myself = lax.axis_index("exp") * lax.axis_size("tile") + lax.axis_index("tile")

    bases = row_taps.shape[0]
    rows = band_matrices(row_taps, BLOCK + 2 * RIM, BLOCK, RIM - HALF, 0)
    rows = rows.reshape(bases * BLOCK, BLOCK + 2 * RIM)
    columns = band_matrices(column_taps, CHUNK + 2 * BLOCK, CHUNK, BLOCK - HALF, 1)
    my_ident = lax.dynamic_slice_in_dim(warp_id.reshape(devices, per_tile), myself, 1, 0)
    my_weight = lax.dynamic_slice_in_dim(weight.reshape(devices, 1), myself, 1, 0)

    above, below = rims(image)
    mine = forward(
        my_ident, my_weight, basis_coef, above, image, below, rows, columns, warp_rows, warp_columns
    )
    arrived = exchange(mine, devices)

    owner = route_device.reshape(-1)
    place = route_slot.reshape(-1)
    block_weight = jnp.repeat(weight.reshape(-1), per_tile)
    by_owner = jnp.where(
        owner[None, :] == jnp.arange(devices, dtype=jnp.int32)[:, None], block_weight[None, :], 0.0
    )
    by_place = (place[:, None] == jnp.arange(slot_count, dtype=jnp.int32)[None, :]).astype(
        jnp.float32
    )
    total = jnp.dot(by_owner, by_place, precision=lax.Precision.HIGHEST)
    total = jnp.broadcast_to(total.reshape(-1, 1), (devices * slot_count, BLOCK))
    slots = (route_device * slot_count + route_slot).reshape(devices, per_tile)

    template_rows, coadd_rows = slot_values(slots, arrived, total)
    returned = exchange(template_rows, devices)
    owned = exchange(coadd_rows, devices)

    template = unwarp(my_ident, returned, warp_rows, warp_columns, tile_rows, width)
    above, below = rims(template)
    difference = subtract(basis_coef, above, template, below, image, rows, columns)
    return patch(owned), difference[None]


def solution(mesh):
    placed = (P("exp", "tile", None), P(), P(), P("exp", None), P(), P(), P(), P(), P(), P())
    return jax.shard_map(
        shards,
        mesh=mesh,
        in_specs=placed,
        out_specs=(P("exp", "tile"), P("exp", "tile", None)),
        check_vma=False,
    )
```

profile of v0, /device:TPU:8, one launch (start us, length us, event | category | flops | bytes accessed | tf_op | source)
XLA Modules:
  0.0 309.1 jit_solution(17417691171173154646)
XLA Ops:
  0.6 0.0 copy-start
  0.6 1.0 slice_bitcast_fusion
  1.7 4.6 %collective-permute-start.1 = (bf16[16,4096]{1,0:T(8,128)(2,1)S(1)}, bf16[16,4096]{1,0:T(8,128)(2,1)S(1)}, u32[]{:S(2)}, u32[]{:S(2)}) collective-permute-start(bf16[16,4096]{1,0:T(8,128)(2,1)S(1)} %get-tuple-element.8), channel_id=1, source_target_pairs={{1,0},{2,1},{3,2},{4,3},{5,4},{6,5},{7,6},{8,7},{9,8},{10,9},{11,1... | collective-permute-start | bytes 393224 | tf_op jit(solution)/shard_map/ppermute | solution.py:42
  6.2 1.9 collective-permute-start
  8.2 1.6 fusion.57
  9.7 2.1 fusion.56
  11.8 2.1 fusion.55
  13.9 2.1 fusion.54
  16.0 1.6 fusion.53
  17.6 2.1 fusion.52
  19.7 2.1 fusion.51
  21.8 2.1 fusion.50
  23.9 0.8 reshape.846
  24.7 0.0 copy-done
  24.7 0.5 constant_dynamic-slice_fusion.1.ident_ref
  25.2 0.6 constant_dynamic-slice_fusion.weight_ref
  25.8 13.3 %select_convert_fusion.5 = bf16[1,128,160]{2,1,0:T(8,128)(2,1)S(1)} fusion(bf16[]{:T(256)} %bitcast.25, bf16[]{:T(256)} %bitcast.24, bf16[]{:T(256)} %bitcast.23, bf16[]{:T(256)} %bitcast.22, bf16[]{:T(256)} %bitcast.21, bf16[]{:T(256)} %bitcast.20, bf16[]{:T(256)} %bitcast.19, bf16[]{:T(256)} %bitcast.18, bf16[]{:T(256)} %bitcast.17, bf16[]{:T(256)} %bitcast.16, ...), kind=kLoop, calls=%fused_computation.37 | loop fusion | flops 901120 | bytes 41002 | tf_op jit(solution)/shard_map/convert.3
  39.1 13.2 %select_convert_fusion.4 = bf16[1,128,160]{2,1,0:T(8,128)(2,1)S(1)} fusion(bf16[]{:T(256)} %bitcast.46, bf16[]{:T(256)} %bitcast.45, bf16[]{:T(256)} %bitcast.44, bf16[]{:T(256)} %bitcast.43, bf16[]{:T(256)} %bitcast.42, bf16[]{:T(256)} %bitcast.41, bf16[]{:T(256)} %bitcast.40, bf16[]{:T(256)} %bitcast.39, bf16[]{:T(256)} %bitcast.38, bf16[]{:T(256)} %bitcast.37, ...), kind=kLoop, calls=%fused_computation.36 | loop fusion | flops 901120 | bytes 41002 | tf_op jit(solution)/shard_map/convert.4
  52.3 13.1 %select_convert_fusion.3 = bf16[1,128,160]{2,1,0:T(8,128)(2,1)S(1)} fusion(bf16[]{:T(256)} %bitcast.67, bf16[]{:T(256)} %bitcast.66, bf16[]{:T(256)} %bitcast.65, bf16[]{:T(256)} %bitcast.64, bf16[]{:T(256)} %bitcast.63, bf16[]{:T(256)} %bitcast.62, bf16[]{:T(256)} %bitcast.61, bf16[]{:T(256)} %bitcast.60, bf16[]{:T(256)} %bitcast.59, bf16[]{:T(256)} %bitcast.58, ...), kind=kLoop, calls=%fused_computation.35 | loop fusion | flops 901120 | bytes 41002 | tf_op jit(solution)/shard_map/convert.5
  65.4 0.7 pad_maximum_fusion.1
  66.1 13.1 %select_convert_fusion.2 = bf16[1,512,256]{2,1,0:T(8,128)(2,1)S(1)} fusion(bf16[]{:T(256)} %bitcast.89, bf16[]{:T(256)} %bitcast.88, bf16[]{:T(256)} %bitcast.87, bf16[]{:T(256)} %bitcast.86, bf16[]{:T(256)} %bitcast.85, bf16[]{:T(256)} %bitcast.84, bf16[]{:T(256)} %bitcast.83, bf16[]{:T(256)} %bitcast.82, bf16[]{:T(256)} %bitcast.81, bf16[]{:T(256)} %bitcast.80, ...), kind=kLoop, calls=%fused_computation.11 | loop fusion | flops 5767168 | bytes 262186 | tf_op jit(solution)/shard_map/convert
  79.2 13.3 %select_convert_fusion.1 = bf16[1,512,256]{2,1,0:T(8,128)(2,1)S(1)} fusion(bf16[]{:T(256)} %bitcast.110, bf16[]{:T(256)} %bitcast.109, bf16[]{:T(256)} %bitcast.108, bf16[]{:T(256)} %bitcast.107, bf16[]{:T(256)} %bitcast.106, bf16[]{:T(256)} %bitcast.105, bf16[]{:T(256)} %bitcast.104, bf16[]{:T(256)} %bitcast.103, bf16[]{:T(256)} %bitcast.102, ...), kind=kLoop, calls=%fused_computation.10 | loop fusion | flops 5767168 | bytes 262186 | tf_op jit(solution)/shard_map/convert.1
  92.5 13.4 %select_convert_fusion = bf16[1,512,256]{2,1,0:T(8,128)(2,1)S(1)} fusion(bf16[]{:T(256)} %bitcast.131, bf16[]{:T(256)} %bitcast.130, bf16[]{:T(256)} %bitcast.129, bf16[]{:T(256)} %bitcast.128, bf16[]{:T(256)} %bitcast.127, bf16[]{:T(256)} %bitcast.126, bf16[]{:T(256)} %bitcast.125, bf16[]{:T(256)} %bitcast.124, bf16[]{:T(256)} %bitcast.123, bf16[]{:T(256)} %bitcast.122, ...), kind=kLoop, calls=%fused_computation.9 | loop fusion | flops 5767168 | bytes 262186 | tf_op jit(solution)/shard_map/convert.2
  105.9 1.0 pad_maximum_fusion.columns_ref
  106.9 0.0 collective-permute-done.1.below_ref
  106.9 0.0 copy-start.5
  106.9 0.0 collective-permute-done.above_ref
  106.9 0.0 copy-start.6
  106.9 0.6 copy-done.5
  107.6 0.0 copy-done.6
  107.6 34.6 %match_warp.1 = bf16[8192,128]{1,0:T(8,128)(2,1)} custom-call(s32[1,64]{1,0:T(1,128)} %constant_dynamic-slice_fusion.1.ident_ref, f32[1,1]{1,0:T(1,128)} %constant_dynamic-slice_fusion.weight_ref, f32[1,3]{1,0:T(1,128)} %coef_ref.3, bf16[16,4096]{1,0:T(8,128)(2,1)} %copy-done.6, bf16[256,4096]{1,0:T(8,128)(2,1)} %bitcast.142, bf16[16,4096]{1,0:T(8,128)(2,1)} %copy-done.5, ...), custom_call_target="tpu_custom_call" | custom-call | tf_op jit(solution)/shard_map/match_warp/pallas_call | solution.py:137
  142.2 0.0 copy-start.9
  142.2 0.0 copy-start.4
  142.2 0.0 copy-start.3
  142.2 11.7 %all-to-all-start = ((bf16[128,64,128]{2,1,0:T(8,128)(2,1)}), bf16[128,64,128]{2,1,0:T(8,128)(2,1)S(1)}, u32[]{:S(2)}, u32[]{:S(2)}) async-start(bf16[128,64,128]{2,1,0:T(8,128)(2,1)} %bitcast.146), calls=%async_computation | async-start | bytes 4194304 | tf_op jit(solution)/shard_map/all_to_all | solution.py:357
  153.9 0.0 copy-done.9
  153.9 0.1 reshape.841
  154.0 0.0 copy-done.4
  154.0 0.1 eq.1143
  154.1 0.0 copy-done.3
  154.1 0.1 eq.1147
  154.1 0.1 broadcast_in_dim.535
  154.2 0.1 broadcast_in_dim.536
  154.3 2.7 fusion
  157.0 0.1 broadcast_in_dim.539
  157.0 0.6 multiply_add_fusion
  157.7 25.7 %all-to-all-done = bf16[128,64,128]{2,1,0:T(8,128)(2,1)S(1)} async-done(((bf16[128,64,128]{2,1,0:T(8,128)(2,1)}), bf16[128,64,128]{2,1,0:T(8,128)(2,1)S(1)}, u32[]{:S(2)}, u32[]{:S(2)}) %all-to-all-start) | async-done | bytes 2097184 | tf_op jit(solution)/shard_map/all_to_all | solution.py:357
  183.3 2.7 broadcast_in_dim.540.total_ref
  186.0 0.0 copy-done.1
  186.0 26.7 %slot_values.1 = (bf16[8192,128]{1,0:T(8,128)(2,1)}, bf16[8192,128]{1,0:T(8,128)(2,1)}) custom-call(s32[128,64]{1,0:T(8,128)} %bitcast.153, bf16[8192,128]{1,0:T(8,128)(2,1)} %bitcast.144, f32[8192,128]{1,0:T(8,128)} %broadcast_in_dim.540.total_ref), custom_call_target="tpu_custom_call" | custom-call | tf_op jit(solution)/shard_map/slot_values/pallas_call | solution.py:211
  212.7 35.4 %all_to_all.15 = bf16[128,64,128]{2,1,0:T(8,128)(2,1)} all-to-all(bf16[128,64,128]{2,1,0:T(8,128)(2,1)} %bitcast.150), channel_id=1, replica_groups=mesh['exp'=8,'tile'=16] {'exp','tile'}, dimensions={0} | all-to-all | bytes 4194304 | tf_op jit(solution)/shard_map/all_to_all | solution.py:357
  248.1 5.0 %all-to-all-start.1 = ((bf16[128,64,128]{2,1,0:T(8,128)(2,1)}), bf16[128,64,128]{2,1,0:T(8,128)(2,1)S(1)}, u32[]{:S(2)}, u32[]{:S(2)}) async-start(bf16[128,64,128]{2,1,0:T(8,128)(2,1)} %bitcast.149), calls=%async_computation.1 | async-start | bytes 4194304 | tf_op jit(solution)/shard_map/all_to_all | solution.py:357
  253.1 12.8 %unwarp.1.image_ref = bf16[256,4096]{1,0:T(8,128)(2,1)} custom-call(s32[1,64]{1,0:T(1,128)} %constant_dynamic-slice_fusion.1.ident_ref, bf16[8192,128]{1,0:T(8,128)(2,1)} %bitcast.147, bf16[64,128,128]{2,1,0:T(8,128)(2,1)} %warp_rows_ref.3, bf16[64,128,128]{2,1,0:T(8,128)(2,1)} %warp_columns_ref.3), custom_call_target="tpu_custom_call" | custom-call | tf_op jit(solution)/shard_map/unwarp/pallas_call | solution.py:256
  265.9 1.0 fusion.49
  266.8 4.6 %collective-permute-start.3 = (bf16[16,4096]{1,0:T(8,128)(2,1)S(1)}, bf16[16,4096]{1,0:T(8,128)(2,1)S(1)}, u32[]{:S(2)}, u32[]{:S(2)}) collective-permute-start(bf16[16,4096]{1,0:T(8,128)(2,1)S(1)} %get-tuple-element.6), channel_id=1, source_target_pairs={{1,0},{2,1},{3,2},{4,3},{5,4},{6,5},{7,6},{8,7},{9,8},{10,9},{11,1... | collective-permute-start | bytes 393224 | tf_op jit(solution)/shard_map/ppermute | solution.py:42
  271.4 1.9 collective-permute-start.2
  273.4 9.1 %all-to-all-done.1 = bf16[128,64,128]{2,1,0:T(8,128)(2,1)S(1)} async-done(((bf16[128,64,128]{2,1,0:T(8,128)(2,1)}), bf16[128,64,128]{2,1,0:T(8,128)(2,1)S(1)}, u32[]{:S(2)}, u32[]{:S(2)}) %all-to-all-start.1) | async-done | bytes 2097184 | tf_op jit(solution)/shard_map/all_to_all | solution.py:357
  282.5 1.3 copy-done.2
  283.8 7.8 %patch.1 = f32[1024,1024]{1,0:T(8,128)} custom-call(bf16[8192,128]{1,0:T(8,128)(2,1)} %bitcast.145), custom_call_target="tpu_custom_call" | custom-call | tf_op jit(solution)/shard_map/patch/pallas_call | solution.py:344
  291.7 0.0 collective-permute-done.3.below_ref
  291.7 0.0 collective-permute-done.2.above_ref
  291.7 0.7 copy-done.7
  292.3 0.6 copy-done.8
  293.0 16.1 %match_subtract.1 = f32[256,4096]{1,0:T(8,128)} custom-call(f32[1,3]{1,0:T(1,128)} %coef_ref.3, bf16[16,4096]{1,0:T(8,128)(2,1)} %copy-done.8, bf16[256,4096]{1,0:T(8,128)(2,1)} %unwarp.1.image_ref, bf16[16,4096]{1,0:T(8,128)(2,1)} %copy-done.7, bf16[256,4096]{1,0:T(8,128)(2,1)} %bitcast.143, bf16[384,160]{1,0:T(8,128)(2,1)} %bitcast.152, ...), custom_call_target="tpu_custom_call" | custom-call | tf_op jit(solution)/shard_map/match_subtract/pallas_call | solution.py:302
  (4 shorter events, 0.0 us)
Async XLA Ops:
  0.6 24.0 %copy-start = (s32[8,16,64]{2,1,0:T(8,128)S(1)}, s32[8,16,64]{2,1,0:T(8,128)}, u32[]{:S(2)}) copy-start(s32[8,16,64]{2,1,0:T(8,128)} %param.16) | copy-start | bytes 98308
  1.7 105.3 %collective-permute-start.1 = (bf16[16,4096]{1,0:T(8,128)(2,1)S(1)}, bf16[16,4096]{1,0:T(8,128)(2,1)S(1)}, u32[]{:S(2)}, u32[]{:S(2)}) collective-permute-start(bf16[16,4096]{1,0:T(8,128)(2,1)S(1)} %get-tuple-element.8), channel_id=1, source_target_pairs={{1,0},{2,1},{3,2},{4,3},{5,4},{6,5},{7,6},{8,7},{9,8},{10,9},{11,1... | collective-permute-start | bytes 393224 | tf_op jit(solution)/shard_map/ppermute | solution.py:42
  6.2 100.7 %collective-permute-start = (bf16[16,4096]{1,0:T(8,128)(2,1)S(1)}, bf16[16,4096]{1,0:T(8,128)(2,1)S(1)}, u32[]{:S(2)}, u32[]{:S(2)}) collective-permute-start(bf16[16,4096]{1,0:T(8,128)(2,1)S(1)} %get-tuple-element.9), channel_id=1, source_target_pairs={{0,1},{1,2},{2,3},{3,4},{4,5},{5,6},{6,7},{7,8},{8,9},{9,10},{10,1... | collective-permute-start | bytes 393224 | tf_op jit(solution)/shard_map/ppermute | solution.py:41
  106.9 0.7 copy-start.5
  106.9 0.7 copy-start.6
  142.2 11.7 %copy-start.9 = (f32[8,16]{1,0:T(8,128)S(1)}, f32[8,16]{1,0:T(8,128)}, u32[]{:S(2)}) copy-start(f32[8,16]{1,0:T(8,128)} %param.19) | copy-start | bytes 1540
  142.2 11.8 %copy-start.4 = (s32[8,16,64]{2,1,0:T(8,128)S(1)}, s32[8,16,64]{2,1,0:T(8,128)}, u32[]{:S(2)}) copy-start(s32[8,16,64]{2,1,0:T(8,128)} %param.17) | copy-start | bytes 98308
  142.2 11.9 %copy-start.3 = (s32[8,16,64]{2,1,0:T(8,128)S(1)}, s32[8,16,64]{2,1,0:T(8,128)}, u32[]{:S(2)}) copy-start(s32[8,16,64]{2,1,0:T(8,128)} %param.18) | copy-start | bytes 98308
  142.2 41.1 %all-to-all-start = ((bf16[128,64,128]{2,1,0:T(8,128)(2,1)}), bf16[128,64,128]{2,1,0:T(8,128)(2,1)S(1)}, u32[]{:S(2)}, u32[]{:S(2)}) async-start(bf16[128,64,128]{2,1,0:T(8,128)(2,1)} %bitcast.146), calls=%async_computation | async-start | bytes 4194304 | tf_op jit(solution)/shard_map/all_to_all | solution.py:357
  183.3 2.7 copy-start.1
  248.1 34.4 %all-to-all-start.1 = ((bf16[128,64,128]{2,1,0:T(8,128)(2,1)}), bf16[128,64,128]{2,1,0:T(8,128)(2,1)S(1)}, u32[]{:S(2)}, u32[]{:S(2)}) async-start(bf16[128,64,128]{2,1,0:T(8,128)(2,1)} %bitcast.149), calls=%async_computation.1 | async-start | bytes 4194304 | tf_op jit(solution)/shard_map/all_to_all | solution.py:357
  266.8 24.8 %collective-permute-start.3 = (bf16[16,4096]{1,0:T(8,128)(2,1)S(1)}, bf16[16,4096]{1,0:T(8,128)(2,1)S(1)}, u32[]{:S(2)}, u32[]{:S(2)}) collective-permute-start(bf16[16,4096]{1,0:T(8,128)(2,1)S(1)} %get-tuple-element.6), channel_id=1, source_target_pairs={{1,0},{2,1},{3,2},{4,3},{5,4},{6,5},{7,6},{8,7},{9,8},{10,9},{11,1... | collective-permute-start | bytes 393224 | tf_op jit(solution)/shard_map/ppermute | solution.py:42
  271.4 20.2 %collective-permute-start.2 = (bf16[16,4096]{1,0:T(8,128)(2,1)S(1)}, bf16[16,4096]{1,0:T(8,128)(2,1)S(1)}, u32[]{:S(2)}, u32[]{:S(2)}) collective-permute-start(bf16[16,4096]{1,0:T(8,128)(2,1)S(1)} %get-tuple-element.7), channel_id=1, source_target_pairs={{0,1},{1,2},{2,3},{3,4},{4,5},{5,6},{6,7},{7,8},{8,9},{9,10},{10,1... | collective-permute-start | bytes 393224 | tf_op jit(solution)/shard_map/ppermute | solution.py:41
  282.5 1.3 copy-start.2
  291.7 0.7 copy-start.7
  292.3 0.6 copy-start.8
where the time goes:
time: 313 us; the launch traced here: 309 us
  Pallas kernels  98 us (31%)
  other arithmetic  81.7 us (26%)
  blocking collectives  35.4 us (11%)
  waiting for transfers between devices  34.8 us (11%)
  starting transfers between devices  29.6 us (9%)
  local copies, waits for them, and re-layouts  26.1 us (8%)
    another operation x6, other arithmetic  79.4 us
    all_to_all x1, blocking collectives, exchange(): lax.all_to_all(shaped, ('exp', 'tile'), split_axis=0, concat_axis=0, tile...  35.4 us
    all_to_all x2, waiting for transfers between devices, exchange(): lax.all_to_all(shaped, ('exp', 'tile'), split_axis=0, concat_axis=0, tile...  34.8 us
    pallas_call x1, Pallas kernels, forward(): pl.pallas_call(functools.partial(forward_kernel, chunks=chunks), out_shap...  34.6 us
    pallas_call x1, Pallas kernels, slot_values(): pl.pallas_call(slots_kernel, out_shape=(shape, shape), in_specs=[SMEM, VM...  26.7 us
    all_to_all x2, starting transfers between devices, exchange(): lax.all_to_all(shaped, ('exp', 'tile'), split_axis=0, concat_axis=0, tile...  16.7 us
    pallas_call x1, Pallas kernels, subtract(): pl.pallas_call(functools.partial(subtract_kernel, chunks=chunks), out_sha...  16.1 us
    slice x8, local copies, waits for them, and re-layouts, band_matrices(): band = jnp.where(grid == tap_index, taps[tap_index], band)  15.7 us
  transfers between devices with their start and end apart: 6, of which 2 were waited for; matrix products, arithmetic and copies ran while one was open for 33% of the time, Pallas kernels for 7%

commit v1 on v0

v1 whole, which is shorter than its diff:
```python
import functools

import jax
import jax.numpy as jnp
from jax import lax
from jax.experimental import pallas as pl
from jax.experimental.pallas import tpu as pltpu
from jax.sharding import PartitionSpec as P

BLOCK = 128
HALF = 10
RIM = 16
CHUNK = 256
WIDE = 512
SPAN = CHUNK + 2 * BLOCK
WINDOW = BLOCK + 2 * RIM
SLOT_ROWS = 8
SLOT_COLS = 8
LANES = 4
PAD = 8
VMEM_BYTES = 60 * 1024 * 1024
VMEM = pl.BlockSpec(memory_space=pltpu.VMEM)
SMEM = pl.BlockSpec(memory_space=pltpu.SMEM)
ANY = pl.BlockSpec(memory_space=pl.ANY)
PARAMS = pltpu.CompilerParams(vmem_limit_bytes=VMEM_BYTES)


def bands_kernel(row_taps_ref, column_taps_ref, rows_ref, columns_ref):
    bases, taps = row_taps_ref.shape
    lead = RIM - HALF

    def banded(taps_ref, offsets):
        bands = [jnp.zeros(offsets.shape, jnp.float32) for _ in range(bases)]
        for tap in range(taps):
            hit = offsets == tap
            bands = [jnp.where(hit, taps_ref[base, tap], bands[base]) for base in range(bases)]
        return [band.astype(jnp.bfloat16) for band in bands]

    shape = (BLOCK, WINDOW)
    across = lax.broadcasted_iota(jnp.int32, shape, 1) - lax.broadcasted_iota(jnp.int32, shape, 0)
    for base, band in enumerate(banded(row_taps_ref, across - lead)):
        rows_ref[base * BLOCK : (base + 1) * BLOCK, :] = band
    shape = (WINDOW, BLOCK)
    down = lax.broadcasted_iota(jnp.int32, shape, 0) - lax.broadcasted_iota(jnp.int32, shape, 1)
    columns_ref[...] = jnp.zeros_like(columns_ref)
    for base, band in enumerate(banded(column_taps_ref, down - lead)):
        for part in range(CHUNK // BLOCK):
            top = base * SPAN + (part + 1) * BLOCK - RIM
            columns_ref[top : top + WINDOW, part * BLOCK : (part + 1) * BLOCK] = band


def band_matrices(row_taps, column_taps):
    bases = row_taps.shape[0]
    return pl.pallas_call(
        bands_kernel,
        out_shape=(
            jax.ShapeDtypeStruct((bases * BLOCK, WINDOW), jnp.bfloat16),
            jax.ShapeDtypeStruct((bases * SPAN, CHUNK), jnp.bfloat16),
        ),
        in_specs=[SMEM, SMEM],
        out_specs=(VMEM, VMEM),
        name="bands",
    )(row_taps.astype(jnp.float32), column_taps.astype(jnp.float32))


def swap_rims(top, bottom):
    count = lax.axis_size("tile")
    forward = [(i, i + 1) for i in range(count - 1)]
    backward = [(target, source) for source, target in forward]
    return lax.ppermute(bottom, "tile", forward), lax.ppermute(top, "tile", backward)


def clear_sides(pass_ref):
    bases, height, width = pass_ref.shape
    side = jnp.zeros((bases, height, BLOCK), pass_ref.dtype)
    pass_ref[:, :, :BLOCK] = side
    pass_ref[:, :, width - BLOCK :] = side


def row_step(index, strips, coef_ref, rows_ref, pass_ref):
    bases = pass_ref.shape[0]
    columns = pl.ds(pl.multiple_of(index * WIDE, WIDE), WIDE)
    for start, count, pieces in strips:
        window = [ref[first : first + size, columns] for ref, first, size in pieces]
        window = window[0] if len(window) == 1 else jnp.concatenate(window, axis=0)
        depth = window.shape[0]
        if count == BLOCK and depth == WINDOW:
            band = rows_ref[...]
        else:
            band = jnp.concatenate(
                [rows_ref[base * BLOCK : base * BLOCK + count, :depth] for base in range(bases)],
                axis=0,
            )
        summed = jnp.dot(band, window, preferred_element_type=jnp.float32)
        to = pl.ds(pl.multiple_of(index * WIDE + BLOCK, BLOCK), WIDE)
        for base in range(bases):
            pass_ref[base, start : start + count, to] = (
                coef_ref[0, base] * summed[base * count : (base + 1) * count]
            ).astype(jnp.bfloat16)


def column_step(index, start, count, columns_ref, pass_ref):
    bases = pass_ref.shape[0]
    parts = []
    for part in range(WIDE // CHUNK):
        window = pl.ds(pl.multiple_of(index * WIDE + part * CHUNK, CHUNK), SPAN)
        parts.append(
            jnp.concatenate(
                [pass_ref[base, start : start + count, window] for base in range(bases)], axis=1
            )
        )
    summed = jnp.dot(
        jnp.concatenate(parts, axis=0), columns_ref[...], preferred_element_type=jnp.float32
    )
    return [summed[part * count : (part + 1) * count] for part in range(WIDE // CHUNK)]


def forward_kernel(
    ident_ref,
    weight_ref,
    coef_ref,
    above_ref,
    image_ref,
    below_ref,
    rows_ref,
    columns_ref,
    bank_rows_ref,
    bank_columns_ref,
    out_ref,
    pass_ref,
    turned_ref,
    warp_rows_ref,
    warp_columns_ref,
    sems,
):
    tile_rows, width = image_ref.shape
    across = width // BLOCK
    per_tile = tile_rows // BLOCK * across
    pitch = per_tile + PAD
    wides = width // WIDE
    loads = [
        pltpu.make_async_copy(bank_rows_ref, warp_rows_ref, sems.at[0]),
        pltpu.make_async_copy(bank_columns_ref, warp_columns_ref, sems.at[1]),
    ]
    for load in loads:
        load.start()

    strips = [
        (0, BLOCK, [(above_ref, 0, RIM), (image_ref, 0, BLOCK + RIM)]),
        (BLOCK, BLOCK, [(image_ref, BLOCK - RIM, BLOCK + RIM), (below_ref, 0, RIM)]),
    ]
    clear_sides(pass_ref)
    row_step(0, strips, coef_ref, rows_ref, pass_ref)
    row_step(1, strips, coef_ref, rows_ref, pass_ref)
    for load in loads:
        load.wait()

    def warp_step(index):
        for half, summed in enumerate(column_step(index, 0, tile_rows, columns_ref, pass_ref)):
            matched = summed.astype(jnp.bfloat16)
            for part in range(tile_rows // BLOCK):
                for inner in range(CHUNK // BLOCK):
                    column = index * (WIDE // BLOCK) + half * (CHUNK // BLOCK) + inner
                    block = part * across + column
                    ident = ident_ref[0, block]
                    piece = matched[
                        part * BLOCK : (part + 1) * BLOCK, inner * BLOCK : (inner + 1) * BLOCK
                    ]
                    first = jnp.dot(
                        warp_rows_ref[ident], piece, preferred_element_type=jnp.float32
                    ).astype(jnp.bfloat16)
                    second = lax.dot_general(
                        first,
                        warp_columns_ref[ident],
                        (((1,), (1,)), ((), ())),
                        preferred_element_type=jnp.float32,
                    )
                    turned_ref[pl.ds(block, BLOCK, stride=pitch), :] = weight_ref[0, 0] * second

    @pl.loop(0, wides - 2)
    def _(index):
        warp_step(index)
        row_step(index + 2, strips, coef_ref, rows_ref, pass_ref)

    @pl.loop(wides - 2, wides)
    def _(index):
        warp_step(index)

    @pl.loop(0, BLOCK, unroll=2)
    def _(row):
        to = pl.ds(pl.multiple_of(row * per_tile, per_tile), per_tile)
        at = pl.ds(pl.multiple_of(row * pitch, PAD), per_tile)
        out_ref[to, :] = turned_ref[at, :].astype(jnp.bfloat16)


def forward(ident, weight, coef, above, image, below, rows, columns, warp_rows, warp_columns):
    tile_rows, width = image.shape
    bases = rows.shape[0] // BLOCK
    items = tile_rows * width // BLOCK
    return pl.pallas_call(
        forward_kernel,
        out_shape=jax.ShapeDtypeStruct((items, BLOCK), jnp.bfloat16),
        in_specs=[SMEM, SMEM, SMEM, VMEM, VMEM, VMEM, VMEM, VMEM, ANY, ANY],
        out_specs=VMEM,
        scratch_shapes=[
            pltpu.VMEM((bases, tile_rows, width + 2 * BLOCK), jnp.bfloat16),
            pltpu.VMEM((items + BLOCK * PAD, BLOCK), jnp.float32),
            pltpu.VMEM(warp_rows.shape, jnp.bfloat16),
            pltpu.VMEM(warp_columns.shape, jnp.bfloat16),
            pltpu.SemaphoreType.DMA((2,)),
        ],
        compiler_params=PARAMS,
        name="match_warp",
    )(ident, weight, coef, above, image, below, rows, columns, warp_rows, warp_columns)


def slots_kernel(slot_ref, arrived_ref, template_ref, coadd_ref, wide_ref, *sums):
    sources, per_tile = slot_ref.shape

    def at(source):
        return pl.ds(pl.multiple_of(source * per_tile, per_tile), per_tile)

    @pl.loop(0, sources)
    def _(source):
        wide_ref[at(source), :] = arrived_ref[at(source), :].astype(jnp.float32)
        for sum_ref in sums:
            sum_ref[at(source), :] = jnp.zeros((per_tile, BLOCK), jnp.float32)

    @pl.loop(0, sources)
    def _(source):
        for first in range(0, per_tile, len(sums)):
            slots = [slot_ref[source, first + lane] for lane in range(len(sums))]
            values = [
                sum_ref[pl.ds(slot, 1), :] + wide_ref[pl.ds(source * per_tile + first + lane, 1), :]
                for lane, (slot, sum_ref) in enumerate(zip(slots, sums))
            ]
            for slot, sum_ref, value in zip(slots, sums, values):
                sum_ref[pl.ds(slot, 1), :] = value

    @pl.loop(0, sources)
    def _(source):
        value = sums[0][at(source), :]
        for sum_ref in sums[1:]:
            value = value + sum_ref[at(source), :]
        sums[0][at(source), :] = value
        coadd_ref[at(source), :] = value.astype(jnp.bfloat16)

    @pl.loop(0, sources)
    def _(source):
        for item in range(per_tile):
            slot = slot_ref[source, item]
            wide_ref[pl.ds(source * per_tile + item, 1), :] = sums[0][pl.ds(slot, 1), :]

    @pl.loop(0, sources)
    def _(source):
        template_ref[at(source), :] = wide_ref[at(source), :].astype(jnp.bfloat16)


def slot_sums(slots, arrived):
    shape = jax.ShapeDtypeStruct(arrived.shape, jnp.bfloat16)
    return pl.pallas_call(
        slots_kernel,
        out_shape=(shape, shape),
        in_specs=[SMEM, VMEM],
        out_specs=(VMEM, VMEM),
        scratch_shapes=[pltpu.VMEM(arrived.shape, jnp.float32)] * (1 + LANES),
        compiler_params=PARAMS,
        name="slot_sums",
    )(slots, arrived)


def unwarp_kernel(
    ident_ref,
    scale_ref,
    returned_ref,
    bank_rows_ref,
    bank_columns_ref,
    out_ref,
    top_ref,
    bottom_ref,
    wide_ref,
    warp_rows_ref,
    warp_columns_ref,
    sems,
):
    tile_rows, width = out_ref.shape
    across = width // BLOCK
    parts = tile_rows // BLOCK
    per_tile = ident_ref.shape[1]
    pitch = per_tile + PAD
    loads = [
        pltpu.make_async_copy(bank_rows_ref, warp_rows_ref, sems.at[0]),
        pltpu.make_async_copy(bank_columns_ref, warp_columns_ref, sems.at[1]),
    ]
    for load in loads:
        load.start()

    @pl.loop(0, BLOCK, unroll=2)
    def _(row):
        to = pl.ds(pl.multiple_of(row * pitch, PAD), per_tile)
        at = pl.ds(pl.multiple_of(row * per_tile, per_tile), per_tile)
        wide_ref[to, :] = returned_ref[at, :].astype(jnp.float32)

    for load in loads:
        load.wait()

    @pl.loop(0, across // 4)
    def _(quad):
        for part in range(parts):
            for inner in range(4):
                column = quad * 4 + inner
                block = part * across + column
                ident = ident_ref[0, block]
                numerator = wide_ref[pl.ds(block, BLOCK, stride=pitch), :].astype(jnp.bfloat16)
                first = lax.dot_general(
                    warp_rows_ref[ident],
                    numerator,
                    (((0,), (0,)), ((), ())),
                    preferred_element_type=jnp.float32,
                )
                image = jnp.dot(
                    (scale_ref[0, block] * first).astype(jnp.bfloat16),
                    warp_columns_ref[ident],
                    preferred_element_type=jnp.float32,
                ).astype(jnp.bfloat16)
                to = pl.ds(pl.multiple_of(column * BLOCK, BLOCK), BLOCK)
                out_ref[part * BLOCK : (part + 1) * BLOCK, to] = image
                if part == 0:
                    top_ref[:, to] = image[:RIM]
                if part == parts - 1:
                    bottom_ref[:, to] = image[BLOCK - RIM :]


def unwarp(ident, scale, returned, warp_rows, warp_columns, tile_rows, width):
    rim = jax.ShapeDtypeStruct((RIM, width), jnp.bfloat16)
    return pl.pallas_call(
        unwarp_kernel,
        out_shape=(jax.ShapeDtypeStruct((tile_rows, width), jnp.bfloat16), rim, rim),
        in_specs=[SMEM, SMEM, VMEM, ANY, ANY],
        out_specs=(VMEM, VMEM, VMEM),
        scratch_shapes=[
            pltpu.VMEM((returned.shape[0] + BLOCK * PAD, BLOCK), jnp.float32),
            pltpu.VMEM(warp_rows.shape, jnp.bfloat16),
            pltpu.VMEM(warp_columns.shape, jnp.bfloat16),
            pltpu.SemaphoreType.DMA((2,)),
        ],
        compiler_params=PARAMS,
        name="unwarp",
    )(ident, scale, returned, warp_rows, warp_columns)


def inner_kernel(
    coef_ref, image_ref, exposure_ref, rows_ref, columns_ref, out_ref, pass_ref, stage_ref, sems
):
    tile_rows, width = image_ref.shape
    wides = width // WIDE
    inner = tile_rows - 2 * RIM
    rest = inner - BLOCK
    strips = [
        (0, BLOCK, [(image_ref, 0, WINDOW)]),
        (BLOCK, rest, [(image_ref, BLOCK, tile_rows - BLOCK)]),
    ]
    clear_sides(pass_ref)
    row_step(0, strips, coef_ref, rows_ref, pass_ref)
    row_step(1, strips, coef_ref, rows_ref, pass_ref)

    def store(index):
        at = pl.ds(pl.multiple_of(index * WIDE, WIDE), WIDE)
        return pltpu.make_async_copy(
            stage_ref.at[:, at], out_ref.at[pl.ds(RIM, inner), at], sems.at[index]
        )

    def subtract_step(index):
        for half, summed in enumerate(column_step(index, 0, inner, columns_ref, pass_ref)):
            at = pl.ds(pl.multiple_of(index * WIDE + half * CHUNK, CHUNK), CHUNK)
            stage_ref[:, at] = (
                exposure_ref[RIM : RIM + inner, at].astype(jnp.float32) - summed
            )
        store(index).start()

    @pl.loop(0, wides - 2)
    def _(index):
        subtract_step(index)
        row_step(index + 2, strips, coef_ref, rows_ref, pass_ref)

    @pl.loop(wides - 2, wides)
    def _(index):
        subtract_step(index)

    @pl.loop(0, wides)
    def _(index):
        store(index).wait()


def subtract_inner(coef, image, exposure, rows, columns):
    tile_rows, width = image.shape
    bases = rows.shape[0] // BLOCK
    inner = tile_rows - 2 * RIM
    return pl.pallas_call(
        inner_kernel,
        out_shape=jax.ShapeDtypeStruct((tile_rows, width), jnp.float32),
        in_specs=[SMEM, VMEM, VMEM, VMEM, VMEM],
        out_specs=ANY,
        scratch_shapes=[
            pltpu.VMEM((bases, inner, width + 2 * BLOCK), jnp.bfloat16),
            pltpu.VMEM((inner, width), jnp.float32),
            pltpu.SemaphoreType.DMA((width // WIDE,)),
        ],
        compiler_params=PARAMS,
        name="subtract_inner",
    )(coef, image, exposure, rows, columns)


def outer_kernel(
    coef_ref,
    above_ref,
    top_ref,
    bottom_ref,
    below_ref,
    exposure_top_ref,
    exposure_bottom_ref,
    rows_ref,
    columns_ref,
    partial_ref,
    out_ref,
    pass_ref,
    stage_ref,
    sems,
):
    del partial_ref
    width = top_ref.shape[1]
    tile_rows = out_ref.shape[0]
    wides = width // WIDE
    strips = [
        (0, RIM, [(above_ref, 0, RIM), (top_ref, 0, 2 * RIM)]),
        (RIM, RIM, [(bottom_ref, 0, 2 * RIM), (below_ref, 0, RIM)]),
    ]
    clear_sides(pass_ref)
    for index in range(wides):
        row_step(index, strips, coef_ref, rows_ref, pass_ref)
    for index in range(wides):
        for half, summed in enumerate(column_step(index, 0, 2 * RIM, columns_ref, pass_ref)):
            at = pl.ds(index * WIDE + half * CHUNK, CHUNK)
            stage_ref[:RIM, at] = exposure_top_ref[:, at].astype(jnp.float32) - summed[:RIM]
            stage_ref[RIM:, at] = exposure_bottom_ref[:, at].astype(jnp.float32) - summed[RIM:]
    stores = [
        pltpu.make_async_copy(stage_ref.at[:RIM], out_ref.at[:RIM], sems.at[0]),
        pltpu.make_async_copy(
            stage_ref.at[RIM:], out_ref.at[pl.ds(tile_rows - RIM, RIM)], sems.at[1]
        ),
    ]
    for store in stores:
        store.start()
    for store in stores:
        store.wait()


def subtract_outer(coef, above, image, below, exposure, rows, columns, partial):
    tile_rows, width = image.shape
    bases = rows.shape[0] // BLOCK
    rim = pl.BlockSpec((RIM, width), lambda _: (0, 0))
    last_rim = pl.BlockSpec((RIM, width), lambda _: (tile_rows // RIM - 1, 0))
    pair = pl.BlockSpec((2 * RIM, width), lambda _: (0, 0))
    last_pair = pl.BlockSpec((2 * RIM, width), lambda _: (tile_rows // (2 * RIM) - 1, 0))
    return pl.pallas_call(
        outer_kernel,
        out_shape=jax.ShapeDtypeStruct((tile_rows, width), jnp.float32),
        grid=(1,),
        in_specs=[SMEM, VMEM, pair, last_pair, VMEM, rim, last_rim, VMEM, VMEM, ANY],
        out_specs=ANY,
        scratch_shapes=[
            pltpu.VMEM((bases, 2 * RIM, width + 2 * BLOCK), jnp.bfloat16),
            pltpu.VMEM((2 * RIM, width), jnp.float32),
            pltpu.SemaphoreType.DMA((2,)),
        ],
        input_output_aliases={9: 0},
        compiler_params=PARAMS,
        name="subtract_outer",
    )(coef, above, image, image, below, exposure, exposure, rows, columns, partial)


def patch_kernel(scale_ref, rows_ref, out_ref, wide_ref, stage_ref, sems):
    slots = SLOT_ROWS * SLOT_COLS
    pitch = slots + PAD

    @pl.loop(0, BLOCK, unroll=2)
    def _(row):
        to = pl.ds(pl.multiple_of(row * pitch, PAD), slots)
        at = pl.ds(pl.multiple_of(row * slots, slots), slots)
        wide_ref[to, :] = rows_ref[at, :].astype(jnp.float32)

    def store(down):
        at = pl.ds(pl.multiple_of(down * BLOCK, BLOCK), BLOCK)
        return pltpu.make_async_copy(stage_ref.at[at], out_ref.at[at], sems.at[down])

    @pl.loop(0, SLOT_ROWS)
    def _(down):
        to = pl.ds(pl.multiple_of(down * BLOCK, BLOCK), BLOCK)
        for across in range(SLOT_COLS):
            slot = down * SLOT_COLS + across
            stage_ref[to, across * BLOCK : (across + 1) * BLOCK] = (
                scale_ref[0, slot] * wide_ref[pl.ds(slot, BLOCK, stride=pitch), :]
            )
        store(down).start()

    @pl.loop(0, SLOT_ROWS)
    def _(down):
        store(down).wait()


def patch(scale, rows):
    shape = (SLOT_ROWS * BLOCK, SLOT_COLS * BLOCK)
    return pl.pallas_call(
        patch_kernel,
        out_shape=jax.ShapeDtypeStruct(shape, jnp.float32),
        in_specs=[SMEM, VMEM],
        out_specs=ANY,
        scratch_shapes=[
            pltpu.VMEM((rows.shape[0] + BLOCK * PAD, BLOCK), jnp.float32),
            pltpu.VMEM(shape, jnp.float32),
            pltpu.SemaphoreType.DMA((SLOT_ROWS,)),
        ],
        compiler_params=PARAMS,
        name="patch",
    )(scale, rows)


def exchange(rows, devices):
    shaped = rows.reshape(devices, -1, BLOCK)
    moved = lax.all_to_all(shaped, ("exp", "tile"), split_axis=0, concat_axis=0, tiled=True)
    return moved.reshape(rows.shape)


def shards(
    exposure,
    row_taps,
    column_taps,
    basis_coef,
    warp_rows,
    warp_columns,
    warp_id,
    route_device,
    route_slot,
    weight,
):
    devices = lax.axis_size("exp") * lax.axis_size("tile")
    image = exposure[0]
    tile_rows, width = image.shape
    per_tile = tile_rows * width // (BLOCK * BLOCK)
    slot_count = SLOT_ROWS * SLOT_COLS
    myself = lax.axis_index("exp") * lax.axis_size("tile") + lax.axis_index("tile")

    def mine(table):
        return lax.dynamic_slice_in_dim(table.reshape(devices, -1), myself, 1, 0)

    above, below = swap_rims(image[:RIM], image[tile_rows - RIM :])
    rows, columns = band_matrices(row_taps, column_taps)
    my_ident = mine(warp_id)
    my_weight = mine(weight)
    weighted = forward(
        my_ident, my_weight, basis_coef, above, image, below, rows, columns, warp_rows, warp_columns
    )
    arrived = exchange(weighted, devices)

    owner = route_device.reshape(-1)
    place = route_slot.reshape(-1)
    block_weight = jnp.repeat(weight.reshape(-1), per_tile)
    by_owner = jnp.where(
        owner[None, :] == jnp.arange(devices, dtype=jnp.int32)[:, None], block_weight[None, :], 0.0
    )
    by_place = (place[:, None] == jnp.arange(slot_count, dtype=jnp.int32)[None, :]).astype(
        jnp.float32
    )
    total = jnp.dot(by_owner, by_place, precision=lax.Precision.HIGHEST)
    scale = 1.0 / jnp.maximum(total, 1.0)
    slots = (route_device * slot_count + route_slot).reshape(devices, per_tile)
    owned_scale = mine(scale)
    block_scale = scale.reshape(-1)[mine(slots)]

    template_rows, coadd_rows = slot_sums(slots, arrived)
    returned = exchange(template_rows, devices)
    owned = exchange(coadd_rows, devices)

    template, top, bottom = unwarp(
        my_ident, block_scale, returned, warp_rows, warp_columns, tile_rows, width
    )
    above, below = swap_rims(top, bottom)
    difference = subtract_inner(basis_coef, template, image, rows, columns)
    difference = subtract_outer(
        basis_coef, above, template, below, image, rows, columns, difference
    )
    return patch(owned_scale, owned), difference[None]


def solution(mesh):
    placed = (P("exp", "tile", None), P(), P(), P("exp", None), P(), P(), P(), P(), P(), P())
    return jax.shard_map(
        shards,
        mesh=mesh,
        in_specs=placed,
        out_specs=(P("exp", "tile"), P("exp", "tile", None)),
        check_vma=False,
    )
```

time: 313 us -> 190 us (0.61); the launches traced: 309 us -> 189 us
  other arithmetic: 81.7 us -> 3.84 us
  Pallas kernels: 98 us -> 78.6 us
  local copies, waits for them, and re-layouts: 26.1 us -> 9.72 us
  waiting for transfers between devices: 34.8 us -> 28.8 us
    another operation x8 -> x0, other arithmetic: 81.1 us -> none
    pallas_call x5 -> x7, Pallas kernels: 98 us -> 78.6 us  [the longest x1 25.3 us: forward(): pl.pallas_call(forward_kernel, out_shape=jax.ShapeDtypeStruct((items, BLO...]
    slice x10 -> x1, local copies, waits for them, and re-layouts: 17.7 us -> 1.02 us  [shards(): above, below = swap_rims(image[:RIM], image[tile_rows - RIM:])]
    all_to_all x2, waiting for transfers between devices: 34.8 us -> 28.8 us  [exchange(): lax.all_to_all(shaped, ('exp', 'tile'), split_axis=0, concat_axis=0, tile...]
    all_to_all x2, starting transfers between devices: 16.7 us -> 13.4 us  [exchange(): lax.all_to_all(shaped, ('exp', 'tile'), split_axis=0, concat_axis=0, tile...]
  transfers between devices with their start and end apart: 6 -> 6, of which waited for: 2 -> 1; matrix products, arithmetic and copies ran while one was open for 33% -> 6% of each run, Pallas kernels for 7% -> 13%
where the time goes in v1:
time: 190 us; the launch traced here: 189 us
  Pallas kernels  78.6 us (41%)
  blocking collectives  35.4 us (19%)
  starting transfers between devices  29.4 us (15%)
  waiting for transfers between devices  28.8 us (15%)
  local copies, waits for them, and re-layouts  9.72 us (5%)
  other arithmetic  3.84 us (2%)
  matrix products  2.66 us (1%)
    all_to_all x1, blocking collectives, exchange(): lax.all_to_all(shaped, ('exp', 'tile'), split_axis=0, concat_axis=0, tile...  35.4 us
    all_to_all x2, waiting for transfers between devices, exchange(): lax.all_to_all(shaped, ('exp', 'tile'), split_axis=0, concat_axis=0, tile...  28.8 us
    pallas_call x1, Pallas kernels, forward(): pl.pallas_call(forward_kernel, out_shape=jax.ShapeDtypeStruct((items, BLO...  25.3 us
    pallas_call x1, Pallas kernels, slot_sums(): pl.pallas_call(slots_kernel, out_shape=(shape, shape), in_specs=[SMEM, VM...  24.9 us
    all_to_all x2, starting transfers between devices, exchange(): lax.all_to_all(shaped, ('exp', 'tile'), split_axis=0, concat_axis=0, tile...  13.4 us
    ppermute x2, starting transfers between devices, swap_rims(): lax.ppermute(top, 'tile', backward)  9.3 us
    pallas_call x1, Pallas kernels, subtract_inner(): pl.pallas_call(inner_kernel, out_shape=jax.ShapeDtypeStruct((tile_rows, w...  9.15 us
    pallas_call x1, Pallas kernels, unwarp(): pl.pallas_call(unwarp_kernel, out_shape=(jax.ShapeDtypeStruct((tile_rows,...  8.69 us
  transfers between devices with their start and end apart: 6, of which 1 were waited for; matrix products, arithmetic and copies ran while one was open for 6% of the time, Pallas kernels for 13%

profile of v1, /device:TPU:8, one launch (start us, length us, event | category | flops | bytes accessed | tf_op | source)
XLA Modules:
  0.0 189.5 jit_solution(6685277033200600369)
XLA Ops:
  0.6 0.0 copy-start
  0.6 1.0 slice_bitcast_fusion
  1.7 3.4 %collective-permute-start = (bf16[16,4096]{1,0:T(8,128)(2,1)S(1)}, bf16[16,4096]{1,0:T(8,128)(2,1)S(1)}, u32[]{:S(2)}, u32[]{:S(2)}) collective-permute-start(bf16[16,4096]{1,0:T(8,128)(2,1)S(1)} %get-tuple-element.17), channel_id=1, source_target_pairs={{0,1},{1,2},{2,3},{3,4},{4,5},{5,6},{6,7},{7,8},{8,9},{9,10},{10,1... | collective-permute-start | bytes 393224 | tf_op jit(solution)/shard_map/ppermute | solution.py:70
  5.1 4.6 %collective-permute-start.1 = (bf16[16,4096]{1,0:T(8,128)(2,1)S(1)}, bf16[16,4096]{1,0:T(8,128)(2,1)S(1)}, u32[]{:S(2)}, u32[]{:S(2)}) collective-permute-start(bf16[16,4096]{1,0:T(8,128)(2,1)S(1)} %get-tuple-element.16), channel_id=1, source_target_pairs={{1,0},{2,1},{3,2},{4,3},{5,4},{6,5},{7,6},{8,7},{9,8},{10,9},{11,1... | collective-permute-start | bytes 393224 | tf_op jit(solution)/shard_map/ppermute | solution.py:70
  9.6 0.8 reshape.62
  10.4 1.3 convert_element_type.7.row_taps_ref
  11.7 1.3 convert_element_type.8.column_taps_ref
  12.9 0.5 constant_dynamic-slice_fusion.1.weight_ref
  13.5 2.5 %bands.1 = (bf16[384,160]{1,0:T(8,128)(2,1)}, bf16[1536,256]{1,0:T(8,128)(2,1)}) custom-call(f32[3,21]{1,0:T(4,128)} %convert_element_type.7.row_taps_ref, f32[3,21]{1,0:T(4,128)} %convert_element_type.8.column_taps_ref), custom_call_target="tpu_custom_call" | custom-call | tf_op jit(solution)/shard_map/bands/pallas_call | solution.py:54
  16.0 0.0 copy-done
  16.0 0.5 constant_dynamic-slice_fusion.2.ident_ref
  16.5 0.0 collective-permute-done.above_ref
  16.5 0.0 copy-start.5
  16.5 0.0 collective-permute-done.1.below_ref
  16.5 0.0 copy-start.6
  16.5 0.6 copy-done.5
  17.1 0.0 copy-done.6
  17.2 25.3 %match_warp.1 = bf16[8192,128]{1,0:T(8,128)(2,1)} custom-call(s32[1,64]{1,0:T(1,128)} %constant_dynamic-slice_fusion.2.ident_ref, f32[1,1]{1,0:T(1,128)} %constant_dynamic-slice_fusion.1.weight_ref, f32[1,3]{1,0:T(1,128)} %coef_ref.5, bf16[16,4096]{1,0:T(8,128)(2,1)} %copy-done.5, bf16[256,4096]{1,0:T(8,128)(2,1)} %bitcast.18, bf16[16,4096]{1,0:T(8,128)(2,1)} %copy-done.6, ...), custom_call_target="tpu_custom_call" | custom-call | tf_op jit(solution)/shard_map/match_warp/pallas_call | solution.py:200
  42.5 0.0 copy-start.3
  42.5 0.0 copy-start.4
  42.5 8.3 %all-to-all-start = ((bf16[128,64,128]{2,1,0:T(8,128)(2,1)}), bf16[128,64,128]{2,1,0:T(8,128)(2,1)S(1)}, u32[]{:S(2)}, u32[]{:S(2)}) async-start(bf16[128,64,128]{2,1,0:T(8,128)(2,1)} %bitcast.24), calls=%async_computation | async-start | bytes 4194304 | tf_op jit(solution)/shard_map/all_to_all | solution.py:530
  50.8 0.0 copy-done.3
  50.8 0.0 copy-done.4
  50.8 0.6 multiply_add_fusion
  51.5 28.8 %all-to-all-done = bf16[128,64,128]{2,1,0:T(8,128)(2,1)S(1)} async-done(((bf16[128,64,128]{2,1,0:T(8,128)(2,1)}), bf16[128,64,128]{2,1,0:T(8,128)(2,1)S(1)}, u32[]{:S(2)}, u32[]{:S(2)}) %all-to-all-start) | async-done | bytes 2097184 | tf_op jit(solution)/shard_map/all_to_all | solution.py:530
  80.3 0.0 copy-start.2
  80.3 1.3 copy-done.2
  81.6 24.9 %slot_sums.1 = (bf16[8192,128]{1,0:T(8,128)(2,1)}, bf16[8192,128]{1,0:T(8,128)(2,1)}) custom-call(s32[128,64]{1,0:T(8,128)} %bitcast.29, bf16[8192,128]{1,0:T(8,128)(2,1)} %bitcast.26), custom_call_target="tpu_custom_call" | custom-call | tf_op jit(solution)/shard_map/slot_sums/pallas_call | solution.py:261
  106.5 35.4 %all_to_all.15 = bf16[128,64,128]{2,1,0:T(8,128)(2,1)} all-to-all(bf16[128,64,128]{2,1,0:T(8,128)(2,1)} %bitcast.28), channel_id=1, replica_groups=mesh['exp'=8,'tile'=16] {'exp','tile'}, dimensions={0} | all-to-all | bytes 4194304 | tf_op jit(solution)/shard_map/all_to_all | solution.py:530
  141.8 0.0 copy-start.9
  141.8 5.0 %all-to-all-start.1 = ((bf16[128,64,128]{2,1,0:T(8,128)(2,1)}), bf16[128,64,128]{2,1,0:T(8,128)(2,1)S(1)}, u32[]{:S(2)}, u32[]{:S(2)}) async-start(bf16[128,64,128]{2,1,0:T(8,128)(2,1)} %bitcast.27), calls=%async_computation.1 | async-start | bytes 4194304 | tf_op jit(solution)/shard_map/all_to_all | solution.py:530
  146.9 0.0 copy-done.9
  146.9 0.1 reshape.42
  147.0 0.1 eq.30
  147.0 0.1 eq.34
  147.1 0.1 broadcast_in_dim.25
  147.2 0.1 broadcast_in_dim.26
  147.3 2.7 %fusion.8 = f32[128,64]{1,0:T(8,128)S(1)} fusion(f32[8192]{0:T(1024)S(1)} %broadcast_in_dim.26, s32[8192]{0:T(1024)S(1)} %eq.30, s32[8192]{0:T(1024)S(1)} %eq.34), kind=kOutput, calls=%fused_computation.9 | convolution fusion | flops 807944192 | bytes 131072 | tf_op jit(solution)/shard_map/dot_general | solution.py:574
  149.9 0.1 reshape.50
  150.0 0.7 fusion.12
  150.7 1.3 gather_fusion
  152.0 8.7 %unwarp.1 = (bf16[256,4096]{1,0:T(8,128)(2,1)}, bf16[16,4096]{1,0:T(8,128)(2,1)}, bf16[16,4096]{1,0:T(8,128)(2,1)}) custom-call(s32[1,64]{1,0:T(1,128)} %constant_dynamic-slice_fusion.2.ident_ref, f32[1,64]{1,0:T(1,128)} %bitcast.31, bf16[8192,128]{1,0:T(8,128)(2,1)} %bitcast.25, bf16[64,128,128]{2,1,0:T(8,128)(2,1)} %bank_rows_ref.3, ...), custom_call_target="tpu_custom_call" | custom-call | tf_op jit(solution)/shard_map/unwarp/pallas_call | solution.py:336
  160.7 3.4 %collective-permute-start.2 = (bf16[16,4096]{1,0:T(8,128)(2,1)}, bf16[16,4096]{1,0:T(8,128)(2,1)S(1)}, u32[]{:S(2)}, u32[]{:S(2)}) collective-permute-start(bf16[16,4096]{1,0:T(8,128)(2,1)} %get-tuple-element.13), channel_id=1, source_target_pairs={{0,1},{1,2},{2,3},{3,4},{4,5},{5,6},{6,7},{7,8},{8,9},{9,10},{10,1... | collective-permute-start | bytes 393224 | tf_op jit(solution)/shard_map/ppermute | solution.py:70
  164.1 4.7 %collective-permute-start.3 = (bf16[16,4096]{1,0:T(8,128)(2,1)}, bf16[16,4096]{1,0:T(8,128)(2,1)S(1)}, u32[]{:S(2)}, u32[]{:S(2)}) collective-permute-start(bf16[16,4096]{1,0:T(8,128)(2,1)} %get-tuple-element.15), channel_id=1, source_target_pairs={{1,0},{2,1},{3,2},{4,3},{5,4},{6,5},{7,6},{8,7},{9,8},{10,9},{11,1... | collective-permute-start | bytes 393224 | tf_op jit(solution)/shard_map/ppermute | solution.py:70
  168.8 0.6 constant_dynamic-slice_fusion.3.scale_ref
  169.4 9.1 %subtract_inner.1.partial_ref = f32[256,4096]{1,0:T(8,128)} custom-call(f32[1,3]{1,0:T(1,128)} %coef_ref.5, bf16[256,4096]{1,0:T(8,128)(2,1)} %get-tuple-element.14.image_ref.top_ref.bottom_ref, bf16[256,4096]{1,0:T(8,128)(2,1)} %bitcast.19, bf16[384,160]{1,0:T(8,128)(2,1)} %get-tuple-element.9.rows_ref, bf16[1536,256]{1,0:T(8,128)(2,1)} %get-tuple-element.10.columns_ref), custom_call_target="tpu_custom_call" | custom-call | tf_op jit(solution)/shard_map/subtract_inner/pallas_call | solution.py:399
  178.6 0.0 all-to-all-done.1
  178.6 0.0 copy-start.1
  178.6 1.3 copy-done.1
  179.9 4.3 %patch.1 = f32[1024,1024]{1,0:T(8,128)} custom-call(f32[1,64]{1,0:T(1,128)} %constant_dynamic-slice_fusion.3.scale_ref, bf16[8192,128]{1,0:T(8,128)(2,1)} %bitcast.23), custom_call_target="tpu_custom_call" | custom-call | tf_op jit(solution)/shard_map/patch/pallas_call | solution.py:513
  184.2 0.0 collective-permute-done.2.above_ref
  184.2 0.0 copy-start.7
  184.2 0.0 collective-permute-done.3.below_ref
  184.2 0.6 copy-done.7
  184.8 0.0 copy-start.8
  184.9 0.6 copy-done.8
  185.5 3.8 %subtract_outer.1 = f32[256,4096]{1,0:T(8,128)} custom-call(f32[1,3]{1,0:T(1,128)} %coef_ref.5, bf16[16,4096]{1,0:T(8,128)(2,1)} %copy-done.7, bf16[256,4096]{1,0:T(8,128)(2,1)} %get-tuple-element.14.image_ref.top_ref.bottom_ref, bf16[256,4096]{1,0:T(8,128)(2,1)} %get-tuple-element.14.image_ref.top_ref.bottom_ref, ...), custom_call_target="tpu_custom_call", output_to_operand_aliasing={{}: (9, {})} | custom-call | tf_op jit(solution)/shard_map/subtract_outer/pallas_call | solution.py:465
  (1 shorter events, 0.0 us)
Async XLA Ops:
  0.6 15.4 %copy-start = (s32[8,16,64]{2,1,0:T(8,128)S(1)}, s32[8,16,64]{2,1,0:T(8,128)}, u32[]{:S(2)}) copy-start(s32[8,16,64]{2,1,0:T(8,128)} %param.16) | copy-start | bytes 98308
  1.7 14.8 %collective-permute-start = (bf16[16,4096]{1,0:T(8,128)(2,1)S(1)}, bf16[16,4096]{1,0:T(8,128)(2,1)S(1)}, u32[]{:S(2)}, u32[]{:S(2)}) collective-permute-start(bf16[16,4096]{1,0:T(8,128)(2,1)S(1)} %get-tuple-element.17), channel_id=1, source_target_pairs={{0,1},{1,2},{2,3},{3,4},{4,5},{5,6},{6,7},{7,8},{8,9},{9,10},{10,1... | collective-permute-start | bytes 393224 | tf_op jit(solution)/shard_map/ppermute | solution.py:70
  5.1 11.4 %collective-permute-start.1 = (bf16[16,4096]{1,0:T(8,128)(2,1)S(1)}, bf16[16,4096]{1,0:T(8,128)(2,1)S(1)}, u32[]{:S(2)}, u32[]{:S(2)}) collective-permute-start(bf16[16,4096]{1,0:T(8,128)(2,1)S(1)} %get-tuple-element.16), channel_id=1, source_target_pairs={{1,0},{2,1},{3,2},{4,3},{5,4},{6,5},{7,6},{8,7},{9,8},{10,9},{11,1... | collective-permute-start | bytes 393224 | tf_op jit(solution)/shard_map/ppermute | solution.py:70
  16.5 0.7 copy-start.5
  16.5 0.7 copy-start.6
  42.5 8.4 %copy-start.3 = (s32[8,16,64]{2,1,0:T(8,128)S(1)}, s32[8,16,64]{2,1,0:T(8,128)}, u32[]{:S(2)}) copy-start(s32[8,16,64]{2,1,0:T(8,128)} %param.17) | copy-start | bytes 98308
  42.5 8.4 %copy-start.4 = (s32[8,16,64]{2,1,0:T(8,128)S(1)}, s32[8,16,64]{2,1,0:T(8,128)}, u32[]{:S(2)}) copy-start(s32[8,16,64]{2,1,0:T(8,128)} %param.18) | copy-start | bytes 98308
  42.5 37.8 %all-to-all-start = ((bf16[128,64,128]{2,1,0:T(8,128)(2,1)}), bf16[128,64,128]{2,1,0:T(8,128)(2,1)S(1)}, u32[]{:S(2)}, u32[]{:S(2)}) async-start(bf16[128,64,128]{2,1,0:T(8,128)(2,1)} %bitcast.24), calls=%async_computation | async-start | bytes 4194304 | tf_op jit(solution)/shard_map/all_to_all | solution.py:530
  80.3 1.3 copy-start.2
  141.8 5.0 %copy-start.9 = (f32[8,16]{1,0:T(8,128)S(1)}, f32[8,16]{1,0:T(8,128)}, u32[]{:S(2)}) copy-start(f32[8,16]{1,0:T(8,128)} %param.19) | copy-start | bytes 1540
  141.8 36.7 %all-to-all-start.1 = ((bf16[128,64,128]{2,1,0:T(8,128)(2,1)}), bf16[128,64,128]{2,1,0:T(8,128)(2,1)S(1)}, u32[]{:S(2)}, u32[]{:S(2)}) async-start(bf16[128,64,128]{2,1,0:T(8,128)(2,1)} %bitcast.27), calls=%async_computation.1 | async-start | bytes 4194304 | tf_op jit(solution)/shard_map/all_to_all | solution.py:530
  160.7 23.5 %collective-permute-start.2 = (bf16[16,4096]{1,0:T(8,128)(2,1)}, bf16[16,4096]{1,0:T(8,128)(2,1)S(1)}, u32[]{:S(2)}, u32[]{:S(2)}) collective-permute-start(bf16[16,4096]{1,0:T(8,128)(2,1)} %get-tuple-element.13), channel_id=1, source_target_pairs={{0,1},{1,2},{2,3},{3,4},{4,5},{5,6},{6,7},{7,8},{8,9},{9,10},{10,1... | collective-permute-start | bytes 393224 | tf_op jit(solution)/shard_map/ppermute | solution.py:70
  164.1 20.1 %collective-permute-start.3 = (bf16[16,4096]{1,0:T(8,128)(2,1)}, bf16[16,4096]{1,0:T(8,128)(2,1)S(1)}, u32[]{:S(2)}, u32[]{:S(2)}) collective-permute-start(bf16[16,4096]{1,0:T(8,128)(2,1)} %get-tuple-element.15), channel_id=1, source_target_pairs={{1,0},{2,1},{3,2},{4,3},{5,4},{6,5},{7,6},{8,7},{9,8},{10,9},{11,1... | collective-permute-start | bytes 393224 | tf_op jit(solution)/shard_map/ppermute | solution.py:70
  178.6 1.3 copy-start.1
  184.2 0.6 copy-start.7
  184.8 0.6 copy-start.8

commit v2 on v1

v2 whole, which is shorter than its diff:
```python
import functools

import jax
import jax.numpy as jnp
from jax import lax
from jax.experimental import pallas as pl
from jax.experimental.pallas import tpu as pltpu
from jax.sharding import PartitionSpec as P

BLOCK = 128
HALF = 10
RIM = 16
CHUNK = 256
WIDE = 512
SPAN = CHUNK + 2 * BLOCK
WINDOW = BLOCK + 2 * RIM
HALVES = 2
LEFT = 3
SLOT_ROWS = 8
SLOT_COLS = 8
LANES = 4
PAD = 8
VMEM_BYTES = 60 * 1024 * 1024
VMEM = pl.BlockSpec(memory_space=pltpu.VMEM)
SMEM = pl.BlockSpec(memory_space=pltpu.SMEM)
ANY = pl.BlockSpec(memory_space=pl.ANY)
PARAMS = pltpu.CompilerParams(vmem_limit_bytes=VMEM_BYTES)


def bands_kernel(row_taps_ref, column_taps_ref, rows_ref, columns_ref):
    bases, taps = row_taps_ref.shape
    lead = RIM - HALF

    def banded(taps_ref, offsets):
        bands = [jnp.zeros(offsets.shape, jnp.float32) for _ in range(bases)]
        for tap in range(taps):
            hit = offsets == tap
            bands = [jnp.where(hit, taps_ref[base, tap], bands[base]) for base in range(bases)]
        return [band.astype(jnp.bfloat16) for band in bands]

    shape = (BLOCK, WINDOW)
    across = lax.broadcasted_iota(jnp.int32, shape, 1) - lax.broadcasted_iota(jnp.int32, shape, 0)
    for base, band in enumerate(banded(row_taps_ref, across - lead)):
        rows_ref[base * BLOCK : (base + 1) * BLOCK, :] = band
    shape = (WINDOW, BLOCK)
    down = lax.broadcasted_iota(jnp.int32, shape, 0) - lax.broadcasted_iota(jnp.int32, shape, 1)
    columns_ref[...] = jnp.zeros_like(columns_ref)
    for base, band in enumerate(banded(column_taps_ref, down - lead)):
        for part in range(CHUNK // BLOCK):
            top = base * SPAN + (part + 1) * BLOCK - RIM
            columns_ref[top : top + WINDOW, part * BLOCK : (part + 1) * BLOCK] = band


def band_matrices(row_taps, column_taps):
    bases = row_taps.shape[0]
    return pl.pallas_call(
        bands_kernel,
        out_shape=(
            jax.ShapeDtypeStruct((bases * BLOCK, WINDOW), jnp.bfloat16),
            jax.ShapeDtypeStruct((bases * SPAN, CHUNK), jnp.bfloat16),
        ),
        in_specs=[SMEM, SMEM],
        out_specs=(VMEM, VMEM),
        name="bands",
    )(row_taps.astype(jnp.float32), column_taps.astype(jnp.float32))


def swap_rims(top, bottom):
    count = lax.axis_size("tile")
    forward = [(i, i + 1) for i in range(count - 1)]
    backward = [(target, source) for source, target in forward]
    return lax.ppermute(bottom, "tile", forward), lax.ppermute(top, "tile", backward)


def clear(pass_ref, start):
    bases, height, _ = pass_ref.shape
    pass_ref[:, :, start : start + BLOCK] = jnp.zeros((bases, height, BLOCK), pass_ref.dtype)


def row_step(lanes, start, to, strips, coef_ref, rows_ref, pass_ref):
    bases = pass_ref.shape[0]
    for first_row, count, pieces in strips:
        window = [
            ref[first : first + size, pl.ds(pl.multiple_of(start + shift, BLOCK), lanes)]
            for ref, first, size, shift in pieces
        ]
        window = window[0] if len(window) == 1 else jnp.concatenate(window, axis=0)
        depth = window.shape[0]
        if count == BLOCK and depth == WINDOW:
            band = rows_ref[...]
        else:
            band = jnp.concatenate(
                [rows_ref[base * BLOCK : base * BLOCK + count, :depth] for base in range(bases)],
                axis=0,
            )
        summed = jnp.dot(band, window, preferred_element_type=jnp.float32)
        for base in range(bases):
            pass_ref[
                base, first_row : first_row + count, pl.ds(pl.multiple_of(to, BLOCK), lanes)
            ] = (coef_ref[0, base] * summed[base * count : (base + 1) * count]).astype(jnp.bfloat16)


def column_step(index, count, columns_ref, pass_ref):
    bases = pass_ref.shape[0]
    parts = []
    for part in range(WIDE // CHUNK):
        window = pl.ds(pl.multiple_of(index * WIDE + part * CHUNK, CHUNK), SPAN)
        parts.append(
            jnp.concatenate([pass_ref[base, :count, window] for base in range(bases)], axis=1)
        )
    summed = jnp.dot(
        jnp.concatenate(parts, axis=0), columns_ref[...], preferred_element_type=jnp.float32
    )
    return [summed[part * count : (part + 1) * count] for part in range(WIDE // CHUNK)]


def forward_kernel(
    ident_ref,
    weight_ref,
    coef_ref,
    above_ref,
    image_hbm,
    below_ref,
    rows_ref,
    columns_ref,
    bank_rows_ref,
    bank_columns_ref,
    out_ref,
    image_ref,
    pass_ref,
    matched_ref,
    turned_ref,
    warp_rows_ref,
    warp_columns_ref,
    sems,
    *,
    half,
):
    tile_rows, width = image_hbm.shape
    part_width = width // HALVES
    parts = tile_rows // BLOCK
    across = part_width // BLOCK
    items = parts * across
    pitch = items + PAD
    wides = part_width // WIDE
    low = max(half * part_width - BLOCK, 0)
    high = min((half + 1) * part_width + BLOCK, width)
    offset = half * part_width - BLOCK
    fetch = pltpu.make_async_copy(
        image_hbm.at[:, low:high], image_ref.at[:, low - offset : high - offset], sems.at[0]
    )
    loads = [
        pltpu.make_async_copy(bank_rows_ref, warp_rows_ref, sems.at[1]),
        pltpu.make_async_copy(bank_columns_ref, warp_columns_ref, sems.at[2]),
    ]
    fetch.start()
    for load in loads:
        load.start()
    fetch.wait()

    strips = [
        (0, BLOCK, [(above_ref, 0, RIM, offset), (image_ref, 0, BLOCK + RIM, 0)]),
        (
            BLOCK,
            BLOCK,
            [(image_ref, BLOCK - RIM, BLOCK + RIM, 0), (below_ref, 0, RIM, offset)],
        ),
    ]
    step = functools.partial(
        row_step, strips=strips, coef_ref=coef_ref, rows_ref=rows_ref, pass_ref=pass_ref
    )
    if low == offset:
        step(BLOCK, 0, 0)
    else:
        clear(pass_ref, 0)
    last = BLOCK + part_width
    if high == (half + 1) * part_width + BLOCK:
        step(BLOCK, last, last)
    else:
        clear(pass_ref, last)

    def wide_step(index):
        step(WIDE, BLOCK + index * WIDE, BLOCK + index * WIDE)

    def match_step(index):
        for inner, summed in enumerate(column_step(index, tile_rows, columns_ref, pass_ref)):
            matched_ref[:, pl.ds(pl.multiple_of(index * WIDE + inner * CHUNK, CHUNK), CHUNK)] = (
                summed.astype(jnp.bfloat16)
            )

    wide_step(0)
    wide_step(1)

    @pl.loop(0, wides - 2)
    def _(index):
        match_step(index)
        wide_step(index + 2)

    @pl.loop(wides - 2, wides)
    def _(index):
        match_step(index)

    for load in loads:
        load.wait()

    @pl.loop(0, across // 4)
    def _(quad):
        todo = []
        for part in range(parts):
            for inner in range(4):
                column = quad * 4 + inner
                ident = ident_ref[0, part * (across * HALVES) + half * across + column]
                piece = matched_ref[
                    part * BLOCK : (part + 1) * BLOCK,
                    pl.ds(pl.multiple_of(column * BLOCK, BLOCK), BLOCK),
                ]
                todo.append((part * across + column, ident, piece))
        todo = [
            (
                item,
                ident,
                jnp.dot(warp_rows_ref[ident], piece, preferred_element_type=jnp.float32).astype(
                    jnp.bfloat16
                ),
            )
            for item, ident, piece in todo
        ]
        todo = [
            (
                item,
                lax.dot_general(
                    first,
                    warp_columns_ref[ident],
                    (((1,), (1,)), ((), ())),
                    preferred_element_type=jnp.float32,
                ),
            )
            for item, ident, first in todo
        ]
        for item, second in todo:
            turned_ref[pl.ds(item, BLOCK, stride=pitch), :] = weight_ref[0, 0] * second

    @pl.loop(0, BLOCK, unroll=4)
    def _(row):
        to = pl.ds(pl.multiple_of(row * items, items), items)
        at = pl.ds(pl.multiple_of(row * pitch, PAD), items)
        out_ref[to, :] = turned_ref[at, :].astype(jnp.bfloat16)


def forward(half, ident, weight, coef, above, image, below, rows, columns, warp_rows, warp_columns):
    tile_rows, width = image.shape
    bases = rows.shape[0] // BLOCK
    part_width = width // HALVES
    lines = tile_rows * part_width // BLOCK
    return pl.pallas_call(
        functools.partial(forward_kernel, half=half),
        out_shape=jax.ShapeDtypeStruct((lines, BLOCK), jnp.bfloat16),
        in_specs=[SMEM, SMEM, SMEM, VMEM, ANY, VMEM, VMEM, VMEM, ANY, ANY],
        out_specs=VMEM,
        scratch_shapes=[
            pltpu.VMEM((tile_rows, part_width + 2 * BLOCK), jnp.bfloat16),
            pltpu.VMEM((bases, tile_rows, part_width + 2 * BLOCK), jnp.bfloat16),
            pltpu.VMEM((tile_rows, part_width), jnp.bfloat16),
            pltpu.VMEM((lines + BLOCK * PAD, BLOCK), jnp.float32),
            pltpu.VMEM(warp_rows.shape, jnp.bfloat16),
            pltpu.VMEM(warp_columns.shape, jnp.bfloat16),
            pltpu.SemaphoreType.DMA((3,)),
        ],
        compiler_params=PARAMS,
        name=f"match_warp_{half}",
    )(ident, weight, coef, above, image, below, rows, columns, warp_rows, warp_columns)


def table_columns(half, per_tile, across):
    items = per_tile // HALVES
    here = across // HALVES
    return [item // here * across + half * here + item % here for item in range(items)]


def add_rows(slot_ref, table, arrived_ref, wide_ref, sums):
    sources = slot_ref.shape[0]
    items = len(table)
    slots_each = wide_ref.shape[0] // sources

    def at(source, count):
        return pl.ds(pl.multiple_of(source * count, count), count)

    @pl.loop(0, sources)
    def _(source):
        wide_ref[at(source, slots_each), :] = arrived_ref[at(source, slots_each), :].astype(
            jnp.float32
        )
        for sum_ref in sums:
            count = sum_ref.shape[0] // sources
            sum_ref[at(source, count), :] = jnp.zeros((count, BLOCK), jnp.float32)

    @pl.loop(0, sources)
    def _(source):
        for first in range(0, items, len(sums)):
            slots = [slot_ref[source, table[first + lane]] for lane in range(len(sums))]
            values = [
                sum_ref[pl.ds(slot, 1), :] + wide_ref[pl.ds(source * items + first + lane, 1), :]
                for lane, (slot, sum_ref) in enumerate(zip(slots, sums))
            ]
            for slot, sum_ref, value in zip(slots, sums, values):
                sum_ref[pl.ds(slot, 1), :] = value


def take_rows(slot_ref, table, value_ref, wide_ref, out_ref):
    sources = slot_ref.shape[0]
    items = len(table)

    @pl.loop(0, sources)
    def _(source):
        for item in range(items):
            slot = slot_ref[source, table[item]]
            wide_ref[pl.ds(source * items + item, 1), :] = value_ref[pl.ds(slot, 1), :]

    @pl.loop(0, sources, unroll=2)
    def _(source):
        at = pl.ds(pl.multiple_of(source * items, items), items)
        out_ref[at, :] = wide_ref[at, :].astype(jnp.bfloat16)


def early_kernel(slot_ref, arrived_ref, sum_ref, wide_ref, *sums, table):
    add_rows(slot_ref, table, arrived_ref, wide_ref, sums)

    @pl.loop(0, sum_ref.shape[0] // BLOCK)
    def _(group):
        at = pl.ds(pl.multiple_of(group * BLOCK, BLOCK), BLOCK)
        value = sums[0][at, :]
        for other in sums[1:]:
            value = value + other[at, :]
        sum_ref[at, :] = value


def early_sums(slots, arrived, across, slot_total):
    table = table_columns(0, slots.shape[1], across)
    return pl.pallas_call(
        functools.partial(early_kernel, table=table),
        out_shape=jax.ShapeDtypeStruct((slot_total, BLOCK), jnp.float32),
        in_specs=[SMEM, VMEM],
        out_specs=VMEM,
        scratch_shapes=[pltpu.VMEM(arrived.shape, jnp.float32)]
        + [pltpu.VMEM((slot_total, BLOCK), jnp.float32)] * LANES,
        compiler_params=PARAMS,
        name="early_sums",
    )(slots, arrived)


def late_kernel(
    slot_ref, arrived_ref, early_ref, template_ref, coadd_ref, wide_ref, *sums, tables
):
    add_rows(slot_ref, tables[1], arrived_ref, wide_ref, sums)

    @pl.loop(0, early_ref.shape[0] // BLOCK)
    def _(group):
        at = pl.ds(pl.multiple_of(group * BLOCK, BLOCK), BLOCK)
        value = early_ref[at, :]
        for other in sums:
            value = value + other[at, :]
        sums[0][at, :] = value
        coadd_ref[at, :] = value.astype(jnp.bfloat16)

    take_rows(slot_ref, tables[0], sums[0], wide_ref, template_ref)


def late_sums(slots, arrived, early, across):
    tables = [table_columns(half, slots.shape[1], across) for half in range(HALVES)]
    return pl.pallas_call(
        functools.partial(late_kernel, tables=tables),
        out_shape=(
            jax.ShapeDtypeStruct(arrived.shape, jnp.bfloat16),
            jax.ShapeDtypeStruct(early.shape, jnp.bfloat16),
        ),
        in_specs=[SMEM, VMEM, VMEM],
        out_specs=(VMEM, VMEM),
        scratch_shapes=[pltpu.VMEM(arrived.shape, jnp.float32)]
        + [pltpu.VMEM(early.shape, jnp.float32)] * LANES,
        compiler_params=PARAMS,
        name="late_sums",
    )(slots, arrived, early)


def more_kernel(slot_ref, coadd_ref, template_ref, value_ref, wide_ref, *, table):
    @pl.loop(0, value_ref.shape[0] // BLOCK)
    def _(group):
        at = pl.ds(pl.multiple_of(group * BLOCK, BLOCK), BLOCK)
        value_ref[at, :] = coadd_ref[at, :].astype(jnp.float32)

    take_rows(slot_ref, table, value_ref, wide_ref, template_ref)


def more_rows(slots, coadd, across):
    table = table_columns(1, slots.shape[1], across)
    shape = (slots.shape[0] * len(table), BLOCK)
    return pl.pallas_call(
        functools.partial(more_kernel, table=table),
        out_shape=jax.ShapeDtypeStruct(shape, jnp.bfloat16),
        in_specs=[SMEM, VMEM],
        out_specs=VMEM,
        scratch_shapes=[pltpu.VMEM(coadd.shape, jnp.float32), pltpu.VMEM(shape, jnp.float32)],
        compiler_params=PARAMS,
        name="more_rows",
    )(slots, coadd)


def unwarp_kernel(
    ident_ref,
    scale_ref,
    returned_ref,
    bank_rows_ref,
    bank_columns_ref,
    out_ref,
    top_ref,
    bottom_ref,
    wide_ref,
    warp_rows_ref,
    warp_columns_ref,
    sems,
    *,
    half,
):
    tile_rows, part_width = out_ref.shape
    across = part_width // BLOCK
    parts = tile_rows // BLOCK
    items = parts * across
    pitch = items + PAD
    loads = [
        pltpu.make_async_copy(bank_rows_ref, warp_rows_ref, sems.at[0]),
        pltpu.make_async_copy(bank_columns_ref, warp_columns_ref, sems.at[1]),
    ]
    for load in loads:
        load.start()

    @pl.loop(0, BLOCK, unroll=4)
    def _(row):
        to = pl.ds(pl.multiple_of(row * pitch, PAD), items)
        at = pl.ds(pl.multiple_of(row * items, items), items)
        wide_ref[to, :] = returned_ref[at, :].astype(jnp.float32)

    for load in loads:
        load.wait()

    @pl.loop(0, across // 4)
    def _(quad):
        todo = []
        for part in range(parts):
            for inner in range(4):
                column = quad * 4 + inner
                item = part * across + column
                block = part * (across * HALVES) + half * across + column
                ident = ident_ref[0, block]
                numerator = wide_ref[pl.ds(item, BLOCK, stride=pitch), :].astype(jnp.bfloat16)
                todo.append((part, column, block, ident, numerator))
        todo = [
            (
                part,
                column,
                ident,
                scale_ref[0, block]
                * lax.dot_general(
                    warp_rows_ref[ident],
                    numerator,
                    (((0,), (0,)), ((), ())),
                    preferred_element_type=jnp.float32,
                ),
            )
            for part, column, block, ident, numerator in todo
        ]
        for part, column, ident, first in todo:
            image = jnp.dot(
                first.astype(jnp.bfloat16),
                warp_columns_ref[ident],
                preferred_element_type=jnp.float32,
            ).astype(jnp.bfloat16)
            to = pl.ds(pl.multiple_of(column * BLOCK, BLOCK), BLOCK)
            out_ref[part * BLOCK : (part + 1) * BLOCK, to] = image
            if part == 0:
                top_ref[:, to] = image[:RIM]
            if part == parts - 1:
                bottom_ref[:, to] = image[BLOCK - RIM :]


def unwarp(half, ident, scale, returned, warp_rows, warp_columns, tile_rows):
    lines = returned.shape[0]
    part_width = lines * BLOCK // tile_rows
    rim = jax.ShapeDtypeStruct((RIM, part_width), jnp.bfloat16)
    return pl.pallas_call(
        functools.partial(unwarp_kernel, half=half),
        out_shape=(jax.ShapeDtypeStruct((tile_rows, part_width), jnp.bfloat16), rim, rim),
        in_specs=[SMEM, SMEM, VMEM, ANY, ANY],
        out_specs=(VMEM, VMEM, VMEM),
        scratch_shapes=[
            pltpu.VMEM((lines + BLOCK * PAD, BLOCK), jnp.float32),
            pltpu.VMEM(warp_rows.shape, jnp.bfloat16),
            pltpu.VMEM(warp_columns.shape, jnp.bfloat16),
            pltpu.SemaphoreType.DMA((2,)),
        ],
        compiler_params=PARAMS,
        name=f"unwarp_{half}",
    )(ident, scale, returned, warp_rows, warp_columns)


def inner_strips(image_ref):
    tile_rows = image_ref.shape[0]
    rest = tile_rows - 2 * RIM - BLOCK
    return [
        (0, BLOCK, [(image_ref, 0, WINDOW, 0)]),
        (BLOCK, rest, [(image_ref, BLOCK, tile_rows - BLOCK, 0)]),
    ]


def inner_parts(first, coef_ref, exposure_hbm, rows_ref, columns_ref, out_ref, refs):
    exposure_ref, pass_ref, stage_ref, sems = refs
    inner, width = stage_ref.shape
    fetch = pltpu.make_async_copy(
        exposure_hbm.at[pl.ds(RIM, inner), pl.ds(first, width)], exposure_ref, sems.at[0]
    )

    def store(index):
        at = pl.multiple_of(index * WIDE, WIDE)
        return pltpu.make_async_copy(
            stage_ref.at[:, pl.ds(at, WIDE)],
            out_ref.at[pl.ds(RIM, inner), pl.ds(first + at, WIDE)],
            sems.at[1 + index],
        )

    def step(image_ref):
        return functools.partial(
            row_step,
            strips=inner_strips(image_ref),
            coef_ref=coef_ref,
            rows_ref=rows_ref,
            pass_ref=pass_ref,
        )

    def subtract_step(index):
        for half, summed in enumerate(column_step(index, inner, columns_ref, pass_ref)):
            at = pl.ds(pl.multiple_of(index * WIDE + half * CHUNK, CHUNK), CHUNK)
            stage_ref[:, at] = exposure_ref[:, at].astype(jnp.float32) - summed
        store(index).start()

    return fetch, step, subtract_step, store


def inner_left_kernel(
    coef_ref, left_ref, exposure_hbm, rows_ref, columns_ref, out_ref, *refs
):
    fetch, step, subtract_step, store = inner_parts(
        0, coef_ref, exposure_hbm, rows_ref, columns_ref, out_ref, refs
    )
    pass_ref = refs[1]
    fetch.start()
    clear(pass_ref, 0)
    step = step(left_ref)

    @pl.loop(0, LEFT)
    def _(index):
        step(WIDE, index * WIDE, BLOCK + index * WIDE)

    step(BLOCK, LEFT * WIDE, BLOCK + LEFT * WIDE)
    fetch.wait()

    @pl.loop(0, LEFT)
    def _(index):
        subtract_step(index)

    @pl.loop(0, LEFT)
    def _(index):
        store(index).wait()


def inner_right_kernel(
    coef_ref, left_ref, right_ref, exposure_hbm, rows_ref, columns_ref, partial_ref, out_ref, *refs
):
    del partial_ref
    first = LEFT * WIDE
    fetch, step, subtract_step, store = inner_parts(
        first, coef_ref, exposure_hbm, rows_ref, columns_ref, out_ref, refs
    )
    pass_ref = refs[1]
    half_width = left_ref.shape[1]
    ahead = half_width - first
    wides = right_ref.shape[1] // WIDE
    total = wides + ahead // WIDE
    fetch.start()
    clear(pass_ref, pass_ref.shape[2] - BLOCK)
    step(left_ref)(BLOCK + ahead, first - BLOCK, 0)
    step = step(right_ref)
    base = BLOCK + ahead
    step(WIDE, 0, base)
    fetch.wait()

    @pl.loop(0, wides - 1)
    def _(index):
        subtract_step(index)
        step(WIDE, (index + 1) * WIDE, base + (index + 1) * WIDE)

    @pl.loop(wides - 1, total)
    def _(index):
        subtract_step(index)

    @pl.loop(0, total)
    def _(index):
        store(index).wait()


def inner_call(kernel, name, width, images, coef, exposure, rows, columns, partial):
    tile_rows = exposure.shape[0]
    bases = rows.shape[0] // BLOCK
    inner = tile_rows - 2 * RIM
    more = [] if partial is None else [partial]
    operands = [coef, *images, exposure, rows, columns, *more]
    return pl.pallas_call(
        kernel,
        out_shape=jax.ShapeDtypeStruct(exposure.shape, jnp.float32),
        in_specs=[SMEM] + [VMEM] * len(images) + [ANY, VMEM, VMEM] + [ANY] * len(more),
        out_specs=ANY,
        scratch_shapes=[
            pltpu.VMEM((inner, width), jnp.bfloat16),
            pltpu.VMEM((bases, inner, width + 2 * BLOCK), jnp.bfloat16),
            pltpu.VMEM((inner, width), jnp.float32),
            pltpu.SemaphoreType.DMA((1 + width // WIDE,)),
        ],
        input_output_aliases={len(operands) - 1: 0} if more else {},
        compiler_params=PARAMS,
        name=name,
    )(*operands)


def outer_kernel(
    coef_ref,
    above_left_ref,
    above_right_ref,
    top_left_ref,
    top_right_ref,
    bottom_left_ref,
    bottom_right_ref,
    below_left_ref,
    below_right_ref,
    exposure_top_ref,
    exposure_bottom_ref,
    rows_ref,
    columns_ref,
    partial_ref,
    out_ref,
    pass_ref,
    stage_ref,
    sems,
):
    del partial_ref
    tile_rows, width = out_ref.shape
    clear(pass_ref, 0)
    clear(pass_ref, BLOCK + width)
    done = 0
    for above_ref, top_ref, bottom_ref, below_ref in (
        (above_left_ref, top_left_ref, bottom_left_ref, below_left_ref),
        (above_right_ref, top_right_ref, bottom_right_ref, below_right_ref),
    ):
        strips = [
            (0, RIM, [(above_ref, 0, RIM, 0), (top_ref, 0, 2 * RIM, 0)]),
            (RIM, RIM, [(bottom_ref, 0, 2 * RIM, 0), (below_ref, 0, RIM, 0)]),
        ]
        for index in range(top_ref.shape[1] // WIDE):
            row_step(
                WIDE, index * WIDE, BLOCK + done * WIDE, strips, coef_ref, rows_ref, pass_ref
            )
            done += 1
    for index in range(width // WIDE):
        for half, summed in enumerate(column_step(index, 2 * RIM, columns_ref, pass_ref)):
            at = pl.ds(index * WIDE + half * CHUNK, CHUNK)
            stage_ref[:RIM, at] = exposure_top_ref[:, at].astype(jnp.float32) - summed[:RIM]
            stage_ref[RIM:, at] = exposure_bottom_ref[:, at].astype(jnp.float32) - summed[RIM:]
    stores = [
        pltpu.make_async_copy(stage_ref.at[:RIM], out_ref.at[:RIM], sems.at[0]),
        pltpu.make_async_copy(
            stage_ref.at[RIM:], out_ref.at[pl.ds(tile_rows - RIM, RIM)], sems.at[1]
        ),
    ]
    for store in stores:
        store.start()
    for store in stores:
        store.wait()


def subtract_outer(coef, above, images, below, exposure, rows, columns, partial):
    tile_rows, width = exposure.shape
    bases = rows.shape[0] // BLOCK
    part_width = images[0].shape[1]
    rim = pl.BlockSpec((RIM, width), lambda _: (0, 0))
    last_rim = pl.BlockSpec((RIM, width), lambda _: (tile_rows // RIM - 1, 0))
    pair = pl.BlockSpec((2 * RIM, part_width), lambda _: (0, 0))
    last_pair = pl.BlockSpec((2 * RIM, part_width), lambda _: (tile_rows // (2 * RIM) - 1, 0))
    specs = [SMEM, VMEM, VMEM, pair, pair, last_pair, last_pair, VMEM, VMEM, rim, last_rim]
    return pl.pallas_call(
        outer_kernel,
        out_shape=jax.ShapeDtypeStruct((tile_rows, width), jnp.float32),
        grid=(1,),
        in_specs=specs + [VMEM, VMEM, ANY],
        out_specs=ANY,
        scratch_shapes=[
            pltpu.VMEM((bases, 2 * RIM, width + 2 * BLOCK), jnp.bfloat16),
            pltpu.VMEM((2 * RIM, width), jnp.float32),
            pltpu.SemaphoreType.DMA((2,)),
        ],
        input_output_aliases={13: 0},
        compiler_params=PARAMS,
        name="subtract_outer",
    )(coef, *above, *images, *images, *below, exposure, exposure, rows, columns, partial)


def patch_kernel(scale_ref, rows_ref, out_ref, wide_ref, stage_ref, sems):
    slots = SLOT_ROWS * SLOT_COLS
    pitch = slots + PAD

    @pl.loop(0, BLOCK, unroll=2)
    def _(row):
        to = pl.ds(pl.multiple_of(row * pitch, PAD), slots)
        at = pl.ds(pl.multiple_of(row * slots, slots), slots)
        wide_ref[to, :] = rows_ref[at, :].astype(jnp.float32)

    def store(down):
        at = pl.ds(pl.multiple_of(down * BLOCK, BLOCK), BLOCK)
        return pltpu.make_async_copy(stage_ref.at[at], out_ref.at[at], sems.at[down])

    @pl.loop(0, SLOT_ROWS)
    def _(down):
        to = pl.ds(pl.multiple_of(down * BLOCK, BLOCK), BLOCK)
        for across in range(SLOT_COLS):
            slot = down * SLOT_COLS + across
            stage_ref[to, across * BLOCK : (across + 1) * BLOCK] = (
                scale_ref[0, slot] * wide_ref[pl.ds(slot, BLOCK, stride=pitch), :]
            )
        store(down).start()

    @pl.loop(0, SLOT_ROWS)
    def _(down):
        store(down).wait()


def patch(scale, rows):
    shape = (SLOT_ROWS * BLOCK, SLOT_COLS * BLOCK)
    return pl.pallas_call(
        patch_kernel,
        out_shape=jax.ShapeDtypeStruct(shape, jnp.float32),
        in_specs=[SMEM, VMEM],
        out_specs=ANY,
        scratch_shapes=[
            pltpu.VMEM((rows.shape[0] + BLOCK * PAD, BLOCK), jnp.float32),
            pltpu.VMEM(shape, jnp.float32),
            pltpu.SemaphoreType.DMA((SLOT_ROWS,)),
        ],
        compiler_params=PARAMS,
        name="patch",
    )(scale, rows)


def exchange(rows, devices):
    shaped = rows.reshape(devices, -1, BLOCK)
    moved = lax.all_to_all(shaped, ("exp", "tile"), split_axis=0, concat_axis=0, tiled=True)
    return moved.reshape(rows.shape)


def shards(
    exposure,
    row_taps,
    column_taps,
    basis_coef,
    warp_rows,
    warp_columns,
    warp_id,
    route_device,
    route_slot,
    weight,
):
    devices = lax.axis_size("exp") * lax.axis_size("tile")
    image = exposure[0]
    tile_rows, width = image.shape
    per_tile = tile_rows * width // (BLOCK * BLOCK)
    slot_count = SLOT_ROWS * SLOT_COLS
    myself = lax.axis_index("exp") * lax.axis_size("tile") + lax.axis_index("tile")

    def mine(table):
        return lax.dynamic_slice_in_dim(table.reshape(devices, -1), myself, 1, 0)

    across = width // BLOCK
    slots = (route_device * slot_count + route_slot).reshape(devices, per_tile)
    above, below = swap_rims(image[:RIM], image[tile_rows - RIM :])
    rows, columns = band_matrices(row_taps, column_taps)
    my_ident = mine(warp_id)
    my_weight = mine(weight)
    arrived = []
    for half in range(HALVES):
        weighted = forward(
            half, my_ident, my_weight, basis_coef, above, image, below, rows, columns,
            warp_rows, warp_columns,
        )
        arrived.append(exchange(weighted, devices))

    owner = route_device.reshape(-1)
    place = route_slot.reshape(-1)
    block_weight = jnp.repeat(weight.reshape(-1), per_tile)
    by_owner = jnp.where(
        owner[None, :] == jnp.arange(devices, dtype=jnp.int32)[:, None], block_weight[None, :], 0.0
    )
    by_place = (place[:, None] == jnp.arange(slot_count, dtype=jnp.int32)[None, :]).astype(
        jnp.float32
    )
    total = jnp.dot(by_owner, by_place, precision=lax.Precision.HIGHEST)
    scale = 1.0 / jnp.maximum(total, 1.0)
    owned_scale = mine(scale)
    block_scale = scale.reshape(-1)[mine(slots)]

    early = early_sums(slots, arrived[0], across, devices * slot_count)
    first_rows, coadd_rows = late_sums(slots, arrived[1], early, across)
    second_rows = more_rows(slots, coadd_rows, across)
    returned = [exchange(first_rows, devices), exchange(second_rows, devices)]
    owned = exchange(coadd_rows, devices)

    images, above, below = [], [], []
    for half in range(HALVES):
        template, top, bottom = unwarp(
            half, my_ident, block_scale, returned[half], warp_rows, warp_columns, tile_rows
        )
        upper, lower = swap_rims(top, bottom)
        images.append(template)
        above.append(upper)
        below.append(lower)
    shared = (basis_coef, image, rows, columns)
    difference = inner_call(
        inner_left_kernel, "inner_left", LEFT * WIDE, images[:1], *shared, None
    )
    difference = inner_call(
        inner_right_kernel, "inner_right", width - LEFT * WIDE, images, *shared, difference
    )
    difference = subtract_outer(
        basis_coef, above, images, below, image, rows, columns, difference
    )
    return patch(owned_scale, owned), difference[None]


def solution(mesh):
    placed = (P("exp", "tile", None), P(), P(), P("exp", None), P(), P(), P(), P(), P(), P())
    return jax.shard_map(
        shards,
        mesh=mesh,
        in_specs=placed,
        out_specs=(P("exp", "tile"), P("exp", "tile", None)),
        check_vma=False,
    )
```

time: 190 us -> 207 us (1.089)
  starting transfers between devices: 29.4 us -> 46.9 us
  Pallas kernels: 78.6 us -> 90.3 us
  blocking collectives: 35.4 us -> 24.6 us
  waiting for transfers between devices: 28.8 us -> 26.6 us
    pallas_call x4 -> x9, Pallas kernels: 68 us -> 79.6 us  [the longest x2 19.3 us: forward(): pl.pallas_call(functools.partial(forward_kernel, half=half), out_shape=ja...]
    all_to_all x1, blocking collectives: 35.4 us -> 24.6 us  [exchange(): lax.all_to_all(shaped, ('exp', 'tile'), split_axis=0, concat_axis=0, tile...]
    all_to_all x2 -> x4, starting transfers between devices: 13.4 us -> 23 us  [exchange(): lax.all_to_all(shaped, ('exp', 'tile'), split_axis=0, concat_axis=0, tile...]
    ppermute x2 -> x3, starting transfers between devices: 9.3 us -> 15.2 us  [swap_rims(): lax.ppermute(top, 'tile', backward)]
    all_to_all x2 -> x4, waiting for transfers between devices: 28.8 us -> 26.6 us  [exchange(): lax.all_to_all(shaped, ('exp', 'tile'), split_axis=0, concat_axis=0, tile...]
    ppermute x2 -> x3, starting transfers between devices: 6.79 us -> 8.7 us  [swap_rims(): lax.ppermute(bottom, 'tile', forward)]
    unnamed x20 -> x32, local copies, waits for them, and re-layouts: 4.58 us -> 4.29 us
  transfers between devices with their start and end apart: 6 -> 10, of which waited for: 1 -> 3; matrix products, arithmetic and copies ran while one was open for 6% -> 5% of each run, Pallas kernels for 13% -> 29%
where the time goes in v2:
time: 207 us; the launch traced here: 205 us
  Pallas kernels  90.3 us (44%)
  starting transfers between devices  46.9 us (23%)
  waiting for transfers between devices  26.6 us (13%)
  blocking collectives  24.6 us (12%)
  local copies, waits for them, and re-layouts  9.43 us (5%)
  other arithmetic  3.85 us (2%)
  matrix products  2.66 us (1%)
    all_to_all x4, waiting for transfers between devices, exchange(): lax.all_to_all(shaped, ('exp', 'tile'), split_axis=0, concat_axis=0, tile...  26.6 us
    all_to_all x1, blocking collectives, exchange(): lax.all_to_all(shaped, ('exp', 'tile'), split_axis=0, concat_axis=0, tile...  24.6 us
    all_to_all x4, starting transfers between devices, exchange(): lax.all_to_all(shaped, ('exp', 'tile'), split_axis=0, concat_axis=0, tile...  23 us
    pallas_call x2, Pallas kernels, forward(): pl.pallas_call(functools.partial(forward_kernel, half=half), out_shape=ja...  19.3 us
    pallas_call x1, Pallas kernels, late_sums(): pl.pallas_call(functools.partial(late_kernel, tables=tables), out_shape=(...  16.5 us
    ppermute x3, starting transfers between devices, swap_rims(): lax.ppermute(top, 'tile', backward)  15.2 us
    pallas_call x2, Pallas kernels, inner_call(): pl.pallas_call(kernel, out_shape=jax.ShapeDtypeStruct(exposure.shape, jnp...  12.3 us
    pallas_call x2, Pallas kernels, unwarp(): pl.pallas_call(functools.partial(unwarp_kernel, half=half), out_shape=(ja...  12.2 us
  transfers between devices with their start and end apart: 10, of which 3 were waited for; matrix products, arithmetic and copies ran while one was open for 5% of the time, Pallas kernels for 29%

profile of v2, /device:TPU:8, one launch (start us, length us, event | category | flops | bytes accessed | tf_op | source)
XLA Modules:
  0.0 205.4 jit_solution(8659678998741989885)
XLA Ops:
  0.6 0.0 copy-start
  0.6 1.0 slice_bitcast_fusion
  1.7 3.4 %collective-permute-start = (bf16[16,4096]{1,0:T(8,128)(2,1)S(1)}, bf16[16,4096]{1,0:T(8,128)(2,1)S(1)}, u32[]{:S(2)}, u32[]{:S(2)}) collective-permute-start(bf16[16,4096]{1,0:T(8,128)(2,1)S(1)} %get-tuple-element.23), channel_id=1, source_target_pairs={{0,1},{1,2},{2,3},{3,4},{4,5},{5,6},{6,7},{7,8},{8,9},{9,10},{10,1... | collective-permute-start | bytes 393224 | tf_op jit(solution)/shard_map/ppermute | solution.py:72
  5.1 4.6 %collective-permute-start.1 = (bf16[16,4096]{1,0:T(8,128)(2,1)S(1)}, bf16[16,4096]{1,0:T(8,128)(2,1)S(1)}, u32[]{:S(2)}, u32[]{:S(2)}) collective-permute-start(bf16[16,4096]{1,0:T(8,128)(2,1)S(1)} %get-tuple-element.22), channel_id=1, source_target_pairs={{1,0},{2,1},{3,2},{4,3},{5,4},{6,5},{7,6},{8,7},{9,8},{10,9},{11,1... | collective-permute-start | bytes 393224 | tf_op jit(solution)/shard_map/ppermute | solution.py:72
  9.6 0.8 reshape.78
  10.4 1.3 convert_element_type.7.row_taps_ref
  11.7 1.3 convert_element_type.8.column_taps_ref
  12.9 0.5 constant_dynamic-slice_fusion.1.weight_ref
  13.4 2.5 %bands.1 = (bf16[384,160]{1,0:T(8,128)(2,1)}, bf16[1536,256]{1,0:T(8,128)(2,1)}) custom-call(f32[3,21]{1,0:T(4,128)} %convert_element_type.7.row_taps_ref, f32[3,21]{1,0:T(4,128)} %convert_element_type.8.column_taps_ref), custom_call_target="tpu_custom_call" | custom-call | tf_op jit(solution)/shard_map/bands/pallas_call | solution.py:56
  15.9 0.6 constant_dynamic-slice_fusion.2.ident_ref
  16.5 0.0 collective-permute-done.above_ref
  16.5 0.0 collective-permute-done.1.below_ref
  16.5 0.6 copy-done.5
  17.2 0.0 copy-done.6
  17.2 9.6 %match_warp_0.1 = bf16[4096,128]{1,0:T(8,128)(2,1)} custom-call(s32[1,64]{1,0:T(1,128)} %constant_dynamic-slice_fusion.2.ident_ref, f32[1,1]{1,0:T(1,128)} %constant_dynamic-slice_fusion.1.weight_ref, f32[1,3]{1,0:T(1,128)} %coef_ref.9, bf16[16,4096]{1,0:T(8,128)(2,1)} %copy-done.5, bf16[256,4096]{1,0:T(8,128)(2,1)} %bitcast.22, bf16[16,4096]{1,0:T(8,128)(2,1)} %copy-done.6, ...), custom_call_target="tpu_custom_call" | custom-call | tf_op jit(solution)/shard_map/match_warp_0/pallas_call | solution.py:255
  26.8 8.3 %all-to-all-start.1 = ((bf16[128,32,128]{2,1,0:T(8,128)(2,1)}), bf16[128,32,128]{2,1,0:T(8,128)(2,1)S(1)}, u32[]{:S(2)}, u32[]{:S(2)}) async-start(bf16[128,32,128]{2,1,0:T(8,128)(2,1)} %bitcast.32), calls=%async_computation.1 | async-start | bytes 2097152 | tf_op jit(solution)/shard_map/all_to_all | solution.py:761
  35.2 0.0 copy-start.7
  35.2 0.0 copy-start.8
  35.2 9.7 %match_warp_1.1 = bf16[4096,128]{1,0:T(8,128)(2,1)} custom-call(s32[1,64]{1,0:T(1,128)} %constant_dynamic-slice_fusion.2.ident_ref, f32[1,1]{1,0:T(1,128)} %constant_dynamic-slice_fusion.1.weight_ref, f32[1,3]{1,0:T(1,128)} %coef_ref.9, bf16[16,4096]{1,0:T(8,128)(2,1)} %copy-done.5, bf16[256,4096]{1,0:T(8,128)(2,1)} %bitcast.23, bf16[16,4096]{1,0:T(8,128)(2,1)} %copy-done.6, ...), custom_call_target="tpu_custom_call" | custom-call | tf_op jit(solution)/shard_map/match_warp_1/pallas_call | solution.py:255
  44.9 9.0 %all-to-all-done.1 = bf16[128,32,128]{2,1,0:T(8,128)(2,1)S(1)} async-done(((bf16[128,32,128]{2,1,0:T(8,128)(2,1)}), bf16[128,32,128]{2,1,0:T(8,128)(2,1)S(1)}, u32[]{:S(2)}, u32[]{:S(2)}) %all-to-all-start.1) | async-done | bytes 1048608 | tf_op jit(solution)/shard_map/all_to_all | solution.py:761
  53.9 4.9 %all-to-all-start = ((bf16[128,32,128]{2,1,0:T(8,128)(2,1)}), bf16[128,32,128]{2,1,0:T(8,128)(2,1)S(1)}, u32[]{:S(2)}, u32[]{:S(2)}) async-start(bf16[128,32,128]{2,1,0:T(8,128)(2,1)} %bitcast.31), calls=%async_computation | async-start | bytes 2097152 | tf_op jit(solution)/shard_map/all_to_all | solution.py:761
  58.8 0.0 copy-done.7
  58.8 0.0 copy-done.8
  58.8 0.6 multiply_add_fusion
  59.4 11.6 %early_sums.1.early_ref = f32[8192,128]{1,0:T(8,128)} custom-call(s32[128,64]{1,0:T(8,128)} %bitcast.39, bf16[4096,128]{1,0:T(8,128)(2,1)} %bitcast.36), custom_call_target="tpu_custom_call" | custom-call | tf_op jit(solution)/shard_map/early_sums/pallas_call | solution.py:339
  71.0 6.6 %all-to-all-done = bf16[128,32,128]{2,1,0:T(8,128)(2,1)S(1)} async-done(((bf16[128,32,128]{2,1,0:T(8,128)(2,1)}), bf16[128,32,128]{2,1,0:T(8,128)(2,1)S(1)}, u32[]{:S(2)}, u32[]{:S(2)}) %all-to-all-start) | async-done | bytes 1048608 | tf_op jit(solution)/shard_map/all_to_all | solution.py:761
  77.6 1.0 copy-done.4
  78.5 16.5 %late_sums.1 = (bf16[4096,128]{1,0:T(8,128)(2,1)}, bf16[8192,128]{1,0:T(8,128)(2,1)}) custom-call(s32[128,64]{1,0:T(8,128)} %bitcast.40, bf16[4096,128]{1,0:T(8,128)(2,1)} %bitcast.37, f32[8192,128]{1,0:T(8,128)} %early_sums.1.early_ref), custom_call_target="tpu_custom_call" | custom-call | tf_op jit(solution)/shard_map/late_sums/pallas_call | solution.py:370
  95.0 4.9 %all-to-all-start.3 = ((bf16[128,32,128]{2,1,0:T(8,128)(2,1)}), bf16[128,32,128]{2,1,0:T(8,128)(2,1)S(1)}, u32[]{:S(2)}, u32[]{:S(2)}) async-start(bf16[128,32,128]{2,1,0:T(8,128)(2,1)} %bitcast.38), calls=%async_computation.3 | async-start | bytes 2097152 | tf_op jit(solution)/shard_map/all_to_all | solution.py:761
  99.9 0.0 copy-start.13
  99.9 7.8 %more_rows.1 = bf16[4096,128]{1,0:T(8,128)(2,1)} custom-call(s32[128,64]{1,0:T(8,128)} %bitcast.41, bf16[8192,128]{1,0:T(8,128)(2,1)} %get-tuple-element.14.coadd_ref), custom_call_target="tpu_custom_call" | custom-call | tf_op jit(solution)/shard_map/more_rows/pallas_call | solution.py:397
  107.7 11.0 %all-to-all-done.3 = bf16[128,32,128]{2,1,0:T(8,128)(2,1)S(1)} async-done(((bf16[128,32,128]{2,1,0:T(8,128)(2,1)}), bf16[128,32,128]{2,1,0:T(8,128)(2,1)S(1)}, u32[]{:S(2)}, u32[]{:S(2)}) %all-to-all-start.3) | async-done | bytes 1048608 | tf_op jit(solution)/shard_map/all_to_all | solution.py:761
  118.7 24.6 %all_to_all.25 = bf16[128,32,128]{2,1,0:T(8,128)(2,1)} all-to-all(bf16[128,32,128]{2,1,0:T(8,128)(2,1)} %bitcast.33), channel_id=1, replica_groups=mesh['exp'=8,'tile'=16] {'exp','tile'}, dimensions={0} | all-to-all | bytes 2097152 | tf_op jit(solution)/shard_map/all_to_all | solution.py:761
  143.3 4.9 %all-to-all-start.2 = ((bf16[128,64,128]{2,1,0:T(8,128)(2,1)}), bf16[128,64,128]{2,1,0:T(8,128)(2,1)S(1)}, u32[]{:S(2)}, u32[]{:S(2)}) async-start(bf16[128,64,128]{2,1,0:T(8,128)(2,1)} %bitcast.30), calls=%async_computation.2 | async-start | bytes 4194304 | tf_op jit(solution)/shard_map/all_to_all | solution.py:761
  148.2 0.1 reshape.54
  148.3 0.1 eq.30
  148.4 0.1 eq.34
  148.4 0.1 broadcast_in_dim.25
  148.5 0.1 broadcast_in_dim.26
  148.6 2.7 %fusion.8 = f32[128,64]{1,0:T(8,128)S(1)} fusion(f32[8192]{0:T(1024)S(1)} %broadcast_in_dim.26, s32[8192]{0:T(1024)S(1)} %eq.30, s32[8192]{0:T(1024)S(1)} %eq.34), kind=kOutput, calls=%fused_computation.9 | convolution fusion | flops 807944192 | bytes 131072 | tf_op jit(solution)/shard_map/dot_general | solution.py:810
  151.3 0.1 reshape.64
  151.3 0.7 fusion.12
  152.0 1.3 gather_fusion
  153.3 6.1 %unwarp_0.1 = (bf16[256,2048]{1,0:T(8,128)(2,1)}, bf16[16,2048]{1,0:T(8,128)(2,1)}, bf16[16,2048]{1,0:T(8,128)(2,1)}) custom-call(s32[1,64]{1,0:T(1,128)} %constant_dynamic-slice_fusion.2.ident_ref, f32[1,64]{1,0:T(1,128)} %bitcast.43, bf16[4096,128]{1,0:T(8,128)(2,1)} %bitcast.34, bf16[64,128,128]{2,1,0:T(8,128)(2,1)} %bank_rows_ref.7, ...), custom_call_target="tpu_custom_call" | custom-call | tf_op jit(solution)/shard_map/unwarp_0/pallas_call | solution.py:489
  159.4 6.1 %unwarp_1.1 = (bf16[256,2048]{1,0:T(8,128)(2,1)}, bf16[16,2048]{1,0:T(8,128)(2,1)}, bf16[16,2048]{1,0:T(8,128)(2,1)}) custom-call(s32[1,64]{1,0:T(1,128)} %constant_dynamic-slice_fusion.2.ident_ref, f32[1,64]{1,0:T(1,128)} %bitcast.44, bf16[4096,128]{1,0:T(8,128)(2,1)} %bitcast.35, bf16[64,128,128]{2,1,0:T(8,128)(2,1)} %bank_rows_ref.7, ...), custom_call_target="tpu_custom_call" | custom-call | tf_op jit(solution)/shard_map/unwarp_1/pallas_call | solution.py:489
  165.5 3.4 %collective-permute-start.3 = (bf16[16,2048]{1,0:T(8,128)(2,1)}, bf16[16,2048]{1,0:T(8,128)(2,1)S(1)}, u32[]{:S(2)}, u32[]{:S(2)}) collective-permute-start(bf16[16,2048]{1,0:T(8,128)(2,1)} %get-tuple-element.17), channel_id=1, source_target_pairs={{0,1},{1,2},{2,3},{3,4},{4,5},{5,6},{6,7},{7,8},{8,9},{9,10},{10,1... | collective-permute-start | bytes 196616 | tf_op jit(solution)/shard_map/ppermute | solution.py:72
  168.9 4.6 %collective-permute-start.5 = (bf16[16,2048]{1,0:T(8,128)(2,1)}, bf16[16,2048]{1,0:T(8,128)(2,1)S(1)}, u32[]{:S(2)}, u32[]{:S(2)}) collective-permute-start(bf16[16,2048]{1,0:T(8,128)(2,1)} %get-tuple-element.21), channel_id=1, source_target_pairs={{1,0},{2,1},{3,2},{4,3},{5,4},{6,5},{7,6},{8,7},{9,8},{10,9},{11,1... | collective-permute-start | bytes 196616 | tf_op jit(solution)/shard_map/ppermute | solution.py:72
  173.5 1.9 collective-permute-start.2
  175.5 6.0 %collective-permute-start.4 = (bf16[16,2048]{1,0:T(8,128)(2,1)S(1)}, bf16[16,2048]{1,0:T(8,128)(2,1)S(1)}, u32[]{:S(2)}, u32[]{:S(2)}) collective-permute-start(bf16[16,2048]{1,0:T(8,128)(2,1)S(1)} %copy-done.14), channel_id=1, source_target_pairs={{1,0},{2,1},{3,2},{4,3},{5,4},{6,5},{7,6},{8,7},{9,8},{10,9},{11,1... | collective-permute-start | bytes 196616 | tf_op jit(solution)/shard_map/ppermute | solution.py:72
  181.5 0.5 constant_dynamic-slice_fusion.3.scale_ref
  182.0 5.2 %inner_left.1.partial_ref = f32[256,4096]{1,0:T(8,128)} custom-call(f32[1,3]{1,0:T(1,128)} %coef_ref.9, bf16[256,2048]{1,0:T(8,128)(2,1)} %get-tuple-element.18.left_ref.top_left_ref.bottom_left_ref, bf16[256,4096]{1,0:T(8,128)(2,1)} %bitcast.24, bf16[384,160]{1,0:T(8,128)(2,1)} %get-tuple-element.12.rows_ref, bf16[1536,256]{1,0:T(8,128)(2,1)} %get-tuple-element.13.columns_ref), custom_call_target="tpu_custom_call" | custom-call | tf_op jit(solution)/shard_map/inner_left/pallas_call | solution.py:615
  187.2 7.1 %inner_right.1.partial_ref = f32[256,4096]{1,0:T(8,128)} custom-call(f32[1,3]{1,0:T(1,128)} %coef_ref.9, bf16[256,2048]{1,0:T(8,128)(2,1)} %get-tuple-element.18.left_ref.top_left_ref.bottom_left_ref, bf16[256,2048]{1,0:T(8,128)(2,1)} %get-tuple-element.19.right_ref.top_right_ref.bottom_right_ref, ...), custom_call_target="tpu_custom_call", output_to_operand_aliasing={{}: (6, {})} | custom-call | tf_op jit(solution)/shard_map/inner_right/pallas_call | solution.py:615
  194.4 0.0 collective-permute-done.3.above_right_ref
  194.4 0.0 collective-permute-done.5.below_right_ref
  194.4 0.0 collective-permute-done.2.above_left_ref
  194.4 0.0 collective-permute-done.4.below_left_ref
  194.4 0.6 copy-done.9
  195.0 0.0 copy-done.10
  195.0 0.0 copy-done.11
  195.1 0.6 copy-done.12
  195.7 3.9 %subtract_outer.1 = f32[256,4096]{1,0:T(8,128)} custom-call(f32[1,3]{1,0:T(1,128)} %coef_ref.9, bf16[16,2048]{1,0:T(8,128)(2,1)} %copy-done.11, bf16[16,2048]{1,0:T(8,128)(2,1)} %copy-done.9, bf16[256,2048]{1,0:T(8,128)(2,1)} %get-tuple-element.18.left_ref.top_left_ref.bottom_left_ref, ...), custom_call_target="tpu_custom_call", output_to_operand_aliasing={{}: (13, {})} | custom-call | tf_op jit(solution)/shard_map/subtract_outer/pallas_call | solution.py:696
  199.6 0.0 all-to-all-done.2
  199.6 1.3 copy-done.1
  201.0 4.3 %patch.1 = f32[1024,1024]{1,0:T(8,128)} custom-call(f32[1,64]{1,0:T(1,128)} %constant_dynamic-slice_fusion.3.scale_ref, bf16[8192,128]{1,0:T(8,128)(2,1)} %bitcast.29), custom_call_target="tpu_custom_call" | custom-call | tf_op jit(solution)/shard_map/patch/pallas_call | solution.py:744
  (19 shorter events, 0.0 us)
Async XLA Ops:
  0.6 15.3 %copy-start = (s32[8,16,64]{2,1,0:T(8,128)S(1)}, s32[8,16,64]{2,1,0:T(8,128)}, u32[]{:S(2)}) copy-start(s32[8,16,64]{2,1,0:T(8,128)} %param.16) | copy-start | bytes 98308
  1.7 14.8 %collective-permute-start = (bf16[16,4096]{1,0:T(8,128)(2,1)S(1)}, bf16[16,4096]{1,0:T(8,128)(2,1)S(1)}, u32[]{:S(2)}, u32[]{:S(2)}) collective-permute-start(bf16[16,4096]{1,0:T(8,128)(2,1)S(1)} %get-tuple-element.23), channel_id=1, source_target_pairs={{0,1},{1,2},{2,3},{3,4},{4,5},{5,6},{6,7},{7,8},{8,9},{9,10},{10,1... | collective-permute-start | bytes 393224 | tf_op jit(solution)/shard_map/ppermute | solution.py:72
  5.1 11.4 %collective-permute-start.1 = (bf16[16,4096]{1,0:T(8,128)(2,1)S(1)}, bf16[16,4096]{1,0:T(8,128)(2,1)S(1)}, u32[]{:S(2)}, u32[]{:S(2)}) collective-permute-start(bf16[16,4096]{1,0:T(8,128)(2,1)S(1)} %get-tuple-element.22), channel_id=1, source_target_pairs={{1,0},{2,1},{3,2},{4,3},{5,4},{6,5},{7,6},{8,7},{9,8},{10,9},{11,1... | collective-permute-start | bytes 393224 | tf_op jit(solution)/shard_map/ppermute | solution.py:72
  16.5 0.6 copy-start.5
  16.5 0.7 copy-start.6
  26.8 27.0 %all-to-all-start.1 = ((bf16[128,32,128]{2,1,0:T(8,128)(2,1)}), bf16[128,32,128]{2,1,0:T(8,128)(2,1)S(1)}, u32[]{:S(2)}, u32[]{:S(2)}) async-start(bf16[128,32,128]{2,1,0:T(8,128)(2,1)} %bitcast.32), calls=%async_computation.1 | async-start | bytes 2097152 | tf_op jit(solution)/shard_map/all_to_all | solution.py:761
  35.2 23.6 %copy-start.7 = (s32[8,16,64]{2,1,0:T(8,128)S(1)}, s32[8,16,64]{2,1,0:T(8,128)}, u32[]{:S(2)}) copy-start(s32[8,16,64]{2,1,0:T(8,128)} %param.17) | copy-start | bytes 98308
  35.2 23.6 %copy-start.8 = (s32[8,16,64]{2,1,0:T(8,128)S(1)}, s32[8,16,64]{2,1,0:T(8,128)}, u32[]{:S(2)}) copy-start(s32[8,16,64]{2,1,0:T(8,128)} %param.18) | copy-start | bytes 98308
  53.9 5.5 %copy-start.3 = (bf16[128,32,128]{2,1,0:T(8,128)(2,1)}, bf16[128,32,128]{2,1,0:T(8,128)(2,1)S(1)}, u32[]{:S(2)}) copy-start(bf16[128,32,128]{2,1,0:T(8,128)(2,1)S(1)} %all-to-all-done.1) | copy-start | bytes 3145732
  53.9 23.7 %all-to-all-start = ((bf16[128,32,128]{2,1,0:T(8,128)(2,1)}), bf16[128,32,128]{2,1,0:T(8,128)(2,1)S(1)}, u32[]{:S(2)}, u32[]{:S(2)}) async-start(bf16[128,32,128]{2,1,0:T(8,128)(2,1)} %bitcast.31), calls=%async_computation | async-start | bytes 2097152 | tf_op jit(solution)/shard_map/all_to_all | solution.py:761
  77.6 1.0 copy-start.4
  95.0 23.7 %all-to-all-start.3 = ((bf16[128,32,128]{2,1,0:T(8,128)(2,1)}), bf16[128,32,128]{2,1,0:T(8,128)(2,1)S(1)}, u32[]{:S(2)}, u32[]{:S(2)}) async-start(bf16[128,32,128]{2,1,0:T(8,128)(2,1)} %bitcast.38), calls=%async_computation.3 | async-start | bytes 2097152 | tf_op jit(solution)/shard_map/all_to_all | solution.py:761
  99.9 48.3 %copy-start.13 = (f32[8,16]{1,0:T(8,128)S(1)}, f32[8,16]{1,0:T(8,128)}, u32[]{:S(2)}) copy-start(f32[8,16]{1,0:T(8,128)} %param.19) | copy-start | bytes 1540
  118.7 32.6 %copy-start.2 = (bf16[128,32,128]{2,1,0:T(8,128)(2,1)}, bf16[128,32,128]{2,1,0:T(8,128)(2,1)S(1)}, u32[]{:S(2)}) copy-start(bf16[128,32,128]{2,1,0:T(8,128)(2,1)S(1)} %all-to-all-done.3) | copy-start | bytes 3145732
  143.3 56.3 %all-to-all-start.2 = ((bf16[128,64,128]{2,1,0:T(8,128)(2,1)}), bf16[128,64,128]{2,1,0:T(8,128)(2,1)S(1)}, u32[]{:S(2)}, u32[]{:S(2)}) async-start(bf16[128,64,128]{2,1,0:T(8,128)(2,1)} %bitcast.30), calls=%async_computation.2 | async-start | bytes 4194304 | tf_op jit(solution)/shard_map/all_to_all | solution.py:761
  159.4 14.1 %copy-start.15 = (bf16[16,2048]{1,0:T(8,128)(2,1)S(1)}, bf16[16,2048]{1,0:T(8,128)(2,1)}, u32[]{:S(2)}) copy-start(bf16[16,2048]{1,0:T(8,128)(2,1)} %get-tuple-element.16) | copy-start | bytes 196612
  159.4 16.0 %copy-start.14 = (bf16[16,2048]{1,0:T(8,128)(2,1)S(1)}, bf16[16,2048]{1,0:T(8,128)(2,1)}, u32[]{:S(2)}) copy-start(bf16[16,2048]{1,0:T(8,128)(2,1)} %get-tuple-element.20) | copy-start | bytes 196612
  165.5 28.8 %collective-permute-start.3 = (bf16[16,2048]{1,0:T(8,128)(2,1)}, bf16[16,2048]{1,0:T(8,128)(2,1)S(1)}, u32[]{:S(2)}, u32[]{:S(2)}) collective-permute-start(bf16[16,2048]{1,0:T(8,128)(2,1)} %get-tuple-element.17), channel_id=1, source_target_pairs={{0,1},{1,2},{2,3},{3,4},{4,5},{5,6},{6,7},{7,8},{8,9},{9,10},{10,1... | collective-permute-start | bytes 196616 | tf_op jit(solution)/shard_map/ppermute | solution.py:72
  168.9 25.5 %collective-permute-start.5 = (bf16[16,2048]{1,0:T(8,128)(2,1)}, bf16[16,2048]{1,0:T(8,128)(2,1)S(1)}, u32[]{:S(2)}, u32[]{:S(2)}) collective-permute-start(bf16[16,2048]{1,0:T(8,128)(2,1)} %get-tuple-element.21), channel_id=1, source_target_pairs={{1,0},{2,1},{3,2},{4,3},{5,4},{6,5},{7,6},{8,7},{9,8},{10,9},{11,1... | collective-permute-start | bytes 196616 | tf_op jit(solution)/shard_map/ppermute | solution.py:72
  173.5 20.9 %collective-permute-start.2 = (bf16[16,2048]{1,0:T(8,128)(2,1)S(1)}, bf16[16,2048]{1,0:T(8,128)(2,1)S(1)}, u32[]{:S(2)}, u32[]{:S(2)}) collective-permute-start(bf16[16,2048]{1,0:T(8,128)(2,1)S(1)} %copy-done.15), channel_id=1, source_target_pairs={{0,1},{1,2},{2,3},{3,4},{4,5},{5,6},{6,7},{7,8},{8,9},{9,10},{10,1... | collective-permute-start | bytes 196616 | tf_op jit(solution)/shard_map/ppermute | solution.py:72
  175.5 19.0 %collective-permute-start.4 = (bf16[16,2048]{1,0:T(8,128)(2,1)S(1)}, bf16[16,2048]{1,0:T(8,128)(2,1)S(1)}, u32[]{:S(2)}, u32[]{:S(2)}) collective-permute-start(bf16[16,2048]{1,0:T(8,128)(2,1)S(1)} %copy-done.14), channel_id=1, source_target_pairs={{1,0},{2,1},{3,2},{4,3},{5,4},{6,5},{7,6},{8,7},{9,8},{10,9},{11,1... | collective-permute-start | bytes 196616 | tf_op jit(solution)/shard_map/ppermute | solution.py:72
  194.4 0.6 copy-start.9
  194.4 0.6 copy-start.10
  194.4 0.6 copy-start.11
  195.1 0.6 copy-start.12
  199.6 1.4 copy-start.1

commit v3 on v1

v3 whole, which is shorter than its diff:
```python
import functools

import jax
import jax.numpy as jnp
from jax import lax
from jax.experimental import pallas as pl
from jax.experimental.pallas import tpu as pltpu
from jax.sharding import PartitionSpec as P

BLOCK = 128
HALF = 10
RIM = 16
CHUNK = 256
WIDE = 1024
SPAN = CHUNK + BLOCK
WINDOW = BLOCK + 2 * RIM
SLOT_ROWS = 8
SLOT_COLS = 8
LANES = 8
PAD = 8
VMEM = pl.BlockSpec(memory_space=pltpu.VMEM)
SMEM = pl.BlockSpec(memory_space=pltpu.SMEM)
ANY = pl.BlockSpec(memory_space=pl.ANY)


def grant(mebibytes):
    return pltpu.CompilerParams(vmem_limit_bytes=mebibytes * 1024 * 1024)


def bands_kernel(row_taps_ref, column_taps_ref, rows_ref, columns_ref):
    bases, taps = row_taps_ref.shape
    lead = RIM - HALF

    def banded(taps_ref, offsets):
        values = taps_ref[...].astype(jnp.float32)
        bands = [jnp.zeros(offsets.shape, jnp.float32) for _ in range(bases)]
        for tap in range(taps):
            hit = offsets == tap
            for base in range(bases):
                value = jnp.broadcast_to(values[base : base + 1, tap : tap + 1], offsets.shape)
                bands[base] = jnp.where(hit, value, bands[base])
        return [band.astype(jnp.bfloat16) for band in bands]

    shape = (BLOCK, WINDOW)
    across = lax.broadcasted_iota(jnp.int32, shape, 1) - lax.broadcasted_iota(jnp.int32, shape, 0)
    for base, band in enumerate(banded(row_taps_ref, across - lead)):
        rows_ref[base * BLOCK : (base + 1) * BLOCK, :] = band
    shape = (WINDOW, BLOCK)
    down = lax.broadcasted_iota(jnp.int32, shape, 0) - lax.broadcasted_iota(jnp.int32, shape, 1)
    columns_ref[...] = jnp.zeros_like(columns_ref)
    for base, band in enumerate(banded(column_taps_ref, down - lead)):
        top = base * CHUNK
        columns_ref[top : top + WINDOW - RIM, :BLOCK] = band[RIM:]
        columns_ref[top + BLOCK - RIM : top + CHUNK, BLOCK:] = band[: WINDOW - RIM]
        top = bases * CHUNK + base * BLOCK
        columns_ref[top : top + RIM, BLOCK:] = band[WINDOW - RIM :]
        columns_ref[top + BLOCK - RIM : top + BLOCK, :BLOCK] = band[:RIM]


def band_matrices(row_taps, column_taps):
    bases = row_taps.shape[0]
    return pl.pallas_call(
        bands_kernel,
        out_shape=(
            jax.ShapeDtypeStruct((bases * BLOCK, WINDOW), jnp.bfloat16),
            jax.ShapeDtypeStruct((bases * SPAN, CHUNK), jnp.bfloat16),
        ),
        in_specs=[VMEM, VMEM],
        out_specs=(VMEM, VMEM),
        compiler_params=grant(58),
        name="bands",
    )(row_taps, column_taps)


def swap_rims(top, bottom):
    count = lax.axis_size("tile")
    forward = [(i, i + 1) for i in range(count - 1)]
    backward = [(target, source) for source, target in forward]
    return lax.ppermute(bottom, "tile", forward), lax.ppermute(top, "tile", backward)


def clear(pass_ref, start):
    bases, height, _ = pass_ref.shape
    pass_ref[:, :, start : start + BLOCK] = jnp.zeros((bases, height, BLOCK), pass_ref.dtype)


def row_step(lanes, start, to, strips, coef_ref, rows_ref, pass_ref):
    bases = pass_ref.shape[0]
    for first_row, count, pieces in strips:
        window = [
            ref[first : first + size, pl.ds(pl.multiple_of(start + shift, BLOCK), lanes)]
            for ref, first, size, shift in pieces
        ]
        window = window[0] if len(window) == 1 else jnp.concatenate(window, axis=0)
        depth = window.shape[0]
        if count == BLOCK and depth == WINDOW:
            band = rows_ref[...]
        else:
            band = jnp.concatenate(
                [rows_ref[base * BLOCK : base * BLOCK + count, :depth] for base in range(bases)],
                axis=0,
            )
        summed = jnp.dot(band, window, preferred_element_type=jnp.float32)
        for base in range(bases):
            pass_ref[
                base, first_row : first_row + count, pl.ds(pl.multiple_of(to, BLOCK), lanes)
            ] = (coef_ref[0, base] * summed[base * count : (base + 1) * count]).astype(jnp.bfloat16)


def column_step(index, count, columns_ref, pass_ref):
    bases = pass_ref.shape[0]
    right = lax.broadcasted_iota(jnp.int32, (count, BLOCK), 1) < BLOCK // 2
    summed = []
    for part in range(WIDE // CHUNK):
        at = index * WIDE + part * CHUNK

        def columns(shift, size):
            return pl.ds(pl.multiple_of(at + shift, BLOCK), size)

        middle = [pass_ref[base, :count, columns(BLOCK, CHUNK)] for base in range(bases)]
        sides = [
            jnp.where(
                right,
                pass_ref[base, :count, columns(BLOCK + CHUNK, BLOCK)],
                pass_ref[base, :count, columns(0, BLOCK)],
            )
            for base in range(bases)
        ]
        summed.append(
            jnp.dot(
                jnp.concatenate(middle + sides, axis=1),
                columns_ref[...],
                preferred_element_type=jnp.float32,
            )
        )
    return summed


def my_device():
    return lax.axis_index("exp") * lax.axis_size("tile") + lax.axis_index("tile")


def wide_copy(source, target, sems, first_row, rows):
    def copy(index):
        at = pl.ds(pl.multiple_of(index * WIDE, WIDE), WIDE)
        return pltpu.make_async_copy(
            source.at[pl.ds(first_row, rows), at], target.at[:, at], sems.at[index]
        )

    return copy


def passes(fetch, step, consume, pass_ref, width):
    wides = width // WIDE

    def wide_step(index):
        fetch(index).wait()
        step(WIDE, index * WIDE, BLOCK + index * WIDE)

    clear(pass_ref, 0)
    clear(pass_ref, BLOCK + width)
    wide_step(0)
    wide_step(1)

    @pl.loop(0, wides - 2)
    def _(index):
        consume(index)
        wide_step(index + 2)

    @pl.loop(wides - 2, wides)
    def _(index):
        consume(index)


def forward_kernel(
    ident_ref,
    weight_ref,
    coef_ref,
    above_ref,
    image_hbm,
    below_ref,
    rows_ref,
    columns_ref,
    bank_rows_ref,
    bank_columns_ref,
    out_ref,
    image_ref,
    pass_ref,
    matched_ref,
    turned_ref,
    warp_rows_ref,
    warp_columns_ref,
    fetch_sems,
    load_sems,
):
    tile_rows, width = image_ref.shape
    parts = tile_rows // BLOCK
    across = width // BLOCK
    items = parts * across
    pitch = items + PAD
    myself = my_device()
    weight = weight_ref[lax.axis_index("exp"), lax.axis_index("tile")]
    fetch = wide_copy(image_hbm, image_ref, fetch_sems, 0, tile_rows)
    loads = [
        pltpu.make_async_copy(bank_rows_ref, warp_rows_ref, load_sems.at[0]),
        pltpu.make_async_copy(bank_columns_ref, warp_columns_ref, load_sems.at[1]),
    ]
    for index in range(width // WIDE):
        fetch(index).start()
    for load in loads:
        load.start()

    strips = [
        (0, BLOCK, [(above_ref, 0, RIM, 0), (image_ref, 0, BLOCK + RIM, 0)]),
        (BLOCK, BLOCK, [(image_ref, BLOCK - RIM, BLOCK + RIM, 0), (below_ref, 0, RIM, 0)]),
    ]
    step = functools.partial(
        row_step, strips=strips, coef_ref=coef_ref, rows_ref=rows_ref, pass_ref=pass_ref
    )

    def match_step(index):
        for inner, summed in enumerate(column_step(index, tile_rows, columns_ref, pass_ref)):
            matched_ref[:, pl.ds(pl.multiple_of(index * WIDE + inner * CHUNK, CHUNK), CHUNK)] = (
                summed.astype(jnp.bfloat16)
            )

    passes(fetch, step, match_step, pass_ref, width)
    for load in loads:
        load.wait()

    @pl.loop(0, across // 4)
    def _(quad):
        todo = []
        for part in range(parts):
            for inner in range(4):
                column = quad * 4 + inner
                ident = ident_ref[myself, part * across + column]
                piece = matched_ref[
                    part * BLOCK : (part + 1) * BLOCK,
                    pl.ds(pl.multiple_of(column * BLOCK, BLOCK), BLOCK),
                ]
                todo.append((part * across + column, ident, piece))
        todo = [
            (
                item,
                ident,
                jnp.dot(warp_rows_ref[ident], piece, preferred_element_type=jnp.float32).astype(
                    jnp.bfloat16
                ),
            )
            for item, ident, piece in todo
        ]
        todo = [
            (
                item,
                lax.dot_general(
                    first,
                    warp_columns_ref[ident],
                    (((1,), (1,)), ((), ())),
                    preferred_element_type=jnp.float32,
                ),
            )
            for item, ident, first in todo
        ]
        for item, second in todo:
            turned_ref[pl.ds(item, BLOCK, stride=pitch), :] = weight * second

    @pl.loop(0, BLOCK, unroll=4)
    def _(row):
        to = pl.ds(pl.multiple_of(row * items, items), items)
        at = pl.ds(pl.multiple_of(row * pitch, PAD), items)
        out_ref[to, :] = turned_ref[at, :].astype(jnp.bfloat16)


def forward(ident, weight, coef, above, image, below, rows, columns, warp_rows, warp_columns):
    tile_rows, width = image.shape
    bases = rows.shape[0] // BLOCK
    lines = tile_rows * width // BLOCK
    return pl.pallas_call(
        forward_kernel,
        out_shape=jax.ShapeDtypeStruct((lines, BLOCK), jnp.bfloat16),
        in_specs=[SMEM, SMEM, SMEM, VMEM, ANY, VMEM, VMEM, VMEM, ANY, ANY],
        out_specs=VMEM,
        scratch_shapes=[
            pltpu.VMEM((tile_rows, width), jnp.bfloat16),
            pltpu.VMEM((bases, tile_rows, width + 2 * BLOCK), jnp.bfloat16),
            pltpu.VMEM((tile_rows, width), jnp.bfloat16),
            pltpu.VMEM((lines + BLOCK * PAD, BLOCK), jnp.float32),
            pltpu.VMEM(warp_rows.shape, jnp.bfloat16),
            pltpu.VMEM(warp_columns.shape, jnp.bfloat16),
            pltpu.SemaphoreType.DMA((width // WIDE,)),
            pltpu.SemaphoreType.DMA((2,)),
        ],
        compiler_params=grant(58),
        name="match_warp",
    )(ident, weight, coef, above, image, below, rows, columns, warp_rows, warp_columns)


def slots_kernel(slot_hbm, arrived_ref, scale_ref, template_ref, coadd_ref, wide_ref, *refs):
    del scale_ref
    items, _, sources = slot_hbm.shape
    sums, tables, sems = refs[:LANES], refs[LANES : LANES + items], refs[LANES + items]
    loads = [pltpu.make_async_copy(slot_hbm.at[k], tables[k], sems.at[k]) for k in range(items)]
    for load in loads:
        load.start()

    def at(source):
        return pl.ds(pl.multiple_of(source * items, items), items)

    @pl.loop(0, sources)
    def _(source):
        wide_ref[at(source), :] = arrived_ref[at(source), :].astype(jnp.float32)
        for sum_ref in sums:
            sum_ref[at(source), :] = jnp.zeros((items, BLOCK), jnp.float32)

    for load in loads:
        load.wait()

    @pl.loop(0, sources)
    def _(source):
        for first in range(0, items, LANES):
            slots = [tables[first + lane][0, source] for lane in range(LANES)]
            values = [
                sum_ref[pl.ds(slot, 1), :] + wide_ref[pl.ds(source * items + first + lane, 1), :]
                for lane, (slot, sum_ref) in enumerate(zip(slots, sums))
            ]
            for slot, sum_ref, value in zip(slots, sums, values):
                sum_ref[pl.ds(slot, 1), :] = value

    @pl.loop(0, sources)
    def _(source):
        value = sums[0][at(source), :]
        for sum_ref in sums[1:]:
            value = value + sum_ref[at(source), :]
        sums[0][at(source), :] = value
        coadd_ref[at(source), :] = value.astype(jnp.bfloat16)

    @pl.loop(0, sources)
    def _(source):
        for item in range(items):
            slot = tables[item][0, source]
            wide_ref[pl.ds(source * items + item, 1), :] = sums[0][pl.ds(slot, 1), :]

    @pl.loop(0, sources)
    def _(source):
        template_ref[at(source), :] = wide_ref[at(source), :].astype(jnp.bfloat16)


def slot_sums(slots, arrived, scale):
    shape = jax.ShapeDtypeStruct(arrived.shape, jnp.bfloat16)
    sources, items = slots.shape
    return pl.pallas_call(
        slots_kernel,
        out_shape=(shape, shape),
        in_specs=[ANY, VMEM, ANY],
        out_specs=(VMEM, VMEM),
        scratch_shapes=[pltpu.VMEM(arrived.shape, jnp.float32)] * (1 + LANES)
        + [pltpu.SMEM((1, sources), jnp.int32)] * items
        + [pltpu.SemaphoreType.DMA((items,))],
        compiler_params=grant(44),
        name="slot_sums",
    )(slots.T.reshape(items, 1, sources), arrived, scale)


def unwarp_kernel(
    ident_ref,
    scale_ref,
    returned_ref,
    bank_rows_ref,
    bank_columns_ref,
    out_ref,
    top_ref,
    bottom_ref,
    wide_ref,
    warp_rows_ref,
    warp_columns_ref,
    sems,
):
    tile_rows, part_width = out_ref.shape
    across = part_width // BLOCK
    parts = tile_rows // BLOCK
    items = parts * across
    pitch = items + PAD
    myself = my_device()
    loads = [
        pltpu.make_async_copy(bank_rows_ref, warp_rows_ref, sems.at[0]),
        pltpu.make_async_copy(bank_columns_ref, warp_columns_ref, sems.at[1]),
    ]
    for load in loads:
        load.start()

    @pl.loop(0, BLOCK, unroll=4)
    def _(row):
        to = pl.ds(pl.multiple_of(row * pitch, PAD), items)
        at = pl.ds(pl.multiple_of(row * items, items), items)
        wide_ref[to, :] = returned_ref[at, :].astype(jnp.float32)

    for load in loads:
        load.wait()

    @pl.loop(0, across // 4)
    def _(quad):
        todo = []
        for part in range(parts):
            for inner in range(4):
                column = quad * 4 + inner
                item = part * across + column
                ident = ident_ref[myself, item]
                numerator = wide_ref[pl.ds(item, BLOCK, stride=pitch), :].astype(jnp.bfloat16)
                todo.append((part, column, item, ident, numerator))
        todo = [
            (
                part,
                column,
                ident,
                scale_ref[0, item]
                * lax.dot_general(
                    warp_rows_ref[ident],
                    numerator,
                    (((0,), (0,)), ((), ())),
                    preferred_element_type=jnp.float32,
                ),
            )
            for part, column, item, ident, numerator in todo
        ]
        for part, column, ident, first in todo:
            image = jnp.dot(
                first.astype(jnp.bfloat16),
                warp_columns_ref[ident],
                preferred_element_type=jnp.float32,
            ).astype(jnp.bfloat16)
            to = pl.ds(pl.multiple_of(column * BLOCK, BLOCK), BLOCK)
            out_ref[part * BLOCK : (part + 1) * BLOCK, to] = image
            if part == 0:
                top_ref[:, to] = image[:RIM]
            if part == parts - 1:
                bottom_ref[:, to] = image[BLOCK - RIM :]


def unwarp(ident, scale, returned, warp_rows, warp_columns, tile_rows):
    lines = returned.shape[0]
    part_width = lines * BLOCK // tile_rows
    rim = jax.ShapeDtypeStruct((RIM, part_width), jnp.bfloat16)
    return pl.pallas_call(
        unwarp_kernel,
        out_shape=(jax.ShapeDtypeStruct((tile_rows, part_width), jnp.bfloat16), rim, rim),
        in_specs=[SMEM, SMEM, VMEM, ANY, ANY],
        out_specs=(VMEM, VMEM, VMEM),
        scratch_shapes=[
            pltpu.VMEM((lines + BLOCK * PAD, BLOCK), jnp.float32),
            pltpu.VMEM(warp_rows.shape, jnp.bfloat16),
            pltpu.VMEM(warp_columns.shape, jnp.bfloat16),
            pltpu.SemaphoreType.DMA((2,)),
        ],
        compiler_params=grant(58),
        name="unwarp",
    )(ident, scale, returned, warp_rows, warp_columns)


def inner_kernel(
    coef_ref,
    image_hbm,
    exposure_hbm,
    rows_ref,
    columns_ref,
    out_ref,
    image_ref,
    exposure_ref,
    pass_ref,
    stage_ref,
    fetch_sems,
    load_sem,
    sems,
):
    tile_rows, width = image_ref.shape
    inner = tile_rows - 2 * RIM
    fetch = wide_copy(image_hbm, image_ref, fetch_sems, 0, tile_rows)
    load = pltpu.make_async_copy(exposure_hbm.at[pl.ds(RIM, inner)], exposure_ref, load_sem)
    for index in range(width // WIDE):
        fetch(index).start()
    load.start()
    strips = [
        (0, BLOCK, [(image_ref, 0, WINDOW, 0)]),
        (BLOCK, inner - BLOCK, [(image_ref, BLOCK, tile_rows - BLOCK, 0)]),
    ]
    step = functools.partial(
        row_step, strips=strips, coef_ref=coef_ref, rows_ref=rows_ref, pass_ref=pass_ref
    )

    def store(index):
        at = pl.ds(pl.multiple_of(index * WIDE, WIDE), WIDE)
        return pltpu.make_async_copy(
            stage_ref.at[:, at], out_ref.at[pl.ds(RIM, inner), at], sems.at[index]
        )

    def subtract_step(index):
        for part, summed in enumerate(column_step(index, inner, columns_ref, pass_ref)):
            at = pl.ds(pl.multiple_of(index * WIDE + part * CHUNK, CHUNK), CHUNK)
            stage_ref[:, at] = exposure_ref[:, at].astype(jnp.float32) - summed
        store(index).start()

    load.wait()
    passes(fetch, step, subtract_step, pass_ref, width)

    @pl.loop(0, width // WIDE)
    def _(index):
        store(index).wait()


def subtract_inner(coef, image, exposure, rows, columns):
    tile_rows, width = image.shape
    bases = rows.shape[0] // BLOCK
    inner = tile_rows - 2 * RIM
    return pl.pallas_call(
        inner_kernel,
        out_shape=jax.ShapeDtypeStruct((tile_rows, width), jnp.float32),
        in_specs=[SMEM, ANY, ANY, VMEM, VMEM],
        out_specs=ANY,
        scratch_shapes=[
            pltpu.VMEM((tile_rows, width), jnp.bfloat16),
            pltpu.VMEM((inner, width), jnp.bfloat16),
            pltpu.VMEM((bases, inner, width + 2 * BLOCK), jnp.bfloat16),
            pltpu.VMEM((inner, width), jnp.float32),
            pltpu.SemaphoreType.DMA((width // WIDE,)),
            pltpu.SemaphoreType.DMA,
            pltpu.SemaphoreType.DMA((width // WIDE,)),
        ],
        compiler_params=grant(58),
        name="subtract_inner",
    )(coef, image, exposure, rows, columns)


def outer_kernel(
    coef_ref,
    above_ref,
    top_ref,
    bottom_ref,
    below_ref,
    exposure_top_ref,
    exposure_bottom_ref,
    rows_ref,
    columns_ref,
    partial_ref,
    out_ref,
    pass_ref,
    stage_ref,
    sems,
):
    del partial_ref
    width = top_ref.shape[1]
    tile_rows = out_ref.shape[0]
    wides = width // WIDE
    strips = [
        (0, RIM, [(above_ref, 0, RIM, 0), (top_ref, 0, 2 * RIM, 0)]),
        (RIM, RIM, [(bottom_ref, 0, 2 * RIM, 0), (below_ref, 0, RIM, 0)]),
    ]
    clear(pass_ref, 0)
    clear(pass_ref, BLOCK + width)
    for index in range(wides):
        row_step(
            WIDE, index * WIDE, BLOCK + index * WIDE, strips, coef_ref, rows_ref, pass_ref
        )
    for index in range(wides):
        for half, summed in enumerate(column_step(index, 2 * RIM, columns_ref, pass_ref)):
            at = pl.ds(index * WIDE + half * CHUNK, CHUNK)
            stage_ref[:RIM, at] = exposure_top_ref[:, at].astype(jnp.float32) - summed[:RIM]
            stage_ref[RIM:, at] = exposure_bottom_ref[:, at].astype(jnp.float32) - summed[RIM:]
    stores = [
        pltpu.make_async_copy(stage_ref.at[:RIM], out_ref.at[:RIM], sems.at[0]),
        pltpu.make_async_copy(
            stage_ref.at[RIM:], out_ref.at[pl.ds(tile_rows - RIM, RIM)], sems.at[1]
        ),
    ]
    for store in stores:
        store.start()
    for store in stores:
        store.wait()


def subtract_outer(coef, above, image, below, exposure, rows, columns, partial):
    tile_rows, width = image.shape
    bases = rows.shape[0] // BLOCK
    rim = pl.BlockSpec((RIM, width), lambda _: (0, 0))
    last_rim = pl.BlockSpec((RIM, width), lambda _: (tile_rows // RIM - 1, 0))
    pair = pl.BlockSpec((2 * RIM, width), lambda _: (0, 0))
    last_pair = pl.BlockSpec((2 * RIM, width), lambda _: (tile_rows // (2 * RIM) - 1, 0))
    return pl.pallas_call(
        outer_kernel,
        out_shape=jax.ShapeDtypeStruct((tile_rows, width), jnp.float32),
        grid=(1,),
        in_specs=[SMEM, VMEM, pair, last_pair, VMEM, rim, last_rim, VMEM, VMEM, ANY],
        out_specs=ANY,
        scratch_shapes=[
            pltpu.VMEM((bases, 2 * RIM, width + 2 * BLOCK), jnp.bfloat16),
            pltpu.VMEM((2 * RIM, width), jnp.float32),
            pltpu.SemaphoreType.DMA((2,)),
        ],
        input_output_aliases={9: 0},
        compiler_params=grant(58),
        name="subtract_outer",
    )(coef, above, image, image, below, exposure, exposure, rows, columns, partial)


def patch_kernel(scale_ref, rows_ref, after_ref, out_ref, wide_ref, stage_ref, sems):
    del after_ref
    slots = SLOT_ROWS * SLOT_COLS
    pitch = slots + PAD
    myself = my_device()

    @pl.loop(0, BLOCK, unroll=2)
    def _(row):
        to = pl.ds(pl.multiple_of(row * pitch, PAD), slots)
        at = pl.ds(pl.multiple_of(row * slots, slots), slots)
        wide_ref[to, :] = rows_ref[at, :].astype(jnp.float32)

    def store(down):
        at = pl.ds(pl.multiple_of(down * BLOCK, BLOCK), BLOCK)
        return pltpu.make_async_copy(stage_ref.at[at], out_ref.at[at], sems.at[down])

    @pl.loop(0, SLOT_ROWS)
    def _(down):
        to = pl.ds(pl.multiple_of(down * BLOCK, BLOCK), BLOCK)
        for across in range(SLOT_COLS):
            slot = down * SLOT_COLS + across
            stage_ref[to, across * BLOCK : (across + 1) * BLOCK] = (
                scale_ref[myself, slot] * wide_ref[pl.ds(slot, BLOCK, stride=pitch), :]
            )
        store(down).start()

    @pl.loop(0, SLOT_ROWS)
    def _(down):
        store(down).wait()


def patch(scale, rows, after):
    shape = (SLOT_ROWS * BLOCK, SLOT_COLS * BLOCK)
    return pl.pallas_call(
        patch_kernel,
        out_shape=jax.ShapeDtypeStruct(shape, jnp.float32),
        in_specs=[SMEM, VMEM, ANY],
        out_specs=ANY,
        scratch_shapes=[
            pltpu.VMEM((rows.shape[0] + BLOCK * PAD, BLOCK), jnp.float32),
            pltpu.VMEM(shape, jnp.float32),
            pltpu.SemaphoreType.DMA((SLOT_ROWS,)),
        ],
        compiler_params=grant(14),
        name="patch",
    )(scale, rows, after)


def exchange(rows, devices):
    shaped = rows.reshape(devices, -1, BLOCK)
    moved = lax.all_to_all(shaped, ("exp", "tile"), split_axis=0, concat_axis=0, tiled=True)
    return moved.reshape(rows.shape)


def shards(
    exposure,
    row_taps,
    column_taps,
    basis_coef,
    warp_rows,
    warp_columns,
    warp_id,
    route_device,
    route_slot,
    weight,
):
    devices = lax.axis_size("exp") * lax.axis_size("tile")
    image = exposure[0]
    tile_rows, width = image.shape
    per_tile = tile_rows * width // (BLOCK * BLOCK)
    slot_count = SLOT_ROWS * SLOT_COLS
    ident = warp_id.reshape(devices, per_tile)

    above, below = swap_rims(image[:RIM], image[tile_rows - RIM :])
    rows, columns = band_matrices(row_taps, column_taps)
    weighted = forward(
        ident, weight, basis_coef, above, image, below, rows, columns, warp_rows, warp_columns
    )
    arrived = exchange(weighted, devices)

    owner = route_device.reshape(-1)
    place = route_slot.reshape(-1)
    block_weight = jnp.repeat(weight.reshape(-1), per_tile)
    by_owner = jnp.where(
        owner[None, :] == jnp.arange(devices, dtype=jnp.int32)[:, None], block_weight[None, :], 0.0
    )
    by_place = (place[:, None] == jnp.arange(slot_count, dtype=jnp.int32)[None, :]).astype(
        jnp.float32
    )
    total = jnp.dot(by_owner, by_place, precision=lax.Precision.HIGHEST)
    scale = 1.0 / jnp.maximum(total, 1.0)
    slots = (route_device * slot_count + route_slot).reshape(devices, per_tile)
    my_slots = lax.dynamic_slice_in_dim(slots, my_device(), 1, 0)
    block_scale = scale.reshape(-1)[my_slots]

    template_rows, coadd_rows = slot_sums(slots, arrived, block_scale)
    returned = exchange(template_rows, devices)
    owned = exchange(coadd_rows, devices)

    template, top, bottom = unwarp(
        ident, block_scale, returned, warp_rows, warp_columns, tile_rows
    )
    above, below = swap_rims(top, bottom)
    difference = subtract_inner(basis_coef, template, image, rows, columns)
    difference = subtract_outer(
        basis_coef, above, template, below, image, rows, columns, difference
    )
    return patch(scale, owned, difference), difference[None]


def solution(mesh):
    placed = (P("exp", "tile", None), P(), P(), P("exp", None), P(), P(), P(), P(), P(), P())
    return jax.shard_map(
        shards,
        mesh=mesh,
        in_specs=placed,
        out_specs=(P("exp", "tile"), P("exp", "tile", None)),
        check_vma=False,
    )
```

time: 190 us -> 166 us (0.87)
  Pallas kernels: 78.6 us -> 61.6 us
  other arithmetic: 3.84 us -> 0.04 us
  local copies, waits for them, and re-layouts: 9.72 us -> 6.44 us
  waiting for transfers between devices: 28.8 us -> 31.7 us
    pallas_call x2, Pallas kernels: 50.2 us -> 32.2 us  [the longest x1 18.2 us: slot_sums(): pl.pallas_call(slots_kernel, out_shape=(shape, shape), in_specs=[ANY, VME...]
    ppermute x2, waiting for transfers between devices: 0.01 us -> 6.28 us  [swap_rims(): lax.ppermute(bottom, 'tile', forward)]
    all_to_all x2, waiting for transfers between devices: 28.8 us -> 25.4 us  [exchange(): lax.all_to_all(shaped, ('exp', 'tile'), split_axis=0, concat_axis=0, tile...]
    convert_element_type x2 -> x0, other arithmetic: 2.52 us -> none  [the longest x1 1.26 us: band_matrices(): row_taps.astype(jnp.float32)]
  transfers between devices with their start and end apart: 6 -> 6, of which waited for: 1 -> 3; matrix products, arithmetic and copies ran while one was open for 6% -> 2% of each run, Pallas kernels for 13% -> 15%
where the time goes in v3:
time: 166 us
  Pallas kernels  61.6 us (37%)
  blocking collectives  34.5 us (21%)
  waiting for transfers between devices  31.7 us (19%)
  starting transfers between devices  27.7 us (17%)
  local copies, waits for them, and re-layouts  6.44 us (4%)
  matrix products  2.66 us (2%)
    all_to_all x1, blocking collectives, exchange(): lax.all_to_all(shaped, ('exp', 'tile'), split_axis=0, concat_axis=0, tile...  34.5 us
    all_to_all x2, waiting for transfers between devices, exchange(): lax.all_to_all(shaped, ('exp', 'tile'), split_axis=0, concat_axis=0, tile...  25.4 us
    pallas_call x1, Pallas kernels, slot_sums(): pl.pallas_call(slots_kernel, out_shape=(shape, shape), in_specs=[ANY, VME...  18.2 us
    pallas_call x1, Pallas kernels, forward(): pl.pallas_call(forward_kernel, out_shape=jax.ShapeDtypeStruct((lines, BLO...  14 us
    all_to_all x2, starting transfers between devices, exchange(): lax.all_to_all(shaped, ('exp', 'tile'), split_axis=0, concat_axis=0, tile...  13.1 us
    pallas_call x1, Pallas kernels, subtract_inner(): pl.pallas_call(inner_kernel, out_shape=jax.ShapeDtypeStruct((tile_rows, w...  9.78 us
    ppermute x2, starting transfers between devices, swap_rims(): lax.ppermute(top, 'tile', backward)  9.31 us
    pallas_call x1, Pallas kernels, unwarp(): pl.pallas_call(unwarp_kernel, out_shape=(jax.ShapeDtypeStruct((tile_rows,...  8.54 us
  transfers between devices with their start and end apart: 6, of which 3 were waited for; matrix products, arithmetic and copies ran while one was open for 2% of the time, Pallas kernels for 15%

profile of v3, /device:TPU:8, one launch (start us, length us, event | category | flops | bytes accessed | tf_op | source)
XLA Modules:
  0.0 165.6 jit_solution(12314838092887384435)
XLA Ops:
  0.6 1.0 slice_bitcast_fusion
  1.6 4.6 %collective-permute-start.1 = (bf16[16,4096]{1,0:T(8,128)(2,1)S(1)}, bf16[16,4096]{1,0:T(8,128)(2,1)S(1)}, u32[]{:S(2)}, u32[]{:S(2)}) collective-permute-start(bf16[16,4096]{1,0:T(8,128)(2,1)S(1)} %get-tuple-element.16), channel_id=1, source_target_pairs={{1,0},{2,1},{3,2},{4,3},{5,4},{6,5},{7,6},{8,7},{9,8},{10,9},{11,1... | collective-permute-start | bytes 393224 | tf_op jit(solution)/shard_map/ppermute | solution.py:79
  6.2 1.9 %collective-permute-start = (bf16[16,4096]{1,0:T(8,128)(2,1)S(1)}, bf16[16,4096]{1,0:T(8,128)(2,1)S(1)}, u32[]{:S(2)}, u32[]{:S(2)}) collective-permute-start(bf16[16,4096]{1,0:T(8,128)(2,1)S(1)} %get-tuple-element.17), channel_id=1, source_target_pairs={{0,1},{1,2},{2,3},{3,4},{4,5},{5,6},{6,7},{7,8},{8,9},{9,10},{10,1... | collective-permute-start | bytes 393224 | tf_op jit(solution)/shard_map/ppermute | solution.py:79
  8.1 2.5 %bands.1 = (bf16[384,160]{1,0:T(8,128)(2,1)}, bf16[1152,256]{1,0:T(8,128)(2,1)}) custom-call(bf16[3,21]{1,0:T(4,128)(2,1)} %row_taps_ref.1, bf16[3,21]{1,0:T(4,128)(2,1)} %column_taps_ref.1), custom_call_target="tpu_custom_call" | custom-call | tf_op jit(solution)/shard_map/bands/pallas_call | solution.py:62
  10.6 0.0 collective-permute-done.1.below_ref
  10.6 0.0 copy-start.5
  10.6 4.5 %collective-permute-done.above_ref = bf16[16,4096]{1,0:T(8,128)(2,1)S(1)} collective-permute-done((bf16[16,4096]{1,0:T(8,128)(2,1)S(1)}, bf16[16,4096]{1,0:T(8,128)(2,1)S(1)}, u32[]{:S(2)}, u32[]{:S(2)}) %collective-permute-start) | collective-permute-done | bytes 131104 | tf_op jit(solution)/shard_map/ppermute | solution.py:79
  15.2 0.0 copy-start.8
  15.2 0.0 copy-done.5
  15.2 0.7 copy-done.8
  15.8 14.0 %match_warp.1 = bf16[8192,128]{1,0:T(8,128)(2,1)} custom-call(s32[128,64]{1,0:T(8,128)} %bitcast.34, f32[8,16]{1,0:T(8,128)} %weight_ref.1, f32[1,3]{1,0:T(1,128)} %coef_ref.5, bf16[16,4096]{1,0:T(8,128)(2,1)} %copy-done.8, bf16[256,4096]{1,0:T(8,128)(2,1)} %bitcast.28, bf16[16,4096]{1,0:T(8,128)(2,1)} %copy-done.5, ...), custom_call_target="tpu_custom_call" | custom-call | tf_op jit(solution)/shard_map/match_warp/pallas_call | solution.py:279
  29.8 0.0 copy-start.9
  29.8 0.0 copy-start.3
  29.9 0.0 copy-start.4
  29.9 8.1 %all-to-all-start = ((bf16[128,64,128]{2,1,0:T(8,128)(2,1)}), bf16[128,64,128]{2,1,0:T(8,128)(2,1)S(1)}, u32[]{:S(2)}, u32[]{:S(2)}) async-start(bf16[128,64,128]{2,1,0:T(8,128)(2,1)} %bitcast.33), calls=%async_computation | async-start | bytes 4194304 | tf_op jit(solution)/shard_map/all_to_all | solution.py:654
  38.0 0.0 copy-done.9
  38.0 0.1 reshape.42
  38.1 0.0 copy-done.3
  38.1 0.1 eq.30
  38.2 0.0 copy-done.4
  38.2 0.1 eq.34
  38.2 0.1 broadcast_in_dim.25
  38.3 0.1 broadcast_in_dim.26
  38.4 2.7 %fusion.8.scale_ref = f32[128,64]{1,0:T(8,128)S(1)} fusion(f32[8192]{0:T(1024)S(1)} %broadcast_in_dim.26, s32[8192]{0:T(1024)S(1)} %eq.30, s32[8192]{0:T(1024)S(1)} %eq.34), kind=kOutput, calls=%fused_computation.9 | convolution fusion | flops 807944192 | bytes 131072 | tf_op jit(solution)/shard_map/dot_general | solution.py:693
  41.1 0.1 reshape.48
  41.2 0.1 copy.18
  41.3 0.8 gather_fusion
  42.0 0.0 copy-start.2
  42.0 25.4 %all-to-all-done = bf16[128,64,128]{2,1,0:T(8,128)(2,1)S(1)} async-done(((bf16[128,64,128]{2,1,0:T(8,128)(2,1)}), bf16[128,64,128]{2,1,0:T(8,128)(2,1)S(1)}, u32[]{:S(2)}, u32[]{:S(2)}) %all-to-all-start) | async-done | bytes 2097184 | tf_op jit(solution)/shard_map/all_to_all | solution.py:654
  67.4 18.2 %slot_sums.1 = (bf16[8192,128]{1,0:T(8,128)(2,1)S(1)}, bf16[8192,128]{1,0:T(8,128)(2,1)S(1)}) custom-call(s32[64,1,128]{2,1,0:T(1,128)S(1)} %bitcast.25, bf16[8192,128]{1,0:T(8,128)(2,1)S(1)} %bitcast.22, f32[1,64]{1,0:T(1,128)S(1)} %bitcast.26), custom_call_target="tpu_custom_call" | custom-call | tf_op jit(solution)/shard_map/slot_sums/pallas_call | solution.py:352
  85.6 0.0 copy-start.1
  85.6 34.5 %all_to_all.15 = bf16[128,64,128]{2,1,0:T(8,128)(2,1)} all-to-all(bf16[128,64,128]{2,1,0:T(8,128)(2,1)S(1)} %bitcast.24), channel_id=1, replica_groups=mesh['exp'=8,'tile'=16] {'exp','tile'}, dimensions={0} | all-to-all | bytes 4194304 | tf_op jit(solution)/shard_map/all_to_all | solution.py:654
  120.1 0.0 copy-done.2
  120.1 0.0 copy-done.1
  120.1 5.0 %all-to-all-start.1 = ((bf16[128,64,128]{2,1,0:T(8,128)(2,1)}), bf16[128,64,128]{2,1,0:T(8,128)(2,1)S(1)}, u32[]{:S(2)}, u32[]{:S(2)}) async-start(bf16[128,64,128]{2,1,0:T(8,128)(2,1)} %bitcast.23), calls=%async_computation.1 | async-start | bytes 4194304 | tf_op jit(solution)/shard_map/all_to_all | solution.py:654
  125.1 8.5 %unwarp.1 = (bf16[256,4096]{1,0:T(8,128)(2,1)}, bf16[16,4096]{1,0:T(8,128)(2,1)}, bf16[16,4096]{1,0:T(8,128)(2,1)}) custom-call(s32[128,64]{1,0:T(8,128)} %bitcast.35, f32[1,64]{1,0:T(1,128)} %bitcast.27, bf16[8192,128]{1,0:T(8,128)(2,1)} %bitcast.32, bf16[64,128,128]{2,1,0:T(8,128)(2,1)} %bank_rows_ref.3, bf16[64,128,128]{2,1,0:T(8,128)(2,1)} %bank_columns_ref.3), custom_call_target="tpu_custom_call" | custom-call | tf_op jit(solution)/shard_map/unwarp/pallas_call | solution.py:444
  133.6 3.4 %collective-permute-start.2 = (bf16[16,4096]{1,0:T(8,128)(2,1)}, bf16[16,4096]{1,0:T(8,128)(2,1)S(1)}, u32[]{:S(2)}, u32[]{:S(2)}) collective-permute-start(bf16[16,4096]{1,0:T(8,128)(2,1)} %get-tuple-element.13), channel_id=1, source_target_pairs={{0,1},{1,2},{2,3},{3,4},{4,5},{5,6},{6,7},{7,8},{8,9},{9,10},{10,1... | collective-permute-start | bytes 393224 | tf_op jit(solution)/shard_map/ppermute | solution.py:79
  137.0 4.8 %collective-permute-start.3 = (bf16[16,4096]{1,0:T(8,128)(2,1)}, bf16[16,4096]{1,0:T(8,128)(2,1)S(1)}, u32[]{:S(2)}, u32[]{:S(2)}) collective-permute-start(bf16[16,4096]{1,0:T(8,128)(2,1)} %get-tuple-element.15), channel_id=1, source_target_pairs={{1,0},{2,1},{3,2},{4,3},{5,4},{6,5},{7,6},{8,7},{9,8},{10,9},{11,1... | collective-permute-start | bytes 393224 | tf_op jit(solution)/shard_map/ppermute | solution.py:79
  141.8 9.8 %subtract_inner.1.partial_ref = f32[256,4096]{1,0:T(8,128)} custom-call(f32[1,3]{1,0:T(1,128)} %coef_ref.5, bf16[256,4096]{1,0:T(8,128)(2,1)} %get-tuple-element.14.image_hbm.top_ref.bottom_ref, bf16[256,4096]{1,0:T(8,128)(2,1)} %bitcast.29, bf16[384,160]{1,0:T(8,128)(2,1)} %get-tuple-element.9.rows_ref, bf16[1152,256]{1,0:T(8,128)(2,1)} %get-tuple-element.10.columns_ref), custom_call_target="tpu_custom_call" | custom-call | tf_op jit(solution)/shard_map/subtract_inner/pallas_call | solution.py:514
  151.6 1.8 %collective-permute-done.2.above_ref = bf16[16,4096]{1,0:T(8,128)(2,1)S(1)} collective-permute-done((bf16[16,4096]{1,0:T(8,128)(2,1)}, bf16[16,4096]{1,0:T(8,128)(2,1)S(1)}, u32[]{:S(2)}, u32[]{:S(2)}) %collective-permute-start.2) | collective-permute-done | bytes 131104 | tf_op jit(solution)/shard_map/ppermute | solution.py:79
  153.4 0.0 copy-start.6
  153.4 0.0 collective-permute-done.3.below_ref
  153.4 0.6 copy-done.6
  154.0 0.0 copy-start.7
  154.0 0.6 copy-done.7
  154.6 4.3 %subtract_outer.1.after_ref = f32[256,4096]{1,0:T(8,128)} custom-call(f32[1,3]{1,0:T(1,128)} %coef_ref.5, bf16[16,4096]{1,0:T(8,128)(2,1)} %copy-done.6, bf16[256,4096]{1,0:T(8,128)(2,1)} %get-tuple-element.14.image_hbm.top_ref.bottom_ref, bf16[256,4096]{1,0:T(8,128)(2,1)} %get-tuple-element.14.image_hbm.top_ref.bottom_ref, ...), custom_call_target="tpu_custom_call", output_to_operand_aliasing={{}: (9, {})} | custom-call | tf_op jit(solution)/shard_map/subtract_outer/pallas_call | solution.py:587
  158.9 0.0 all-to-all-done.1
  158.9 0.0 copy-start
  158.9 2.2 %copy-done = f32[256,4096]{1,0:T(8,128)S(1)} copy-done((f32[256,4096]{1,0:T(8,128)S(1)}, f32[256,4096]{1,0:T(8,128)}, u32[]{:S(2)}) %copy-start) | copy-done | bytes 4194328
  161.1 4.3 %patch.1 = f32[1024,1024]{1,0:T(8,128)} custom-call(f32[128,64]{1,0:T(8,128)S(1)} %fusion.8.scale_ref, bf16[8192,128]{1,0:T(8,128)(2,1)S(1)} %bitcast.21, f32[256,4096]{1,0:T(8,128)S(1)} %copy-done), custom_call_target="tpu_custom_call" | custom-call | tf_op jit(solution)/shard_map/patch/pallas_call | solution.py:637
  (3 shorter events, 0.0 us)
Async XLA Ops:
  1.6 9.0 %collective-permute-start.1 = (bf16[16,4096]{1,0:T(8,128)(2,1)S(1)}, bf16[16,4096]{1,0:T(8,128)(2,1)S(1)}, u32[]{:S(2)}, u32[]{:S(2)}) collective-permute-start(bf16[16,4096]{1,0:T(8,128)(2,1)S(1)} %get-tuple-element.16), channel_id=1, source_target_pairs={{1,0},{2,1},{3,2},{4,3},{5,4},{6,5},{7,6},{8,7},{9,8},{10,9},{11,1... | collective-permute-start | bytes 393224 | tf_op jit(solution)/shard_map/ppermute | solution.py:79
  6.2 9.0 %collective-permute-start = (bf16[16,4096]{1,0:T(8,128)(2,1)S(1)}, bf16[16,4096]{1,0:T(8,128)(2,1)S(1)}, u32[]{:S(2)}, u32[]{:S(2)}) collective-permute-start(bf16[16,4096]{1,0:T(8,128)(2,1)S(1)} %get-tuple-element.17), channel_id=1, source_target_pairs={{0,1},{1,2},{2,3},{3,4},{4,5},{5,6},{6,7},{7,8},{8,9},{9,10},{10,1... | collective-permute-start | bytes 393224 | tf_op jit(solution)/shard_map/ppermute | solution.py:79
  10.6 4.5 %copy-start.5 = (bf16[16,4096]{1,0:T(8,128)(2,1)}, bf16[16,4096]{1,0:T(8,128)(2,1)S(1)}, u32[]{:S(2)}) copy-start(bf16[16,4096]{1,0:T(8,128)(2,1)S(1)} %collective-permute-done.1.below_ref) | copy-start | bytes 393220
  15.2 0.7 copy-start.8
  29.8 8.2 %copy-start.9 = (f32[8,16]{1,0:T(8,128)S(1)}, f32[8,16]{1,0:T(8,128)}, u32[]{:S(2)}) copy-start(f32[8,16]{1,0:T(8,128)} %weight_ref.1) | copy-start | bytes 1540
  29.8 8.2 %copy-start.3 = (s32[8,16,64]{2,1,0:T(8,128)S(1)}, s32[8,16,64]{2,1,0:T(8,128)}, u32[]{:S(2)}) copy-start(s32[8,16,64]{2,1,0:T(8,128)} %param.17) | copy-start | bytes 98308
  29.9 8.3 %copy-start.4 = (s32[8,16,64]{2,1,0:T(8,128)S(1)}, s32[8,16,64]{2,1,0:T(8,128)}, u32[]{:S(2)}) copy-start(s32[8,16,64]{2,1,0:T(8,128)} %param.18) | copy-start | bytes 98308
  29.9 37.6 %all-to-all-start = ((bf16[128,64,128]{2,1,0:T(8,128)(2,1)}), bf16[128,64,128]{2,1,0:T(8,128)(2,1)S(1)}, u32[]{:S(2)}, u32[]{:S(2)}) async-start(bf16[128,64,128]{2,1,0:T(8,128)(2,1)} %bitcast.33), calls=%async_computation | async-start | bytes 4194304 | tf_op jit(solution)/shard_map/all_to_all | solution.py:654
  42.0 78.1 %copy-start.2 = (f32[64]{0:T(128)}, f32[64]{0:T(128)S(1)}, u32[]{:S(2)}) copy-start(f32[64]{0:T(128)S(1)} %gather_fusion) | copy-start | bytes 772
  85.6 34.5 %copy-start.1 = (bf16[8192,128]{1,0:T(8,128)(2,1)}, bf16[8192,128]{1,0:T(8,128)(2,1)S(1)}, u32[]{:S(2)}) copy-start(bf16[8192,128]{1,0:T(8,128)(2,1)S(1)} %get-tuple-element.11) | copy-start | bytes 6291460
  120.1 38.8 %all-to-all-start.1 = ((bf16[128,64,128]{2,1,0:T(8,128)(2,1)}), bf16[128,64,128]{2,1,0:T(8,128)(2,1)S(1)}, u32[]{:S(2)}, u32[]{:S(2)}) async-start(bf16[128,64,128]{2,1,0:T(8,128)(2,1)} %bitcast.23), calls=%async_computation.1 | async-start | bytes 4194304 | tf_op jit(solution)/shard_map/all_to_all | solution.py:654
  133.6 19.7 %collective-permute-start.2 = (bf16[16,4096]{1,0:T(8,128)(2,1)}, bf16[16,4096]{1,0:T(8,128)(2,1)S(1)}, u32[]{:S(2)}, u32[]{:S(2)}) collective-permute-start(bf16[16,4096]{1,0:T(8,128)(2,1)} %get-tuple-element.13), channel_id=1, source_target_pairs={{0,1},{1,2},{2,3},{3,4},{4,5},{5,6},{6,7},{7,8},{8,9},{9,10},{10,1... | collective-permute-start | bytes 393224 | tf_op jit(solution)/shard_map/ppermute | solution.py:79
  137.0 16.3 %collective-permute-start.3 = (bf16[16,4096]{1,0:T(8,128)(2,1)}, bf16[16,4096]{1,0:T(8,128)(2,1)S(1)}, u32[]{:S(2)}, u32[]{:S(2)}) collective-permute-start(bf16[16,4096]{1,0:T(8,128)(2,1)} %get-tuple-element.15), channel_id=1, source_target_pairs={{1,0},{2,1},{3,2},{4,3},{5,4},{6,5},{7,6},{8,7},{9,8},{10,9},{11,1... | collective-permute-start | bytes 393224 | tf_op jit(solution)/shard_map/ppermute | solution.py:79
  153.4 0.6 copy-start.6
  154.0 0.6 copy-start.7
  158.9 2.2 %copy-start = (f32[256,4096]{1,0:T(8,128)S(1)}, f32[256,4096]{1,0:T(8,128)}, u32[]{:S(2)}) copy-start(f32[256,4096]{1,0:T(8,128)} %subtract_outer.1.after_ref) | copy-start | bytes 12582916

commit v4 on v3

--- a/solution.py
+++ b/solution.py
@@ -21,13 +21,15 @@
 VMEM = pl.BlockSpec(memory_space=pltpu.VMEM)
 SMEM = pl.BlockSpec(memory_space=pltpu.SMEM)
 ANY = pl.BlockSpec(memory_space=pl.ANY)
+HBM = pl.BlockSpec(memory_space=pltpu.HBM)
+GROUPS = 4
 
 
 def grant(mebibytes):
     return pltpu.CompilerParams(vmem_limit_bytes=mebibytes * 1024 * 1024)
 
 
-def bands_kernel(row_taps_ref, column_taps_ref, rows_ref, columns_ref):
+def make_bands(row_taps_ref, column_taps_ref, rows_ref, columns_ref):
     bases, taps = row_taps_ref.shape
     lead = RIM - HALF
 
@@ -55,21 +57,6 @@
         top = bases * CHUNK + base * BLOCK
         columns_ref[top : top + RIM, BLOCK:] = band[WINDOW - RIM :]
         columns_ref[top + BLOCK - RIM : top + BLOCK, :BLOCK] = band[:RIM]
-
-
-def band_matrices(row_taps, column_taps):
-    bases = row_taps.shape[0]
-    return pl.pallas_call(
-        bands_kernel,
-        out_shape=(
-            jax.ShapeDtypeStruct((bases * BLOCK, WINDOW), jnp.bfloat16),
-            jax.ShapeDtypeStruct((bases * SPAN, CHUNK), jnp.bfloat16),
-        ),
-        in_specs=[VMEM, VMEM],
-        out_specs=(VMEM, VMEM),
-        compiler_params=grant(58),
-        name="bands",
-    )(row_taps, column_taps)
 
 
 def swap_rims(top, bottom):
@@ -150,7 +137,7 @@
     return copy
 
 
-def passes(fetch, step, consume, pass_ref, width):
+def passes(fetch, step, consume, pass_ref, width, load=None):
     wides = width // WIDE
 
     def wide_step(index):
@@ -161,6 +148,8 @@
     clear(pass_ref, BLOCK + width)
     wide_step(0)
     wide_step(1)
+    if load is not None:
+        load.wait()
 
     @pl.loop(0, wides - 2)
     def _(index):
@@ -179,19 +168,23 @@
     above_ref,
     image_hbm,
     below_ref,
+    row_taps_ref,
+    column_taps_ref,
+    bank_rows_ref,
+    bank_columns_ref,
+    out_hbm,
     rows_ref,
     columns_ref,
-    bank_rows_ref,
-    bank_columns_ref,
-    out_ref,
     image_ref,
     pass_ref,
     matched_ref,
     turned_ref,
+    out_ref,
     warp_rows_ref,
     warp_columns_ref,
     fetch_sems,
     load_sems,
+    store_sems,
 ):
     tile_rows, width = image_ref.shape
     parts = tile_rows // BLOCK
@@ -209,6 +202,7 @@
         fetch(index).start()
     for load in loads:
         load.start()
+    make_bands(row_taps_ref, column_taps_ref, rows_ref, columns_ref)
 
     strips = [
         (0, BLOCK, [(above_ref, 0, RIM, 0), (image_ref, 0, BLOCK + RIM, 0)]),
@@ -265,35 +259,55 @@
         for item, second in todo:
             turned_ref[pl.ds(item, BLOCK, stride=pitch), :] = weight * second
 
-    @pl.loop(0, BLOCK, unroll=4)
-    def _(row):
-        to = pl.ds(pl.multiple_of(row * items, items), items)
-        at = pl.ds(pl.multiple_of(row * pitch, PAD), items)
-        out_ref[to, :] = turned_ref[at, :].astype(jnp.bfloat16)
-
-
-def forward(ident, weight, coef, above, image, below, rows, columns, warp_rows, warp_columns):
+    lines = out_ref.shape[0] // GROUPS
+
+    def store(group):
+        at = pl.ds(pl.multiple_of(group * lines, lines), lines)
+        return pltpu.make_async_copy(out_ref.at[at], out_hbm.at[at], store_sems.at[group])
+
+    for group in range(GROUPS):
+
+        @pl.loop(group * BLOCK // GROUPS, (group + 1) * BLOCK // GROUPS, unroll=2)
+        def _(row):
+            to = pl.ds(pl.multiple_of(row * items, items), items)
+            at = pl.ds(pl.multiple_of(row * pitch, PAD), items)
+            out_ref[to, :] = turned_ref[at, :].astype(jnp.bfloat16)
+
+        store(group).start()
+    for group in range(GROUPS):
+        store(group).wait()
+
+
+def forward(
+    ident, weight, coef, above, image, below, row_taps, column_taps, warp_rows, warp_columns
+):
     tile_rows, width = image.shape
-    bases = rows.shape[0] // BLOCK
+    bases = row_taps.shape[0]
     lines = tile_rows * width // BLOCK
     return pl.pallas_call(
         forward_kernel,
-        out_shape=jax.ShapeDtypeStruct((lines, BLOCK), jnp.bfloat16),
-        in_specs=[SMEM, SMEM, SMEM, VMEM, ANY, VMEM, VMEM, VMEM, ANY, ANY],
-        out_specs=VMEM,
+        out_shape=(
+            jax.ShapeDtypeStruct((lines, BLOCK), jnp.bfloat16),
+            jax.ShapeDtypeStruct((bases * BLOCK, WINDOW), jnp.bfloat16),
+            jax.ShapeDtypeStruct((bases * SPAN, CHUNK), jnp.bfloat16),
+        ),
+        in_specs=[SMEM, SMEM, SMEM, VMEM, HBM, VMEM, VMEM, VMEM, HBM, HBM],
+        out_specs=(HBM, VMEM, VMEM),
         scratch_shapes=[
             pltpu.VMEM((tile_rows, width), jnp.bfloat16),
             pltpu.VMEM((bases, tile_rows, width + 2 * BLOCK), jnp.bfloat16),
             pltpu.VMEM((tile_rows, width), jnp.bfloat16),
             pltpu.VMEM((lines + BLOCK * PAD, BLOCK), jnp.float32),
+            pltpu.VMEM((lines, BLOCK), jnp.bfloat16),
             pltpu.VMEM(warp_rows.shape, jnp.bfloat16),
             pltpu.VMEM(warp_columns.shape, jnp.bfloat16),
             pltpu.SemaphoreType.DMA((width // WIDE,)),
             pltpu.SemaphoreType.DMA((2,)),
+            pltpu.SemaphoreType.DMA((GROUPS,)),
         ],
         compiler_params=grant(58),
         name="match_warp",
-    )(ident, weight, coef, above, image, below, rows, columns, warp_rows, warp_columns)
+    )(ident, weight, coef, above, image, below, row_taps, column_taps, warp_rows, warp_columns)
 
 
 def slots_kernel(slot_hbm, arrived_ref, scale_ref, template_ref, coadd_ref, wide_ref, *refs):
@@ -352,7 +366,7 @@
     return pl.pallas_call(
         slots_kernel,
         out_shape=(shape, shape),
-        in_specs=[ANY, VMEM, ANY],
+        in_specs=[ANY, VMEM, SMEM],
         out_specs=(VMEM, VMEM),
         scratch_shapes=[pltpu.VMEM(arrived.shape, jnp.float32)] * (1 + LANES)
         + [pltpu.SMEM((1, sources), jnp.int32)] * items
@@ -365,38 +379,58 @@
 def unwarp_kernel(
     ident_ref,
     scale_ref,
-    returned_ref,
+    returned_hbm,
     bank_rows_ref,
     bank_columns_ref,
-    out_ref,
+    out_hbm,
     top_ref,
     bottom_ref,
+    returned_ref,
+    out_ref,
     wide_ref,
     warp_rows_ref,
     warp_columns_ref,
-    sems,
+    fetch_sems,
+    load_sems,
+    store_sems,
 ):
-    tile_rows, part_width = out_ref.shape
-    across = part_width // BLOCK
+    tile_rows, width = out_ref.shape
+    across = width // BLOCK
     parts = tile_rows // BLOCK
     items = parts * across
     pitch = items + PAD
     myself = my_device()
+    lines = returned_ref.shape[0] // GROUPS
+
+    def fetch(group):
+        at = pl.ds(group * lines, lines)
+        return pltpu.make_async_copy(
+            returned_hbm.at[at], returned_ref.at[at], fetch_sems.at[group]
+        )
+
     loads = [
-        pltpu.make_async_copy(bank_rows_ref, warp_rows_ref, sems.at[0]),
-        pltpu.make_async_copy(bank_columns_ref, warp_columns_ref, sems.at[1]),
+        pltpu.make_async_copy(bank_rows_ref, warp_rows_ref, load_sems.at[0]),
+        pltpu.make_async_copy(bank_columns_ref, warp_columns_ref, load_sems.at[1]),
     ]
+    for group in range(GROUPS):
+        fetch(group).start()
     for load in loads:
         load.start()
-
-    @pl.loop(0, BLOCK, unroll=4)
-    def _(row):
-        to = pl.ds(pl.multiple_of(row * pitch, PAD), items)
-        at = pl.ds(pl.multiple_of(row * items, items), items)
-        wide_ref[to, :] = returned_ref[at, :].astype(jnp.float32)
+    for group in range(GROUPS):
+        fetch(group).wait()
+
+        @pl.loop(group * BLOCK // GROUPS, (group + 1) * BLOCK // GROUPS, unroll=2)
+        def _(row):
+            to = pl.ds(pl.multiple_of(row * pitch, PAD), items)
+            at = pl.ds(pl.multiple_of(row * items, items), items)
+            wide_ref[to, :] = returned_ref[at, :].astype(jnp.float32)
 
     for load in loads:
         load.wait()
+
+    def store(quad):
+        at = pl.ds(pl.multiple_of(quad * 4 * BLOCK, 4 * BLOCK), 4 * BLOCK)
+        return pltpu.make_async_copy(out_ref.at[:, at], out_hbm.at[:, at], store_sems.at[quad])
 
     @pl.loop(0, across // 4)
     def _(quad):
@@ -435,22 +469,31 @@
                 top_ref[:, to] = image[:RIM]
             if part == parts - 1:
                 bottom_ref[:, to] = image[BLOCK - RIM :]
+        store(quad).start()
+
+    @pl.loop(0, across // 4)
+    def _(quad):
+        store(quad).wait()
 
 
 def unwarp(ident, scale, returned, warp_rows, warp_columns, tile_rows):
     lines = returned.shape[0]
-    part_width = lines * BLOCK // tile_rows
-    rim = jax.ShapeDtypeStruct((RIM, part_width), jnp.bfloat16)
+    width = lines * BLOCK // tile_rows
+    rim = jax.ShapeDtypeStruct((RIM, width), jnp.bfloat16)
     return pl.pallas_call(
         unwarp_kernel,
-        out_shape=(jax.ShapeDtypeStruct((tile_rows, part_width), jnp.bfloat16), rim, rim),
-        in_specs=[SMEM, SMEM, VMEM, ANY, ANY],
-        out_specs=(VMEM, VMEM, VMEM),
+        out_shape=(jax.ShapeDtypeStruct((tile_rows, width), jnp.bfloat16), rim, rim),
+        in_specs=[SMEM, SMEM, HBM, HBM, HBM],
+        out_specs=(HBM, VMEM, VMEM),
         scratch_shapes=[
+            pltpu.VMEM((lines, BLOCK), jnp.bfloat16),
+            pltpu.VMEM((tile_rows, width), jnp.bfloat16),
             pltpu.VMEM((lines + BLOCK * PAD, BLOCK), jnp.float32),
             pltpu.VMEM(warp_rows.shape, jnp.bfloat16),
             pltpu.VMEM(warp_columns.shape, jnp.bfloat16),
+            pltpu.SemaphoreType.DMA((GROUPS,)),
             pltpu.SemaphoreType.DMA((2,)),
+            pltpu.SemaphoreType.DMA((width // (4 * BLOCK),)),
         ],
         compiler_params=grant(58),
         name="unwarp",
@@ -499,8 +542,7 @@
             stage_ref[:, at] = exposure_ref[:, at].astype(jnp.float32) - summed
         store(index).start()
 
-    load.wait()
-    passes(fetch, step, subtract_step, pass_ref, width)
+    passes(fetch, step, subtract_step, pass_ref, width, load)
 
     @pl.loop(0, width // WIDE)
     def _(index):
@@ -514,8 +556,8 @@
     return pl.pallas_call(
         inner_kernel,
         out_shape=jax.ShapeDtypeStruct((tile_rows, width), jnp.float32),
-        in_specs=[SMEM, ANY, ANY, VMEM, VMEM],
-        out_specs=ANY,
+        in_specs=[SMEM, HBM, HBM, VMEM, VMEM],
+        out_specs=HBM,
         scratch_shapes=[
             pltpu.VMEM((tile_rows, width), jnp.bfloat16),
             pltpu.VMEM((inner, width), jnp.bfloat16),
@@ -530,123 +572,131 @@
     )(coef, image, exposure, rows, columns)
 
 
-def outer_kernel(
+def finish_kernel(
     coef_ref,
+    scale_ref,
+    owned_ref,
     above_ref,
-    top_ref,
-    bottom_ref,
+    image_hbm,
     below_ref,
-    exposure_top_ref,
-    exposure_bottom_ref,
+    exposure_hbm,
     rows_ref,
     columns_ref,
-    partial_ref,
-    out_ref,
+    partial_hbm,
+    patch_hbm,
+    out_hbm,
+    ends_ref,
+    exposure_ref,
     pass_ref,
     stage_ref,
-    sems,
+    wide_ref,
+    patch_ref,
+    fetch_sems,
+    rim_sems,
+    patch_sems,
 ):
-    del partial_ref
-    width = top_ref.shape[1]
-    tile_rows = out_ref.shape[0]
-    wides = width // WIDE
-    strips = [
-        (0, RIM, [(above_ref, 0, RIM, 0), (top_ref, 0, 2 * RIM, 0)]),
-        (RIM, RIM, [(bottom_ref, 0, 2 * RIM, 0), (below_ref, 0, RIM, 0)]),
-    ]
-    clear(pass_ref, 0)
-    clear(pass_ref, BLOCK + width)
-    for index in range(wides):
-        row_step(
-            WIDE, index * WIDE, BLOCK + index * WIDE, strips, coef_ref, rows_ref, pass_ref
-        )
-    for index in range(wides):
-        for half, summed in enumerate(column_step(index, 2 * RIM, columns_ref, pass_ref)):
-            at = pl.ds(index * WIDE + half * CHUNK, CHUNK)
-            stage_ref[:RIM, at] = exposure_top_ref[:, at].astype(jnp.float32) - summed[:RIM]
-            stage_ref[RIM:, at] = exposure_bottom_ref[:, at].astype(jnp.float32) - summed[RIM:]
-    stores = [
-        pltpu.make_async_copy(stage_ref.at[:RIM], out_ref.at[:RIM], sems.at[0]),
-        pltpu.make_async_copy(
-            stage_ref.at[RIM:], out_ref.at[pl.ds(tile_rows - RIM, RIM)], sems.at[1]
-        ),
-    ]
-    for store in stores:
-        store.start()
-    for store in stores:
-        store.wait()
-
-
-def subtract_outer(coef, above, image, below, exposure, rows, columns, partial):
-    tile_rows, width = image.shape
-    bases = rows.shape[0] // BLOCK
-    rim = pl.BlockSpec((RIM, width), lambda _: (0, 0))
-    last_rim = pl.BlockSpec((RIM, width), lambda _: (tile_rows // RIM - 1, 0))
-    pair = pl.BlockSpec((2 * RIM, width), lambda _: (0, 0))
-    last_pair = pl.BlockSpec((2 * RIM, width), lambda _: (tile_rows // (2 * RIM) - 1, 0))
-    return pl.pallas_call(
-        outer_kernel,
-        out_shape=jax.ShapeDtypeStruct((tile_rows, width), jnp.float32),
-        grid=(1,),
-        in_specs=[SMEM, VMEM, pair, last_pair, VMEM, rim, last_rim, VMEM, VMEM, ANY],
-        out_specs=ANY,
-        scratch_shapes=[
-            pltpu.VMEM((bases, 2 * RIM, width + 2 * BLOCK), jnp.bfloat16),
-            pltpu.VMEM((2 * RIM, width), jnp.float32),
-            pltpu.SemaphoreType.DMA((2,)),
-        ],
-        input_output_aliases={9: 0},
-        compiler_params=grant(58),
-        name="subtract_outer",
-    )(coef, above, image, image, below, exposure, exposure, rows, columns, partial)
-
-
-def patch_kernel(scale_ref, rows_ref, after_ref, out_ref, wide_ref, stage_ref, sems):
-    del after_ref
+    del partial_hbm
+    tile_rows, width = out_hbm.shape
     slots = SLOT_ROWS * SLOT_COLS
     pitch = slots + PAD
     myself = my_device()
+    pair = 2 * RIM
+
+    def ends(source, target, size, first):
+        return [
+            pltpu.make_async_copy(
+                source.at[pl.ds(0, size)], target.at[pl.ds(0, size)], fetch_sems.at[first]
+            ),
+            pltpu.make_async_copy(
+                source.at[pl.ds(tile_rows - size, size)],
+                target.at[pl.ds(size, size)],
+                fetch_sems.at[first + 1],
+            ),
+        ]
+
+    fetches = ends(image_hbm, ends_ref, pair, 0) + ends(exposure_hbm, exposure_ref, RIM, 2)
+    for fetch in fetches:
+        fetch.start()
 
     @pl.loop(0, BLOCK, unroll=2)
     def _(row):
         to = pl.ds(pl.multiple_of(row * pitch, PAD), slots)
         at = pl.ds(pl.multiple_of(row * slots, slots), slots)
-        wide_ref[to, :] = rows_ref[at, :].astype(jnp.float32)
+        wide_ref[to, :] = owned_ref[at, :].astype(jnp.float32)
 
     def store(down):
         at = pl.ds(pl.multiple_of(down * BLOCK, BLOCK), BLOCK)
-        return pltpu.make_async_copy(stage_ref.at[at], out_ref.at[at], sems.at[down])
+        return pltpu.make_async_copy(patch_ref.at[at], patch_hbm.at[at], patch_sems.at[down])
 
     @pl.loop(0, SLOT_ROWS)
     def _(down):
         to = pl.ds(pl.multiple_of(down * BLOCK, BLOCK), BLOCK)
         for across in range(SLOT_COLS):
             slot = down * SLOT_COLS + across
-            stage_ref[to, across * BLOCK : (across + 1) * BLOCK] = (
+            patch_ref[to, across * BLOCK : (across + 1) * BLOCK] = (
                 scale_ref[myself, slot] * wide_ref[pl.ds(slot, BLOCK, stride=pitch), :]
             )
         store(down).start()
 
+    for fetch in fetches:
+        fetch.wait()
+    strips = [
+        (0, RIM, [(above_ref, 0, RIM, 0), (ends_ref, 0, pair, 0)]),
+        (RIM, RIM, [(ends_ref, pair, pair, 0), (below_ref, 0, RIM, 0)]),
+    ]
+    clear(pass_ref, 0)
+    clear(pass_ref, BLOCK + width)
+    for index in range(width // WIDE):
+        row_step(
+            WIDE, index * WIDE, BLOCK + index * WIDE, strips, coef_ref, rows_ref, pass_ref
+        )
+    for index in range(width // WIDE):
+        for part, summed in enumerate(column_step(index, pair, columns_ref, pass_ref)):
+            at = pl.ds(index * WIDE + part * CHUNK, CHUNK)
+            stage_ref[:, at] = exposure_ref[:, at].astype(jnp.float32) - summed
+    rims = [
+        pltpu.make_async_copy(stage_ref.at[:RIM], out_hbm.at[:RIM], rim_sems.at[0]),
+        pltpu.make_async_copy(
+            stage_ref.at[RIM:], out_hbm.at[pl.ds(tile_rows - RIM, RIM)], rim_sems.at[1]
+        ),
+    ]
+    for rim in rims:
+        rim.start()
+    for rim in rims:
+        rim.wait()
+
     @pl.loop(0, SLOT_ROWS)
     def _(down):
         store(down).wait()
 
 
-def patch(scale, rows, after):
+def finish(coef, scale, owned, above, image, below, exposure, rows, columns, partial):
+    tile_rows, width = image.shape
+    bases = rows.shape[0] // BLOCK
     shape = (SLOT_ROWS * BLOCK, SLOT_COLS * BLOCK)
     return pl.pallas_call(
-        patch_kernel,
-        out_shape=jax.ShapeDtypeStruct(shape, jnp.float32),
-        in_specs=[SMEM, VMEM, ANY],
-        out_specs=ANY,
+        finish_kernel,
+        out_shape=(
+            jax.ShapeDtypeStruct(shape, jnp.float32),
+            jax.ShapeDtypeStruct((tile_rows, width), jnp.float32),
+        ),
+        in_specs=[SMEM, SMEM, VMEM, VMEM, HBM, VMEM, HBM, VMEM, VMEM, HBM],
+        out_specs=(HBM, HBM),
         scratch_shapes=[
-            pltpu.VMEM((rows.shape[0] + BLOCK * PAD, BLOCK), jnp.float32),
+            pltpu.VMEM((4 * RIM, width), jnp.bfloat16),
+            pltpu.VMEM((2 * RIM, width), jnp.bfloat16),
+            pltpu.VMEM((bases, 2 * RIM, width + 2 * BLOCK), jnp.bfloat16),
+            pltpu.VMEM((2 * RIM, width), jnp.float32),
+            pltpu.VMEM((owned.shape[0] + BLOCK * PAD, BLOCK), jnp.float32),
             pltpu.VMEM(shape, jnp.float32),
+            pltpu.SemaphoreType.DMA((4,)),
+            pltpu.SemaphoreType.DMA((2,)),
             pltpu.SemaphoreType.DMA((SLOT_ROWS,)),
         ],
-        compiler_params=grant(14),
-        name="patch",
-    )(scale, rows, after)
+        input_output_aliases={9: 1},
+        compiler_params=grant(16),
+        name="finish",
+    )(coef, scale, owned, above, image, below, exposure, rows, columns, partial)
 
 
 def exchange(rows, devices):
@@ -675,9 +725,17 @@
     ident = warp_id.reshape(devices, per_tile)
 
     above, below = swap_rims(image[:RIM], image[tile_rows - RIM :])
-    rows, columns = band_matrices(row_taps, column_taps)
-    weighted = forward(
-        ident, weight, basis_coef, above, image, below, rows, columns, warp_rows, warp_columns
+    weighted, rows, columns = forward(
+        ident,
+        weight,
+        basis_coef,
+        above,
+        image,
+        below,
+        row_taps,
+        column_taps,
+        warp_rows,
+        warp_columns,
     )
     arrived = exchange(weighted, devices)
 
@@ -705,10 +763,10 @@
     )
     above, below = swap_rims(top, bottom)
     difference = subtract_inner(basis_coef, template, image, rows, columns)
-    difference = subtract_outer(
-        basis_coef, above, template, below, image, rows, columns, difference
+    coadd, difference = finish(
+        basis_coef, scale, owned, above, template, below, image, rows, columns, difference
     )
-    return patch(scale, owned, difference), difference[None]
+    return coadd, difference[None]
 
 
 def solution(mesh):

time: 166 us -> 168 us (1.012); the launches traced: 166 us -> 166 us
  waiting for transfers between devices: 31.7 us -> 35.2 us
  Pallas kernels: 61.6 us -> 59.1 us
  local copies, waits for them, and re-layouts: 6.44 us -> 4.58 us
    pallas_call x4 -> x2, Pallas kernels: 25.1 us -> 22.1 us  [the longest x1 15.8 us: forward(): pl.pallas_call(forward_kernel, out_shape=(jax.ShapeDtypeStruct((lines, BL...]
    all_to_all x2, waiting for transfers between devices: 25.4 us -> 28.1 us  [exchange(): lax.all_to_all(shaped, ('exp', 'tile'), split_axis=0, concat_axis=0, tile...]
    unnamed x20 -> x24, local copies, waits for them, and re-layouts: 4.15 us -> 2.29 us
  transfers between devices with their start and end apart: 6 -> 6, of which waited for: 3 -> 4; matrix products, arithmetic and copies ran while one was open for 2% -> 2% of each run, Pallas kernels for 15% -> 11%
where the time goes in v4:
time: 168 us; the launch traced here: 166 us
  Pallas kernels  59.1 us (35%)
  waiting for transfers between devices  35.2 us (21%)
  blocking collectives  34.5 us (21%)
  starting transfers between devices  28.7 us (17%)
  local copies, waits for them, and re-layouts  4.58 us (3%)
  matrix products  2.66 us (2%)
    all_to_all x1, blocking collectives, exchange(): lax.all_to_all(shaped, ('exp', 'tile'), split_axis=0, concat_axis=0, tile...  34.5 us
    all_to_all x2, waiting for transfers between devices, exchange(): lax.all_to_all(shaped, ('exp', 'tile'), split_axis=0, concat_axis=0, tile...  28.1 us
    pallas_call x1, Pallas kernels, slot_sums(): pl.pallas_call(slots_kernel, out_shape=(shape, shape), in_specs=[ANY, VME...  18.7 us
    pallas_call x1, Pallas kernels, forward(): pl.pallas_call(forward_kernel, out_shape=(jax.ShapeDtypeStruct((lines, BL...  15.8 us
    all_to_all x2, starting transfers between devices, exchange(): lax.all_to_all(shaped, ('exp', 'tile'), split_axis=0, concat_axis=0, tile...  14 us
    pallas_call x1, Pallas kernels, unwarp(): pl.pallas_call(unwarp_kernel, out_shape=(jax.ShapeDtypeStruct((tile_rows,...  9.42 us
    ppermute x2, starting transfers between devices, swap_rims(): lax.ppermute(top, 'tile', backward)  9.3 us
    pallas_call x1, Pallas kernels, subtract_inner(): pl.pallas_call(inner_kernel, out_shape=jax.ShapeDtypeStruct((tile_rows, w...  8.85 us
  transfers between devices with their start and end apart: 6, of which 4 were waited for; matrix products, arithmetic and copies ran while one was open for 2% of the time, Pallas kernels for 11%

profile of v4, /device:TPU:8, one launch (start us, length us, event | category | flops | bytes accessed | tf_op | source)
XLA Modules:
  0.0 165.7 jit_solution(34529937239234444)
XLA Ops:
  0.6 1.0 slice_bitcast_fusion
  1.6 4.6 %collective-permute-start.1 = (bf16[16,4096]{1,0:T(8,128)(2,1)S(1)}, bf16[16,4096]{1,0:T(8,128)(2,1)S(1)}, u32[]{:S(2)}, u32[]{:S(2)}) collective-permute-start(bf16[16,4096]{1,0:T(8,128)(2,1)S(1)} %get-tuple-element.22), channel_id=1, source_target_pairs={{1,0},{2,1},{3,2},{4,3},{5,4},{6,5},{7,6},{8,7},{9,8},{10,9},{11,1... | collective-permute-start | bytes 393224 | tf_op jit(solution)/shard_map/ppermute | solution.py:66
  6.2 1.9 %collective-permute-start = (bf16[16,4096]{1,0:T(8,128)(2,1)S(1)}, bf16[16,4096]{1,0:T(8,128)(2,1)S(1)}, u32[]{:S(2)}, u32[]{:S(2)}) collective-permute-start(bf16[16,4096]{1,0:T(8,128)(2,1)S(1)} %get-tuple-element.23), channel_id=1, source_target_pairs={{0,1},{1,2},{2,3},{3,4},{4,5},{5,6},{6,7},{7,8},{8,9},{9,10},{10,1... | collective-permute-start | bytes 393224 | tf_op jit(solution)/shard_map/ppermute | solution.py:66
  8.1 0.8 collective-permute-done.1.below_ref
  8.9 0.0 copy-start.9
  8.9 6.2 %collective-permute-done.above_ref = bf16[16,4096]{1,0:T(8,128)(2,1)S(1)} collective-permute-done((bf16[16,4096]{1,0:T(8,128)(2,1)S(1)}, bf16[16,4096]{1,0:T(8,128)(2,1)S(1)}, u32[]{:S(2)}, u32[]{:S(2)}) %collective-permute-start) | collective-permute-done | bytes 131104 | tf_op jit(solution)/shard_map/ppermute | solution.py:66
  15.2 0.0 copy-start.10
  15.2 0.0 copy-done.9
  15.2 0.7 copy-done.10
  15.8 15.8 %match_warp.1 = (bf16[8192,128]{1,0:T(8,128)(2,1)}, bf16[384,160]{1,0:T(8,128)(2,1)}, bf16[1152,256]{1,0:T(8,128)(2,1)}) custom-call(s32[128,64]{1,0:T(8,128)} %bitcast.32, f32[8,16]{1,0:T(8,128)} %weight_ref.1, f32[1,3]{1,0:T(1,128)} %coef_ref.5, bf16[16,4096]{1,0:T(8,128)(2,1)} %copy-done.10, bf16[256,4096]{1,0:T(8,128)(2,1)} %bitcast.20, ...), custom_call_target="tpu_custom_call" | custom-call | tf_op jit(solution)/shard_map/match_warp/pallas_call | solution.py:287
  31.7 0.0 copy-start.11
  31.7 0.0 copy-start.7
  31.7 0.0 copy-start.8
  31.7 8.1 %all-to-all-start = ((bf16[128,64,128]{2,1,0:T(8,128)(2,1)}), bf16[128,64,128]{2,1,0:T(8,128)(2,1)S(1)}, u32[]{:S(2)}, u32[]{:S(2)}) async-start(bf16[128,64,128]{2,1,0:T(8,128)(2,1)} %bitcast.31), calls=%async_computation | async-start | bytes 4194304 | tf_op jit(solution)/shard_map/all_to_all | solution.py:704
  39.8 0.0 copy-done.11
  39.8 0.1 reshape.42
  39.9 0.0 copy-done.7
  39.9 0.1 eq.30
  40.0 0.0 copy-done.8
  40.0 0.1 eq.34
  40.1 0.1 broadcast_in_dim.25
  40.1 0.1 broadcast_in_dim.26
  40.2 2.7 %fusion.8.scale_ref = f32[128,64]{1,0:T(8,128)S(1)} fusion(f32[8192]{0:T(1024)S(1)} %broadcast_in_dim.26, s32[8192]{0:T(1024)S(1)} %eq.30, s32[8192]{0:T(1024)S(1)} %eq.34), kind=kOutput, calls=%fused_computation.9 | convolution fusion | flops 807944192 | bytes 131072 | tf_op jit(solution)/shard_map/dot_general | solution.py:751
  42.9 0.1 reshape.48
  43.0 0.1 copy.18
  43.1 0.8 gather_fusion
  43.9 0.0 copy-start.6
  43.9 25.4 %all-to-all-done = bf16[128,64,128]{2,1,0:T(8,128)(2,1)S(1)} async-done(((bf16[128,64,128]{2,1,0:T(8,128)(2,1)}), bf16[128,64,128]{2,1,0:T(8,128)(2,1)S(1)}, u32[]{:S(2)}, u32[]{:S(2)}) %all-to-all-start) | async-done | bytes 2097184 | tf_op jit(solution)/shard_map/all_to_all | solution.py:704
  69.3 18.7 %slot_sums.1 = (bf16[8192,128]{1,0:T(8,128)(2,1)S(1)}, bf16[8192,128]{1,0:T(8,128)(2,1)S(1)}) custom-call(s32[64,1,128]{2,1,0:T(1,128)S(1)} %bitcast.26, bf16[8192,128]{1,0:T(8,128)(2,1)S(1)} %bitcast.23, f32[1,64]{1,0:T(1,128)S(1)} %bitcast.27), custom_call_target="tpu_custom_call" | custom-call | tf_op jit(solution)/shard_map/slot_sums/pallas_call | solution.py:366
  88.0 0.0 copy-start.3
  88.0 34.5 %all_to_all.15 = bf16[128,64,128]{2,1,0:T(8,128)(2,1)} all-to-all(bf16[128,64,128]{2,1,0:T(8,128)(2,1)S(1)} %bitcast.25), channel_id=1, replica_groups=mesh['exp'=8,'tile'=16] {'exp','tile'}, dimensions={0} | all-to-all | bytes 4194304 | tf_op jit(solution)/shard_map/all_to_all | solution.py:704
  122.5 0.0 copy-done.6
  122.5 0.0 copy-done.3
  122.5 5.9 %all-to-all-start.1 = ((bf16[128,64,128]{2,1,0:T(8,128)(2,1)}), bf16[128,64,128]{2,1,0:T(8,128)(2,1)}, u32[]{:S(2)}, u32[]{:S(2)}) async-start(bf16[128,64,128]{2,1,0:T(8,128)(2,1)} %bitcast.24), calls=%async_computation.1 | async-start | bytes 4194304 | tf_op jit(solution)/shard_map/all_to_all | solution.py:704
  128.4 9.4 %unwarp.1 = (bf16[256,4096]{1,0:T(8,128)(2,1)}, bf16[16,4096]{1,0:T(8,128)(2,1)}, bf16[16,4096]{1,0:T(8,128)(2,1)}) custom-call(s32[128,64]{1,0:T(8,128)} %bitcast.33, f32[1,64]{1,0:T(1,128)} %bitcast.28, bf16[8192,128]{1,0:T(8,128)(2,1)} %bitcast.30, bf16[64,128,128]{2,1,0:T(8,128)(2,1)} %bank_rows_ref.3, bf16[64,128,128]{2,1,0:T(8,128)(2,1)} %bank_columns_ref.3), custom_call_target="tpu_custom_call" | custom-call | tf_op jit(solution)/shard_map/unwarp/pallas_call | solution.py:483
  137.9 3.4 %collective-permute-start.2 = (bf16[16,4096]{1,0:T(8,128)(2,1)}, bf16[16,4096]{1,0:T(8,128)(2,1)S(1)}, u32[]{:S(2)}, u32[]{:S(2)}) collective-permute-start(bf16[16,4096]{1,0:T(8,128)(2,1)} %get-tuple-element.15), channel_id=1, source_target_pairs={{0,1},{1,2},{2,3},{3,4},{4,5},{5,6},{6,7},{7,8},{8,9},{9,10},{10,1... | collective-permute-start | bytes 393224 | tf_op jit(solution)/shard_map/ppermute | solution.py:66
  141.3 4.7 %collective-permute-start.3 = (bf16[16,4096]{1,0:T(8,128)(2,1)}, bf16[16,4096]{1,0:T(8,128)(2,1)S(1)}, u32[]{:S(2)}, u32[]{:S(2)}) collective-permute-start(bf16[16,4096]{1,0:T(8,128)(2,1)} %get-tuple-element.17), channel_id=1, source_target_pairs={{1,0},{2,1},{3,2},{4,3},{5,4},{6,5},{7,6},{8,7},{9,8},{10,9},{11,1... | collective-permute-start | bytes 393224 | tf_op jit(solution)/shard_map/ppermute | solution.py:66
  146.0 0.0 copy-start
  146.0 0.0 copy-start.2
  146.0 0.0 copy-start.4
  146.0 0.0 copy-start.5
  146.1 8.8 %subtract_inner.1.partial_hbm = f32[256,4096]{1,0:T(8,128)} custom-call(f32[1,3]{1,0:T(1,128)} %coef_ref.5, bf16[256,4096]{1,0:T(8,128)(2,1)} %get-tuple-element.16.image_hbm, bf16[256,4096]{1,0:T(8,128)(2,1)} %bitcast.21, bf16[384,160]{1,0:T(8,128)(2,1)} %get-tuple-element.18.rows_ref, bf16[1152,256]{1,0:T(8,128)(2,1)} %get-tuple-element.19.columns_ref), custom_call_target="tpu_custom_call" | custom-call | tf_op jit(solution)/shard_map/subtract_inner/pallas_call | solution.py:556
  154.9 2.7 %all-to-all-done.1 = bf16[128,64,128]{2,1,0:T(8,128)(2,1)} async-done(((bf16[128,64,128]{2,1,0:T(8,128)(2,1)}), bf16[128,64,128]{2,1,0:T(8,128)(2,1)}, u32[]{:S(2)}, u32[]{:S(2)}) %all-to-all-start.1) | async-done | bytes 2097184 | tf_op jit(solution)/shard_map/all_to_all | solution.py:704
  157.6 0.0 collective-permute-done.2.above_ref
  157.6 0.0 collective-permute-done.3.below_ref
  157.6 0.0 copy-done
  157.6 0.0 copy-done.2
  157.6 0.0 copy-done.4
  157.7 0.0 copy-done.5
  157.7 0.0 copy-start.1
  157.7 1.6 copy-done.1
  159.3 6.2 %finish.1 = (f32[1024,1024]{1,0:T(8,128)}, f32[256,4096]{1,0:T(8,128)}) custom-call(f32[1,3]{1,0:T(1,128)S(1)} %copy-done.5, f32[128,64]{1,0:T(8,128)S(1)} %fusion.8.scale_ref, bf16[8192,128]{1,0:T(8,128)(2,1)} %bitcast.12.owned_ref, bf16[16,4096]{1,0:T(8,128)(2,1)S(1)} %collective-permute-done.2.above_ref, ...), custom_call_target="tpu_custom_call", output_to_operand_aliasing={{1}: (9, {})} | custom-call | tf_op jit(solution)/shard_map/finish/pallas_call | solution.py:677
  (3 shorter events, 0.0 us)
Async XLA Ops:
  1.6 7.3 %collective-permute-start.1 = (bf16[16,4096]{1,0:T(8,128)(2,1)S(1)}, bf16[16,4096]{1,0:T(8,128)(2,1)S(1)}, u32[]{:S(2)}, u32[]{:S(2)}) collective-permute-start(bf16[16,4096]{1,0:T(8,128)(2,1)S(1)} %get-tuple-element.22), channel_id=1, source_target_pairs={{1,0},{2,1},{3,2},{4,3},{5,4},{6,5},{7,6},{8,7},{9,8},{10,9},{11,1... | collective-permute-start | bytes 393224 | tf_op jit(solution)/shard_map/ppermute | solution.py:66
  6.2 9.0 %collective-permute-start = (bf16[16,4096]{1,0:T(8,128)(2,1)S(1)}, bf16[16,4096]{1,0:T(8,128)(2,1)S(1)}, u32[]{:S(2)}, u32[]{:S(2)}) collective-permute-start(bf16[16,4096]{1,0:T(8,128)(2,1)S(1)} %get-tuple-element.23), channel_id=1, source_target_pairs={{0,1},{1,2},{2,3},{3,4},{4,5},{5,6},{6,7},{7,8},{8,9},{9,10},{10,1... | collective-permute-start | bytes 393224 | tf_op jit(solution)/shard_map/ppermute | solution.py:66
  8.9 6.2 %copy-start.9 = (bf16[16,4096]{1,0:T(8,128)(2,1)}, bf16[16,4096]{1,0:T(8,128)(2,1)S(1)}, u32[]{:S(2)}) copy-start(bf16[16,4096]{1,0:T(8,128)(2,1)S(1)} %collective-permute-done.1.below_ref) | copy-start | bytes 393220
  15.2 0.7 copy-start.10
  31.7 8.2 %copy-start.11 = (f32[8,16]{1,0:T(8,128)S(1)}, f32[8,16]{1,0:T(8,128)}, u32[]{:S(2)}) copy-start(f32[8,16]{1,0:T(8,128)} %weight_ref.1) | copy-start | bytes 1540
  31.7 8.2 %copy-start.7 = (s32[8,16,64]{2,1,0:T(8,128)S(1)}, s32[8,16,64]{2,1,0:T(8,128)}, u32[]{:S(2)}) copy-start(s32[8,16,64]{2,1,0:T(8,128)} %param.17) | copy-start | bytes 98308
  31.7 8.3 %copy-start.8 = (s32[8,16,64]{2,1,0:T(8,128)S(1)}, s32[8,16,64]{2,1,0:T(8,128)}, u32[]{:S(2)}) copy-start(s32[8,16,64]{2,1,0:T(8,128)} %param.18) | copy-start | bytes 98308
  31.7 37.6 %all-to-all-start = ((bf16[128,64,128]{2,1,0:T(8,128)(2,1)}), bf16[128,64,128]{2,1,0:T(8,128)(2,1)S(1)}, u32[]{:S(2)}, u32[]{:S(2)}) async-start(bf16[128,64,128]{2,1,0:T(8,128)(2,1)} %bitcast.31), calls=%async_computation | async-start | bytes 4194304 | tf_op jit(solution)/shard_map/all_to_all | solution.py:704
  43.9 78.6 %copy-start.6 = (f32[64]{0:T(128)}, f32[64]{0:T(128)S(1)}, u32[]{:S(2)}) copy-start(f32[64]{0:T(128)S(1)} %gather_fusion) | copy-start | bytes 772
  88.0 34.5 %copy-start.3 = (bf16[8192,128]{1,0:T(8,128)(2,1)}, bf16[8192,128]{1,0:T(8,128)(2,1)S(1)}, u32[]{:S(2)}) copy-start(bf16[8192,128]{1,0:T(8,128)(2,1)S(1)} %get-tuple-element.13) | copy-start | bytes 6291460
  122.5 35.1 %all-to-all-start.1 = ((bf16[128,64,128]{2,1,0:T(8,128)(2,1)}), bf16[128,64,128]{2,1,0:T(8,128)(2,1)}, u32[]{:S(2)}, u32[]{:S(2)}) async-start(bf16[128,64,128]{2,1,0:T(8,128)(2,1)} %bitcast.24), calls=%async_computation.1 | async-start | bytes 4194304 | tf_op jit(solution)/shard_map/all_to_all | solution.py:704
  137.9 19.8 %collective-permute-start.2 = (bf16[16,4096]{1,0:T(8,128)(2,1)}, bf16[16,4096]{1,0:T(8,128)(2,1)S(1)}, u32[]{:S(2)}, u32[]{:S(2)}) collective-permute-start(bf16[16,4096]{1,0:T(8,128)(2,1)} %get-tuple-element.15), channel_id=1, source_target_pairs={{0,1},{1,2},{2,3},{3,4},{4,5},{5,6},{6,7},{7,8},{8,9},{9,10},{10,1... | collective-permute-start | bytes 393224 | tf_op jit(solution)/shard_map/ppermute | solution.py:66
  141.3 16.4 %collective-permute-start.3 = (bf16[16,4096]{1,0:T(8,128)(2,1)}, bf16[16,4096]{1,0:T(8,128)(2,1)S(1)}, u32[]{:S(2)}, u32[]{:S(2)}) collective-permute-start(bf16[16,4096]{1,0:T(8,128)(2,1)} %get-tuple-element.17), channel_id=1, source_target_pairs={{1,0},{2,1},{3,2},{4,3},{5,4},{6,5},{7,6},{8,7},{9,8},{10,9},{11,1... | collective-permute-start | bytes 393224 | tf_op jit(solution)/shard_map/ppermute | solution.py:66
  146.0 11.6 %copy-start = (bf16[1,256,4096]{2,1,0:T(8,128)(2,1)S(1)}, bf16[1,256,4096]{2,1,0:T(8,128)(2,1)}, u32[]{:S(2)}) copy-start(bf16[1,256,4096]{2,1,0:T(8,128)(2,1)} %param.10) | copy-start | bytes 6291460
  146.0 11.6 %copy-start.2 = (bf16[1152,256]{1,0:T(8,128)(2,1)S(1)}, bf16[1152,256]{1,0:T(8,128)(2,1)}, u32[]{:S(2)}) copy-start(bf16[1152,256]{1,0:T(8,128)(2,1)} %get-tuple-element.19.columns_ref) | copy-start | bytes 1769476
  146.0 11.6 %copy-start.4 = (bf16[384,160]{1,0:T(8,128)(2,1)S(1)}, bf16[384,160]{1,0:T(8,128)(2,1)}, u32[]{:S(2)}) copy-start(bf16[384,160]{1,0:T(8,128)(2,1)} %get-tuple-element.18.rows_ref) | copy-start | bytes 368644
  146.0 11.6 %copy-start.5 = (f32[1,3]{1,0:T(1,128)S(1)}, f32[1,3]{1,0:T(1,128)}, u32[]{:S(2)}) copy-start(f32[1,3]{1,0:T(1,128)} %coef_ref.5) | copy-start | bytes 40
  157.7 1.6 copy-start.1

commit v5 on v3

--- a/solution.py
+++ b/solution.py
@@ -16,11 +16,13 @@
 WINDOW = BLOCK + 2 * RIM
 SLOT_ROWS = 8
 SLOT_COLS = 8
-LANES = 8
+LANES = 4
 PAD = 8
 VMEM = pl.BlockSpec(memory_space=pltpu.VMEM)
 SMEM = pl.BlockSpec(memory_space=pltpu.SMEM)
 ANY = pl.BlockSpec(memory_space=pl.ANY)
+HBM = pl.BlockSpec(memory_space=pltpu.HBM)
+GROUPS = 4
 
 
 def grant(mebibytes):
@@ -150,7 +152,7 @@
     return copy
 
 
-def passes(fetch, step, consume, pass_ref, width):
+def passes(fetch, step, consume, pass_ref, width, load=None):
     wides = width // WIDE
 
     def wide_step(index):
@@ -161,6 +163,8 @@
     clear(pass_ref, BLOCK + width)
     wide_step(0)
     wide_step(1)
+    if load is not None:
+        load.wait()
 
     @pl.loop(0, wides - 2)
     def _(index):
@@ -183,15 +187,17 @@
     columns_ref,
     bank_rows_ref,
     bank_columns_ref,
-    out_ref,
+    out_hbm,
     image_ref,
     pass_ref,
     matched_ref,
     turned_ref,
+    out_ref,
     warp_rows_ref,
     warp_columns_ref,
     fetch_sems,
     load_sems,
+    store_sems,
 ):
     tile_rows, width = image_ref.shape
     parts = tile_rows // BLOCK
@@ -265,38 +271,56 @@
         for item, second in todo:
             turned_ref[pl.ds(item, BLOCK, stride=pitch), :] = weight * second
 
-    @pl.loop(0, BLOCK, unroll=4)
-    def _(row):
-        to = pl.ds(pl.multiple_of(row * items, items), items)
-        at = pl.ds(pl.multiple_of(row * pitch, PAD), items)
-        out_ref[to, :] = turned_ref[at, :].astype(jnp.bfloat16)
-
-
-def forward(ident, weight, coef, above, image, below, rows, columns, warp_rows, warp_columns):
+    lines = out_ref.shape[0] // GROUPS
+
+    def store(group):
+        at = pl.ds(pl.multiple_of(group * lines, lines), lines)
+        return pltpu.make_async_copy(out_ref.at[at], out_hbm.at[at], store_sems.at[group])
+
+    for group in range(GROUPS):
+
+        @pl.loop(group * BLOCK // GROUPS, (group + 1) * BLOCK // GROUPS, unroll=2)
+        def _(row):
+            to = pl.ds(pl.multiple_of(row * items, items), items)
+            at = pl.ds(pl.multiple_of(row * pitch, PAD), items)
+            out_ref[to, :] = turned_ref[at, :].astype(jnp.bfloat16)
+
+        store(group).start()
+    for group in range(GROUPS):
+        store(group).wait()
+
+
+def forward(
+    ident, weight, coef, above, image, below, rows, columns, warp_rows, warp_columns
+):
     tile_rows, width = image.shape
     bases = rows.shape[0] // BLOCK
     lines = tile_rows * width // BLOCK
     return pl.pallas_call(
         forward_kernel,
         out_shape=jax.ShapeDtypeStruct((lines, BLOCK), jnp.bfloat16),
-        in_specs=[SMEM, SMEM, SMEM, VMEM, ANY, VMEM, VMEM, VMEM, ANY, ANY],
-        out_specs=VMEM,
+        in_specs=[SMEM, SMEM, SMEM, VMEM, HBM, VMEM, VMEM, VMEM, HBM, HBM],
+        out_specs=HBM,
         scratch_shapes=[
             pltpu.VMEM((tile_rows, width), jnp.bfloat16),
             pltpu.VMEM((bases, tile_rows, width + 2 * BLOCK), jnp.bfloat16),
             pltpu.VMEM((tile_rows, width), jnp.bfloat16),
             pltpu.VMEM((lines + BLOCK * PAD, BLOCK), jnp.float32),
+            pltpu.VMEM((lines, BLOCK), jnp.bfloat16),
             pltpu.VMEM(warp_rows.shape, jnp.bfloat16),
             pltpu.VMEM(warp_columns.shape, jnp.bfloat16),
             pltpu.SemaphoreType.DMA((width // WIDE,)),
             pltpu.SemaphoreType.DMA((2,)),
+            pltpu.SemaphoreType.DMA((GROUPS,)),
         ],
         compiler_params=grant(58),
         name="match_warp",
     )(ident, weight, coef, above, image, below, rows, columns, warp_rows, warp_columns)
 
 
-def slots_kernel(slot_hbm, arrived_ref, scale_ref, template_ref, coadd_ref, wide_ref, *refs):
+def slots_kernel(
+    slot_hbm, repeat_ref, arrived_ref, scale_ref, template_ref, coadd_ref, wide_ref, *refs
+):
     del scale_ref
     items, _, sources = slot_hbm.shape
     sums, tables, sems = refs[:LANES], refs[LANES : LANES + items], refs[LANES + items]
@@ -316,16 +340,39 @@
     for load in loads:
         load.wait()
 
+    def add(source, blocks, sum_ref):
+        slots = [tables[block][0, source] for block in blocks]
+        values = [
+            sum_ref[pl.ds(slot, 1), :] + wide_ref[pl.ds(source * items + block, 1), :]
+            for slot, block in zip(slots, blocks)
+        ]
+        for slot, value in zip(slots, values):
+            sum_ref[pl.ds(slot, 1), :] = value
+
+    groups = [list(range(first, first + LANES)) for first in range(0, items, LANES)]
+
     @pl.loop(0, sources)
     def _(source):
-        for first in range(0, items, LANES):
-            slots = [tables[first + lane][0, source] for lane in range(LANES)]
-            values = [
-                sum_ref[pl.ds(slot, 1), :] + wide_ref[pl.ds(source * items + first + lane, 1), :]
-                for lane, (slot, sum_ref) in enumerate(zip(slots, sums))
-            ]
-            for slot, sum_ref, value in zip(slots, sums, values):
-                sum_ref[pl.ds(slot, 1), :] = value
+        repeats = repeat_ref[0, source]
+
+        @pl.when(repeats == 0)
+        def _():
+            for index, blocks in enumerate(groups):
+                add(source, blocks, sums[index % LANES])
+
+        @pl.when(repeats != 0)
+        def _():
+            for index, blocks in enumerate(groups):
+                repeated = (repeats // 2**index) % 2
+
+                @pl.when(repeated == 0)
+                def _():
+                    add(source, blocks, sums[index % LANES])
+
+                @pl.when(repeated != 0)
+                def _():
+                    for lane, block in enumerate(blocks):
+                        add(source, [block], sums[lane])
 
     @pl.loop(0, sources)
     def _(source):
@@ -341,9 +388,19 @@
             slot = tables[item][0, source]
             wide_ref[pl.ds(source * items + item, 1), :] = sums[0][pl.ds(slot, 1), :]
 
-    @pl.loop(0, sources)
+    @pl.loop(0, sources, unroll=2)
     def _(source):
         template_ref[at(source), :] = wide_ref[at(source), :].astype(jnp.bfloat16)
+
+
+def group_repeats(slots):
+    grouped = slots.T.reshape(-1, LANES, slots.shape[0])
+    repeated = jnp.zeros(grouped[:, 0].shape, jnp.bool_)
+    for later in range(1, LANES):
+        for earlier in range(later):
+            repeated = repeated | (grouped[:, later] == grouped[:, earlier])
+    bits = 2 ** jnp.arange(grouped.shape[0], dtype=jnp.int32)
+    return jnp.sum(jnp.where(repeated, bits[:, None], 0), axis=0, keepdims=True)
 
 
 def slot_sums(slots, arrived, scale):
@@ -352,14 +409,14 @@
     return pl.pallas_call(
         slots_kernel,
         out_shape=(shape, shape),
-        in_specs=[ANY, VMEM, ANY],
+        in_specs=[ANY, SMEM, VMEM, SMEM],
         out_specs=(VMEM, VMEM),
         scratch_shapes=[pltpu.VMEM(arrived.shape, jnp.float32)] * (1 + LANES)
         + [pltpu.SMEM((1, sources), jnp.int32)] * items
         + [pltpu.SemaphoreType.DMA((items,))],
         compiler_params=grant(44),
         name="slot_sums",
-    )(slots.T.reshape(items, 1, sources), arrived, scale)
+    )(slots.T.reshape(items, 1, sources), group_repeats(slots), arrived, scale)
 
 
 def unwarp_kernel(
@@ -370,6 +427,8 @@
     bank_columns_ref,
     out_ref,
     top_ref,
+    under_top_ref,
+    over_bottom_ref,
     bottom_ref,
     wide_ref,
     warp_rows_ref,
@@ -433,7 +492,9 @@
             out_ref[part * BLOCK : (part + 1) * BLOCK, to] = image
             if part == 0:
                 top_ref[:, to] = image[:RIM]
+                under_top_ref[:, to] = image[RIM : 2 * RIM]
             if part == parts - 1:
+                over_bottom_ref[:, to] = image[BLOCK - 2 * RIM : BLOCK - RIM]
                 bottom_ref[:, to] = image[BLOCK - RIM :]
 
 
@@ -443,9 +504,9 @@
     rim = jax.ShapeDtypeStruct((RIM, part_width), jnp.bfloat16)
     return pl.pallas_call(
         unwarp_kernel,
-        out_shape=(jax.ShapeDtypeStruct((tile_rows, part_width), jnp.bfloat16), rim, rim),
+        out_shape=(jax.ShapeDtypeStruct((tile_rows, part_width), jnp.bfloat16),) + (rim,) * 4,
         in_specs=[SMEM, SMEM, VMEM, ANY, ANY],
-        out_specs=(VMEM, VMEM, VMEM),
+        out_specs=(VMEM,) * 5,
         scratch_shapes=[
             pltpu.VMEM((lines + BLOCK * PAD, BLOCK), jnp.float32),
             pltpu.VMEM(warp_rows.shape, jnp.bfloat16),
@@ -499,8 +560,7 @@
             stage_ref[:, at] = exposure_ref[:, at].astype(jnp.float32) - summed
         store(index).start()
 
-    load.wait()
-    passes(fetch, step, subtract_step, pass_ref, width)
+    passes(fetch, step, subtract_step, pass_ref, width, load)
 
     @pl.loop(0, width // WIDE)
     def _(index):
@@ -514,8 +574,8 @@
     return pl.pallas_call(
         inner_kernel,
         out_shape=jax.ShapeDtypeStruct((tile_rows, width), jnp.float32),
-        in_specs=[SMEM, ANY, ANY, VMEM, VMEM],
-        out_specs=ANY,
+        in_specs=[SMEM, HBM, HBM, VMEM, VMEM],
+        out_specs=HBM,
         scratch_shapes=[
             pltpu.VMEM((tile_rows, width), jnp.bfloat16),
             pltpu.VMEM((inner, width), jnp.bfloat16),
@@ -534,88 +594,112 @@
     coef_ref,
     above_ref,
     top_ref,
+    under_top_ref,
+    over_bottom_ref,
     bottom_ref,
     below_ref,
-    exposure_top_ref,
-    exposure_bottom_ref,
+    exposure_hbm,
     rows_ref,
     columns_ref,
-    partial_ref,
-    out_ref,
+    partial_hbm,
+    out_hbm,
+    order_ref,
+    exposure_ref,
     pass_ref,
     stage_ref,
-    sems,
+    fetch_sems,
+    store_sems,
 ):
-    del partial_ref
-    width = top_ref.shape[1]
-    tile_rows = out_ref.shape[0]
-    wides = width // WIDE
+    del partial_hbm
+    tile_rows, width = out_hbm.shape
+    order_ref[...] = jnp.zeros_like(order_ref)
+
+    def ends(index):
+        first = index * (tile_rows - RIM)
+        here, there = pl.ds(index * RIM, RIM), pl.ds(first, RIM)
+        return (
+            pltpu.make_async_copy(
+                exposure_hbm.at[there], exposure_ref.at[here], fetch_sems.at[index]
+            ),
+            pltpu.make_async_copy(stage_ref.at[here], out_hbm.at[there], store_sems.at[index]),
+        )
+
+    for index in range(2):
+        ends(index)[0].start()
     strips = [
-        (0, RIM, [(above_ref, 0, RIM, 0), (top_ref, 0, 2 * RIM, 0)]),
-        (RIM, RIM, [(bottom_ref, 0, 2 * RIM, 0), (below_ref, 0, RIM, 0)]),
+        (0, RIM, [(ref, 0, RIM, 0) for ref in (above_ref, top_ref, under_top_ref)]),
+        (RIM, RIM, [(ref, 0, RIM, 0) for ref in (over_bottom_ref, bottom_ref, below_ref)]),
     ]
     clear(pass_ref, 0)
     clear(pass_ref, BLOCK + width)
-    for index in range(wides):
+    for index in range(width // WIDE):
         row_step(
             WIDE, index * WIDE, BLOCK + index * WIDE, strips, coef_ref, rows_ref, pass_ref
         )
-    for index in range(wides):
-        for half, summed in enumerate(column_step(index, 2 * RIM, columns_ref, pass_ref)):
-            at = pl.ds(index * WIDE + half * CHUNK, CHUNK)
-            stage_ref[:RIM, at] = exposure_top_ref[:, at].astype(jnp.float32) - summed[:RIM]
-            stage_ref[RIM:, at] = exposure_bottom_ref[:, at].astype(jnp.float32) - summed[RIM:]
-    stores = [
-        pltpu.make_async_copy(stage_ref.at[:RIM], out_ref.at[:RIM], sems.at[0]),
-        pltpu.make_async_copy(
-            stage_ref.at[RIM:], out_ref.at[pl.ds(tile_rows - RIM, RIM)], sems.at[1]
-        ),
-    ]
-    for store in stores:
-        store.start()
-    for store in stores:
-        store.wait()
-
-
-def subtract_outer(coef, above, image, below, exposure, rows, columns, partial):
-    tile_rows, width = image.shape
+    for index in range(2):
+        ends(index)[0].wait()
+    for index in range(width // WIDE):
+        for part, summed in enumerate(column_step(index, 2 * RIM, columns_ref, pass_ref)):
+            at = pl.ds(index * WIDE + part * CHUNK, CHUNK)
+            stage_ref[:, at] = exposure_ref[:, at].astype(jnp.float32) - summed
+    for index in range(2):
+        ends(index)[1].start()
+    for index in range(2):
+        ends(index)[1].wait()
+
+
+def subtract_outer(coef, rims, exposure, rows, columns, partial):
+    tile_rows, width = exposure.shape
     bases = rows.shape[0] // BLOCK
-    rim = pl.BlockSpec((RIM, width), lambda _: (0, 0))
-    last_rim = pl.BlockSpec((RIM, width), lambda _: (tile_rows // RIM - 1, 0))
-    pair = pl.BlockSpec((2 * RIM, width), lambda _: (0, 0))
-    last_pair = pl.BlockSpec((2 * RIM, width), lambda _: (tile_rows // (2 * RIM) - 1, 0))
+    operands = (coef, *rims, exposure, rows, columns, partial)
     return pl.pallas_call(
         outer_kernel,
-        out_shape=jax.ShapeDtypeStruct((tile_rows, width), jnp.float32),
-        grid=(1,),
-        in_specs=[SMEM, VMEM, pair, last_pair, VMEM, rim, last_rim, VMEM, VMEM, ANY],
-        out_specs=ANY,
+        out_shape=(
+            jax.ShapeDtypeStruct((tile_rows, width), jnp.float32),
+            jax.ShapeDtypeStruct((SLOT_ROWS, BLOCK), jnp.float32),
+        ),
+        in_specs=[SMEM] + [VMEM] * len(rims) + [HBM, VMEM, VMEM, HBM],
+        out_specs=(HBM, VMEM),
         scratch_shapes=[
+            pltpu.VMEM((2 * RIM, width), jnp.bfloat16),
             pltpu.VMEM((bases, 2 * RIM, width + 2 * BLOCK), jnp.bfloat16),
             pltpu.VMEM((2 * RIM, width), jnp.float32),
             pltpu.SemaphoreType.DMA((2,)),
+            pltpu.SemaphoreType.DMA((2,)),
         ],
-        input_output_aliases={9: 0},
-        compiler_params=grant(58),
+        input_output_aliases={len(operands) - 1: 0},
+        compiler_params=grant(16),
         name="subtract_outer",
-    )(coef, above, image, image, below, exposure, exposure, rows, columns, partial)
-
-
-def patch_kernel(scale_ref, rows_ref, after_ref, out_ref, wide_ref, stage_ref, sems):
-    del after_ref
+    )(*operands)
+
+
+def patch_kernel(
+    scale_ref, owned_hbm, order_ref, out_hbm, owned_ref, wide_ref, stage_ref, fetch_sems, store_sems
+):
+    del order_ref
     slots = SLOT_ROWS * SLOT_COLS
     pitch = slots + PAD
     myself = my_device()
-
-    @pl.loop(0, BLOCK, unroll=2)
-    def _(row):
-        to = pl.ds(pl.multiple_of(row * pitch, PAD), slots)
-        at = pl.ds(pl.multiple_of(row * slots, slots), slots)
-        wide_ref[to, :] = rows_ref[at, :].astype(jnp.float32)
+    lines = owned_ref.shape[0] // GROUPS
+
+    def fetch(group):
+        at = pl.ds(group * lines, lines)
+        return pltpu.make_async_copy(owned_hbm.at[at], owned_ref.at[at], fetch_sems.at[group])
+
+    for group in range(GROUPS):
+        fetch(group).start()
+    for group in range(GROUPS):
+        fetch(group).wait()
+
+        @pl.loop(group * BLOCK // GROUPS, (group + 1) * BLOCK // GROUPS, unroll=4)
+        def _(row):
+            to = pl.ds(pl.multiple_of(row * pitch, PAD), slots)
+            at = pl.ds(pl.multiple_of(row * slots, slots), slots)
+            wide_ref[to, :] = owned_ref[at, :].astype(jnp.float32)
 
     def store(down):
         at = pl.ds(pl.multiple_of(down * BLOCK, BLOCK), BLOCK)
-        return pltpu.make_async_copy(stage_ref.at[at], out_ref.at[at], sems.at[down])
+        return pltpu.make_async_copy(stage_ref.at[at], out_hbm.at[at], store_sems.at[down])
 
     @pl.loop(0, SLOT_ROWS)
     def _(down):
@@ -632,21 +716,23 @@
         store(down).wait()
 
 
-def patch(scale, rows, after):
+def patch(scale, owned, order):
     shape = (SLOT_ROWS * BLOCK, SLOT_COLS * BLOCK)
     return pl.pallas_call(
         patch_kernel,
         out_shape=jax.ShapeDtypeStruct(shape, jnp.float32),
-        in_specs=[SMEM, VMEM, ANY],
-        out_specs=ANY,
+        in_specs=[SMEM, HBM, VMEM],
+        out_specs=HBM,
         scratch_shapes=[
-            pltpu.VMEM((rows.shape[0] + BLOCK * PAD, BLOCK), jnp.float32),
+            pltpu.VMEM(owned.shape, jnp.bfloat16),
+            pltpu.VMEM((owned.shape[0] + BLOCK * PAD, BLOCK), jnp.float32),
             pltpu.VMEM(shape, jnp.float32),
+            pltpu.SemaphoreType.DMA((GROUPS,)),
             pltpu.SemaphoreType.DMA((SLOT_ROWS,)),
         ],
         compiler_params=grant(14),
         name="patch",
-    )(scale, rows, after)
+    )(scale, owned, order)
 
 
 def exchange(rows, devices):
@@ -677,7 +763,16 @@
     above, below = swap_rims(image[:RIM], image[tile_rows - RIM :])
     rows, columns = band_matrices(row_taps, column_taps)
     weighted = forward(
-        ident, weight, basis_coef, above, image, below, rows, columns, warp_rows, warp_columns
+        ident,
+        weight,
+        basis_coef,
+        above,
+        image,
+        below,
+        rows,
+        columns,
+        warp_rows,
+        warp_columns,
     )
     arrived = exchange(weighted, devices)
 
@@ -700,15 +795,14 @@
     returned = exchange(template_rows, devices)
     owned = exchange(coadd_rows, devices)
 
-    template, top, bottom = unwarp(
+    template, top, under_top, over_bottom, bottom = unwarp(
         ident, block_scale, returned, warp_rows, warp_columns, tile_rows
     )
     above, below = swap_rims(top, bottom)
     difference = subtract_inner(basis_coef, template, image, rows, columns)
-    difference = subtract_outer(
-        basis_coef, above, template, below, image, rows, columns, difference
-    )
-    return patch(scale, owned, difference), difference[None]
+    rims = (above, top, under_top, over_bottom, bottom, below)
+    difference, order = subtract_outer(basis_coef, rims, image, rows, columns, difference)
+    return patch(scale, owned, order), difference[None]
 
 
 def solution(mesh):

time: 166 us -> 163 us (0.982)
  local copies, waits for them, and re-layouts: 6.44 us -> 3.03 us
    unnamed x20 -> x30, local copies, waits for them, and re-layouts: 4.15 us -> 0.72 us
  transfers between devices with their start and end apart: 6 -> 6, of which waited for: 3 -> 3; matrix products, arithmetic and copies ran while one was open for 2% -> 3% of each run, Pallas kernels for 15% -> 15%
where the time goes in v5:
time: 163 us; the launch traced here: 162 us
  Pallas kernels  60.8 us (37%)
  blocking collectives  34.5 us (21%)
  waiting for transfers between devices  32.2 us (20%)
  starting transfers between devices  27.7 us (17%)
  local copies, waits for them, and re-layouts  3.03 us (2%)
  matrix products  2.66 us (2%)
    all_to_all x1, blocking collectives, exchange(): lax.all_to_all(shaped, ('exp', 'tile'), split_axis=0, concat_axis=0, tile...  34.5 us
    all_to_all x2, waiting for transfers between devices, exchange(): lax.all_to_all(shaped, ('exp', 'tile'), split_axis=0, concat_axis=0, tile...  25.3 us
    pallas_call x1, Pallas kernels, slot_sums(): pl.pallas_call(slots_kernel, out_shape=(shape, shape), in_specs=[ANY, SME...  18.7 us
    pallas_call x1, Pallas kernels, forward(): pl.pallas_call(forward_kernel, out_shape=jax.ShapeDtypeStruct((lines, BLO...  13.8 us
    all_to_all x2, starting transfers between devices, exchange(): lax.all_to_all(shaped, ('exp', 'tile'), split_axis=0, concat_axis=0, tile...  13.1 us
    ppermute x2, starting transfers between devices, swap_rims(): lax.ppermute(top, 'tile', backward)  9.31 us
    pallas_call x1, Pallas kernels, subtract_inner(): pl.pallas_call(inner_kernel, out_shape=jax.ShapeDtypeStruct((tile_rows, w...  8.84 us
    pallas_call x1, Pallas kernels, unwarp(): pl.pallas_call(unwarp_kernel, out_shape=(jax.ShapeDtypeStruct((tile_rows,...  8.68 us
  transfers between devices with their start and end apart: 6, of which 3 were waited for; matrix products, arithmetic and copies ran while one was open for 3% of the time, Pallas kernels for 15%

profile of v5, /device:TPU:8, one launch (start us, length us, event | category | flops | bytes accessed | tf_op | source)
XLA Modules:
  0.0 162.2 jit_solution(5687738849732202371)
XLA Ops:
  0.6 1.0 slice_bitcast_fusion
  1.6 4.6 %collective-permute-start.1 = (bf16[16,4096]{1,0:T(8,128)(2,1)S(1)}, bf16[16,4096]{1,0:T(8,128)(2,1)S(1)}, u32[]{:S(2)}, u32[]{:S(2)}) collective-permute-start(bf16[16,4096]{1,0:T(8,128)(2,1)S(1)} %get-tuple-element.24), channel_id=1, source_target_pairs={{1,0},{2,1},{3,2},{4,3},{5,4},{6,5},{7,6},{8,7},{9,8},{10,9},{11,1... | collective-permute-start | bytes 393224 | tf_op jit(solution)/shard_map/ppermute | solution.py:81
  6.2 1.9 %collective-permute-start = (bf16[16,4096]{1,0:T(8,128)(2,1)S(1)}, bf16[16,4096]{1,0:T(8,128)(2,1)S(1)}, u32[]{:S(2)}, u32[]{:S(2)}) collective-permute-start(bf16[16,4096]{1,0:T(8,128)(2,1)S(1)} %get-tuple-element.25), channel_id=1, source_target_pairs={{0,1},{1,2},{2,3},{3,4},{4,5},{5,6},{6,7},{7,8},{8,9},{9,10},{10,1... | collective-permute-start | bytes 393224 | tf_op jit(solution)/shard_map/ppermute | solution.py:81
  8.1 2.5 %bands.1 = (bf16[384,160]{1,0:T(8,128)(2,1)}, bf16[1152,256]{1,0:T(8,128)(2,1)}) custom-call(bf16[3,21]{1,0:T(4,128)(2,1)} %row_taps_ref.1, bf16[3,21]{1,0:T(4,128)(2,1)} %column_taps_ref.1), custom_call_target="tpu_custom_call" | custom-call | tf_op jit(solution)/shard_map/bands/pallas_call | solution.py:64
  10.7 0.0 collective-permute-done.1.below_ref
  10.7 0.0 copy-start.12
  10.7 4.5 %collective-permute-done.above_ref = bf16[16,4096]{1,0:T(8,128)(2,1)S(1)} collective-permute-done((bf16[16,4096]{1,0:T(8,128)(2,1)S(1)}, bf16[16,4096]{1,0:T(8,128)(2,1)S(1)}, u32[]{:S(2)}, u32[]{:S(2)}) %collective-permute-start) | collective-permute-done | bytes 131104 | tf_op jit(solution)/shard_map/ppermute | solution.py:81
  15.2 0.0 copy-start.13
  15.2 0.0 copy-done.12
  15.2 0.7 copy-done.13
  15.8 13.8 %match_warp.1 = bf16[8192,128]{1,0:T(8,128)(2,1)} custom-call(s32[128,64]{1,0:T(8,128)} %bitcast.44, f32[8,16]{1,0:T(8,128)} %weight_ref.1, f32[1,3]{1,0:T(1,128)} %coef_ref.5, bf16[16,4096]{1,0:T(8,128)(2,1)} %copy-done.13, bf16[256,4096]{1,0:T(8,128)(2,1)} %bitcast.29, bf16[16,4096]{1,0:T(8,128)(2,1)} %copy-done.12, ...), custom_call_target="tpu_custom_call" | custom-call | tf_op jit(solution)/shard_map/match_warp/pallas_call | solution.py:299
  29.7 0.0 copy-start.14
  29.7 0.0 copy-start.10
  29.7 0.0 copy-start.11
  29.7 8.1 %all-to-all-start = ((bf16[128,64,128]{2,1,0:T(8,128)(2,1)}), bf16[128,64,128]{2,1,0:T(8,128)(2,1)S(1)}, u32[]{:S(2)}, u32[]{:S(2)}) async-start(bf16[128,64,128]{2,1,0:T(8,128)(2,1)} %bitcast.43), calls=%async_computation | async-start | bytes 4194304 | tf_op jit(solution)/shard_map/all_to_all | solution.py:740
  37.8 0.0 copy-done.14
  37.8 0.1 reshape.85
  37.9 0.0 copy-done.10
  37.9 0.1 eq.58
  38.0 0.0 copy-done.11
  38.0 0.1 eq.62
  38.0 0.1 broadcast_in_dim.45
  38.1 0.1 broadcast_in_dim.46
  38.2 2.7 %fusion.8.scale_ref = f32[128,64]{1,0:T(8,128)S(1)} fusion(f32[8192]{0:T(1024)S(1)} %broadcast_in_dim.46, s32[8192]{0:T(1024)S(1)} %eq.58, s32[8192]{0:T(1024)S(1)} %eq.62), kind=kOutput, calls=%fused_computation.9 | convolution fusion | flops 807944192 | bytes 131072 | tf_op jit(solution)/shard_map/dot_general | solution.py:788
  40.9 0.1 reshape.92
  41.0 0.1 copy.22
  41.1 0.8 gather_fusion
  41.8 0.0 copy-start.9
  41.9 0.1 select_reduce_fusion
  42.0 25.3 %all-to-all-done = bf16[128,64,128]{2,1,0:T(8,128)(2,1)S(1)} async-done(((bf16[128,64,128]{2,1,0:T(8,128)(2,1)}), bf16[128,64,128]{2,1,0:T(8,128)(2,1)S(1)}, u32[]{:S(2)}, u32[]{:S(2)}) %all-to-all-start) | async-done | bytes 2097184 | tf_op jit(solution)/shard_map/all_to_all | solution.py:740
  67.3 18.7 %slot_sums.1 = (bf16[8192,128]{1,0:T(8,128)(2,1)S(1)}, bf16[8192,128]{1,0:T(8,128)(2,1)S(1)}) custom-call(s32[64,1,128]{2,1,0:T(1,128)S(1)} %bitcast.37, s32[1,128]{1,0:T(1,128)S(1)} %bitcast.40, bf16[8192,128]{1,0:T(8,128)(2,1)S(1)} %bitcast.32, f32[1,64]{1,0:T(1,128)S(1)} %bitcast.38), custom_call_target="tpu_custom_call" | custom-call | tf_op jit(solution)/shard_map/slot_sums/pallas_call | solution.py:409
  86.0 0.0 copy-start.2
  86.0 34.5 %all_to_all.15 = bf16[128,64,128]{2,1,0:T(8,128)(2,1)} all-to-all(bf16[128,64,128]{2,1,0:T(8,128)(2,1)S(1)} %bitcast.35), channel_id=1, replica_groups=mesh['exp'=8,'tile'=16] {'exp','tile'}, dimensions={0} | all-to-all | bytes 4194304 | tf_op jit(solution)/shard_map/all_to_all | solution.py:740
  120.5 0.0 copy-done.9
  120.5 0.0 copy-done.2
  120.5 5.0 %all-to-all-start.1 = ((bf16[128,64,128]{2,1,0:T(8,128)(2,1)}), bf16[128,64,128]{2,1,0:T(8,128)(2,1)S(1)}, u32[]{:S(2)}, u32[]{:S(2)}) async-start(bf16[128,64,128]{2,1,0:T(8,128)(2,1)} %bitcast.34), calls=%async_computation.1 | async-start | bytes 4194304 | tf_op jit(solution)/shard_map/all_to_all | solution.py:740
  125.5 8.7 %unwarp.1 = (bf16[256,4096]{1,0:T(8,128)(2,1)}, bf16[16,4096]{1,0:T(8,128)(2,1)}, bf16[16,4096]{1,0:T(8,128)(2,1)}, bf16[16,4096]{1,0:T(8,128)(2,1)}, bf16[16,4096]{1,0:T(8,128)(2,1)}) custom-call(s32[128,64]{1,0:T(8,128)} %bitcast.45, f32[1,64]{1,0:T(1,128)} %bitcast.39, bf16[8192,128]{1,0:T(8,128)(2,1)} %bitcast.42, bf16[64,128,128]{2,1,0:T(8,128)(2,1)} %bank_rows_ref.3, ...), custom_call_target="tpu_custom_call" | custom-call | tf_op jit(solution)/shard_map/unwarp/pallas_call | solution.py:505
  134.2 3.4 %collective-permute-start.2 = (bf16[16,4096]{1,0:T(8,128)(2,1)}, bf16[16,4096]{1,0:T(8,128)(2,1)S(1)}, u32[]{:S(2)}, u32[]{:S(2)}) collective-permute-start(bf16[16,4096]{1,0:T(8,128)(2,1)} %get-tuple-element.17.bottom_ref), channel_id=1, source_target_pairs={{0,1},{1,2},{2,3},{3,4},{4,5},{5,6},{6,7},{7,8},{8,9},{9,10},{10,1... | collective-permute-start | bytes 393224 | tf_op jit(solution)/shard_map/ppermute | solution.py:81
  137.6 4.8 %collective-permute-start.3 = (bf16[16,4096]{1,0:T(8,128)(2,1)}, bf16[16,4096]{1,0:T(8,128)(2,1)S(1)}, u32[]{:S(2)}, u32[]{:S(2)}) collective-permute-start(bf16[16,4096]{1,0:T(8,128)(2,1)} %get-tuple-element.18.top_ref), channel_id=1, source_target_pairs={{1,0},{2,1},{3,2},{4,3},{5,4},{6,5},{7,6},{8,7},{9,8},{10,9},{11,1... | collective-permute-start | bytes 393224 | tf_op jit(solution)/shard_map/ppermute | solution.py:81
  142.3 0.0 copy-start
  142.3 0.0 copy-start.1
  142.4 0.0 copy-start.3
  142.4 0.0 copy-start.4
  142.4 0.0 copy-start.5
  142.4 0.0 copy-start.6
  142.4 0.0 copy-start.7
  142.4 0.0 copy-start.8
  142.4 8.8 %subtract_inner.1.partial_hbm = f32[256,4096]{1,0:T(8,128)} custom-call(f32[1,3]{1,0:T(1,128)} %coef_ref.5, bf16[256,4096]{1,0:T(8,128)(2,1)} %get-tuple-element.21.image_hbm, bf16[256,4096]{1,0:T(8,128)(2,1)} %bitcast.30, bf16[384,160]{1,0:T(8,128)(2,1)} %get-tuple-element.13.rows_ref, bf16[1152,256]{1,0:T(8,128)(2,1)} %get-tuple-element.14.columns_ref), custom_call_target="tpu_custom_call" | custom-call | tf_op jit(solution)/shard_map/subtract_inner/pallas_call | solution.py:574
  151.3 2.5 %collective-permute-done.2.above_ref = bf16[16,4096]{1,0:T(8,128)(2,1)S(1)} collective-permute-done((bf16[16,4096]{1,0:T(8,128)(2,1)}, bf16[16,4096]{1,0:T(8,128)(2,1)S(1)}, u32[]{:S(2)}, u32[]{:S(2)}) %collective-permute-start.2) | collective-permute-done | bytes 131104 | tf_op jit(solution)/shard_map/ppermute | solution.py:81
  153.8 0.0 collective-permute-done.3.below_ref
  153.8 0.0 copy-done
  153.8 0.0 copy-done.1
  153.8 0.0 copy-done.3
  153.8 0.0 copy-done.4
  153.8 0.0 copy-done.5
  153.8 0.0 copy-done.6
  153.8 0.0 copy-done.7
  153.8 0.0 copy-done.8
  153.8 3.8 %subtract_outer.1 = (f32[256,4096]{1,0:T(8,128)}, f32[8,128]{1,0:T(8,128)S(1)}) custom-call(f32[1,3]{1,0:T(1,128)S(1)} %copy-done.8, bf16[16,4096]{1,0:T(8,128)(2,1)S(1)} %collective-permute-done.2.above_ref, bf16[16,4096]{1,0:T(8,128)(2,1)S(1)} %copy-done.4, bf16[16,4096]{1,0:T(8,128)(2,1)S(1)} %copy-done.5, ...), custom_call_target="tpu_custom_call", output_to_operand_aliasing={{0}: (10, {})} | custom-call | tf_op jit(solution)/shard_map/subtract_outer/pallas_call | solution.py:655
  157.6 0.0 all-to-all-done.1
  157.6 4.4 %patch.1 = f32[1024,1024]{1,0:T(8,128)} custom-call(f32[128,64]{1,0:T(8,128)S(1)} %fusion.8.scale_ref, bf16[8192,128]{1,0:T(8,128)(2,1)S(1)} %bitcast.33, f32[8,128]{1,0:T(8,128)S(1)} %get-tuple-element.22.order_ref), custom_call_target="tpu_custom_call" | custom-call | tf_op jit(solution)/shard_map/patch/pallas_call | solution.py:721
  (5 shorter events, 0.1 us)
Async XLA Ops:
  1.6 9.0 %collective-permute-start.1 = (bf16[16,4096]{1,0:T(8,128)(2,1)S(1)}, bf16[16,4096]{1,0:T(8,128)(2,1)S(1)}, u32[]{:S(2)}, u32[]{:S(2)}) collective-permute-start(bf16[16,4096]{1,0:T(8,128)(2,1)S(1)} %get-tuple-element.24), channel_id=1, source_target_pairs={{1,0},{2,1},{3,2},{4,3},{5,4},{6,5},{7,6},{8,7},{9,8},{10,9},{11,1... | collective-permute-start | bytes 393224 | tf_op jit(solution)/shard_map/ppermute | solution.py:81
  6.2 9.0 %collective-permute-start = (bf16[16,4096]{1,0:T(8,128)(2,1)S(1)}, bf16[16,4096]{1,0:T(8,128)(2,1)S(1)}, u32[]{:S(2)}, u32[]{:S(2)}) collective-permute-start(bf16[16,4096]{1,0:T(8,128)(2,1)S(1)} %get-tuple-element.25), channel_id=1, source_target_pairs={{0,1},{1,2},{2,3},{3,4},{4,5},{5,6},{6,7},{7,8},{8,9},{9,10},{10,1... | collective-permute-start | bytes 393224 | tf_op jit(solution)/shard_map/ppermute | solution.py:81
  10.7 4.5 %copy-start.12 = (bf16[16,4096]{1,0:T(8,128)(2,1)}, bf16[16,4096]{1,0:T(8,128)(2,1)S(1)}, u32[]{:S(2)}) copy-start(bf16[16,4096]{1,0:T(8,128)(2,1)S(1)} %collective-permute-done.1.below_ref) | copy-start | bytes 393220
  15.2 0.7 copy-start.13
  29.7 8.2 %copy-start.14 = (f32[8,16]{1,0:T(8,128)S(1)}, f32[8,16]{1,0:T(8,128)}, u32[]{:S(2)}) copy-start(f32[8,16]{1,0:T(8,128)} %weight_ref.1) | copy-start | bytes 1540
  29.7 8.2 %copy-start.10 = (s32[8,16,64]{2,1,0:T(8,128)S(1)}, s32[8,16,64]{2,1,0:T(8,128)}, u32[]{:S(2)}) copy-start(s32[8,16,64]{2,1,0:T(8,128)} %param.17) | copy-start | bytes 98308
  29.7 8.3 %copy-start.11 = (s32[8,16,64]{2,1,0:T(8,128)S(1)}, s32[8,16,64]{2,1,0:T(8,128)}, u32[]{:S(2)}) copy-start(s32[8,16,64]{2,1,0:T(8,128)} %param.18) | copy-start | bytes 98308
  29.7 37.6 %all-to-all-start = ((bf16[128,64,128]{2,1,0:T(8,128)(2,1)}), bf16[128,64,128]{2,1,0:T(8,128)(2,1)S(1)}, u32[]{:S(2)}, u32[]{:S(2)}) async-start(bf16[128,64,128]{2,1,0:T(8,128)(2,1)} %bitcast.43), calls=%async_computation | async-start | bytes 4194304 | tf_op jit(solution)/shard_map/all_to_all | solution.py:740
  41.8 78.7 %copy-start.9 = (f32[64]{0:T(128)}, f32[64]{0:T(128)S(1)}, u32[]{:S(2)}) copy-start(f32[64]{0:T(128)S(1)} %gather_fusion) | copy-start | bytes 772
  86.0 34.5 %copy-start.2 = (bf16[8192,128]{1,0:T(8,128)(2,1)}, bf16[8192,128]{1,0:T(8,128)(2,1)S(1)}, u32[]{:S(2)}) copy-start(bf16[8192,128]{1,0:T(8,128)(2,1)S(1)} %get-tuple-element.15) | copy-start | bytes 6291460
  120.5 37.1 %all-to-all-start.1 = ((bf16[128,64,128]{2,1,0:T(8,128)(2,1)}), bf16[128,64,128]{2,1,0:T(8,128)(2,1)S(1)}, u32[]{:S(2)}, u32[]{:S(2)}) async-start(bf16[128,64,128]{2,1,0:T(8,128)(2,1)} %bitcast.34), calls=%async_computation.1 | async-start | bytes 4194304 | tf_op jit(solution)/shard_map/all_to_all | solution.py:740
  134.2 19.6 %collective-permute-start.2 = (bf16[16,4096]{1,0:T(8,128)(2,1)}, bf16[16,4096]{1,0:T(8,128)(2,1)S(1)}, u32[]{:S(2)}, u32[]{:S(2)}) collective-permute-start(bf16[16,4096]{1,0:T(8,128)(2,1)} %get-tuple-element.17.bottom_ref), channel_id=1, source_target_pairs={{0,1},{1,2},{2,3},{3,4},{4,5},{5,6},{6,7},{7,8},{8,9},{9,10},{10,1... | collective-permute-start | bytes 393224 | tf_op jit(solution)/shard_map/ppermute | solution.py:81
  137.6 16.2 %collective-permute-start.3 = (bf16[16,4096]{1,0:T(8,128)(2,1)}, bf16[16,4096]{1,0:T(8,128)(2,1)S(1)}, u32[]{:S(2)}, u32[]{:S(2)}) collective-permute-start(bf16[16,4096]{1,0:T(8,128)(2,1)} %get-tuple-element.18.top_ref), channel_id=1, source_target_pairs={{1,0},{2,1},{3,2},{4,3},{5,4},{6,5},{7,6},{8,7},{9,8},{10,9},{11,1... | collective-permute-start | bytes 393224 | tf_op jit(solution)/shard_map/ppermute | solution.py:81
  142.3 11.4 %copy-start = (bf16[1,256,4096]{2,1,0:T(8,128)(2,1)S(1)}, bf16[1,256,4096]{2,1,0:T(8,128)(2,1)}, u32[]{:S(2)}) copy-start(bf16[1,256,4096]{2,1,0:T(8,128)(2,1)} %param.10) | copy-start | bytes 6291460
  142.3 11.4 %copy-start.1 = (bf16[1152,256]{1,0:T(8,128)(2,1)S(1)}, bf16[1152,256]{1,0:T(8,128)(2,1)}, u32[]{:S(2)}) copy-start(bf16[1152,256]{1,0:T(8,128)(2,1)} %get-tuple-element.14.columns_ref) | copy-start | bytes 1769476
  142.4 11.4 %copy-start.3 = (bf16[384,160]{1,0:T(8,128)(2,1)S(1)}, bf16[384,160]{1,0:T(8,128)(2,1)}, u32[]{:S(2)}) copy-start(bf16[384,160]{1,0:T(8,128)(2,1)} %get-tuple-element.13.rows_ref) | copy-start | bytes 368644
  142.4 11.4 %copy-start.4 = (bf16[16,4096]{1,0:T(8,128)(2,1)S(1)}, bf16[16,4096]{1,0:T(8,128)(2,1)}, u32[]{:S(2)}) copy-start(bf16[16,4096]{1,0:T(8,128)(2,1)} %get-tuple-element.18.top_ref) | copy-start | bytes 393220
  142.4 11.4 %copy-start.5 = (bf16[16,4096]{1,0:T(8,128)(2,1)S(1)}, bf16[16,4096]{1,0:T(8,128)(2,1)}, u32[]{:S(2)}) copy-start(bf16[16,4096]{1,0:T(8,128)(2,1)} %get-tuple-element.19.under_top_ref) | copy-start | bytes 393220
  142.4 11.4 %copy-start.6 = (bf16[16,4096]{1,0:T(8,128)(2,1)S(1)}, bf16[16,4096]{1,0:T(8,128)(2,1)}, u32[]{:S(2)}) copy-start(bf16[16,4096]{1,0:T(8,128)(2,1)} %get-tuple-element.20.over_bottom_ref) | copy-start | bytes 393220
  142.4 11.4 %copy-start.7 = (bf16[16,4096]{1,0:T(8,128)(2,1)S(1)}, bf16[16,4096]{1,0:T(8,128)(2,1)}, u32[]{:S(2)}) copy-start(bf16[16,4096]{1,0:T(8,128)(2,1)} %get-tuple-element.17.bottom_ref) | copy-start | bytes 393220
  142.4 11.4 %copy-start.8 = (f32[1,3]{1,0:T(1,128)S(1)}, f32[1,3]{1,0:T(1,128)}, u32[]{:S(2)}) copy-start(f32[1,3]{1,0:T(1,128)} %coef_ref.5) | copy-start | bytes 40

commit v6 on v5

--- a/solution.py
+++ b/solution.py
@@ -16,7 +16,7 @@
 WINDOW = BLOCK + 2 * RIM
 SLOT_ROWS = 8
 SLOT_COLS = 8
-LANES = 4
+LANES = 8
 PAD = 8
 VMEM = pl.BlockSpec(memory_space=pltpu.VMEM)
 SMEM = pl.BlockSpec(memory_space=pltpu.SMEM)
@@ -29,7 +29,7 @@
     return pltpu.CompilerParams(vmem_limit_bytes=mebibytes * 1024 * 1024)
 
 
-def bands_kernel(row_taps_ref, column_taps_ref, rows_ref, columns_ref):
+def make_bands(row_taps_ref, column_taps_ref, rows_ref, columns_ref):
     bases, taps = row_taps_ref.shape
     lead = RIM - HALF
 
@@ -57,21 +57,6 @@
         top = bases * CHUNK + base * BLOCK
         columns_ref[top : top + RIM, BLOCK:] = band[WINDOW - RIM :]
         columns_ref[top + BLOCK - RIM : top + BLOCK, :BLOCK] = band[:RIM]
-
-
-def band_matrices(row_taps, column_taps):
-    bases = row_taps.shape[0]
-    return pl.pallas_call(
-        bands_kernel,
-        out_shape=(
-            jax.ShapeDtypeStruct((bases * BLOCK, WINDOW), jnp.bfloat16),
-            jax.ShapeDtypeStruct((bases * SPAN, CHUNK), jnp.bfloat16),
-        ),
-        in_specs=[VMEM, VMEM],
-        out_specs=(VMEM, VMEM),
-        compiler_params=grant(58),
-        name="bands",
-    )(row_taps, column_taps)
 
 
 def swap_rims(top, bottom):
@@ -109,33 +94,54 @@
             ] = (coef_ref[0, base] * summed[base * count : (base + 1) * count]).astype(jnp.bfloat16)
 
 
-def column_step(index, count, columns_ref, pass_ref):
+def column_window(at, count, pass_ref):
     bases = pass_ref.shape[0]
     right = lax.broadcasted_iota(jnp.int32, (count, BLOCK), 1) < BLOCK // 2
-    summed = []
-    for part in range(WIDE // CHUNK):
-        at = index * WIDE + part * CHUNK
-
-        def columns(shift, size):
-            return pl.ds(pl.multiple_of(at + shift, BLOCK), size)
-
-        middle = [pass_ref[base, :count, columns(BLOCK, CHUNK)] for base in range(bases)]
-        sides = [
-            jnp.where(
-                right,
-                pass_ref[base, :count, columns(BLOCK + CHUNK, BLOCK)],
-                pass_ref[base, :count, columns(0, BLOCK)],
+
+    def columns(shift, size):
+        return pl.ds(pl.multiple_of(at + shift, BLOCK), size)
+
+    middle = [pass_ref[base, :count, columns(BLOCK, CHUNK)] for base in range(bases)]
+    sides = [
+        jnp.where(
+            right,
+            pass_ref[base, :count, columns(BLOCK + CHUNK, BLOCK)],
+            pass_ref[base, :count, columns(0, BLOCK)],
+        )
+        for base in range(bases)
+    ]
+    return jnp.concatenate(middle + sides, axis=1)
+
+
+def column_step(index, count, columns_ref, pass_ref):
+    return [
+        jnp.dot(
+            column_window(index * WIDE + part * CHUNK, count, pass_ref),
+            columns_ref[...],
+            preferred_element_type=jnp.float32,
+        )
+        for part in range(WIDE // CHUNK)
+    ]
+
+
+def column_strip(count, columns_ref, pass_ref, consume):
+    width = pass_ref.shape[2] - 2 * BLOCK
+    chunks = width // CHUNK // 2
+    for half in range(2):
+        windows = [
+            column_window((half * chunks + chunk) * CHUNK, count, pass_ref)
+            for chunk in range(chunks)
+        ]
+        summed = jnp.dot(
+            jnp.concatenate(windows, axis=0),
+            columns_ref[...],
+            preferred_element_type=jnp.float32,
+        )
+        for chunk in range(chunks):
+            consume(
+                pl.ds((half * chunks + chunk) * CHUNK, CHUNK),
+                summed[chunk * count : (chunk + 1) * count],
             )
-            for base in range(bases)
-        ]
-        summed.append(
-            jnp.dot(
-                jnp.concatenate(middle + sides, axis=1),
-                columns_ref[...],
-                preferred_element_type=jnp.float32,
-            )
-        )
-    return summed
 
 
 def my_device():
@@ -174,6 +180,84 @@
     @pl.loop(wides - 2, wides)
     def _(index):
         consume(index)
+
+
+def match_inner_kernel(
+    coef_ref,
+    row_taps_ref,
+    column_taps_ref,
+    image_hbm,
+    rows_ref,
+    columns_ref,
+    out_hbm,
+    image_ref,
+    pass_ref,
+    stage_ref,
+    fetch_sems,
+    store_sems,
+):
+    tile_rows, width = image_ref.shape
+    inner = tile_rows - 2 * RIM
+    fetch = wide_copy(image_hbm, image_ref, fetch_sems, 0, tile_rows)
+    for index in range(width // WIDE):
+        fetch(index).start()
+    make_bands(row_taps_ref, column_taps_ref, rows_ref, columns_ref)
+    step = functools.partial(
+        row_step,
+        strips=inner_strips(image_ref),
+        coef_ref=coef_ref,
+        rows_ref=rows_ref,
+        pass_ref=pass_ref,
+    )
+
+    def store(index):
+        at = pl.ds(pl.multiple_of(index * WIDE, WIDE), WIDE)
+        return pltpu.make_async_copy(stage_ref.at[:, at], out_hbm.at[:, at], store_sems.at[index])
+
+    def match_step(index):
+        for part, summed in enumerate(column_step(index, inner, columns_ref, pass_ref)):
+            at = pl.ds(pl.multiple_of(index * WIDE + part * CHUNK, CHUNK), CHUNK)
+            stage_ref[:, at] = summed.astype(jnp.bfloat16)
+        store(index).start()
+
+    passes(fetch, step, match_step, pass_ref, width)
+
+    @pl.loop(0, width // WIDE)
+    def _(index):
+        store(index).wait()
+
+
+def inner_strips(image_ref):
+    tile_rows = image_ref.shape[0]
+    return [
+        (0, BLOCK, [(image_ref, 0, WINDOW, 0)]),
+        (BLOCK, tile_rows - 2 * RIM - BLOCK, [(image_ref, BLOCK, tile_rows - BLOCK, 0)]),
+    ]
+
+
+def match_inner(coef, row_taps, column_taps, image):
+    tile_rows, width = image.shape
+    bases = row_taps.shape[0]
+    inner = tile_rows - 2 * RIM
+    return pl.pallas_call(
+        match_inner_kernel,
+        out_shape=(
+            jax.ShapeDtypeStruct((bases * BLOCK, WINDOW), jnp.bfloat16),
+            jax.ShapeDtypeStruct((bases * SPAN, CHUNK), jnp.bfloat16),
+            jax.ShapeDtypeStruct((inner, width), jnp.bfloat16),
+        ),
+        in_specs=[SMEM, VMEM, VMEM, HBM],
+        out_specs=(VMEM, VMEM, HBM),
+        scratch_shapes=[
+            pltpu.VMEM((tile_rows, width), jnp.bfloat16),
+            pltpu.VMEM((bases, inner, width + 2 * BLOCK), jnp.bfloat16),
+            pltpu.VMEM((inner, width), jnp.bfloat16),
+            pltpu.SemaphoreType.DMA((width // WIDE,)),
+            pltpu.SemaphoreType.DMA((width // WIDE,)),
+        ],
+        compiler_params=grant(58),
+        name="match_inner",
+    )(coef, row_taps, column_taps, image)
 
 
 def forward_kernel(
@@ -183,12 +267,13 @@
     above_ref,
     image_hbm,
     below_ref,
+    inner_hbm,
     rows_ref,
     columns_ref,
     bank_rows_ref,
     bank_columns_ref,
     out_hbm,
-    image_ref,
+    ends_ref,
     pass_ref,
     matched_ref,
     turned_ref,
@@ -199,38 +284,49 @@
     load_sems,
     store_sems,
 ):
-    tile_rows, width = image_ref.shape
+    tile_rows, width = matched_ref.shape
     parts = tile_rows // BLOCK
     across = width // BLOCK
     items = parts * across
     pitch = items + PAD
+    pair = 2 * RIM
     myself = my_device()
     weight = weight_ref[lax.axis_index("exp"), lax.axis_index("tile")]
-    fetch = wide_copy(image_hbm, image_ref, fetch_sems, 0, tile_rows)
+    fetches = [
+        pltpu.make_async_copy(
+            image_hbm.at[pl.ds(end * (tile_rows - pair), pair)],
+            ends_ref.at[pl.ds(end * pair, pair)],
+            fetch_sems.at[end],
+        )
+        for end in range(2)
+    ]
     loads = [
-        pltpu.make_async_copy(bank_rows_ref, warp_rows_ref, load_sems.at[0]),
-        pltpu.make_async_copy(bank_columns_ref, warp_columns_ref, load_sems.at[1]),
+        pltpu.make_async_copy(
+            inner_hbm, matched_ref.at[pl.ds(RIM, tile_rows - pair)], load_sems.at[0]
+        ),
+        pltpu.make_async_copy(bank_rows_ref, warp_rows_ref, load_sems.at[1]),
+        pltpu.make_async_copy(bank_columns_ref, warp_columns_ref, load_sems.at[2]),
     ]
+    for copy in fetches + loads:
+        copy.start()
+    for fetch in fetches:
+        fetch.wait()
+    strips = [
+        (0, RIM, [(above_ref, 0, RIM, 0), (ends_ref, 0, pair, 0)]),
+        (RIM, RIM, [(ends_ref, pair, pair, 0), (below_ref, 0, RIM, 0)]),
+    ]
+    clear(pass_ref, 0)
+    clear(pass_ref, BLOCK + width)
     for index in range(width // WIDE):
-        fetch(index).start()
-    for load in loads:
-        load.start()
-
-    strips = [
-        (0, BLOCK, [(above_ref, 0, RIM, 0), (image_ref, 0, BLOCK + RIM, 0)]),
-        (BLOCK, BLOCK, [(image_ref, BLOCK - RIM, BLOCK + RIM, 0), (below_ref, 0, RIM, 0)]),
-    ]
-    step = functools.partial(
-        row_step, strips=strips, coef_ref=coef_ref, rows_ref=rows_ref, pass_ref=pass_ref
-    )
-
-    def match_step(index):
-        for inner, summed in enumerate(column_step(index, tile_rows, columns_ref, pass_ref)):
-            matched_ref[:, pl.ds(pl.multiple_of(index * WIDE + inner * CHUNK, CHUNK), CHUNK)] = (
-                summed.astype(jnp.bfloat16)
-            )
-
-    passes(fetch, step, match_step, pass_ref, width)
+        row_step(
+            WIDE, index * WIDE, BLOCK + index * WIDE, strips, coef_ref, rows_ref, pass_ref
+        )
+
+    def match(at, summed):
+        matched_ref[:RIM, at] = summed[:RIM].astype(jnp.bfloat16)
+        matched_ref[tile_rows - RIM :, at] = summed[RIM:].astype(jnp.bfloat16)
+
+    column_strip(pair, columns_ref, pass_ref, match)
     for load in loads:
         load.wait()
 
@@ -291,7 +387,7 @@
 
 
 def forward(
-    ident, weight, coef, above, image, below, rows, columns, warp_rows, warp_columns
+    ident, weight, coef, above, image, below, inner, rows, columns, warp_rows, warp_columns
 ):
     tile_rows, width = image.shape
     bases = rows.shape[0] // BLOCK
@@ -299,28 +395,26 @@
     return pl.pallas_call(
         forward_kernel,
         out_shape=jax.ShapeDtypeStruct((lines, BLOCK), jnp.bfloat16),
-        in_specs=[SMEM, SMEM, SMEM, VMEM, HBM, VMEM, VMEM, VMEM, HBM, HBM],
+        in_specs=[SMEM, SMEM, SMEM, VMEM, HBM, VMEM, HBM, VMEM, VMEM, HBM, HBM],
         out_specs=HBM,
         scratch_shapes=[
-            pltpu.VMEM((tile_rows, width), jnp.bfloat16),
-            pltpu.VMEM((bases, tile_rows, width + 2 * BLOCK), jnp.bfloat16),
+            pltpu.VMEM((4 * RIM, width), jnp.bfloat16),
+            pltpu.VMEM((bases, 2 * RIM, width + 2 * BLOCK), jnp.bfloat16),
             pltpu.VMEM((tile_rows, width), jnp.bfloat16),
             pltpu.VMEM((lines + BLOCK * PAD, BLOCK), jnp.float32),
             pltpu.VMEM((lines, BLOCK), jnp.bfloat16),
             pltpu.VMEM(warp_rows.shape, jnp.bfloat16),
             pltpu.VMEM(warp_columns.shape, jnp.bfloat16),
-            pltpu.SemaphoreType.DMA((width // WIDE,)),
             pltpu.SemaphoreType.DMA((2,)),
+            pltpu.SemaphoreType.DMA((3,)),
             pltpu.SemaphoreType.DMA((GROUPS,)),
         ],
         compiler_params=grant(58),
         name="match_warp",
-    )(ident, weight, coef, above, image, below, rows, columns, warp_rows, warp_columns)
-
-
-def slots_kernel(
-    slot_hbm, repeat_ref, arrived_ref, scale_ref, template_ref, coadd_ref, wide_ref, *refs
-):
+    )(ident, weight, coef, above, image, below, inner, rows, columns, warp_rows, warp_columns)
+
+
+def slots_kernel(slot_hbm, arrived_ref, scale_ref, template_ref, coadd_ref, wide_ref, *refs):
     del scale_ref
     items, _, sources = slot_hbm.shape
     sums, tables, sems = refs[:LANES], refs[LANES : LANES + items], refs[LANES + items]
@@ -340,39 +434,16 @@
     for load in loads:
         load.wait()
 
-    def add(source, blocks, sum_ref):
-        slots = [tables[block][0, source] for block in blocks]
-        values = [
-            sum_ref[pl.ds(slot, 1), :] + wide_ref[pl.ds(source * items + block, 1), :]
-            for slot, block in zip(slots, blocks)
-        ]
-        for slot, value in zip(slots, values):
-            sum_ref[pl.ds(slot, 1), :] = value
-
-    groups = [list(range(first, first + LANES)) for first in range(0, items, LANES)]
-
     @pl.loop(0, sources)
     def _(source):
-        repeats = repeat_ref[0, source]
-
-        @pl.when(repeats == 0)
-        def _():
-            for index, blocks in enumerate(groups):
-                add(source, blocks, sums[index % LANES])
-
-        @pl.when(repeats != 0)
-        def _():
-            for index, blocks in enumerate(groups):
-                repeated = (repeats // 2**index) % 2
-
-                @pl.when(repeated == 0)
-                def _():
-                    add(source, blocks, sums[index % LANES])
-
-                @pl.when(repeated != 0)
-                def _():
-                    for lane, block in enumerate(blocks):
-                        add(source, [block], sums[lane])
+        for first in range(0, items, LANES):
+            slots = [tables[first + lane][0, source] for lane in range(LANES)]
+            values = [
+                sum_ref[pl.ds(slot, 1), :] + wide_ref[pl.ds(source * items + first + lane, 1), :]
+                for lane, (slot, sum_ref) in enumerate(zip(slots, sums))
+            ]
+            for slot, sum_ref, value in zip(slots, sums, values):
+                sum_ref[pl.ds(slot, 1), :] = value
 
     @pl.loop(0, sources)
     def _(source):
@@ -388,19 +459,9 @@
             slot = tables[item][0, source]
             wide_ref[pl.ds(source * items + item, 1), :] = sums[0][pl.ds(slot, 1), :]
 
-    @pl.loop(0, sources, unroll=2)
+    @pl.loop(0, sources)
     def _(source):
         template_ref[at(source), :] = wide_ref[at(source), :].astype(jnp.bfloat16)
-
-
-def group_repeats(slots):
-    grouped = slots.T.reshape(-1, LANES, slots.shape[0])
-    repeated = jnp.zeros(grouped[:, 0].shape, jnp.bool_)
-    for later in range(1, LANES):
-        for earlier in range(later):
-            repeated = repeated | (grouped[:, later] == grouped[:, earlier])
-    bits = 2 ** jnp.arange(grouped.shape[0], dtype=jnp.int32)
-    return jnp.sum(jnp.where(repeated, bits[:, None], 0), axis=0, keepdims=True)
 
 
 def slot_sums(slots, arrived, scale):
@@ -409,14 +470,14 @@
     return pl.pallas_call(
         slots_kernel,
         out_shape=(shape, shape),
-        in_specs=[ANY, SMEM, VMEM, SMEM],
+        in_specs=[ANY, VMEM, SMEM],
         out_specs=(VMEM, VMEM),
         scratch_shapes=[pltpu.VMEM(arrived.shape, jnp.float32)] * (1 + LANES)
         + [pltpu.SMEM((1, sources), jnp.int32)] * items
         + [pltpu.SemaphoreType.DMA((items,))],
         compiler_params=grant(44),
         name="slot_sums",
-    )(slots.T.reshape(items, 1, sources), group_repeats(slots), arrived, scale)
+    )(slots.T.reshape(items, 1, sources), arrived, scale)
 
 
 def unwarp_kernel(
@@ -540,12 +601,12 @@
     for index in range(width // WIDE):
         fetch(index).start()
     load.start()
-    strips = [
-        (0, BLOCK, [(image_ref, 0, WINDOW, 0)]),
-        (BLOCK, inner - BLOCK, [(image_ref, BLOCK, tile_rows - BLOCK, 0)]),
-    ]
     step = functools.partial(
-        row_step, strips=strips, coef_ref=coef_ref, rows_ref=rows_ref, pass_ref=pass_ref
+        row_step,
+        strips=inner_strips(image_ref),
+        coef_ref=coef_ref,
+        rows_ref=rows_ref,
+        pass_ref=pass_ref,
     )
 
     def store(index):
@@ -624,8 +685,9 @@
             pltpu.make_async_copy(stage_ref.at[here], out_hbm.at[there], store_sems.at[index]),
         )
 
-    for index in range(2):
-        ends(index)[0].start()
+    fetches, stores = zip(*(ends(index) for index in range(2)))
+    for fetch in fetches:
+        fetch.start()
     strips = [
         (0, RIM, [(ref, 0, RIM, 0) for ref in (above_ref, top_ref, under_top_ref)]),
         (RIM, RIM, [(ref, 0, RIM, 0) for ref in (over_bottom_ref, bottom_ref, below_ref)]),
@@ -636,16 +698,17 @@
         row_step(
             WIDE, index * WIDE, BLOCK + index * WIDE, strips, coef_ref, rows_ref, pass_ref
         )
-    for index in range(2):
-        ends(index)[0].wait()
-    for index in range(width // WIDE):
-        for part, summed in enumerate(column_step(index, 2 * RIM, columns_ref, pass_ref)):
-            at = pl.ds(index * WIDE + part * CHUNK, CHUNK)
-            stage_ref[:, at] = exposure_ref[:, at].astype(jnp.float32) - summed
-    for index in range(2):
-        ends(index)[1].start()
-    for index in range(2):
-        ends(index)[1].wait()
+    for fetch in fetches:
+        fetch.wait()
+
+    def subtract(at, summed):
+        stage_ref[:, at] = exposure_ref[:, at].astype(jnp.float32) - summed
+
+    column_strip(2 * RIM, columns_ref, pass_ref, subtract)
+    for store in stores:
+        store.start()
+    for store in stores:
+        store.wait()
 
 
 def subtract_outer(coef, rims, exposure, rows, columns, partial):
@@ -681,39 +744,45 @@
     pitch = slots + PAD
     myself = my_device()
     lines = owned_ref.shape[0] // GROUPS
+    count = BLOCK // GROUPS
 
     def fetch(group):
         at = pl.ds(group * lines, lines)
         return pltpu.make_async_copy(owned_hbm.at[at], owned_ref.at[at], fetch_sems.at[group])
+
+    def store(group, down):
+        at = pl.ds(pl.multiple_of(down * BLOCK + group * count, count), count)
+        return pltpu.make_async_copy(
+            stage_ref.at[at], out_hbm.at[at], store_sems.at[group, down]
+        )
 
     for group in range(GROUPS):
         fetch(group).start()
     for group in range(GROUPS):
         fetch(group).wait()
 
-        @pl.loop(group * BLOCK // GROUPS, (group + 1) * BLOCK // GROUPS, unroll=4)
+        @pl.loop(group * count, (group + 1) * count, unroll=4)
         def _(row):
             to = pl.ds(pl.multiple_of(row * pitch, PAD), slots)
             at = pl.ds(pl.multiple_of(row * slots, slots), slots)
             wide_ref[to, :] = owned_ref[at, :].astype(jnp.float32)
 
-    def store(down):
-        at = pl.ds(pl.multiple_of(down * BLOCK, BLOCK), BLOCK)
-        return pltpu.make_async_copy(stage_ref.at[at], out_hbm.at[at], store_sems.at[down])
-
-    @pl.loop(0, SLOT_ROWS)
-    def _(down):
-        to = pl.ds(pl.multiple_of(down * BLOCK, BLOCK), BLOCK)
-        for across in range(SLOT_COLS):
-            slot = down * SLOT_COLS + across
-            stage_ref[to, across * BLOCK : (across + 1) * BLOCK] = (
-                scale_ref[myself, slot] * wide_ref[pl.ds(slot, BLOCK, stride=pitch), :]
-            )
-        store(down).start()
-
-    @pl.loop(0, SLOT_ROWS)
-    def _(down):
-        store(down).wait()
+        @pl.loop(0, SLOT_ROWS)
+        def _(down):
+            to = pl.ds(pl.multiple_of(down * BLOCK + group * count, count), count)
+            for across in range(SLOT_COLS):
+                slot = down * SLOT_COLS + across
+                stage_ref[to, across * BLOCK : (across + 1) * BLOCK] = (
+                    scale_ref[myself, slot]
+                    * wide_ref[pl.ds(group * count * pitch + slot, count, stride=pitch), :]
+                )
+            store(group, down).start()
+
+    for group in range(GROUPS):
+
+        @pl.loop(0, SLOT_ROWS)
+        def _(down):
+            store(group, down).wait()
 
 
 def patch(scale, owned, order):
@@ -728,7 +797,7 @@
             pltpu.VMEM((owned.shape[0] + BLOCK * PAD, BLOCK), jnp.float32),
             pltpu.VMEM(shape, jnp.float32),
             pltpu.SemaphoreType.DMA((GROUPS,)),
-            pltpu.SemaphoreType.DMA((SLOT_ROWS,)),
+            pltpu.SemaphoreType.DMA((GROUPS, SLOT_ROWS)),
         ],
         compiler_params=grant(14),
         name="patch",
@@ -761,7 +830,7 @@
     ident = warp_id.reshape(devices, per_tile)
 
     above, below = swap_rims(image[:RIM], image[tile_rows - RIM :])
-    rows, columns = band_matrices(row_taps, column_taps)
+    rows, columns, inner = match_inner(basis_coef, row_taps, column_taps, image)
     weighted = forward(
         ident,
         weight,
@@ -769,6 +838,7 @@
         above,
         image,
         below,
+        inner,
         rows,
         columns,
         warp_rows,

time: 163 us -> 164 us (level)
  waiting for transfers between devices: 32.2 us -> 27.9 us
  starting transfers between devices: 27.7 us -> 31.3 us
    pallas_call x2, Pallas kernels: 21.3 us -> 28.3 us  [the longest x1 18.7 us: slot_sums(): pl.pallas_call(slots_kernel, out_shape=(shape, shape), in_specs=[ANY, VME...]
    ppermute x2, waiting for transfers between devices: 6.97 us -> 2.53 us  [swap_rims(): lax.ppermute(bottom, 'tile', forward)]
    pallas_call x1, Pallas kernels: 13.8 us -> 9.86 us  [forward(): pl.pallas_call(forward_kernel, out_shape=jax.ShapeDtypeStruct((lines, BLO...]
    all_to_all x2, starting transfers between devices: 13.1 us -> 16.7 us  [exchange(): lax.all_to_all(shaped, ('exp', 'tile'), split_axis=0, concat_axis=0, tile...]
  transfers between devices with their start and end apart: 6 -> 6, of which waited for: 3 -> 2; matrix products, arithmetic and copies ran while one was open for 3% -> 2% of each run, Pallas kernels for 15% -> 18%
where the time goes in v6:
time: 164 us; the launch traced here: 163 us
  Pallas kernels  62.4 us (38%)
  blocking collectives  34.5 us (21%)
  starting transfers between devices  31.3 us (19%)
  waiting for transfers between devices  27.9 us (17%)
  local copies, waits for them, and re-layouts  3.02 us (2%)
  matrix products  2.66 us (2%)
    all_to_all x1, blocking collectives, exchange(): lax.all_to_all(shaped, ('exp', 'tile'), split_axis=0, concat_axis=0, tile...  34.5 us
    all_to_all x2, waiting for transfers between devices, exchange(): lax.all_to_all(shaped, ('exp', 'tile'), split_axis=0, concat_axis=0, tile...  25.4 us
    pallas_call x1, Pallas kernels, slot_sums(): pl.pallas_call(slots_kernel, out_shape=(shape, shape), in_specs=[ANY, VME...  18.7 us
    all_to_all x2, starting transfers between devices, exchange(): lax.all_to_all(shaped, ('exp', 'tile'), split_axis=0, concat_axis=0, tile...  16.7 us
    pallas_call x1, Pallas kernels, forward(): pl.pallas_call(forward_kernel, out_shape=jax.ShapeDtypeStruct((lines, BLO...  9.86 us
    pallas_call x1, Pallas kernels, match_inner(): pl.pallas_call(match_inner_kernel, out_shape=(jax.ShapeDtypeStruct((bases...  9.57 us
    ppermute x2, starting transfers between devices, swap_rims(): lax.ppermute(top, 'tile', backward)  9.31 us
    pallas_call x1, Pallas kernels, subtract_inner(): pl.pallas_call(inner_kernel, out_shape=jax.ShapeDtypeStruct((tile_rows, w...  8.85 us
  transfers between devices with their start and end apart: 6, of which 2 were waited for; matrix products, arithmetic and copies ran while one was open for 2% of the time, Pallas kernels for 18%

profile of v6, /device:TPU:8, one launch (start us, length us, event | category | flops | bytes accessed | tf_op | source)
XLA Modules:
  0.0 163.0 jit_solution(12775351982382508030)
XLA Ops:
  0.6 1.0 slice_bitcast_fusion
  1.6 4.6 %collective-permute-start.1 = (bf16[16,4096]{1,0:T(8,128)(2,1)S(1)}, bf16[16,4096]{1,0:T(8,128)(2,1)S(1)}, u32[]{:S(2)}, u32[]{:S(2)}) collective-permute-start(bf16[16,4096]{1,0:T(8,128)(2,1)S(1)} %get-tuple-element.26), channel_id=1, source_target_pairs={{1,0},{2,1},{3,2},{4,3},{5,4},{6,5},{7,6},{8,7},{9,8},{10,9},{11,1... | collective-permute-start | bytes 393224 | tf_op jit(solution)/shard_map/ppermute | solution.py:66
  6.2 1.9 %collective-permute-start = (bf16[16,4096]{1,0:T(8,128)(2,1)S(1)}, bf16[16,4096]{1,0:T(8,128)(2,1)S(1)}, u32[]{:S(2)}, u32[]{:S(2)}) collective-permute-start(bf16[16,4096]{1,0:T(8,128)(2,1)S(1)} %get-tuple-element.27), channel_id=1, source_target_pairs={{0,1},{1,2},{2,3},{3,4},{4,5},{5,6},{6,7},{7,8},{8,9},{9,10},{10,1... | collective-permute-start | bytes 393224 | tf_op jit(solution)/shard_map/ppermute | solution.py:66
  8.1 9.6 %match_inner.1 = (bf16[384,160]{1,0:T(8,128)(2,1)}, bf16[1152,256]{1,0:T(8,128)(2,1)}, bf16[224,4096]{1,0:T(8,128)(2,1)}) custom-call(f32[1,3]{1,0:T(1,128)} %coef_ref.7, bf16[3,21]{1,0:T(4,128)(2,1)} %row_taps_ref.1, bf16[3,21]{1,0:T(4,128)(2,1)} %column_taps_ref.1, bf16[256,4096]{1,0:T(8,128)(2,1)} %bitcast.20), custom_call_target="tpu_custom_call" | custom-call | tf_op jit(solution)/shard_map/match_inner/pallas_call | solution.py:242
  17.7 0.0 collective-permute-done.1.below_ref
  17.7 0.0 copy-start.12
  17.7 0.0 collective-permute-done.above_ref
  17.7 0.0 copy-start.13
  17.7 0.6 copy-done.12
  18.3 0.1 copy-done.13
  18.4 9.9 %match_warp.1 = bf16[8192,128]{1,0:T(8,128)(2,1)} custom-call(s32[128,64]{1,0:T(8,128)} %bitcast.34, f32[8,16]{1,0:T(8,128)} %weight_ref.1, f32[1,3]{1,0:T(1,128)} %coef_ref.7, bf16[16,4096]{1,0:T(8,128)(2,1)} %copy-done.13, bf16[256,4096]{1,0:T(8,128)(2,1)} %bitcast.21, bf16[16,4096]{1,0:T(8,128)(2,1)} %copy-done.12, ...), custom_call_target="tpu_custom_call" | custom-call | tf_op jit(solution)/shard_map/match_warp/pallas_call | solution.py:395
  28.3 0.0 copy-start.14
  28.3 0.0 copy-start.10
  28.3 0.0 copy-start.11
  28.3 11.7 %all-to-all-start = ((bf16[128,64,128]{2,1,0:T(8,128)(2,1)}), bf16[128,64,128]{2,1,0:T(8,128)(2,1)S(1)}, u32[]{:S(2)}, u32[]{:S(2)}) async-start(bf16[128,64,128]{2,1,0:T(8,128)(2,1)} %bitcast.33), calls=%async_computation | async-start | bytes 4194304 | tf_op jit(solution)/shard_map/all_to_all | solution.py:809
  40.0 0.0 copy-done.14
  40.0 0.1 reshape.42
  40.1 0.0 copy-done.10
  40.1 0.1 eq.30
  40.2 0.0 copy-done.11
  40.2 0.1 eq.34
  40.2 0.1 broadcast_in_dim.25
  40.3 0.1 broadcast_in_dim.26
  40.4 2.7 %fusion.8.scale_ref = f32[128,64]{1,0:T(8,128)S(1)} fusion(f32[8192]{0:T(1024)S(1)} %broadcast_in_dim.26, s32[8192]{0:T(1024)S(1)} %eq.30, s32[8192]{0:T(1024)S(1)} %eq.34), kind=kOutput, calls=%fused_computation.9 | convolution fusion | flops 807944192 | bytes 131072 | tf_op jit(solution)/shard_map/dot_general | solution.py:858
  43.1 0.1 reshape.48
  43.2 0.1 copy.18
  43.3 0.8 gather_fusion
  44.0 0.0 copy-start.9
  44.0 25.4 %all-to-all-done = bf16[128,64,128]{2,1,0:T(8,128)(2,1)S(1)} async-done(((bf16[128,64,128]{2,1,0:T(8,128)(2,1)}), bf16[128,64,128]{2,1,0:T(8,128)(2,1)S(1)}, u32[]{:S(2)}, u32[]{:S(2)}) %all-to-all-start) | async-done | bytes 2097184 | tf_op jit(solution)/shard_map/all_to_all | solution.py:809
  69.4 18.7 %slot_sums.1 = (bf16[8192,128]{1,0:T(8,128)(2,1)S(1)}, bf16[8192,128]{1,0:T(8,128)(2,1)S(1)}) custom-call(s32[64,1,128]{2,1,0:T(1,128)S(1)} %bitcast.28, bf16[8192,128]{1,0:T(8,128)(2,1)S(1)} %bitcast.24, f32[1,64]{1,0:T(1,128)S(1)} %bitcast.29), custom_call_target="tpu_custom_call" | custom-call | tf_op jit(solution)/shard_map/slot_sums/pallas_call | solution.py:470
  88.2 0.0 copy-start.2
  88.2 34.5 %all_to_all.15 = bf16[128,64,128]{2,1,0:T(8,128)(2,1)} all-to-all(bf16[128,64,128]{2,1,0:T(8,128)(2,1)S(1)} %bitcast.27), channel_id=1, replica_groups=mesh['exp'=8,'tile'=16] {'exp','tile'}, dimensions={0} | all-to-all | bytes 4194304 | tf_op jit(solution)/shard_map/all_to_all | solution.py:809
  122.7 0.0 copy-done.9
  122.7 0.0 copy-done.2
  122.7 5.0 %all-to-all-start.1 = ((bf16[128,64,128]{2,1,0:T(8,128)(2,1)}), bf16[128,64,128]{2,1,0:T(8,128)(2,1)S(1)}, u32[]{:S(2)}, u32[]{:S(2)}) async-start(bf16[128,64,128]{2,1,0:T(8,128)(2,1)} %bitcast.26), calls=%async_computation.1 | async-start | bytes 4194304 | tf_op jit(solution)/shard_map/all_to_all | solution.py:809
  127.7 8.6 %unwarp.1 = (bf16[256,4096]{1,0:T(8,128)(2,1)}, bf16[16,4096]{1,0:T(8,128)(2,1)}, bf16[16,4096]{1,0:T(8,128)(2,1)}, bf16[16,4096]{1,0:T(8,128)(2,1)}, bf16[16,4096]{1,0:T(8,128)(2,1)}) custom-call(s32[128,64]{1,0:T(8,128)} %bitcast.35, f32[1,64]{1,0:T(1,128)} %bitcast.30, bf16[8192,128]{1,0:T(8,128)(2,1)} %bitcast.32, bf16[64,128,128]{2,1,0:T(8,128)(2,1)} %bank_rows_ref.3, ...), custom_call_target="tpu_custom_call" | custom-call | tf_op jit(solution)/shard_map/unwarp/pallas_call | solution.py:566
  136.3 3.4 %collective-permute-start.2 = (bf16[16,4096]{1,0:T(8,128)(2,1)}, bf16[16,4096]{1,0:T(8,128)(2,1)S(1)}, u32[]{:S(2)}, u32[]{:S(2)}) collective-permute-start(bf16[16,4096]{1,0:T(8,128)(2,1)} %get-tuple-element.19.bottom_ref), channel_id=1, source_target_pairs={{0,1},{1,2},{2,3},{3,4},{4,5},{5,6},{6,7},{7,8},{8,9},{9,10},{10,1... | collective-permute-start | bytes 393224 | tf_op jit(solution)/shard_map/ppermute | solution.py:66
  139.7 4.8 %collective-permute-start.3 = (bf16[16,4096]{1,0:T(8,128)(2,1)}, bf16[16,4096]{1,0:T(8,128)(2,1)S(1)}, u32[]{:S(2)}, u32[]{:S(2)}) collective-permute-start(bf16[16,4096]{1,0:T(8,128)(2,1)} %get-tuple-element.20.top_ref), channel_id=1, source_target_pairs={{1,0},{2,1},{3,2},{4,3},{5,4},{6,5},{7,6},{8,7},{9,8},{10,9},{11,1... | collective-permute-start | bytes 393224 | tf_op jit(solution)/shard_map/ppermute | solution.py:66
  144.4 0.0 copy-start
  144.5 0.0 copy-start.1
  144.5 0.0 copy-start.3
  144.5 0.0 copy-start.4
  144.5 0.0 copy-start.5
  144.5 0.0 copy-start.6
  144.5 0.0 copy-start.7
  144.5 0.0 copy-start.8
  144.5 8.8 %subtract_inner.1.partial_hbm = f32[256,4096]{1,0:T(8,128)} custom-call(f32[1,3]{1,0:T(1,128)} %coef_ref.7, bf16[256,4096]{1,0:T(8,128)(2,1)} %get-tuple-element.23.image_hbm, bf16[256,4096]{1,0:T(8,128)(2,1)} %bitcast.22, bf16[384,160]{1,0:T(8,128)(2,1)} %get-tuple-element.15.rows_ref, bf16[1152,256]{1,0:T(8,128)(2,1)} %get-tuple-element.16.columns_ref), custom_call_target="tpu_custom_call" | custom-call | tf_op jit(solution)/shard_map/subtract_inner/pallas_call | solution.py:635
  153.4 2.5 %collective-permute-done.2.above_ref = bf16[16,4096]{1,0:T(8,128)(2,1)S(1)} collective-permute-done((bf16[16,4096]{1,0:T(8,128)(2,1)}, bf16[16,4096]{1,0:T(8,128)(2,1)S(1)}, u32[]{:S(2)}, u32[]{:S(2)}) %collective-permute-start.2) | collective-permute-done | bytes 131104 | tf_op jit(solution)/shard_map/ppermute | solution.py:66
  155.9 0.0 collective-permute-done.3.below_ref
  155.9 0.0 copy-done
  155.9 0.0 copy-done.1
  155.9 0.0 copy-done.3
  155.9 0.0 copy-done.4
  155.9 0.0 copy-done.5
  156.0 0.0 copy-done.6
  156.0 0.0 copy-done.7
  156.0 0.0 copy-done.8
  156.0 2.6 %subtract_outer.1 = (f32[256,4096]{1,0:T(8,128)}, f32[8,128]{1,0:T(8,128)S(1)}) custom-call(f32[1,3]{1,0:T(1,128)S(1)} %copy-done.8, bf16[16,4096]{1,0:T(8,128)(2,1)S(1)} %collective-permute-done.2.above_ref, bf16[16,4096]{1,0:T(8,128)(2,1)S(1)} %copy-done.4, bf16[16,4096]{1,0:T(8,128)(2,1)S(1)} %copy-done.5, ...), custom_call_target="tpu_custom_call", output_to_operand_aliasing={{0}: (10, {})} | custom-call | tf_op jit(solution)/shard_map/subtract_outer/pallas_call | solution.py:718
  158.6 0.0 all-to-all-done.1
  158.6 4.2 %patch.1 = f32[1024,1024]{1,0:T(8,128)} custom-call(f32[128,64]{1,0:T(8,128)S(1)} %fusion.8.scale_ref, bf16[8192,128]{1,0:T(8,128)(2,1)S(1)} %bitcast.25, f32[8,128]{1,0:T(8,128)S(1)} %get-tuple-element.24.order_ref), custom_call_target="tpu_custom_call" | custom-call | tf_op jit(solution)/shard_map/patch/pallas_call | solution.py:790
  (3 shorter events, 0.0 us)
Async XLA Ops:
  1.6 16.1 %collective-permute-start.1 = (bf16[16,4096]{1,0:T(8,128)(2,1)S(1)}, bf16[16,4096]{1,0:T(8,128)(2,1)S(1)}, u32[]{:S(2)}, u32[]{:S(2)}) collective-permute-start(bf16[16,4096]{1,0:T(8,128)(2,1)S(1)} %get-tuple-element.26), channel_id=1, source_target_pairs={{1,0},{2,1},{3,2},{4,3},{5,4},{6,5},{7,6},{8,7},{9,8},{10,9},{11,1... | collective-permute-start | bytes 393224 | tf_op jit(solution)/shard_map/ppermute | solution.py:66
  6.2 11.5 %collective-permute-start = (bf16[16,4096]{1,0:T(8,128)(2,1)S(1)}, bf16[16,4096]{1,0:T(8,128)(2,1)S(1)}, u32[]{:S(2)}, u32[]{:S(2)}) collective-permute-start(bf16[16,4096]{1,0:T(8,128)(2,1)S(1)} %get-tuple-element.27), channel_id=1, source_target_pairs={{0,1},{1,2},{2,3},{3,4},{4,5},{5,6},{6,7},{7,8},{8,9},{9,10},{10,1... | collective-permute-start | bytes 393224 | tf_op jit(solution)/shard_map/ppermute | solution.py:66
  17.7 0.6 copy-start.12
  17.7 0.7 copy-start.13
  28.3 11.7 %copy-start.14 = (f32[8,16]{1,0:T(8,128)S(1)}, f32[8,16]{1,0:T(8,128)}, u32[]{:S(2)}) copy-start(f32[8,16]{1,0:T(8,128)} %weight_ref.1) | copy-start | bytes 1540
  28.3 11.8 %copy-start.10 = (s32[8,16,64]{2,1,0:T(8,128)S(1)}, s32[8,16,64]{2,1,0:T(8,128)}, u32[]{:S(2)}) copy-start(s32[8,16,64]{2,1,0:T(8,128)} %param.17) | copy-start | bytes 98308
  28.3 11.9 %copy-start.11 = (s32[8,16,64]{2,1,0:T(8,128)S(1)}, s32[8,16,64]{2,1,0:T(8,128)}, u32[]{:S(2)}) copy-start(s32[8,16,64]{2,1,0:T(8,128)} %param.18) | copy-start | bytes 98308
  28.3 41.1 %all-to-all-start = ((bf16[128,64,128]{2,1,0:T(8,128)(2,1)}), bf16[128,64,128]{2,1,0:T(8,128)(2,1)S(1)}, u32[]{:S(2)}, u32[]{:S(2)}) async-start(bf16[128,64,128]{2,1,0:T(8,128)(2,1)} %bitcast.33), calls=%async_computation | async-start | bytes 4194304 | tf_op jit(solution)/shard_map/all_to_all | solution.py:809
  44.0 78.6 %copy-start.9 = (f32[64]{0:T(128)}, f32[64]{0:T(128)S(1)}, u32[]{:S(2)}) copy-start(f32[64]{0:T(128)S(1)} %gather_fusion) | copy-start | bytes 772
  88.2 34.5 %copy-start.2 = (bf16[8192,128]{1,0:T(8,128)(2,1)}, bf16[8192,128]{1,0:T(8,128)(2,1)S(1)}, u32[]{:S(2)}) copy-start(bf16[8192,128]{1,0:T(8,128)(2,1)S(1)} %get-tuple-element.17) | copy-start | bytes 6291460
  122.7 35.9 %all-to-all-start.1 = ((bf16[128,64,128]{2,1,0:T(8,128)(2,1)}), bf16[128,64,128]{2,1,0:T(8,128)(2,1)S(1)}, u32[]{:S(2)}, u32[]{:S(2)}) async-start(bf16[128,64,128]{2,1,0:T(8,128)(2,1)} %bitcast.26), calls=%async_computation.1 | async-start | bytes 4194304 | tf_op jit(solution)/shard_map/all_to_all | solution.py:809
  136.3 19.6 %collective-permute-start.2 = (bf16[16,4096]{1,0:T(8,128)(2,1)}, bf16[16,4096]{1,0:T(8,128)(2,1)S(1)}, u32[]{:S(2)}, u32[]{:S(2)}) collective-permute-start(bf16[16,4096]{1,0:T(8,128)(2,1)} %get-tuple-element.19.bottom_ref), channel_id=1, source_target_pairs={{0,1},{1,2},{2,3},{3,4},{4,5},{5,6},{6,7},{7,8},{8,9},{9,10},{10,1... | collective-permute-start | bytes 393224 | tf_op jit(solution)/shard_map/ppermute | solution.py:66
  139.7 16.2 %collective-permute-start.3 = (bf16[16,4096]{1,0:T(8,128)(2,1)}, bf16[16,4096]{1,0:T(8,128)(2,1)S(1)}, u32[]{:S(2)}, u32[]{:S(2)}) collective-permute-start(bf16[16,4096]{1,0:T(8,128)(2,1)} %get-tuple-element.20.top_ref), channel_id=1, source_target_pairs={{1,0},{2,1},{3,2},{4,3},{5,4},{6,5},{7,6},{8,7},{9,8},{10,9},{11,1... | collective-permute-start | bytes 393224 | tf_op jit(solution)/shard_map/ppermute | solution.py:66
  144.4 11.5 %copy-start = (bf16[1,256,4096]{2,1,0:T(8,128)(2,1)S(1)}, bf16[1,256,4096]{2,1,0:T(8,128)(2,1)}, u32[]{:S(2)}) copy-start(bf16[1,256,4096]{2,1,0:T(8,128)(2,1)} %param.10) | copy-start | bytes 6291460
  144.5 11.5 %copy-start.1 = (bf16[1152,256]{1,0:T(8,128)(2,1)S(1)}, bf16[1152,256]{1,0:T(8,128)(2,1)}, u32[]{:S(2)}) copy-start(bf16[1152,256]{1,0:T(8,128)(2,1)} %get-tuple-element.16.columns_ref) | copy-start | bytes 1769476
  144.5 11.5 %copy-start.3 = (bf16[384,160]{1,0:T(8,128)(2,1)S(1)}, bf16[384,160]{1,0:T(8,128)(2,1)}, u32[]{:S(2)}) copy-start(bf16[384,160]{1,0:T(8,128)(2,1)} %get-tuple-element.15.rows_ref) | copy-start | bytes 368644
  144.5 11.5 %copy-start.4 = (bf16[16,4096]{1,0:T(8,128)(2,1)S(1)}, bf16[16,4096]{1,0:T(8,128)(2,1)}, u32[]{:S(2)}) copy-start(bf16[16,4096]{1,0:T(8,128)(2,1)} %get-tuple-element.20.top_ref) | copy-start | bytes 393220
  144.5 11.5 %copy-start.5 = (bf16[16,4096]{1,0:T(8,128)(2,1)S(1)}, bf16[16,4096]{1,0:T(8,128)(2,1)}, u32[]{:S(2)}) copy-start(bf16[16,4096]{1,0:T(8,128)(2,1)} %get-tuple-element.21.under_top_ref) | copy-start | bytes 393220
  144.5 11.5 %copy-start.6 = (bf16[16,4096]{1,0:T(8,128)(2,1)S(1)}, bf16[16,4096]{1,0:T(8,128)(2,1)}, u32[]{:S(2)}) copy-start(bf16[16,4096]{1,0:T(8,128)(2,1)} %get-tuple-element.22.over_bottom_ref) | copy-start | bytes 393220
  144.5 11.5 %copy-start.7 = (bf16[16,4096]{1,0:T(8,128)(2,1)S(1)}, bf16[16,4096]{1,0:T(8,128)(2,1)}, u32[]{:S(2)}) copy-start(bf16[16,4096]{1,0:T(8,128)(2,1)} %get-tuple-element.19.bottom_ref) | copy-start | bytes 393220
  144.5 11.5 %copy-start.8 = (f32[1,3]{1,0:T(1,128)S(1)}, f32[1,3]{1,0:T(1,128)}, u32[]{:S(2)}) copy-start(f32[1,3]{1,0:T(1,128)} %coef_ref.7) | copy-start | bytes 40

commit v7 on v5

--- a/solution.py
+++ b/solution.py
@@ -16,7 +16,7 @@
 WINDOW = BLOCK + 2 * RIM
 SLOT_ROWS = 8
 SLOT_COLS = 8
-LANES = 4
+LANES = 8
 PAD = 8
 VMEM = pl.BlockSpec(memory_space=pltpu.VMEM)
 SMEM = pl.BlockSpec(memory_space=pltpu.SMEM)
@@ -26,7 +26,7 @@
 
 
 def grant(mebibytes):
-    return pltpu.CompilerParams(vmem_limit_bytes=mebibytes * 1024 * 1024)
+    return pltpu.CompilerParams(vmem_limit_bytes=int(mebibytes * 1024 * 1024))
 
 
 def bands_kernel(row_taps_ref, column_taps_ref, rows_ref, columns_ref):
@@ -109,33 +109,54 @@
             ] = (coef_ref[0, base] * summed[base * count : (base + 1) * count]).astype(jnp.bfloat16)
 
 
-def column_step(index, count, columns_ref, pass_ref):
+def column_window(at, count, pass_ref):
     bases = pass_ref.shape[0]
     right = lax.broadcasted_iota(jnp.int32, (count, BLOCK), 1) < BLOCK // 2
-    summed = []
-    for part in range(WIDE // CHUNK):
-        at = index * WIDE + part * CHUNK
-
-        def columns(shift, size):
-            return pl.ds(pl.multiple_of(at + shift, BLOCK), size)
-
-        middle = [pass_ref[base, :count, columns(BLOCK, CHUNK)] for base in range(bases)]
-        sides = [
-            jnp.where(
-                right,
-                pass_ref[base, :count, columns(BLOCK + CHUNK, BLOCK)],
-                pass_ref[base, :count, columns(0, BLOCK)],
+
+    def columns(shift, size):
+        return pl.ds(pl.multiple_of(at + shift, BLOCK), size)
+
+    middle = [pass_ref[base, :count, columns(BLOCK, CHUNK)] for base in range(bases)]
+    sides = [
+        jnp.where(
+            right,
+            pass_ref[base, :count, columns(BLOCK + CHUNK, BLOCK)],
+            pass_ref[base, :count, columns(0, BLOCK)],
+        )
+        for base in range(bases)
+    ]
+    return jnp.concatenate(middle + sides, axis=1)
+
+
+def column_step(index, count, columns_ref, pass_ref):
+    return [
+        jnp.dot(
+            column_window(index * WIDE + part * CHUNK, count, pass_ref),
+            columns_ref[...],
+            preferred_element_type=jnp.float32,
+        )
+        for part in range(WIDE // CHUNK)
+    ]
+
+
+def column_strip(count, columns_ref, pass_ref, consume):
+    width = pass_ref.shape[2] - 2 * BLOCK
+    chunks = width // CHUNK // 2
+    for half in range(2):
+        windows = [
+            column_window((half * chunks + chunk) * CHUNK, count, pass_ref)
+            for chunk in range(chunks)
+        ]
+        summed = jnp.dot(
+            jnp.concatenate(windows, axis=0),
+            columns_ref[...],
+            preferred_element_type=jnp.float32,
+        )
+        for chunk in range(chunks):
+            consume(
+                pl.ds((half * chunks + chunk) * CHUNK, CHUNK),
+                summed[chunk * count : (chunk + 1) * count],
             )
-            for base in range(bases)
-        ]
-        summed.append(
-            jnp.dot(
-                jnp.concatenate(middle + sides, axis=1),
-                columns_ref[...],
-                preferred_element_type=jnp.float32,
-            )
-        )
-    return summed
 
 
 def my_device():
@@ -318,9 +339,7 @@
     )(ident, weight, coef, above, image, below, rows, columns, warp_rows, warp_columns)
 
 
-def slots_kernel(
-    slot_hbm, repeat_ref, arrived_ref, scale_ref, template_ref, coadd_ref, wide_ref, *refs
-):
+def slots_kernel(slot_hbm, arrived_ref, scale_ref, template_ref, coadd_ref, wide_ref, *refs):
     del scale_ref
     items, _, sources = slot_hbm.shape
     sums, tables, sems = refs[:LANES], refs[LANES : LANES + items], refs[LANES + items]
@@ -340,39 +359,16 @@
     for load in loads:
         load.wait()
 
-    def add(source, blocks, sum_ref):
-        slots = [tables[block][0, source] for block in blocks]
-        values = [
-            sum_ref[pl.ds(slot, 1), :] + wide_ref[pl.ds(source * items + block, 1), :]
-            for slot, block in zip(slots, blocks)
-        ]
-        for slot, value in zip(slots, values):
-            sum_ref[pl.ds(slot, 1), :] = value
-
-    groups = [list(range(first, first + LANES)) for first in range(0, items, LANES)]
-
     @pl.loop(0, sources)
     def _(source):
-        repeats = repeat_ref[0, source]
-
-        @pl.when(repeats == 0)
-        def _():
-            for index, blocks in enumerate(groups):
-                add(source, blocks, sums[index % LANES])
-
-        @pl.when(repeats != 0)
-        def _():
-            for index, blocks in enumerate(groups):
-                repeated = (repeats // 2**index) % 2
-
-                @pl.when(repeated == 0)
-                def _():
-                    add(source, blocks, sums[index % LANES])
-
-                @pl.when(repeated != 0)
-                def _():
-                    for lane, block in enumerate(blocks):
-                        add(source, [block], sums[lane])
+        for first in range(0, items, LANES):
+            slots = [tables[first + lane][0, source] for lane in range(LANES)]
+            values = [
+                sum_ref[pl.ds(slot, 1), :] + wide_ref[pl.ds(source * items + first + lane, 1), :]
+                for lane, (slot, sum_ref) in enumerate(zip(slots, sums))
+            ]
+            for slot, sum_ref, value in zip(slots, sums, values):
+                sum_ref[pl.ds(slot, 1), :] = value
 
     @pl.loop(0, sources)
     def _(source):
@@ -388,19 +384,9 @@
             slot = tables[item][0, source]
             wide_ref[pl.ds(source * items + item, 1), :] = sums[0][pl.ds(slot, 1), :]
 
-    @pl.loop(0, sources, unroll=2)
+    @pl.loop(0, sources)
     def _(source):
         template_ref[at(source), :] = wide_ref[at(source), :].astype(jnp.bfloat16)
-
-
-def group_repeats(slots):
-    grouped = slots.T.reshape(-1, LANES, slots.shape[0])
-    repeated = jnp.zeros(grouped[:, 0].shape, jnp.bool_)
-    for later in range(1, LANES):
-        for earlier in range(later):
-            repeated = repeated | (grouped[:, later] == grouped[:, earlier])
-    bits = 2 ** jnp.arange(grouped.shape[0], dtype=jnp.int32)
-    return jnp.sum(jnp.where(repeated, bits[:, None], 0), axis=0, keepdims=True)
 
 
 def slot_sums(slots, arrived, scale):
@@ -409,14 +395,14 @@
     return pl.pallas_call(
         slots_kernel,
         out_shape=(shape, shape),
-        in_specs=[ANY, SMEM, VMEM, SMEM],
+        in_specs=[ANY, VMEM, SMEM],
         out_specs=(VMEM, VMEM),
         scratch_shapes=[pltpu.VMEM(arrived.shape, jnp.float32)] * (1 + LANES)
         + [pltpu.SMEM((1, sources), jnp.int32)] * items
         + [pltpu.SemaphoreType.DMA((items,))],
         compiler_params=grant(44),
         name="slot_sums",
-    )(slots.T.reshape(items, 1, sources), group_repeats(slots), arrived, scale)
+    )(slots.T.reshape(items, 1, sources), arrived, scale)
 
 
 def unwarp_kernel(
@@ -518,6 +504,14 @@
     )(ident, scale, returned, warp_rows, warp_columns)
 
 
+def inner_strips(image_ref):
+    tile_rows = image_ref.shape[0]
+    return [
+        (0, BLOCK, [(image_ref, 0, WINDOW, 0)]),
+        (BLOCK, tile_rows - 2 * RIM - BLOCK, [(image_ref, BLOCK, tile_rows - BLOCK, 0)]),
+    ]
+
+
 def inner_kernel(
     coef_ref,
     image_hbm,
@@ -540,12 +534,12 @@
     for index in range(width // WIDE):
         fetch(index).start()
     load.start()
-    strips = [
-        (0, BLOCK, [(image_ref, 0, WINDOW, 0)]),
-        (BLOCK, inner - BLOCK, [(image_ref, BLOCK, tile_rows - BLOCK, 0)]),
-    ]
     step = functools.partial(
-        row_step, strips=strips, coef_ref=coef_ref, rows_ref=rows_ref, pass_ref=pass_ref
+        row_step,
+        strips=inner_strips(image_ref),
+        coef_ref=coef_ref,
+        rows_ref=rows_ref,
+        pass_ref=pass_ref,
     )
 
     def store(index):
@@ -624,8 +618,9 @@
             pltpu.make_async_copy(stage_ref.at[here], out_hbm.at[there], store_sems.at[index]),
         )
 
-    for index in range(2):
-        ends(index)[0].start()
+    fetches, stores = zip(*(ends(index) for index in range(2)))
+    for fetch in fetches:
+        fetch.start()
     strips = [
         (0, RIM, [(ref, 0, RIM, 0) for ref in (above_ref, top_ref, under_top_ref)]),
         (RIM, RIM, [(ref, 0, RIM, 0) for ref in (over_bottom_ref, bottom_ref, below_ref)]),
@@ -636,16 +631,17 @@
         row_step(
             WIDE, index * WIDE, BLOCK + index * WIDE, strips, coef_ref, rows_ref, pass_ref
         )
-    for index in range(2):
-        ends(index)[0].wait()
-    for index in range(width // WIDE):
-        for part, summed in enumerate(column_step(index, 2 * RIM, columns_ref, pass_ref)):
-            at = pl.ds(index * WIDE + part * CHUNK, CHUNK)
-            stage_ref[:, at] = exposure_ref[:, at].astype(jnp.float32) - summed
-    for index in range(2):
-        ends(index)[1].start()
-    for index in range(2):
-        ends(index)[1].wait()
+    for fetch in fetches:
+        fetch.wait()
+
+    def subtract(at, summed):
+        stage_ref[:, at] = exposure_ref[:, at].astype(jnp.float32) - summed
+
+    column_strip(2 * RIM, columns_ref, pass_ref, subtract)
+    for store in stores:
+        store.start()
+    for store in stores:
+        store.wait()
 
 
 def subtract_outer(coef, rims, exposure, rows, columns, partial):
@@ -673,29 +669,17 @@
     )(*operands)
 
 
-def patch_kernel(
-    scale_ref, owned_hbm, order_ref, out_hbm, owned_ref, wide_ref, stage_ref, fetch_sems, store_sems
-):
+def patch_kernel(scale_ref, owned_ref, order_ref, out_hbm, wide_ref, stage_ref, store_sems):
     del order_ref
     slots = SLOT_ROWS * SLOT_COLS
     pitch = slots + PAD
     myself = my_device()
-    lines = owned_ref.shape[0] // GROUPS
-
-    def fetch(group):
-        at = pl.ds(group * lines, lines)
-        return pltpu.make_async_copy(owned_hbm.at[at], owned_ref.at[at], fetch_sems.at[group])
-
-    for group in range(GROUPS):
-        fetch(group).start()
-    for group in range(GROUPS):
-        fetch(group).wait()
-
-        @pl.loop(group * BLOCK // GROUPS, (group + 1) * BLOCK // GROUPS, unroll=4)
-        def _(row):
-            to = pl.ds(pl.multiple_of(row * pitch, PAD), slots)
-            at = pl.ds(pl.multiple_of(row * slots, slots), slots)
-            wide_ref[to, :] = owned_ref[at, :].astype(jnp.float32)
+
+    @pl.loop(0, BLOCK, unroll=4)
+    def _(row):
+        to = pl.ds(pl.multiple_of(row * pitch, PAD), slots)
+        at = pl.ds(pl.multiple_of(row * slots, slots), slots)
+        wide_ref[to, :] = owned_ref[at, :].astype(jnp.float32)
 
     def store(down):
         at = pl.ds(pl.multiple_of(down * BLOCK, BLOCK), BLOCK)
@@ -721,16 +705,14 @@
     return pl.pallas_call(
         patch_kernel,
         out_shape=jax.ShapeDtypeStruct(shape, jnp.float32),
-        in_specs=[SMEM, HBM, VMEM],
+        in_specs=[SMEM, VMEM, VMEM],
         out_specs=HBM,
         scratch_shapes=[
-            pltpu.VMEM(owned.shape, jnp.bfloat16),
             pltpu.VMEM((owned.shape[0] + BLOCK * PAD, BLOCK), jnp.float32),
             pltpu.VMEM(shape, jnp.float32),
-            pltpu.SemaphoreType.DMA((GROUPS,)),
             pltpu.SemaphoreType.DMA((SLOT_ROWS,)),
         ],
-        compiler_params=grant(14),
+        compiler_params=grant(12),
         name="patch",
     )(scale, owned, order)
 

time: 163 us -> 162 us (level)
  transfers between devices with their start and end apart: 6 -> 6, of which waited for: 3 -> 3; matrix products, arithmetic and copies ran while one was open for 3% -> 2% of each run, Pallas kernels for 15% -> 14%
where the time goes in v7:
time: 162 us; the launch traced here: 161 us
  Pallas kernels  59.3 us (37%)
  blocking collectives  34.5 us (21%)
  waiting for transfers between devices  32.4 us (20%)
  starting transfers between devices  27.7 us (17%)
  local copies, waits for them, and re-layouts  3.01 us (2%)
  matrix products  2.66 us (2%)
    all_to_all x1, blocking collectives, exchange(): lax.all_to_all(shaped, ('exp', 'tile'), split_axis=0, concat_axis=0, tile...  34.5 us
    all_to_all x2, waiting for transfers between devices, exchange(): lax.all_to_all(shaped, ('exp', 'tile'), split_axis=0, concat_axis=0, tile...  25.4 us
    pallas_call x1, Pallas kernels, slot_sums(): pl.pallas_call(slots_kernel, out_shape=(shape, shape), in_specs=[ANY, VME...  18.7 us
    pallas_call x1, Pallas kernels, forward(): pl.pallas_call(forward_kernel, out_shape=jax.ShapeDtypeStruct((lines, BLO...  13.8 us
    all_to_all x2, starting transfers between devices, exchange(): lax.all_to_all(shaped, ('exp', 'tile'), split_axis=0, concat_axis=0, tile...  13.1 us
    ppermute x2, starting transfers between devices, swap_rims(): lax.ppermute(top, 'tile', backward)  9.31 us
    pallas_call x1, Pallas kernels, subtract_inner(): pl.pallas_call(inner_kernel, out_shape=jax.ShapeDtypeStruct((tile_rows, w...  8.85 us
    pallas_call x1, Pallas kernels, unwarp(): pl.pallas_call(unwarp_kernel, out_shape=(jax.ShapeDtypeStruct((tile_rows,...  8.63 us
  transfers between devices with their start and end apart: 6, of which 3 were waited for; matrix products, arithmetic and copies ran while one was open for 2% of the time, Pallas kernels for 14%

profile of v7, /device:TPU:8, one launch (start us, length us, event | category | flops | bytes accessed | tf_op | source)
XLA Modules:
  0.0 160.7 jit_solution(893013910719811779)
XLA Ops:
  0.6 1.0 slice_bitcast_fusion
  1.6 4.6 %collective-permute-start.1 = (bf16[16,4096]{1,0:T(8,128)(2,1)S(1)}, bf16[16,4096]{1,0:T(8,128)(2,1)S(1)}, u32[]{:S(2)}, u32[]{:S(2)}) collective-permute-start(bf16[16,4096]{1,0:T(8,128)(2,1)S(1)} %get-tuple-element.24), channel_id=1, source_target_pairs={{1,0},{2,1},{3,2},{4,3},{5,4},{6,5},{7,6},{8,7},{9,8},{10,9},{11,1... | collective-permute-start | bytes 393224 | tf_op jit(solution)/shard_map/ppermute | solution.py:81
  6.2 1.9 %collective-permute-start = (bf16[16,4096]{1,0:T(8,128)(2,1)S(1)}, bf16[16,4096]{1,0:T(8,128)(2,1)S(1)}, u32[]{:S(2)}, u32[]{:S(2)}) collective-permute-start(bf16[16,4096]{1,0:T(8,128)(2,1)S(1)} %get-tuple-element.25), channel_id=1, source_target_pairs={{0,1},{1,2},{2,3},{3,4},{4,5},{5,6},{6,7},{7,8},{8,9},{9,10},{10,1... | collective-permute-start | bytes 393224 | tf_op jit(solution)/shard_map/ppermute | solution.py:81
  8.1 2.5 %bands.1 = (bf16[384,160]{1,0:T(8,128)(2,1)}, bf16[1152,256]{1,0:T(8,128)(2,1)}) custom-call(bf16[3,21]{1,0:T(4,128)(2,1)} %row_taps_ref.1, bf16[3,21]{1,0:T(4,128)(2,1)} %column_taps_ref.1), custom_call_target="tpu_custom_call" | custom-call | tf_op jit(solution)/shard_map/bands/pallas_call | solution.py:64
  10.7 0.0 collective-permute-done.1.below_ref
  10.7 0.0 copy-start.12
  10.7 4.5 %collective-permute-done.above_ref = bf16[16,4096]{1,0:T(8,128)(2,1)S(1)} collective-permute-done((bf16[16,4096]{1,0:T(8,128)(2,1)S(1)}, bf16[16,4096]{1,0:T(8,128)(2,1)S(1)}, u32[]{:S(2)}, u32[]{:S(2)}) %collective-permute-start) | collective-permute-done | bytes 131104 | tf_op jit(solution)/shard_map/ppermute | solution.py:81
  15.2 0.0 copy-start.13
  15.2 0.0 copy-done.12
  15.2 0.7 copy-done.13
  15.8 13.8 %match_warp.1 = bf16[8192,128]{1,0:T(8,128)(2,1)} custom-call(s32[128,64]{1,0:T(8,128)} %bitcast.33, f32[8,16]{1,0:T(8,128)} %weight_ref.1, f32[1,3]{1,0:T(1,128)} %coef_ref.5, bf16[16,4096]{1,0:T(8,128)(2,1)} %copy-done.13, bf16[256,4096]{1,0:T(8,128)(2,1)} %bitcast.20, bf16[16,4096]{1,0:T(8,128)(2,1)} %copy-done.12, ...), custom_call_target="tpu_custom_call" | custom-call | tf_op jit(solution)/shard_map/match_warp/pallas_call | solution.py:320
  29.7 0.0 copy-start.14
  29.7 0.0 copy-start.10
  29.7 0.0 copy-start.11
  29.7 8.1 %all-to-all-start = ((bf16[128,64,128]{2,1,0:T(8,128)(2,1)}), bf16[128,64,128]{2,1,0:T(8,128)(2,1)S(1)}, u32[]{:S(2)}, u32[]{:S(2)}) async-start(bf16[128,64,128]{2,1,0:T(8,128)(2,1)} %bitcast.32), calls=%async_computation | async-start | bytes 4194304 | tf_op jit(solution)/shard_map/all_to_all | solution.py:722
  37.8 0.0 copy-done.14
  37.8 0.1 reshape.42
  37.9 0.0 copy-done.10
  37.9 0.1 eq.30
  38.0 0.0 copy-done.11
  38.0 0.1 eq.34
  38.0 0.1 broadcast_in_dim.25
  38.1 0.1 broadcast_in_dim.26
  38.2 2.7 %fusion.8.scale_ref = f32[128,64]{1,0:T(8,128)S(1)} fusion(f32[8192]{0:T(1024)S(1)} %broadcast_in_dim.26, s32[8192]{0:T(1024)S(1)} %eq.30, s32[8192]{0:T(1024)S(1)} %eq.34), kind=kOutput, calls=%fused_computation.9 | convolution fusion | flops 807944192 | bytes 131072 | tf_op jit(solution)/shard_map/dot_general | solution.py:770
  40.9 0.1 reshape.48
  41.0 0.1 copy.18
  41.1 0.8 gather_fusion
  41.8 0.0 copy-start.9
  41.9 25.4 %all-to-all-done = bf16[128,64,128]{2,1,0:T(8,128)(2,1)S(1)} async-done(((bf16[128,64,128]{2,1,0:T(8,128)(2,1)}), bf16[128,64,128]{2,1,0:T(8,128)(2,1)S(1)}, u32[]{:S(2)}, u32[]{:S(2)}) %all-to-all-start) | async-done | bytes 2097184 | tf_op jit(solution)/shard_map/all_to_all | solution.py:722
  67.3 18.7 %slot_sums.1 = (bf16[8192,128]{1,0:T(8,128)(2,1)S(1)}, bf16[8192,128]{1,0:T(8,128)(2,1)S(1)}) custom-call(s32[64,1,128]{2,1,0:T(1,128)S(1)} %bitcast.27, bf16[8192,128]{1,0:T(8,128)(2,1)S(1)} %bitcast.23, f32[1,64]{1,0:T(1,128)S(1)} %bitcast.28), custom_call_target="tpu_custom_call" | custom-call | tf_op jit(solution)/shard_map/slot_sums/pallas_call | solution.py:395
  86.0 0.0 copy-start.2
  86.0 34.5 %all_to_all.15 = bf16[128,64,128]{2,1,0:T(8,128)(2,1)} all-to-all(bf16[128,64,128]{2,1,0:T(8,128)(2,1)S(1)} %bitcast.26), channel_id=1, replica_groups=mesh['exp'=8,'tile'=16] {'exp','tile'}, dimensions={0} | all-to-all | bytes 4194304 | tf_op jit(solution)/shard_map/all_to_all | solution.py:722
  120.5 0.0 copy-done.9
  120.5 0.0 copy-done.2
  120.5 5.0 %all-to-all-start.1 = ((bf16[128,64,128]{2,1,0:T(8,128)(2,1)}), bf16[128,64,128]{2,1,0:T(8,128)(2,1)S(1)}, u32[]{:S(2)}, u32[]{:S(2)}) async-start(bf16[128,64,128]{2,1,0:T(8,128)(2,1)} %bitcast.25), calls=%async_computation.1 | async-start | bytes 4194304 | tf_op jit(solution)/shard_map/all_to_all | solution.py:722
  125.5 8.6 %unwarp.1 = (bf16[256,4096]{1,0:T(8,128)(2,1)}, bf16[16,4096]{1,0:T(8,128)(2,1)}, bf16[16,4096]{1,0:T(8,128)(2,1)}, bf16[16,4096]{1,0:T(8,128)(2,1)}, bf16[16,4096]{1,0:T(8,128)(2,1)}) custom-call(s32[128,64]{1,0:T(8,128)} %bitcast.34, f32[1,64]{1,0:T(1,128)} %bitcast.29, bf16[8192,128]{1,0:T(8,128)(2,1)} %bitcast.31, bf16[64,128,128]{2,1,0:T(8,128)(2,1)} %bank_rows_ref.3, ...), custom_call_target="tpu_custom_call" | custom-call | tf_op jit(solution)/shard_map/unwarp/pallas_call | solution.py:491
  134.1 3.4 %collective-permute-start.2 = (bf16[16,4096]{1,0:T(8,128)(2,1)}, bf16[16,4096]{1,0:T(8,128)(2,1)S(1)}, u32[]{:S(2)}, u32[]{:S(2)}) collective-permute-start(bf16[16,4096]{1,0:T(8,128)(2,1)} %get-tuple-element.17.bottom_ref), channel_id=1, source_target_pairs={{0,1},{1,2},{2,3},{3,4},{4,5},{5,6},{6,7},{7,8},{8,9},{9,10},{10,1... | collective-permute-start | bytes 393224 | tf_op jit(solution)/shard_map/ppermute | solution.py:81
  137.5 4.8 %collective-permute-start.3 = (bf16[16,4096]{1,0:T(8,128)(2,1)}, bf16[16,4096]{1,0:T(8,128)(2,1)S(1)}, u32[]{:S(2)}, u32[]{:S(2)}) collective-permute-start(bf16[16,4096]{1,0:T(8,128)(2,1)} %get-tuple-element.18.top_ref), channel_id=1, source_target_pairs={{1,0},{2,1},{3,2},{4,3},{5,4},{6,5},{7,6},{8,7},{9,8},{10,9},{11,1... | collective-permute-start | bytes 393224 | tf_op jit(solution)/shard_map/ppermute | solution.py:81
  142.3 0.0 copy-start
  142.3 0.0 copy-start.1
  142.3 0.0 copy-start.3
  142.3 0.0 copy-start.4
  142.3 0.0 copy-start.5
  142.3 0.0 copy-start.6
  142.3 0.0 copy-start.7
  142.3 0.0 copy-start.8
  142.3 8.8 %subtract_inner.1.partial_hbm = f32[256,4096]{1,0:T(8,128)} custom-call(f32[1,3]{1,0:T(1,128)} %coef_ref.5, bf16[256,4096]{1,0:T(8,128)(2,1)} %get-tuple-element.21.image_hbm, bf16[256,4096]{1,0:T(8,128)(2,1)} %bitcast.21, bf16[384,160]{1,0:T(8,128)(2,1)} %get-tuple-element.13.rows_ref, bf16[1152,256]{1,0:T(8,128)(2,1)} %get-tuple-element.14.columns_ref), custom_call_target="tpu_custom_call" | custom-call | tf_op jit(solution)/shard_map/subtract_inner/pallas_call | solution.py:568
  151.2 2.5 %collective-permute-done.2.above_ref = bf16[16,4096]{1,0:T(8,128)(2,1)S(1)} collective-permute-done((bf16[16,4096]{1,0:T(8,128)(2,1)}, bf16[16,4096]{1,0:T(8,128)(2,1)S(1)}, u32[]{:S(2)}, u32[]{:S(2)}) %collective-permute-start.2) | collective-permute-done | bytes 131104 | tf_op jit(solution)/shard_map/ppermute | solution.py:81
  153.7 0.0 collective-permute-done.3.below_ref
  153.7 0.0 copy-done
  153.7 0.0 copy-done.1
  153.7 0.0 copy-done.3
  153.7 0.0 copy-done.4
  153.8 0.0 copy-done.5
  153.8 0.0 copy-done.6
  153.8 0.0 copy-done.7
  153.8 0.0 copy-done.8
  153.8 2.6 %subtract_outer.1 = (f32[256,4096]{1,0:T(8,128)}, f32[8,128]{1,0:T(8,128)S(1)}) custom-call(f32[1,3]{1,0:T(1,128)S(1)} %copy-done.8, bf16[16,4096]{1,0:T(8,128)(2,1)S(1)} %collective-permute-done.2.above_ref, bf16[16,4096]{1,0:T(8,128)(2,1)S(1)} %copy-done.4, bf16[16,4096]{1,0:T(8,128)(2,1)S(1)} %copy-done.5, ...), custom_call_target="tpu_custom_call", output_to_operand_aliasing={{0}: (10, {})} | custom-call | tf_op jit(solution)/shard_map/subtract_outer/pallas_call | solution.py:651
  156.4 0.0 all-to-all-done.1
  156.4 4.2 %patch.1 = f32[1024,1024]{1,0:T(8,128)} custom-call(f32[128,64]{1,0:T(8,128)S(1)} %fusion.8.scale_ref, bf16[8192,128]{1,0:T(8,128)(2,1)S(1)} %bitcast.24, f32[8,128]{1,0:T(8,128)S(1)} %get-tuple-element.22.order_ref), custom_call_target="tpu_custom_call" | custom-call | tf_op jit(solution)/shard_map/patch/pallas_call | solution.py:705
  (3 shorter events, 0.0 us)
Async XLA Ops:
  1.6 9.0 %collective-permute-start.1 = (bf16[16,4096]{1,0:T(8,128)(2,1)S(1)}, bf16[16,4096]{1,0:T(8,128)(2,1)S(1)}, u32[]{:S(2)}, u32[]{:S(2)}) collective-permute-start(bf16[16,4096]{1,0:T(8,128)(2,1)S(1)} %get-tuple-element.24), channel_id=1, source_target_pairs={{1,0},{2,1},{3,2},{4,3},{5,4},{6,5},{7,6},{8,7},{9,8},{10,9},{11,1... | collective-permute-start | bytes 393224 | tf_op jit(solution)/shard_map/ppermute | solution.py:81
  6.2 9.0 %collective-permute-start = (bf16[16,4096]{1,0:T(8,128)(2,1)S(1)}, bf16[16,4096]{1,0:T(8,128)(2,1)S(1)}, u32[]{:S(2)}, u32[]{:S(2)}) collective-permute-start(bf16[16,4096]{1,0:T(8,128)(2,1)S(1)} %get-tuple-element.25), channel_id=1, source_target_pairs={{0,1},{1,2},{2,3},{3,4},{4,5},{5,6},{6,7},{7,8},{8,9},{9,10},{10,1... | collective-permute-start | bytes 393224 | tf_op jit(solution)/shard_map/ppermute | solution.py:81
  10.7 4.5 %copy-start.12 = (bf16[16,4096]{1,0:T(8,128)(2,1)}, bf16[16,4096]{1,0:T(8,128)(2,1)S(1)}, u32[]{:S(2)}) copy-start(bf16[16,4096]{1,0:T(8,128)(2,1)S(1)} %collective-permute-done.1.below_ref) | copy-start | bytes 393220
  15.2 0.7 copy-start.13
  29.7 8.2 %copy-start.14 = (f32[8,16]{1,0:T(8,128)S(1)}, f32[8,16]{1,0:T(8,128)}, u32[]{:S(2)}) copy-start(f32[8,16]{1,0:T(8,128)} %weight_ref.1) | copy-start | bytes 1540
  29.7 8.2 %copy-start.10 = (s32[8,16,64]{2,1,0:T(8,128)S(1)}, s32[8,16,64]{2,1,0:T(8,128)}, u32[]{:S(2)}) copy-start(s32[8,16,64]{2,1,0:T(8,128)} %param.17) | copy-start | bytes 98308
  29.7 8.3 %copy-start.11 = (s32[8,16,64]{2,1,0:T(8,128)S(1)}, s32[8,16,64]{2,1,0:T(8,128)}, u32[]{:S(2)}) copy-start(s32[8,16,64]{2,1,0:T(8,128)} %param.18) | copy-start | bytes 98308
  29.7 37.6 %all-to-all-start = ((bf16[128,64,128]{2,1,0:T(8,128)(2,1)}), bf16[128,64,128]{2,1,0:T(8,128)(2,1)S(1)}, u32[]{:S(2)}, u32[]{:S(2)}) async-start(bf16[128,64,128]{2,1,0:T(8,128)(2,1)} %bitcast.32), calls=%async_computation | async-start | bytes 4194304 | tf_op jit(solution)/shard_map/all_to_all | solution.py:722
  41.8 78.6 %copy-start.9 = (f32[64]{0:T(128)}, f32[64]{0:T(128)S(1)}, u32[]{:S(2)}) copy-start(f32[64]{0:T(128)S(1)} %gather_fusion) | copy-start | bytes 772
  86.0 34.5 %copy-start.2 = (bf16[8192,128]{1,0:T(8,128)(2,1)}, bf16[8192,128]{1,0:T(8,128)(2,1)S(1)}, u32[]{:S(2)}) copy-start(bf16[8192,128]{1,0:T(8,128)(2,1)S(1)} %get-tuple-element.15) | copy-start | bytes 6291460
  120.5 35.9 %all-to-all-start.1 = ((bf16[128,64,128]{2,1,0:T(8,128)(2,1)}), bf16[128,64,128]{2,1,0:T(8,128)(2,1)S(1)}, u32[]{:S(2)}, u32[]{:S(2)}) async-start(bf16[128,64,128]{2,1,0:T(8,128)(2,1)} %bitcast.25), calls=%async_computation.1 | async-start | bytes 4194304 | tf_op jit(solution)/shard_map/all_to_all | solution.py:722
  134.1 19.6 %collective-permute-start.2 = (bf16[16,4096]{1,0:T(8,128)(2,1)}, bf16[16,4096]{1,0:T(8,128)(2,1)S(1)}, u32[]{:S(2)}, u32[]{:S(2)}) collective-permute-start(bf16[16,4096]{1,0:T(8,128)(2,1)} %get-tuple-element.17.bottom_ref), channel_id=1, source_target_pairs={{0,1},{1,2},{2,3},{3,4},{4,5},{5,6},{6,7},{7,8},{8,9},{9,10},{10,1... | collective-permute-start | bytes 393224 | tf_op jit(solution)/shard_map/ppermute | solution.py:81
  137.5 16.2 %collective-permute-start.3 = (bf16[16,4096]{1,0:T(8,128)(2,1)}, bf16[16,4096]{1,0:T(8,128)(2,1)S(1)}, u32[]{:S(2)}, u32[]{:S(2)}) collective-permute-start(bf16[16,4096]{1,0:T(8,128)(2,1)} %get-tuple-element.18.top_ref), channel_id=1, source_target_pairs={{1,0},{2,1},{3,2},{4,3},{5,4},{6,5},{7,6},{8,7},{9,8},{10,9},{11,1... | collective-permute-start | bytes 393224 | tf_op jit(solution)/shard_map/ppermute | solution.py:81
  142.3 11.5 %copy-start = (bf16[1,256,4096]{2,1,0:T(8,128)(2,1)S(1)}, bf16[1,256,4096]{2,1,0:T(8,128)(2,1)}, u32[]{:S(2)}) copy-start(bf16[1,256,4096]{2,1,0:T(8,128)(2,1)} %param.10) | copy-start | bytes 6291460
  142.3 11.5 %copy-start.1 = (bf16[1152,256]{1,0:T(8,128)(2,1)S(1)}, bf16[1152,256]{1,0:T(8,128)(2,1)}, u32[]{:S(2)}) copy-start(bf16[1152,256]{1,0:T(8,128)(2,1)} %get-tuple-element.14.columns_ref) | copy-start | bytes 1769476
  142.3 11.5 %copy-start.3 = (bf16[384,160]{1,0:T(8,128)(2,1)S(1)}, bf16[384,160]{1,0:T(8,128)(2,1)}, u32[]{:S(2)}) copy-start(bf16[384,160]{1,0:T(8,128)(2,1)} %get-tuple-element.13.rows_ref) | copy-start | bytes 368644
  142.3 11.5 %copy-start.4 = (bf16[16,4096]{1,0:T(8,128)(2,1)S(1)}, bf16[16,4096]{1,0:T(8,128)(2,1)}, u32[]{:S(2)}) copy-start(bf16[16,4096]{1,0:T(8,128)(2,1)} %get-tuple-element.18.top_ref) | copy-start | bytes 393220
  142.3 11.5 %copy-start.5 = (bf16[16,4096]{1,0:T(8,128)(2,1)S(1)}, bf16[16,4096]{1,0:T(8,128)(2,1)}, u32[]{:S(2)}) copy-start(bf16[16,4096]{1,0:T(8,128)(2,1)} %get-tuple-element.19.under_top_ref) | copy-start | bytes 393220
  142.3 11.5 %copy-start.6 = (bf16[16,4096]{1,0:T(8,128)(2,1)S(1)}, bf16[16,4096]{1,0:T(8,128)(2,1)}, u32[]{:S(2)}) copy-start(bf16[16,4096]{1,0:T(8,128)(2,1)} %get-tuple-element.20.over_bottom_ref) | copy-start | bytes 393220
  142.3 11.5 %copy-start.7 = (bf16[16,4096]{1,0:T(8,128)(2,1)S(1)}, bf16[16,4096]{1,0:T(8,128)(2,1)}, u32[]{:S(2)}) copy-start(bf16[16,4096]{1,0:T(8,128)(2,1)} %get-tuple-element.17.bottom_ref) | copy-start | bytes 393220
  142.3 11.5 %copy-start.8 = (f32[1,3]{1,0:T(1,128)S(1)}, f32[1,3]{1,0:T(1,128)}, u32[]{:S(2)}) copy-start(f32[1,3]{1,0:T(1,128)} %coef_ref.5) | copy-start | bytes 40

commit v8 on v7

--- a/solution.py
+++ b/solution.py
@@ -370,7 +370,7 @@
             for slot, sum_ref, value in zip(slots, sums, values):
                 sum_ref[pl.ds(slot, 1), :] = value
 
-    @pl.loop(0, sources)
+    @pl.loop(0, sources, unroll=2)
     def _(source):
         value = sums[0][at(source), :]
         for sum_ref in sums[1:]:
@@ -384,7 +384,7 @@
             slot = tables[item][0, source]
             wide_ref[pl.ds(source * items + item, 1), :] = sums[0][pl.ds(slot, 1), :]
 
-    @pl.loop(0, sources)
+    @pl.loop(0, sources, unroll=4)
     def _(source):
         template_ref[at(source), :] = wide_ref[at(source), :].astype(jnp.bfloat16)
 

time: 162 us -> 161 us (level)
  transfers between devices with their start and end apart: 6 -> 6, of which waited for: 3 -> 3; matrix products, arithmetic and copies ran while one was open for 2% -> 3% of each run, Pallas kernels for 14% -> 14%
where the time goes in v8:
time: 161 us; the launch traced here: 160 us
  Pallas kernels  58.3 us (36%)
  blocking collectives  34.5 us (21%)
  waiting for transfers between devices  32.4 us (20%)
  starting transfers between devices  27.7 us (17%)
  local copies, waits for them, and re-layouts  3.01 us (2%)
  matrix products  2.66 us (2%)
    all_to_all x1, blocking collectives, exchange(): lax.all_to_all(shaped, ('exp', 'tile'), split_axis=0, concat_axis=0, tile...  34.5 us
    all_to_all x2, waiting for transfers between devices, exchange(): lax.all_to_all(shaped, ('exp', 'tile'), split_axis=0, concat_axis=0, tile...  25.4 us
    pallas_call x1, Pallas kernels, slot_sums(): pl.pallas_call(slots_kernel, out_shape=(shape, shape), in_specs=[ANY, VME...  17.7 us
    pallas_call x1, Pallas kernels, forward(): pl.pallas_call(forward_kernel, out_shape=jax.ShapeDtypeStruct((lines, BLO...  13.8 us
    all_to_all x2, starting transfers between devices, exchange(): lax.all_to_all(shaped, ('exp', 'tile'), split_axis=0, concat_axis=0, tile...  13.1 us
    ppermute x2, starting transfers between devices, swap_rims(): lax.ppermute(top, 'tile', backward)  9.31 us
    pallas_call x1, Pallas kernels, subtract_inner(): pl.pallas_call(inner_kernel, out_shape=jax.ShapeDtypeStruct((tile_rows, w...  8.85 us
    pallas_call x1, Pallas kernels, unwarp(): pl.pallas_call(unwarp_kernel, out_shape=(jax.ShapeDtypeStruct((tile_rows,...  8.63 us
  transfers between devices with their start and end apart: 6, of which 3 were waited for; matrix products, arithmetic and copies ran while one was open for 3% of the time, Pallas kernels for 14%

profile of v8, /device:TPU:8, one launch (start us, length us, event | category | flops | bytes accessed | tf_op | source)
XLA Modules:
  0.0 159.7 jit_solution(7189222081638467780)
XLA Ops:
  0.6 1.0 slice_bitcast_fusion
  1.6 4.6 %collective-permute-start.1 = (bf16[16,4096]{1,0:T(8,128)(2,1)S(1)}, bf16[16,4096]{1,0:T(8,128)(2,1)S(1)}, u32[]{:S(2)}, u32[]{:S(2)}) collective-permute-start(bf16[16,4096]{1,0:T(8,128)(2,1)S(1)} %get-tuple-element.24), channel_id=1, source_target_pairs={{1,0},{2,1},{3,2},{4,3},{5,4},{6,5},{7,6},{8,7},{9,8},{10,9},{11,1... | collective-permute-start | bytes 393224 | tf_op jit(solution)/shard_map/ppermute | solution.py:81
  6.2 1.9 %collective-permute-start = (bf16[16,4096]{1,0:T(8,128)(2,1)S(1)}, bf16[16,4096]{1,0:T(8,128)(2,1)S(1)}, u32[]{:S(2)}, u32[]{:S(2)}) collective-permute-start(bf16[16,4096]{1,0:T(8,128)(2,1)S(1)} %get-tuple-element.25), channel_id=1, source_target_pairs={{0,1},{1,2},{2,3},{3,4},{4,5},{5,6},{6,7},{7,8},{8,9},{9,10},{10,1... | collective-permute-start | bytes 393224 | tf_op jit(solution)/shard_map/ppermute | solution.py:81
  8.1 2.5 %bands.1 = (bf16[384,160]{1,0:T(8,128)(2,1)}, bf16[1152,256]{1,0:T(8,128)(2,1)}) custom-call(bf16[3,21]{1,0:T(4,128)(2,1)} %row_taps_ref.1, bf16[3,21]{1,0:T(4,128)(2,1)} %column_taps_ref.1), custom_call_target="tpu_custom_call" | custom-call | tf_op jit(solution)/shard_map/bands/pallas_call | solution.py:64
  10.7 0.0 collective-permute-done.1.below_ref
  10.7 0.0 copy-start.12
  10.7 4.5 %collective-permute-done.above_ref = bf16[16,4096]{1,0:T(8,128)(2,1)S(1)} collective-permute-done((bf16[16,4096]{1,0:T(8,128)(2,1)S(1)}, bf16[16,4096]{1,0:T(8,128)(2,1)S(1)}, u32[]{:S(2)}, u32[]{:S(2)}) %collective-permute-start) | collective-permute-done | bytes 131104 | tf_op jit(solution)/shard_map/ppermute | solution.py:81
  15.2 0.0 copy-start.13
  15.2 0.0 copy-done.12
  15.2 0.7 copy-done.13
  15.8 13.8 %match_warp.1 = bf16[8192,128]{1,0:T(8,128)(2,1)} custom-call(s32[128,64]{1,0:T(8,128)} %bitcast.33, f32[8,16]{1,0:T(8,128)} %weight_ref.1, f32[1,3]{1,0:T(1,128)} %coef_ref.5, bf16[16,4096]{1,0:T(8,128)(2,1)} %copy-done.13, bf16[256,4096]{1,0:T(8,128)(2,1)} %bitcast.20, bf16[16,4096]{1,0:T(8,128)(2,1)} %copy-done.12, ...), custom_call_target="tpu_custom_call" | custom-call | tf_op jit(solution)/shard_map/match_warp/pallas_call | solution.py:320
  29.7 0.0 copy-start.14
  29.7 0.0 copy-start.10
  29.7 0.0 copy-start.11
  29.7 8.1 %all-to-all-start = ((bf16[128,64,128]{2,1,0:T(8,128)(2,1)}), bf16[128,64,128]{2,1,0:T(8,128)(2,1)S(1)}, u32[]{:S(2)}, u32[]{:S(2)}) async-start(bf16[128,64,128]{2,1,0:T(8,128)(2,1)} %bitcast.32), calls=%async_computation | async-start | bytes 4194304 | tf_op jit(solution)/shard_map/all_to_all | solution.py:722
  37.8 0.0 copy-done.14
  37.8 0.1 reshape.42
  37.9 0.0 copy-done.10
  37.9 0.1 eq.30
  38.0 0.0 copy-done.11
  38.0 0.1 eq.34
  38.0 0.1 broadcast_in_dim.25
  38.1 0.1 broadcast_in_dim.26
  38.2 2.7 %fusion.8.scale_ref = f32[128,64]{1,0:T(8,128)S(1)} fusion(f32[8192]{0:T(1024)S(1)} %broadcast_in_dim.26, s32[8192]{0:T(1024)S(1)} %eq.30, s32[8192]{0:T(1024)S(1)} %eq.34), kind=kOutput, calls=%fused_computation.9 | convolution fusion | flops 807944192 | bytes 131072 | tf_op jit(solution)/shard_map/dot_general | solution.py:770
  40.9 0.1 reshape.48
  41.0 0.1 copy.18
  41.1 0.8 gather_fusion
  41.8 0.0 copy-start.9
  41.9 25.4 %all-to-all-done = bf16[128,64,128]{2,1,0:T(8,128)(2,1)S(1)} async-done(((bf16[128,64,128]{2,1,0:T(8,128)(2,1)}), bf16[128,64,128]{2,1,0:T(8,128)(2,1)S(1)}, u32[]{:S(2)}, u32[]{:S(2)}) %all-to-all-start) | async-done | bytes 2097184 | tf_op jit(solution)/shard_map/all_to_all | solution.py:722
  67.3 17.7 %slot_sums.1 = (bf16[8192,128]{1,0:T(8,128)(2,1)S(1)}, bf16[8192,128]{1,0:T(8,128)(2,1)S(1)}) custom-call(s32[64,1,128]{2,1,0:T(1,128)S(1)} %bitcast.27, bf16[8192,128]{1,0:T(8,128)(2,1)S(1)} %bitcast.23, f32[1,64]{1,0:T(1,128)S(1)} %bitcast.28), custom_call_target="tpu_custom_call" | custom-call | tf_op jit(solution)/shard_map/slot_sums/pallas_call | solution.py:395
  85.0 0.0 copy-start.2
  85.0 34.5 %all_to_all.15 = bf16[128,64,128]{2,1,0:T(8,128)(2,1)} all-to-all(bf16[128,64,128]{2,1,0:T(8,128)(2,1)S(1)} %bitcast.26), channel_id=1, replica_groups=mesh['exp'=8,'tile'=16] {'exp','tile'}, dimensions={0} | all-to-all | bytes 4194304 | tf_op jit(solution)/shard_map/all_to_all | solution.py:722
  119.5 0.0 copy-done.9
  119.5 0.0 copy-done.2
  119.5 5.0 %all-to-all-start.1 = ((bf16[128,64,128]{2,1,0:T(8,128)(2,1)}), bf16[128,64,128]{2,1,0:T(8,128)(2,1)S(1)}, u32[]{:S(2)}, u32[]{:S(2)}) async-start(bf16[128,64,128]{2,1,0:T(8,128)(2,1)} %bitcast.25), calls=%async_computation.1 | async-start | bytes 4194304 | tf_op jit(solution)/shard_map/all_to_all | solution.py:722
  124.5 8.6 %unwarp.1 = (bf16[256,4096]{1,0:T(8,128)(2,1)}, bf16[16,4096]{1,0:T(8,128)(2,1)}, bf16[16,4096]{1,0:T(8,128)(2,1)}, bf16[16,4096]{1,0:T(8,128)(2,1)}, bf16[16,4096]{1,0:T(8,128)(2,1)}) custom-call(s32[128,64]{1,0:T(8,128)} %bitcast.34, f32[1,64]{1,0:T(1,128)} %bitcast.29, bf16[8192,128]{1,0:T(8,128)(2,1)} %bitcast.31, bf16[64,128,128]{2,1,0:T(8,128)(2,1)} %bank_rows_ref.3, ...), custom_call_target="tpu_custom_call" | custom-call | tf_op jit(solution)/shard_map/unwarp/pallas_call | solution.py:491
  133.1 3.4 %collective-permute-start.2 = (bf16[16,4096]{1,0:T(8,128)(2,1)}, bf16[16,4096]{1,0:T(8,128)(2,1)S(1)}, u32[]{:S(2)}, u32[]{:S(2)}) collective-permute-start(bf16[16,4096]{1,0:T(8,128)(2,1)} %get-tuple-element.17.bottom_ref), channel_id=1, source_target_pairs={{0,1},{1,2},{2,3},{3,4},{4,5},{5,6},{6,7},{7,8},{8,9},{9,10},{10,1... | collective-permute-start | bytes 393224 | tf_op jit(solution)/shard_map/ppermute | solution.py:81
  136.5 4.8 %collective-permute-start.3 = (bf16[16,4096]{1,0:T(8,128)(2,1)}, bf16[16,4096]{1,0:T(8,128)(2,1)S(1)}, u32[]{:S(2)}, u32[]{:S(2)}) collective-permute-start(bf16[16,4096]{1,0:T(8,128)(2,1)} %get-tuple-element.18.top_ref), channel_id=1, source_target_pairs={{1,0},{2,1},{3,2},{4,3},{5,4},{6,5},{7,6},{8,7},{9,8},{10,9},{11,1... | collective-permute-start | bytes 393224 | tf_op jit(solution)/shard_map/ppermute | solution.py:81
  141.3 0.0 copy-start
  141.3 0.0 copy-start.1
  141.3 0.0 copy-start.3
  141.3 0.0 copy-start.4
  141.3 0.0 copy-start.5
  141.3 0.0 copy-start.6
  141.3 0.0 copy-start.7
  141.3 0.0 copy-start.8
  141.3 8.8 %subtract_inner.1.partial_hbm = f32[256,4096]{1,0:T(8,128)} custom-call(f32[1,3]{1,0:T(1,128)} %coef_ref.5, bf16[256,4096]{1,0:T(8,128)(2,1)} %get-tuple-element.21.image_hbm, bf16[256,4096]{1,0:T(8,128)(2,1)} %bitcast.21, bf16[384,160]{1,0:T(8,128)(2,1)} %get-tuple-element.13.rows_ref, bf16[1152,256]{1,0:T(8,128)(2,1)} %get-tuple-element.14.columns_ref), custom_call_target="tpu_custom_call" | custom-call | tf_op jit(solution)/shard_map/subtract_inner/pallas_call | solution.py:568
  150.2 2.5 %collective-permute-done.2.above_ref = bf16[16,4096]{1,0:T(8,128)(2,1)S(1)} collective-permute-done((bf16[16,4096]{1,0:T(8,128)(2,1)}, bf16[16,4096]{1,0:T(8,128)(2,1)S(1)}, u32[]{:S(2)}, u32[]{:S(2)}) %collective-permute-start.2) | collective-permute-done | bytes 131104 | tf_op jit(solution)/shard_map/ppermute | solution.py:81
  152.7 0.0 collective-permute-done.3.below_ref
  152.7 0.0 copy-done
  152.7 0.0 copy-done.1
  152.7 0.0 copy-done.3
  152.8 0.0 copy-done.4
  152.8 0.0 copy-done.5
  152.8 0.0 copy-done.6
  152.8 0.0 copy-done.7
  152.8 0.0 copy-done.8
  152.8 2.6 %subtract_outer.1 = (f32[256,4096]{1,0:T(8,128)}, f32[8,128]{1,0:T(8,128)S(1)}) custom-call(f32[1,3]{1,0:T(1,128)S(1)} %copy-done.8, bf16[16,4096]{1,0:T(8,128)(2,1)S(1)} %collective-permute-done.2.above_ref, bf16[16,4096]{1,0:T(8,128)(2,1)S(1)} %copy-done.4, bf16[16,4096]{1,0:T(8,128)(2,1)S(1)} %copy-done.5, ...), custom_call_target="tpu_custom_call", output_to_operand_aliasing={{0}: (10, {})} | custom-call | tf_op jit(solution)/shard_map/subtract_outer/pallas_call | solution.py:651
  155.4 0.0 all-to-all-done.1
  155.4 4.2 %patch.1 = f32[1024,1024]{1,0:T(8,128)} custom-call(f32[128,64]{1,0:T(8,128)S(1)} %fusion.8.scale_ref, bf16[8192,128]{1,0:T(8,128)(2,1)S(1)} %bitcast.24, f32[8,128]{1,0:T(8,128)S(1)} %get-tuple-element.22.order_ref), custom_call_target="tpu_custom_call" | custom-call | tf_op jit(solution)/shard_map/patch/pallas_call | solution.py:705
  (3 shorter events, 0.0 us)
Async XLA Ops:
  1.6 9.0 %collective-permute-start.1 = (bf16[16,4096]{1,0:T(8,128)(2,1)S(1)}, bf16[16,4096]{1,0:T(8,128)(2,1)S(1)}, u32[]{:S(2)}, u32[]{:S(2)}) collective-permute-start(bf16[16,4096]{1,0:T(8,128)(2,1)S(1)} %get-tuple-element.24), channel_id=1, source_target_pairs={{1,0},{2,1},{3,2},{4,3},{5,4},{6,5},{7,6},{8,7},{9,8},{10,9},{11,1... | collective-permute-start | bytes 393224 | tf_op jit(solution)/shard_map/ppermute | solution.py:81
  6.2 9.0 %collective-permute-start = (bf16[16,4096]{1,0:T(8,128)(2,1)S(1)}, bf16[16,4096]{1,0:T(8,128)(2,1)S(1)}, u32[]{:S(2)}, u32[]{:S(2)}) collective-permute-start(bf16[16,4096]{1,0:T(8,128)(2,1)S(1)} %get-tuple-element.25), channel_id=1, source_target_pairs={{0,1},{1,2},{2,3},{3,4},{4,5},{5,6},{6,7},{7,8},{8,9},{9,10},{10,1... | collective-permute-start | bytes 393224 | tf_op jit(solution)/shard_map/ppermute | solution.py:81
  10.7 4.5 %copy-start.12 = (bf16[16,4096]{1,0:T(8,128)(2,1)}, bf16[16,4096]{1,0:T(8,128)(2,1)S(1)}, u32[]{:S(2)}) copy-start(bf16[16,4096]{1,0:T(8,128)(2,1)S(1)} %collective-permute-done.1.below_ref) | copy-start | bytes 393220
  15.2 0.7 copy-start.13
  29.7 8.2 %copy-start.14 = (f32[8,16]{1,0:T(8,128)S(1)}, f32[8,16]{1,0:T(8,128)}, u32[]{:S(2)}) copy-start(f32[8,16]{1,0:T(8,128)} %weight_ref.1) | copy-start | bytes 1540
  29.7 8.2 %copy-start.10 = (s32[8,16,64]{2,1,0:T(8,128)S(1)}, s32[8,16,64]{2,1,0:T(8,128)}, u32[]{:S(2)}) copy-start(s32[8,16,64]{2,1,0:T(8,128)} %param.17) | copy-start | bytes 98308
  29.7 8.3 %copy-start.11 = (s32[8,16,64]{2,1,0:T(8,128)S(1)}, s32[8,16,64]{2,1,0:T(8,128)}, u32[]{:S(2)}) copy-start(s32[8,16,64]{2,1,0:T(8,128)} %param.18) | copy-start | bytes 98308
  29.7 37.6 %all-to-all-start = ((bf16[128,64,128]{2,1,0:T(8,128)(2,1)}), bf16[128,64,128]{2,1,0:T(8,128)(2,1)S(1)}, u32[]{:S(2)}, u32[]{:S(2)}) async-start(bf16[128,64,128]{2,1,0:T(8,128)(2,1)} %bitcast.32), calls=%async_computation | async-start | bytes 4194304 | tf_op jit(solution)/shard_map/all_to_all | solution.py:722
  41.8 77.6 %copy-start.9 = (f32[64]{0:T(128)}, f32[64]{0:T(128)S(1)}, u32[]{:S(2)}) copy-start(f32[64]{0:T(128)S(1)} %gather_fusion) | copy-start | bytes 772
  85.0 34.5 %copy-start.2 = (bf16[8192,128]{1,0:T(8,128)(2,1)}, bf16[8192,128]{1,0:T(8,128)(2,1)S(1)}, u32[]{:S(2)}) copy-start(bf16[8192,128]{1,0:T(8,128)(2,1)S(1)} %get-tuple-element.15) | copy-start | bytes 6291460
  119.5 35.9 %all-to-all-start.1 = ((bf16[128,64,128]{2,1,0:T(8,128)(2,1)}), bf16[128,64,128]{2,1,0:T(8,128)(2,1)S(1)}, u32[]{:S(2)}, u32[]{:S(2)}) async-start(bf16[128,64,128]{2,1,0:T(8,128)(2,1)} %bitcast.25), calls=%async_computation.1 | async-start | bytes 4194304 | tf_op jit(solution)/shard_map/all_to_all | solution.py:722
  133.1 19.6 %collective-permute-start.2 = (bf16[16,4096]{1,0:T(8,128)(2,1)}, bf16[16,4096]{1,0:T(8,128)(2,1)S(1)}, u32[]{:S(2)}, u32[]{:S(2)}) collective-permute-start(bf16[16,4096]{1,0:T(8,128)(2,1)} %get-tuple-element.17.bottom_ref), channel_id=1, source_target_pairs={{0,1},{1,2},{2,3},{3,4},{4,5},{5,6},{6,7},{7,8},{8,9},{9,10},{10,1... | collective-permute-start | bytes 393224 | tf_op jit(solution)/shard_map/ppermute | solution.py:81
  136.5 16.2 %collective-permute-start.3 = (bf16[16,4096]{1,0:T(8,128)(2,1)}, bf16[16,4096]{1,0:T(8,128)(2,1)S(1)}, u32[]{:S(2)}, u32[]{:S(2)}) collective-permute-start(bf16[16,4096]{1,0:T(8,128)(2,1)} %get-tuple-element.18.top_ref), channel_id=1, source_target_pairs={{1,0},{2,1},{3,2},{4,3},{5,4},{6,5},{7,6},{8,7},{9,8},{10,9},{11,1... | collective-permute-start | bytes 393224 | tf_op jit(solution)/shard_map/ppermute | solution.py:81
  141.3 11.5 %copy-start = (bf16[1,256,4096]{2,1,0:T(8,128)(2,1)S(1)}, bf16[1,256,4096]{2,1,0:T(8,128)(2,1)}, u32[]{:S(2)}) copy-start(bf16[1,256,4096]{2,1,0:T(8,128)(2,1)} %param.10) | copy-start | bytes 6291460
  141.3 11.5 %copy-start.1 = (bf16[1152,256]{1,0:T(8,128)(2,1)S(1)}, bf16[1152,256]{1,0:T(8,128)(2,1)}, u32[]{:S(2)}) copy-start(bf16[1152,256]{1,0:T(8,128)(2,1)} %get-tuple-element.14.columns_ref) | copy-start | bytes 1769476
  141.3 11.5 %copy-start.3 = (bf16[384,160]{1,0:T(8,128)(2,1)S(1)}, bf16[384,160]{1,0:T(8,128)(2,1)}, u32[]{:S(2)}) copy-start(bf16[384,160]{1,0:T(8,128)(2,1)} %get-tuple-element.13.rows_ref) | copy-start | bytes 368644
  141.3 11.5 %copy-start.4 = (bf16[16,4096]{1,0:T(8,128)(2,1)S(1)}, bf16[16,4096]{1,0:T(8,128)(2,1)}, u32[]{:S(2)}) copy-start(bf16[16,4096]{1,0:T(8,128)(2,1)} %get-tuple-element.18.top_ref) | copy-start | bytes 393220
  141.3 11.5 %copy-start.5 = (bf16[16,4096]{1,0:T(8,128)(2,1)S(1)}, bf16[16,4096]{1,0:T(8,128)(2,1)}, u32[]{:S(2)}) copy-start(bf16[16,4096]{1,0:T(8,128)(2,1)} %get-tuple-element.19.under_top_ref) | copy-start | bytes 393220
  141.3 11.5 %copy-start.6 = (bf16[16,4096]{1,0:T(8,128)(2,1)S(1)}, bf16[16,4096]{1,0:T(8,128)(2,1)}, u32[]{:S(2)}) copy-start(bf16[16,4096]{1,0:T(8,128)(2,1)} %get-tuple-element.20.over_bottom_ref) | copy-start | bytes 393220
  141.3 11.5 %copy-start.7 = (bf16[16,4096]{1,0:T(8,128)(2,1)S(1)}, bf16[16,4096]{1,0:T(8,128)(2,1)}, u32[]{:S(2)}) copy-start(bf16[16,4096]{1,0:T(8,128)(2,1)} %get-tuple-element.17.bottom_ref) | copy-start | bytes 393220
  141.3 11.5 %copy-start.8 = (f32[1,3]{1,0:T(1,128)S(1)}, f32[1,3]{1,0:T(1,128)}, u32[]{:S(2)}) copy-start(f32[1,3]{1,0:T(1,128)} %coef_ref.5) | copy-start | bytes 40

commit v9 on v8

--- a/solution.py
+++ b/solution.py
@@ -17,6 +17,7 @@
 SLOT_ROWS = 8
 SLOT_COLS = 8
 LANES = 8
+SUMS = 2
 PAD = 8
 VMEM = pl.BlockSpec(memory_space=pltpu.VMEM)
 SMEM = pl.BlockSpec(memory_space=pltpu.SMEM)
@@ -339,10 +340,12 @@
     )(ident, weight, coef, above, image, below, rows, columns, warp_rows, warp_columns)
 
 
-def slots_kernel(slot_hbm, arrived_ref, scale_ref, template_ref, coadd_ref, wide_ref, *refs):
+def slots_kernel(
+    slot_hbm, repeat_ref, arrived_ref, scale_ref, template_ref, coadd_ref, wide_ref, *refs
+):
     del scale_ref
     items, _, sources = slot_hbm.shape
-    sums, tables, sems = refs[:LANES], refs[LANES : LANES + items], refs[LANES + items]
+    sums, tables, sems = refs[:SUMS], refs[SUMS : SUMS + items], refs[SUMS + items]
     loads = [pltpu.make_async_copy(slot_hbm.at[k], tables[k], sems.at[k]) for k in range(items)]
     for load in loads:
         load.start()
@@ -350,7 +353,7 @@
     def at(source):
         return pl.ds(pl.multiple_of(source * items, items), items)
 
-    @pl.loop(0, sources)
+    @pl.loop(0, sources, unroll=2)
     def _(source):
         wide_ref[at(source), :] = arrived_ref[at(source), :].astype(jnp.float32)
         for sum_ref in sums:
@@ -359,16 +362,39 @@
     for load in loads:
         load.wait()
 
+    def add(source, blocks, sum_ref):
+        slots = [tables[block][0, source] for block in blocks]
+        values = [
+            sum_ref[pl.ds(slot, 1), :] + wide_ref[pl.ds(source * items + block, 1), :]
+            for slot, block in zip(slots, blocks)
+        ]
+        for slot, value in zip(slots, values):
+            sum_ref[pl.ds(slot, 1), :] = value
+
+    groups = [list(range(first, first + LANES)) for first in range(0, items, LANES)]
+
     @pl.loop(0, sources)
     def _(source):
-        for first in range(0, items, LANES):
-            slots = [tables[first + lane][0, source] for lane in range(LANES)]
-            values = [
-                sum_ref[pl.ds(slot, 1), :] + wide_ref[pl.ds(source * items + first + lane, 1), :]
-                for lane, (slot, sum_ref) in enumerate(zip(slots, sums))
-            ]
-            for slot, sum_ref, value in zip(slots, sums, values):
-                sum_ref[pl.ds(slot, 1), :] = value
+        repeats = repeat_ref[0, source]
+
+        @pl.when(repeats == 0)
+        def _():
+            for index, blocks in enumerate(groups):
+                add(source, blocks, sums[index % SUMS])
+
+        @pl.when(repeats != 0)
+        def _():
+            for index, blocks in enumerate(groups):
+                repeated = (repeats // 2**index) % 2
+
+                @pl.when(repeated == 0)
+                def _():
+                    add(source, blocks, sums[index % SUMS])
+
+                @pl.when(repeated != 0)
+                def _():
+                    for lane, block in enumerate(blocks):
+                        add(source, [block], sums[lane % SUMS])
 
     @pl.loop(0, sources, unroll=2)
     def _(source):
@@ -389,20 +415,30 @@
         template_ref[at(source), :] = wide_ref[at(source), :].astype(jnp.bfloat16)
 
 
+def group_repeats(slots):
+    grouped = slots.T.reshape(-1, LANES, slots.shape[0])
+    repeated = jnp.zeros(grouped[:, 0].shape, jnp.bool_)
+    for later in range(1, LANES):
+        for earlier in range(later):
+            repeated = repeated | (grouped[:, later] == grouped[:, earlier])
+    bits = 2 ** jnp.arange(grouped.shape[0], dtype=jnp.int32)
+    return jnp.sum(jnp.where(repeated, bits[:, None], 0), axis=0, keepdims=True)
+
+
 def slot_sums(slots, arrived, scale):
     shape = jax.ShapeDtypeStruct(arrived.shape, jnp.bfloat16)
     sources, items = slots.shape
     return pl.pallas_call(
         slots_kernel,
         out_shape=(shape, shape),
-        in_specs=[ANY, VMEM, SMEM],
+        in_specs=[ANY, SMEM, VMEM, SMEM],
         out_specs=(VMEM, VMEM),
-        scratch_shapes=[pltpu.VMEM(arrived.shape, jnp.float32)] * (1 + LANES)
+        scratch_shapes=[pltpu.VMEM(arrived.shape, jnp.float32)] * (1 + SUMS)
         + [pltpu.SMEM((1, sources), jnp.int32)] * items
         + [pltpu.SemaphoreType.DMA((items,))],
-        compiler_params=grant(44),
+        compiler_params=grant(28),
         name="slot_sums",
-    )(slots.T.reshape(items, 1, sources), arrived, scale)
+    )(slots.T.reshape(items, 1, sources), group_repeats(slots), arrived, scale)
 
 
 def unwarp_kernel(

time: 161 us -> 161 us (level)
  no operation moved by 1% of the time
where the time goes in v9:
time: 161 us; the launch traced here: 160 us
  Pallas kernels  58.7 us (36%)
  blocking collectives  34.5 us (21%)
  waiting for transfers between devices  32.2 us (20%)
  starting transfers between devices  27.7 us (17%)
  local copies, waits for them, and re-layouts  3.03 us (2%)
  matrix products  2.66 us (2%)
    all_to_all x1, blocking collectives, exchange(): lax.all_to_all(shaped, ('exp', 'tile'), split_axis=0, concat_axis=0, tile...  34.5 us
    all_to_all x2, waiting for transfers between devices, exchange(): lax.all_to_all(shaped, ('exp', 'tile'), split_axis=0, concat_axis=0, tile...  25.3 us
    pallas_call x1, Pallas kernels, slot_sums(): pl.pallas_call(slots_kernel, out_shape=(shape, shape), in_specs=[ANY, SME...  18 us
    pallas_call x1, Pallas kernels, forward(): pl.pallas_call(forward_kernel, out_shape=jax.ShapeDtypeStruct((lines, BLO...  13.8 us
    all_to_all x2, starting transfers between devices, exchange(): lax.all_to_all(shaped, ('exp', 'tile'), split_axis=0, concat_axis=0, tile...  13.1 us
    ppermute x2, starting transfers between devices, swap_rims(): lax.ppermute(top, 'tile', backward)  9.31 us
    pallas_call x1, Pallas kernels, subtract_inner(): pl.pallas_call(inner_kernel, out_shape=jax.ShapeDtypeStruct((tile_rows, w...  8.85 us
    pallas_call x1, Pallas kernels, unwarp(): pl.pallas_call(unwarp_kernel, out_shape=(jax.ShapeDtypeStruct((tile_rows,...  8.68 us
  transfers between devices with their start and end apart: 6, of which 3 were waited for; matrix products, arithmetic and copies ran while one was open for 3% of the time, Pallas kernels for 14%

profile of v9, /device:TPU:8, one launch (start us, length us, event | category | flops | bytes accessed | tf_op | source)
XLA Modules:
  0.0 160.0 jit_solution(11181698213475535543)
XLA Ops:
  0.6 1.0 slice_bitcast_fusion
  1.6 4.6 %collective-permute-start.1 = (bf16[16,4096]{1,0:T(8,128)(2,1)S(1)}, bf16[16,4096]{1,0:T(8,128)(2,1)S(1)}, u32[]{:S(2)}, u32[]{:S(2)}) collective-permute-start(bf16[16,4096]{1,0:T(8,128)(2,1)S(1)} %get-tuple-element.24), channel_id=1, source_target_pairs={{1,0},{2,1},{3,2},{4,3},{5,4},{6,5},{7,6},{8,7},{9,8},{10,9},{11,1... | collective-permute-start | bytes 393224 | tf_op jit(solution)/shard_map/ppermute | solution.py:82
  6.2 1.9 %collective-permute-start = (bf16[16,4096]{1,0:T(8,128)(2,1)S(1)}, bf16[16,4096]{1,0:T(8,128)(2,1)S(1)}, u32[]{:S(2)}, u32[]{:S(2)}) collective-permute-start(bf16[16,4096]{1,0:T(8,128)(2,1)S(1)} %get-tuple-element.25), channel_id=1, source_target_pairs={{0,1},{1,2},{2,3},{3,4},{4,5},{5,6},{6,7},{7,8},{8,9},{9,10},{10,1... | collective-permute-start | bytes 393224 | tf_op jit(solution)/shard_map/ppermute | solution.py:82
  8.1 2.5 %bands.1 = (bf16[384,160]{1,0:T(8,128)(2,1)}, bf16[1152,256]{1,0:T(8,128)(2,1)}) custom-call(bf16[3,21]{1,0:T(4,128)(2,1)} %row_taps_ref.1, bf16[3,21]{1,0:T(4,128)(2,1)} %column_taps_ref.1), custom_call_target="tpu_custom_call" | custom-call | tf_op jit(solution)/shard_map/bands/pallas_call | solution.py:65
  10.7 0.0 collective-permute-done.1.below_ref
  10.7 0.0 copy-start.12
  10.7 4.5 %collective-permute-done.above_ref = bf16[16,4096]{1,0:T(8,128)(2,1)S(1)} collective-permute-done((bf16[16,4096]{1,0:T(8,128)(2,1)S(1)}, bf16[16,4096]{1,0:T(8,128)(2,1)S(1)}, u32[]{:S(2)}, u32[]{:S(2)}) %collective-permute-start) | collective-permute-done | bytes 131104 | tf_op jit(solution)/shard_map/ppermute | solution.py:82
  15.2 0.0 copy-start.13
  15.2 0.0 copy-done.12
  15.2 0.7 copy-done.13
  15.8 13.8 %match_warp.1 = bf16[8192,128]{1,0:T(8,128)(2,1)} custom-call(s32[128,64]{1,0:T(8,128)} %bitcast.96, f32[8,16]{1,0:T(8,128)} %weight_ref.1, f32[1,3]{1,0:T(1,128)} %coef_ref.5, bf16[16,4096]{1,0:T(8,128)(2,1)} %copy-done.13, bf16[256,4096]{1,0:T(8,128)(2,1)} %bitcast.81, bf16[16,4096]{1,0:T(8,128)(2,1)} %copy-done.12, ...), custom_call_target="tpu_custom_call" | custom-call | tf_op jit(solution)/shard_map/match_warp/pallas_call | solution.py:321
  29.7 0.0 copy-start.14
  29.7 0.0 copy-start.10
  29.7 0.0 copy-start.11
  29.7 8.1 %all-to-all-start = ((bf16[128,64,128]{2,1,0:T(8,128)(2,1)}), bf16[128,64,128]{2,1,0:T(8,128)(2,1)S(1)}, u32[]{:S(2)}, u32[]{:S(2)}) async-start(bf16[128,64,128]{2,1,0:T(8,128)(2,1)} %bitcast.95), calls=%async_computation | async-start | bytes 4194304 | tf_op jit(solution)/shard_map/all_to_all | solution.py:758
  37.8 0.0 copy-done.14
  37.8 0.1 reshape.107
  37.9 0.0 copy-done.10
  37.9 0.1 eq.190
  38.0 0.0 copy-done.11
  38.0 0.1 eq.194
  38.0 0.1 broadcast_in_dim.45
  38.1 0.1 broadcast_in_dim.46
  38.2 2.7 %fusion.8.scale_ref = f32[128,64]{1,0:T(8,128)S(1)} fusion(f32[8192]{0:T(1024)S(1)} %broadcast_in_dim.46, s32[8192]{0:T(1024)S(1)} %eq.190, s32[8192]{0:T(1024)S(1)} %eq.194), kind=kOutput, calls=%fused_computation.9 | convolution fusion | flops 807944192 | bytes 131072 | tf_op jit(solution)/shard_map/dot_general | solution.py:806
  40.9 0.1 reshape.114
  41.0 0.1 copy.40
  41.1 0.8 gather_fusion
  41.8 0.0 copy-start.9
  41.9 0.1 select_reduce_fusion
  42.0 25.3 %all-to-all-done = bf16[128,64,128]{2,1,0:T(8,128)(2,1)S(1)} async-done(((bf16[128,64,128]{2,1,0:T(8,128)(2,1)}), bf16[128,64,128]{2,1,0:T(8,128)(2,1)S(1)}, u32[]{:S(2)}, u32[]{:S(2)}) %all-to-all-start) | async-done | bytes 2097184 | tf_op jit(solution)/shard_map/all_to_all | solution.py:758
  67.3 18.0 %slot_sums.1 = (bf16[8192,128]{1,0:T(8,128)(2,1)S(1)}, bf16[8192,128]{1,0:T(8,128)(2,1)S(1)}) custom-call(s32[64,1,128]{2,1,0:T(1,128)S(1)} %bitcast.89, s32[1,128]{1,0:T(1,128)S(1)} %bitcast.92, bf16[8192,128]{1,0:T(8,128)(2,1)S(1)} %bitcast.84, f32[1,64]{1,0:T(1,128)S(1)} %bitcast.90), custom_call_target="tpu_custom_call" | custom-call | tf_op jit(solution)/shard_map/slot_sums/pallas_call | solution.py:431
  85.3 0.0 copy-start.2
  85.3 34.5 %all_to_all.15 = bf16[128,64,128]{2,1,0:T(8,128)(2,1)} all-to-all(bf16[128,64,128]{2,1,0:T(8,128)(2,1)S(1)} %bitcast.87), channel_id=1, replica_groups=mesh['exp'=8,'tile'=16] {'exp','tile'}, dimensions={0} | all-to-all | bytes 4194304 | tf_op jit(solution)/shard_map/all_to_all | solution.py:758
  119.8 0.0 copy-done.9
  119.8 0.0 copy-done.2
  119.8 5.0 %all-to-all-start.1 = ((bf16[128,64,128]{2,1,0:T(8,128)(2,1)}), bf16[128,64,128]{2,1,0:T(8,128)(2,1)S(1)}, u32[]{:S(2)}, u32[]{:S(2)}) async-start(bf16[128,64,128]{2,1,0:T(8,128)(2,1)} %bitcast.86), calls=%async_computation.1 | async-start | bytes 4194304 | tf_op jit(solution)/shard_map/all_to_all | solution.py:758
  124.8 8.7 %unwarp.1 = (bf16[256,4096]{1,0:T(8,128)(2,1)}, bf16[16,4096]{1,0:T(8,128)(2,1)}, bf16[16,4096]{1,0:T(8,128)(2,1)}, bf16[16,4096]{1,0:T(8,128)(2,1)}, bf16[16,4096]{1,0:T(8,128)(2,1)}) custom-call(s32[128,64]{1,0:T(8,128)} %bitcast.97, f32[1,64]{1,0:T(1,128)} %bitcast.91, bf16[8192,128]{1,0:T(8,128)(2,1)} %bitcast.94, bf16[64,128,128]{2,1,0:T(8,128)(2,1)} %bank_rows_ref.3, ...), custom_call_target="tpu_custom_call" | custom-call | tf_op jit(solution)/shard_map/unwarp/pallas_call | solution.py:527
  133.5 3.4 %collective-permute-start.2 = (bf16[16,4096]{1,0:T(8,128)(2,1)}, bf16[16,4096]{1,0:T(8,128)(2,1)S(1)}, u32[]{:S(2)}, u32[]{:S(2)}) collective-permute-start(bf16[16,4096]{1,0:T(8,128)(2,1)} %get-tuple-element.17.bottom_ref), channel_id=1, source_target_pairs={{0,1},{1,2},{2,3},{3,4},{4,5},{5,6},{6,7},{7,8},{8,9},{9,10},{10,1... | collective-permute-start | bytes 393224 | tf_op jit(solution)/shard_map/ppermute | solution.py:82
  136.8 4.8 %collective-permute-start.3 = (bf16[16,4096]{1,0:T(8,128)(2,1)}, bf16[16,4096]{1,0:T(8,128)(2,1)S(1)}, u32[]{:S(2)}, u32[]{:S(2)}) collective-permute-start(bf16[16,4096]{1,0:T(8,128)(2,1)} %get-tuple-element.18.top_ref), channel_id=1, source_target_pairs={{1,0},{2,1},{3,2},{4,3},{5,4},{6,5},{7,6},{8,7},{9,8},{10,9},{11,1... | collective-permute-start | bytes 393224 | tf_op jit(solution)/shard_map/ppermute | solution.py:82
  141.6 0.0 copy-start
  141.6 0.0 copy-start.1
  141.6 0.0 copy-start.3
  141.6 0.0 copy-start.4
  141.6 0.0 copy-start.5
  141.7 0.0 copy-start.6
  141.7 0.0 copy-start.7
  141.7 0.0 copy-start.8
  141.7 8.8 %subtract_inner.1.partial_hbm = f32[256,4096]{1,0:T(8,128)} custom-call(f32[1,3]{1,0:T(1,128)} %coef_ref.5, bf16[256,4096]{1,0:T(8,128)(2,1)} %get-tuple-element.21.image_hbm, bf16[256,4096]{1,0:T(8,128)(2,1)} %bitcast.82, bf16[384,160]{1,0:T(8,128)(2,1)} %get-tuple-element.13.rows_ref, bf16[1152,256]{1,0:T(8,128)(2,1)} %get-tuple-element.14.columns_ref), custom_call_target="tpu_custom_call" | custom-call | tf_op jit(solution)/shard_map/subtract_inner/pallas_call | solution.py:604
  150.5 2.5 %collective-permute-done.2.above_ref = bf16[16,4096]{1,0:T(8,128)(2,1)S(1)} collective-permute-done((bf16[16,4096]{1,0:T(8,128)(2,1)}, bf16[16,4096]{1,0:T(8,128)(2,1)S(1)}, u32[]{:S(2)}, u32[]{:S(2)}) %collective-permute-start.2) | collective-permute-done | bytes 131104 | tf_op jit(solution)/shard_map/ppermute | solution.py:82
  153.0 0.0 collective-permute-done.3.below_ref
  153.0 0.0 copy-done
  153.0 0.0 copy-done.1
  153.0 0.0 copy-done.3
  153.0 0.0 copy-done.4
  153.1 0.0 copy-done.5
  153.1 0.0 copy-done.6
  153.1 0.0 copy-done.7
  153.1 0.0 copy-done.8
  153.1 2.6 %subtract_outer.1 = (f32[256,4096]{1,0:T(8,128)}, f32[8,128]{1,0:T(8,128)S(1)}) custom-call(f32[1,3]{1,0:T(1,128)S(1)} %copy-done.8, bf16[16,4096]{1,0:T(8,128)(2,1)S(1)} %collective-permute-done.2.above_ref, bf16[16,4096]{1,0:T(8,128)(2,1)S(1)} %copy-done.4, bf16[16,4096]{1,0:T(8,128)(2,1)S(1)} %copy-done.5, ...), custom_call_target="tpu_custom_call", output_to_operand_aliasing={{0}: (10, {})} | custom-call | tf_op jit(solution)/shard_map/subtract_outer/pallas_call | solution.py:687
  155.7 0.0 all-to-all-done.1
  155.7 4.2 %patch.1 = f32[1024,1024]{1,0:T(8,128)} custom-call(f32[128,64]{1,0:T(8,128)S(1)} %fusion.8.scale_ref, bf16[8192,128]{1,0:T(8,128)(2,1)S(1)} %bitcast.85, f32[8,128]{1,0:T(8,128)S(1)} %get-tuple-element.22.order_ref), custom_call_target="tpu_custom_call" | custom-call | tf_op jit(solution)/shard_map/patch/pallas_call | solution.py:741
  (5 shorter events, 0.1 us)
Async XLA Ops:
  1.6 9.0 %collective-permute-start.1 = (bf16[16,4096]{1,0:T(8,128)(2,1)S(1)}, bf16[16,4096]{1,0:T(8,128)(2,1)S(1)}, u32[]{:S(2)}, u32[]{:S(2)}) collective-permute-start(bf16[16,4096]{1,0:T(8,128)(2,1)S(1)} %get-tuple-element.24), channel_id=1, source_target_pairs={{1,0},{2,1},{3,2},{4,3},{5,4},{6,5},{7,6},{8,7},{9,8},{10,9},{11,1... | collective-permute-start | bytes 393224 | tf_op jit(solution)/shard_map/ppermute | solution.py:82
  6.2 9.0 %collective-permute-start = (bf16[16,4096]{1,0:T(8,128)(2,1)S(1)}, bf16[16,4096]{1,0:T(8,128)(2,1)S(1)}, u32[]{:S(2)}, u32[]{:S(2)}) collective-permute-start(bf16[16,4096]{1,0:T(8,128)(2,1)S(1)} %get-tuple-element.25), channel_id=1, source_target_pairs={{0,1},{1,2},{2,3},{3,4},{4,5},{5,6},{6,7},{7,8},{8,9},{9,10},{10,1... | collective-permute-start | bytes 393224 | tf_op jit(solution)/shard_map/ppermute | solution.py:82
  10.7 4.5 %copy-start.12 = (bf16[16,4096]{1,0:T(8,128)(2,1)}, bf16[16,4096]{1,0:T(8,128)(2,1)S(1)}, u32[]{:S(2)}) copy-start(bf16[16,4096]{1,0:T(8,128)(2,1)S(1)} %collective-permute-done.1.below_ref) | copy-start | bytes 393220
  15.2 0.7 copy-start.13
  29.7 8.2 %copy-start.14 = (f32[8,16]{1,0:T(8,128)S(1)}, f32[8,16]{1,0:T(8,128)}, u32[]{:S(2)}) copy-start(f32[8,16]{1,0:T(8,128)} %weight_ref.1) | copy-start | bytes 1540
  29.7 8.2 %copy-start.10 = (s32[8,16,64]{2,1,0:T(8,128)S(1)}, s32[8,16,64]{2,1,0:T(8,128)}, u32[]{:S(2)}) copy-start(s32[8,16,64]{2,1,0:T(8,128)} %param.17) | copy-start | bytes 98308
  29.7 8.3 %copy-start.11 = (s32[8,16,64]{2,1,0:T(8,128)S(1)}, s32[8,16,64]{2,1,0:T(8,128)}, u32[]{:S(2)}) copy-start(s32[8,16,64]{2,1,0:T(8,128)} %param.18) | copy-start | bytes 98308
  29.7 37.6 %all-to-all-start = ((bf16[128,64,128]{2,1,0:T(8,128)(2,1)}), bf16[128,64,128]{2,1,0:T(8,128)(2,1)S(1)}, u32[]{:S(2)}, u32[]{:S(2)}) async-start(bf16[128,64,128]{2,1,0:T(8,128)(2,1)} %bitcast.95), calls=%async_computation | async-start | bytes 4194304 | tf_op jit(solution)/shard_map/all_to_all | solution.py:758
  41.8 77.9 %copy-start.9 = (f32[64]{0:T(128)}, f32[64]{0:T(128)S(1)}, u32[]{:S(2)}) copy-start(f32[64]{0:T(128)S(1)} %gather_fusion) | copy-start | bytes 772
  85.3 34.5 %copy-start.2 = (bf16[8192,128]{1,0:T(8,128)(2,1)}, bf16[8192,128]{1,0:T(8,128)(2,1)S(1)}, u32[]{:S(2)}) copy-start(bf16[8192,128]{1,0:T(8,128)(2,1)S(1)} %get-tuple-element.15) | copy-start | bytes 6291460
  119.8 35.9 %all-to-all-start.1 = ((bf16[128,64,128]{2,1,0:T(8,128)(2,1)}), bf16[128,64,128]{2,1,0:T(8,128)(2,1)S(1)}, u32[]{:S(2)}, u32[]{:S(2)}) async-start(bf16[128,64,128]{2,1,0:T(8,128)(2,1)} %bitcast.86), calls=%async_computation.1 | async-start | bytes 4194304 | tf_op jit(solution)/shard_map/all_to_all | solution.py:758
  133.5 19.6 %collective-permute-start.2 = (bf16[16,4096]{1,0:T(8,128)(2,1)}, bf16[16,4096]{1,0:T(8,128)(2,1)S(1)}, u32[]{:S(2)}, u32[]{:S(2)}) collective-permute-start(bf16[16,4096]{1,0:T(8,128)(2,1)} %get-tuple-element.17.bottom_ref), channel_id=1, source_target_pairs={{0,1},{1,2},{2,3},{3,4},{4,5},{5,6},{6,7},{7,8},{8,9},{9,10},{10,1... | collective-permute-start | bytes 393224 | tf_op jit(solution)/shard_map/ppermute | solution.py:82
  136.8 16.2 %collective-permute-start.3 = (bf16[16,4096]{1,0:T(8,128)(2,1)}, bf16[16,4096]{1,0:T(8,128)(2,1)S(1)}, u32[]{:S(2)}, u32[]{:S(2)}) collective-permute-start(bf16[16,4096]{1,0:T(8,128)(2,1)} %get-tuple-element.18.top_ref), channel_id=1, source_target_pairs={{1,0},{2,1},{3,2},{4,3},{5,4},{6,5},{7,6},{8,7},{9,8},{10,9},{11,1... | collective-permute-start | bytes 393224 | tf_op jit(solution)/shard_map/ppermute | solution.py:82
  141.6 11.4 %copy-start = (bf16[1,256,4096]{2,1,0:T(8,128)(2,1)S(1)}, bf16[1,256,4096]{2,1,0:T(8,128)(2,1)}, u32[]{:S(2)}) copy-start(bf16[1,256,4096]{2,1,0:T(8,128)(2,1)} %param.10) | copy-start | bytes 6291460
  141.6 11.4 %copy-start.1 = (bf16[1152,256]{1,0:T(8,128)(2,1)S(1)}, bf16[1152,256]{1,0:T(8,128)(2,1)}, u32[]{:S(2)}) copy-start(bf16[1152,256]{1,0:T(8,128)(2,1)} %get-tuple-element.14.columns_ref) | copy-start | bytes 1769476
  141.6 11.4 %copy-start.3 = (bf16[384,160]{1,0:T(8,128)(2,1)S(1)}, bf16[384,160]{1,0:T(8,128)(2,1)}, u32[]{:S(2)}) copy-start(bf16[384,160]{1,0:T(8,128)(2,1)} %get-tuple-element.13.rows_ref) | copy-start | bytes 368644
  141.6 11.4 %copy-start.4 = (bf16[16,4096]{1,0:T(8,128)(2,1)S(1)}, bf16[16,4096]{1,0:T(8,128)(2,1)}, u32[]{:S(2)}) copy-start(bf16[16,4096]{1,0:T(8,128)(2,1)} %get-tuple-element.18.top_ref) | copy-start | bytes 393220
  141.6 11.4 %copy-start.5 = (bf16[16,4096]{1,0:T(8,128)(2,1)S(1)}, bf16[16,4096]{1,0:T(8,128)(2,1)}, u32[]{:S(2)}) copy-start(bf16[16,4096]{1,0:T(8,128)(2,1)} %get-tuple-element.19.under_top_ref) | copy-start | bytes 393220
  141.7 11.4 %copy-start.6 = (bf16[16,4096]{1,0:T(8,128)(2,1)S(1)}, bf16[16,4096]{1,0:T(8,128)(2,1)}, u32[]{:S(2)}) copy-start(bf16[16,4096]{1,0:T(8,128)(2,1)} %get-tuple-element.20.over_bottom_ref) | copy-start | bytes 393220
  141.7 11.4 %copy-start.7 = (bf16[16,4096]{1,0:T(8,128)(2,1)S(1)}, bf16[16,4096]{1,0:T(8,128)(2,1)}, u32[]{:S(2)}) copy-start(bf16[16,4096]{1,0:T(8,128)(2,1)} %get-tuple-element.17.bottom_ref) | copy-start | bytes 393220
  141.7 11.4 %copy-start.8 = (f32[1,3]{1,0:T(1,128)S(1)}, f32[1,3]{1,0:T(1,128)}, u32[]{:S(2)}) copy-start(f32[1,3]{1,0:T(1,128)} %coef_ref.5) | copy-start | bytes 40
